TPU v7x, 32 devices: a whole 2x2x4 slice. The times are simulated.
32 devices in a mesh: group: 4 (over y, core), fsdp: 8 (over z, x).
Axes of the slice: x: 2, y: 2, z: 4, core: 2. Of those that a mesh axis runs over, the one named last changes fastest.
Arguments:
- tokens: bfloat16 [16384, 768], P(('group', 'fsdp')), may hold values from -6 to 6
- cotangent: bfloat16 [16384, 768], P(('group', 'fsdp')), may hold values from -6 to 6
- parent_seg: int32 [4, 16], P('group'), may hold values from -1 to 15, as said below
- w_qkv: bfloat16 [768, 2304], P(('group', 'fsdp')), may hold values from -0.21875 to 0.21875
- w_out: bfloat16 [768, 768], P(('group', 'fsdp')), may hold values from -3 to 3
- b_out: bfloat16 [768], P(('group', 'fsdp')), may hold values from -4 to 4
- norm1_gain: bfloat16 [768], P(('group', 'fsdp')), may hold values from 0.5 to 1.5
- norm1_bias: bfloat16 [768], P(('group', 'fsdp')), may hold values from -4 to 4
- w_up: bfloat16 [768, 3072], P(('group', 'fsdp')), may hold values from -0.21875 to 0.21875
- b_up: bfloat16 [3072], P(('group', 'fsdp')), may hold values from -4 to 4
- w_down: bfloat16 [3072, 768], P(('group', 'fsdp')), may hold values from -0.109375 to 0.109375
- b_down: bfloat16 [768], P(('group', 'fsdp')), may hold values from -4 to 4
- norm2_gain: bfloat16 [768], P(('group', 'fsdp')), may hold values from 0.5 to 1.5
- norm2_bias: bfloat16 [768], P(('group', 'fsdp')), may hold values from -4 to 4
Outputs:
- output: bfloat16 [16384, 768], P(('group', 'fsdp'))
- tokens_grad: float32 [16384, 768], P(('group', 'fsdp'))
- w_qkv_grad: float32 [768, 2304], P('fsdp')
- w_out_grad: float32 [768, 768], P('fsdp')
- b_out_grad: float32 [768], P('fsdp')
- norm1_gain_grad: float32 [768], P('fsdp')
- norm1_bias_grad: float32 [768], P('fsdp')
- w_up_grad: float32 [768, 3072], P('fsdp')
- b_up_grad: float32 [3072], P('fsdp')
- w_down_grad: float32 [3072, 768], P('fsdp')
- b_down_grad: float32 [768], P('fsdp')
- norm2_gain_grad: float32 [768], P('fsdp')
- norm2_bias_grad: float32 [768], P('fsdp')
Inputs may be any that keep to these rules, and one draw needn't show every extreme that they name: parent_seg[g, p] is the position within group row g of the segment whose end state seeds segment p, or -1 for a root. Each row is a forest of trees of 20 segments placed in random positions: a trunk chain of 8, four branches off the trunk's last segment, and two leaves on each branch; where 16 is not a multiple of 20, the row's last tree keeps only its first segments. Following parents reaches a root after at most 9 steps, which some segment of every row needs.
All inputs are finite; a program needn't handle non-finite values.
Results may differ from a plain program's by a relative error of at most 0.018.
Values may be sent and summed in bfloat16 or wider, within the bound.
No kernel may reach another device: no remote copies, remote signals or barrier semaphores. Data moves between devices by JAX's collectives and lax.ppermute only.
A program may use at most 128 MiB of HBM per device.

v0:
```python
from functools import partial
import math

import jax
import jax.numpy as jnp
from jax import lax
from jax.sharding import PartitionSpec as P

D = 768
H = 12
HD = 64
SEG = 256
TREE_DEPTH = 10
HORIZON = 2560


ln_epsilon = 1e-05
highest = lax.Precision.HIGHEST


def ancestor_rows(parents, first_block, blocks):
    row_count = parents.shape[0]
    columns = jnp.arange(row_count, dtype=jnp.int32)
    step_one = (parents[:, None] == columns[None, :]).astype(jnp.float32)
    own_rows = first_block + jnp.arange(blocks, dtype=jnp.int32)
    current = (own_rows[:, None] == columns[None, :]).astype(jnp.float32)
    reached = jnp.zeros((blocks, row_count), jnp.float32)
    for depth_step in range(TREE_DEPTH):
        current = jnp.dot(current, step_one, precision=highest)
        reached = reached + current
    return reached


def norm_forward(resid, gain, shift):
    centred = resid - jnp.mean(resid, axis=-1, keepdims=True)
    inv_std = lax.rsqrt(jnp.mean(centred * centred, axis=-1, keepdims=True) + ln_epsilon)
    norm_hat = centred * inv_std
    return (norm_hat * gain + shift, norm_hat, inv_std)


def norm_backward(grad_out, gain, norm_hat, inv_std):
    d_hat = grad_out * gain
    d_resid = inv_std * (
        d_hat
        - jnp.mean(d_hat, axis=-1, keepdims=True)
        - norm_hat * jnp.mean(d_hat * norm_hat, axis=-1, keepdims=True)
    )
    return (d_resid, jnp.sum(grad_out * norm_hat, axis=0), jnp.sum(grad_out, axis=0))


def body(
    tokens,
    cotangent,
    parent_seg,
    w_qkv,
    w_out,
    b_out,
    norm1_gain,
    norm1_bias,
    w_up,
    b_up,
    w_down,
    b_down,
    norm2_gain,
    norm2_bias,
):
    gathered = (
        lax.all_gather(w_qkv, ("group", "fsdp"), axis=0, tiled=True),
        lax.all_gather(w_out, ("group", "fsdp"), axis=0, tiled=True),
        lax.all_gather(w_up, ("group", "fsdp"), axis=0, tiled=True),
        lax.all_gather(w_down, ("group", "fsdp"), axis=0, tiled=True),
        lax.all_gather(b_out, ("group", "fsdp"), axis=0, tiled=True),
        lax.all_gather(b_up, ("group", "fsdp"), axis=0, tiled=True),
        lax.all_gather(b_down, ("group", "fsdp"), axis=0, tiled=True),
        lax.all_gather(norm1_gain, ("group", "fsdp"), axis=0, tiled=True),
        lax.all_gather(norm1_bias, ("group", "fsdp"), axis=0, tiled=True),
        lax.all_gather(norm2_gain, ("group", "fsdp"), axis=0, tiled=True),
        lax.all_gather(norm2_bias, ("group", "fsdp"), axis=0, tiled=True),
    )
    qkv_full, out_full, up_full, down_full = (gathered[0], gathered[1], gathered[2], gathered[3])
    out_bias = gathered[4].astype(jnp.float32)
    up_bias = gathered[5].astype(jnp.float32)
    down_bias = gathered[6].astype(jnp.float32)
    gain_one = gathered[7].astype(jnp.float32)
    shift_one = gathered[8].astype(jnp.float32)
    gain_two = gathered[9].astype(jnp.float32)
    shift_two = gathered[10].astype(jnp.float32)
    row_total = tokens.shape[0]
    blocks = row_total // SEG
    ancestry = ancestor_rows(parent_seg[0], lax.axis_index("fsdp") * blocks, blocks)
    depths = jnp.sum(ancestry, axis=1)
    angles = (depths[:, None] * SEG + jnp.arange(SEG, dtype=jnp.float32)[None, :]) * (
        math.pi / (2.0 * HORIZON)
    )
    cos_col = jnp.cos(angles)[:, :, None, None]
    sin_col = jnp.sin(angles)[:, :, None, None]
    projected = jnp.dot(tokens, qkv_full, preferred_element_type=jnp.float32)
    query_pre = projected[:, :D].reshape(blocks, SEG, H, HD)
    key_pre = projected[:, D : 2 * D].reshape(blocks, SEG, H, HD)
    value_act = projected[:, 2 * D :].astype(jnp.bfloat16).reshape(blocks, SEG, H, HD)
    query_act = jax.nn.relu(query_pre)
    key_act = jax.nn.relu(key_pre)
    query_feat = jnp.concatenate([query_act * cos_col, query_act * sin_col], axis=-1).astype(
        jnp.bfloat16
    )
    key_feat = jnp.concatenate([key_act * cos_col, key_act * sin_col], axis=-1).astype(jnp.bfloat16)
    incr_state = jnp.einsum(
        "bshf,bshe->bhfe", key_feat, value_act, preferred_element_type=jnp.float32
    )
    incr_norm = jnp.sum(key_feat, axis=1, dtype=jnp.float32)
    state_width = H * 2 * HD * HD
    norm_width = H * 2 * HD
    columns = ancestry.astype(jnp.bfloat16)
    path_state = jnp.dot(
        columns,
        lax.all_gather(
            incr_state.astype(jnp.bfloat16).reshape(blocks, state_width), "fsdp", axis=0, tiled=True
        ),
        preferred_element_type=jnp.float32,
    )
    path_norm = jnp.dot(
        columns,
        lax.all_gather(
            incr_norm.astype(jnp.bfloat16).reshape(blocks, norm_width), "fsdp", axis=0, tiled=True
        ),
        preferred_element_type=jnp.float32,
    )
    state_low = path_state.astype(jnp.bfloat16).reshape(blocks, H, 2 * HD, HD)
    norm_low = path_norm.astype(jnp.bfloat16).reshape(blocks, H, 2 * HD)
    positions = jnp.arange(SEG, dtype=jnp.int32)
    causal = positions[:, None] >= positions[None, :]
    scores = jnp.where(
        causal,
        jnp.einsum("bshf,bthf->bhst", query_feat, key_feat, preferred_element_type=jnp.float32),
        0.0,
    )
    scores_low = scores.astype(jnp.bfloat16)
    numerator = jnp.einsum(
        "bhst,bthe->bshe", scores_low, value_act, preferred_element_type=jnp.float32
    )
    numerator = numerator + jnp.einsum(
        "bshf,bhfe->bshe", query_feat, state_low, preferred_element_type=jnp.float32
    )
    denominator = (
        jnp.transpose(jnp.sum(scores, axis=-1), (0, 2, 1))
        + jnp.einsum("bshf,bhf->bsh", query_feat, norm_low, preferred_element_type=jnp.float32)
        + 1.0
    )
    attended = numerator / denominator[..., None]
    att_low = attended.reshape(row_total, D).astype(jnp.bfloat16)
    mixed_out = jnp.dot(att_low, out_full, preferred_element_type=jnp.float32) + out_bias
    normed, hat_one, inv_one = norm_forward(
        tokens.astype(jnp.float32) + mixed_out, gain_one, shift_one
    )
    normed_low = normed.astype(jnp.bfloat16)
    upper_pre = jnp.dot(normed_low, up_full, preferred_element_type=jnp.float32) + up_bias
    gelu_out, gelu_pull = jax.vjp(partial(jax.nn.gelu, approximate=False), upper_pre)
    gelu_low = gelu_out.astype(jnp.bfloat16)
    lowered = jnp.dot(gelu_low, down_full, preferred_element_type=jnp.float32) + down_bias
    result, hat_two, inv_two = norm_forward(normed + lowered, gain_two, shift_two)
    output = result.astype(jnp.bfloat16)
    again = (
        lax.all_gather(w_qkv, ("group", "fsdp"), axis=0, tiled=True),
        lax.all_gather(w_out, ("group", "fsdp"), axis=0, tiled=True),
        lax.all_gather(w_up, ("group", "fsdp"), axis=0, tiled=True),
        lax.all_gather(w_down, ("group", "fsdp"), axis=0, tiled=True),
        lax.all_gather(b_out, ("group", "fsdp"), axis=0, tiled=True),
        lax.all_gather(b_up, ("group", "fsdp"), axis=0, tiled=True),
        lax.all_gather(b_down, ("group", "fsdp"), axis=0, tiled=True),
        lax.all_gather(norm1_gain, ("group", "fsdp"), axis=0, tiled=True),
        lax.all_gather(norm1_bias, ("group", "fsdp"), axis=0, tiled=True),
        lax.all_gather(norm2_gain, ("group", "fsdp"), axis=0, tiled=True),
        lax.all_gather(norm2_bias, ("group", "fsdp"), axis=0, tiled=True),
    )
    qkv_back, out_back, up_back, down_back = (again[0], again[1], again[2], again[3])
    gain_one_back = again[7].astype(jnp.float32)
    gain_two_back = again[9].astype(jnp.float32)
    d_resid2, norm2_gain_grad, norm2_bias_grad = norm_backward(
        cotangent.astype(jnp.float32), gain_two_back, hat_two, inv_two
    )
    d_lower = d_resid2.astype(jnp.bfloat16)
    w_down_grad = jnp.einsum("rf,rd->fd", gelu_low, d_lower, preferred_element_type=jnp.float32)
    b_down_grad = jnp.sum(d_lower, axis=0, dtype=jnp.float32)
    d_gelu = jnp.einsum("rd,fd->rf", d_lower, down_back, preferred_element_type=jnp.float32)
    d_upper = gelu_pull(d_gelu)[0].astype(jnp.bfloat16)
    w_up_grad = jnp.einsum("rd,rf->df", normed_low, d_upper, preferred_element_type=jnp.float32)
    b_up_grad = jnp.sum(d_upper, axis=0, dtype=jnp.float32)
    d_normed = d_resid2 + jnp.einsum(
        "rf,df->rd", d_upper, up_back, preferred_element_type=jnp.float32
    )
    d_resid1, norm1_gain_grad, norm1_bias_grad = norm_backward(
        d_normed, gain_one_back, hat_one, inv_one
    )
    d_mixed = d_resid1.astype(jnp.bfloat16)
    w_out_grad = jnp.einsum("rd,re->de", att_low, d_mixed, preferred_element_type=jnp.float32)
    b_out_grad = jnp.sum(d_mixed, axis=0, dtype=jnp.float32)
    d_att = jnp.einsum("re,de->rd", d_mixed, out_back, preferred_element_type=jnp.float32).reshape(
        blocks, SEG, H, HD
    )
    d_numer = (d_att / denominator[..., None]).astype(jnp.bfloat16)
    d_denom = -jnp.sum(d_att * attended, axis=-1) / denominator
    d_scores = (
        jnp.einsum("bshe,bthe->bhst", d_numer, value_act, preferred_element_type=jnp.float32)
        + jnp.transpose(d_denom, (0, 2, 1))[..., None]
    )
    d_scores_low = jnp.where(causal, d_scores, 0.0).astype(jnp.bfloat16)
    d_value = jnp.einsum("bhst,bshe->bthe", scores_low, d_numer, preferred_element_type=jnp.float32)
    d_query = jnp.einsum("bshe,bhfe->bshf", d_numer, state_low, preferred_element_type=jnp.float32)
    d_query = d_query + d_denom[..., None] * norm_low.astype(jnp.float32)[:, None, :, :]
    d_query = d_query + jnp.einsum(
        "bhst,bthf->bshf", d_scores_low, key_feat, preferred_element_type=jnp.float32
    )
    d_key = jnp.einsum(
        "bhst,bshf->bthf", d_scores_low, query_feat, preferred_element_type=jnp.float32
    )
    d_state = jnp.einsum("bshf,bshe->bhfe", query_feat, d_numer, preferred_element_type=jnp.float32)
    d_norm = jnp.einsum("bsh,bshf->bhf", d_denom, query_feat, preferred_element_type=jnp.float32)
    path_grad = jnp.concatenate(
        [d_state.reshape(blocks, state_width), d_norm.reshape(blocks, norm_width)], axis=1
    ).astype(jnp.bfloat16)
    whole_ancestry = ancestor_rows(parent_seg[0], 0, parent_seg.shape[1])
    own_columns = lax.dynamic_slice_in_dim(
        whole_ancestry, lax.axis_index("fsdp") * blocks, blocks, 1
    ).astype(jnp.bfloat16)
    incoming = jnp.einsum(
        "pc,pw->cw",
        own_columns,
        lax.all_gather(path_grad, "fsdp", axis=0, tiled=True),
        preferred_element_type=jnp.float32,
    )
    d_incr_state = incoming[:, :state_width].astype(jnp.bfloat16).reshape(blocks, H, 2 * HD, HD)
    d_incr_norm = incoming[:, state_width:].reshape(blocks, 1, H, 2 * HD)
    d_key = (
        d_key
        + jnp.einsum("bhfe,bshe->bshf", d_incr_state, value_act, preferred_element_type=jnp.float32)
        + d_incr_norm
    )
    d_value = d_value + jnp.einsum(
        "bshf,bhfe->bshe", key_feat, d_incr_state, preferred_element_type=jnp.float32
    )
    d_query_act = d_query[..., :HD] * cos_col + d_query[..., HD:] * sin_col
    d_key_act = d_key[..., :HD] * cos_col + d_key[..., HD:] * sin_col
    d_projected = jnp.concatenate(
        [
            jnp.where(query_pre > 0, d_query_act, 0.0).reshape(row_total, D),
            jnp.where(key_pre > 0, d_key_act, 0.0).reshape(row_total, D),
            d_value.reshape(row_total, D),
        ],
        axis=1,
    ).astype(jnp.bfloat16)
    w_qkv_grad = jnp.einsum("rd,rc->dc", tokens, d_projected, preferred_element_type=jnp.float32)
    tokens_grad = d_resid1 + jnp.einsum(
        "rc,dc->rd", d_projected, qkv_back, preferred_element_type=jnp.float32
    )
    partial_rows = (
        lax.psum_scatter(
            w_qkv_grad.astype(jnp.bfloat16), "fsdp", scatter_dimension=0, tiled=True
        ).astype(jnp.float32),
        lax.psum_scatter(
            w_out_grad.astype(jnp.bfloat16), "fsdp", scatter_dimension=0, tiled=True
        ).astype(jnp.float32),
        lax.psum_scatter(
            b_out_grad.astype(jnp.bfloat16), "fsdp", scatter_dimension=0, tiled=True
        ).astype(jnp.float32),
        lax.psum_scatter(
            norm1_gain_grad.astype(jnp.bfloat16), "fsdp", scatter_dimension=0, tiled=True
        ).astype(jnp.float32),
        lax.psum_scatter(
            norm1_bias_grad.astype(jnp.bfloat16), "fsdp", scatter_dimension=0, tiled=True
        ).astype(jnp.float32),
        lax.psum_scatter(
            w_up_grad.astype(jnp.bfloat16), "fsdp", scatter_dimension=0, tiled=True
        ).astype(jnp.float32),
        lax.psum_scatter(
            b_up_grad.astype(jnp.bfloat16), "fsdp", scatter_dimension=0, tiled=True
        ).astype(jnp.float32),
        lax.psum_scatter(
            w_down_grad.astype(jnp.bfloat16), "fsdp", scatter_dimension=0, tiled=True
        ).astype(jnp.float32),
        lax.psum_scatter(
            b_down_grad.astype(jnp.bfloat16), "fsdp", scatter_dimension=0, tiled=True
        ).astype(jnp.float32),
        lax.psum_scatter(
            norm2_gain_grad.astype(jnp.bfloat16), "fsdp", scatter_dimension=0, tiled=True
        ).astype(jnp.float32),
        lax.psum_scatter(
            norm2_bias_grad.astype(jnp.bfloat16), "fsdp", scatter_dimension=0, tiled=True
        ).astype(jnp.float32),
    )
    reduced = (
        lax.psum(partial_rows[0].astype(jnp.bfloat16), "group").astype(jnp.float32),
        lax.psum(partial_rows[1].astype(jnp.bfloat16), "group").astype(jnp.float32),
        lax.psum(partial_rows[2].astype(jnp.bfloat16), "group").astype(jnp.float32),
        lax.psum(partial_rows[3].astype(jnp.bfloat16), "group").astype(jnp.float32),
        lax.psum(partial_rows[4].astype(jnp.bfloat16), "group").astype(jnp.float32),
        lax.psum(partial_rows[5].astype(jnp.bfloat16), "group").astype(jnp.float32),
        lax.psum(partial_rows[6].astype(jnp.bfloat16), "group").astype(jnp.float32),
        lax.psum(partial_rows[7].astype(jnp.bfloat16), "group").astype(jnp.float32),
        lax.psum(partial_rows[8].astype(jnp.bfloat16), "group").astype(jnp.float32),
        lax.psum(partial_rows[9].astype(jnp.bfloat16), "group").astype(jnp.float32),
        lax.psum(partial_rows[10].astype(jnp.bfloat16), "group").astype(jnp.float32),
    )
    return (
        output,
        tokens_grad,
        reduced[0],
        reduced[1],
        reduced[2],
        reduced[3],
        reduced[4],
        reduced[5],
        reduced[6],
        reduced[7],
        reduced[8],
        reduced[9],
        reduced[10],
    )


def solution(mesh):
    in_specs = (
        P(("group", "fsdp"), None),
        P(("group", "fsdp"), None),
        P("group", None),
        P(("group", "fsdp"), None),
        P(("group", "fsdp"), None),
        P(("group", "fsdp")),
        P(("group", "fsdp")),
        P(("group", "fsdp")),
        P(("group", "fsdp"), None),
        P(("group", "fsdp")),
        P(("group", "fsdp"), None),
        P(("group", "fsdp")),
        P(("group", "fsdp")),
        P(("group", "fsdp")),
    )
    out_specs = (
        P(("group", "fsdp"), None),
        P(("group", "fsdp"), None),
        P("fsdp", None),
        P("fsdp", None),
        P("fsdp"),
        P("fsdp"),
        P("fsdp"),
        P("fsdp", None),
        P("fsdp"),
        P("fsdp", None),
        P("fsdp"),
        P("fsdp"),
        P("fsdp"),
    )
    return jax.shard_map(body, mesh=mesh, in_specs=in_specs, out_specs=out_specs, check_vma=False)
```

profile of v0, /device:TPU:0, one launch (start us, length us, event | category | flops | bytes accessed | tf_op | source)
XLA Modules:
  0.0 879.1 jit_solution(8862627342162834473)
XLA Ops:
  17.2 56.7 %all-gather.10.cloned.1.call-done = bf16[768,2304]{1,0:T(8,128)(2,1)} async-done(((bf16[24,2304]{1,0:T(8,128)(2,1)}), bf16[768,2304]{1,0:T(8,128)(2,1)}) %all-gather.10.cloned.1.call-update) | async-done | bytes 3538960 | tf_op jit(solution)/shard_map/all_gather | solution.py:68
  73.9 4.3 fusion.113
  78.3 2.0 copy-done.9
  84.9 2.1 max.22
  87.5 2.1 max.24
  89.6 2.8 multiply_convert_fusion.2
  94.4 2.5 reshape.212
  102.3 39.7 %all-reduce.14 = (bf16[768]{0:T(1024)(128)(2,1)S(1)}, bf16[768]{0:T(1024)(128)(2,1)S(1)}, bf16[768]{0:T(1024)(128)(2,1)S(1)}, bf16[3072]{0:T(1024)(128)(2,1)S(1)...) all-reduce(bf16[768]{0:T(1024)(128)(2,1)S(1)} %dynamic-update-slice, ...), channel_id=1, replica_groups=mesh['group'=4,'fsdp'=8] {'group','fsdp'}, use_global_device_ids=true, to_apply=%add | all-reduce | flops 7680 | bytes 30720
  145.5 30.9 %all-gather.1 = bf16[8,2,1536]{2,1,0:T(2,128)(2,1)S(1)} all-gather(bf16[1,2,1536]{2,1,0:T(2,128)(2,1)S(1)} %reshape.214), channel_id=1, replica_groups=mesh['group'=4,'fsdp'=8] {'fsdp'}, dimensions={0}, use_global_device_ids=true | all-gather | bytes 55296 | tf_op jit(solution)/shard_map/all_gather | solution.py:123
  177.0 2.5 select_reduce_fusion
  180.8 2.6 reshape.213
  185.2 2.0 fusion.105
  191.4 21.6 %all-gather.12.cloned.1.call-done = bf16[768,768]{1,0:T(8,128)(2,1)} async-done(((bf16[24,768]{1,0:T(8,128)(2,1)}), bf16[768,768]{1,0:T(8,128)(2,1)}) %all-gather.12.cloned.1.call-update) | async-done | bytes 1179664 | tf_op jit(solution)/shard_map/all_gather | solution.py:69
  213.1 2.7 fusion.110
  216.1 62.5 %all-gather.14.cloned.1.call-done = bf16[768,3072]{1,0:T(8,128)(2,1)} async-done(((bf16[24,3072]{1,0:T(8,128)(2,1)}), bf16[768,3072]{1,0:T(8,128)(2,1)}) %all-gather.14.cloned.1.call-update) | async-done | bytes 4718608 | tf_op jit(solution)/shard_map/all_gather | solution.py:70
  278.5 20.1 %multiply_convert_fusion = (bf16[512,3072]{1,0:T(8,128)(2,1)}, f32[512,3072]{1,0:T(8,128)}, f32[512,3072]{1,0:T(8,128)}) fusion(f32[3072]{0:T(1024)S(1)} %copy-done.52, bf16[768,3072]{1,0:T(8,128)(2,1)} %all-gather.14.cloned.1.call-done, f32[512,768]{1,0:T(8,128)S(1)} %get-tuple-element.128, f32[768]{0:T(1024)S(1)} %copy-done.60, ...), kind=kOutput, calls=%fused_computation.5 | convolution fusion | flops 2521694208 | bytes 22042624 | tf_op jit(solution)/shard_map/dot_general | solution.py:156
  298.6 45.3 %all-gather.16.cloned.1.call-done = bf16[3072,768]{1,0:T(8,128)(2,1)} async-done(((bf16[96,768]{1,0:T(8,128)(2,1)}), bf16[3072,768]{1,0:T(8,128)(2,1)}) %all-gather.16.cloned.1.call-update) | async-done | bytes 4718608 | tf_op jit(solution)/shard_map/all_gather | solution.py:71
  343.9 6.1 fusion.111
  350.4 2.1 fusion.14
  353.8 8.8 fusion.112
  362.5 3.6 multiply_reduce_fusion
  368.5 2.0 fusion.89
  370.5 3.3 reshape.191
  373.8 2.2 multiply_reduce_fusion.1
  383.1 2.3 slice_compare_fusion
  386.7 2.5 copy.166
  390.5 2.5 copy.158
  397.6 2.1 bitcast_add_fusion.1
  399.7 40.0 %all-gather.20.cloned.1.call-done = bf16[8,2,99840]{2,1,0:T(2,128)(2,1)} async-done(((bf16[1,2,99840]{2,1,0:T(2,128)(2,1)}), bf16[8,2,99840]{2,1,0:T(2,128)(2,1)}) %all-gather.20.cloned.1.call-update) | async-done | bytes 3194896 | tf_op jit(solution)/shard_map/all_gather | solution.py:228
  439.7 2.7 reshape.217
  445.4 2.9 fusion.98
  448.3 1.9 fusion.23
  450.3 3.8 fusion.22
  462.7 2.0 fusion.6
  464.7 4.0 copy.197
  470.2 2.9 convolution_convert_fusion.5
  473.2 6.8 convolution_convert_fusion.2
  481.4 6.8 convolution_convert_fusion.1
  488.3 58.4 %reduce-scatter.13.cloned.1.call-done = bf16[96,2304]{1,0:T(8,128)(2,1)} async-done(((bf16[768,2304]{1,0:T(8,128)(2,1)}), bf16[96,2304]{1,0:T(8,128)(2,1)}) %reduce-scatter.13.cloned.1.call-update) | async-done | bytes 442384
  546.7 2.1 copy.198
  548.7 65.4 %reduce-scatter.7.cloned.1.call-done = bf16[96,768]{1,0:T(8,128)(2,1)} async-done(((bf16[768,768]{1,0:T(8,128)(2,1)}), bf16[96,768]{1,0:T(8,128)(2,1)}) %reduce-scatter.7.cloned.1.call-update) | async-done | bytes 147472 | tf_op jit(solution)/shard_map/reduce_scatter | solution.py:259
  614.2 97.9 %reduce-scatter.9.cloned.1.call-done = bf16[96,3072]{1,0:T(8,128)(2,1)} async-done(((bf16[768,3072]{1,0:T(8,128)(2,1)}), bf16[96,3072]{1,0:T(8,128)(2,1)}) %reduce-scatter.9.cloned.1.call-update) | async-done | bytes 589840 | tf_op jit(solution)/shard_map/reduce_scatter | solution.py:271
  712.1 98.5 %reduce-scatter.11.cloned.1.call-done = bf16[384,768]{1,0:T(8,128)(2,1)} async-done(((bf16[3072,768]{1,0:T(8,128)(2,1)}), bf16[384,768]{1,0:T(8,128)(2,1)}) %reduce-scatter.11.cloned.1.call-update) | async-done | bytes 589840 | tf_op jit(solution)/shard_map/reduce_scatter | solution.py:277
  812.6 35.9 %all-reduce.15 = (bf16[768]{0:T(1024)(128)(2,1)S(1)}, bf16[768]{0:T(1024)(128)(2,1)S(1)}, bf16[768]{0:T(1024)(128)(2,1)S(1)}, bf16[3072]{0:T(1024)(128)(2,1)S(1)...) all-reduce(bf16[768]{0:T(1024)(128)(2,1)S(1)} %copy-done.53, ...), channel_id=4, replica_groups=mesh['group'=4,'fsdp'=8] {'fsdp'}, use_global_device_ids=true, to_apply=%region_17.18.clone | all-reduce | flops 7680 | bytes 30720
  849.0 6.4 all-reduce.16
  859.1 5.9 convolution_add_fusion
  865.0 2.3 copy.172
  868.9 2.2 convert_element_type.219
  (316 shorter events, 73.7 us)
Async XLA Ops:
  7.2 66.7 %all-gather.10.cloned.1.call-start = ((), (), s32[]{:S(2)}) async-start(), calls=%async_computation.4 | async-start | bytes 3649536 | tf_op jit(solution)/shard_map/all_gather | solution.py:68
  7.9 172.9 %all-gather.18.cloned.1.call-start = ((), (), s32[]{:S(2)}) async-start(), calls=%async_computation.11 | async-start | bytes 3538944 | tf_op jit(solution)/shard_map/all_gather | solution.py:116
  17.2 72.3 %copy-start.45 = (f32[2,256]{1,0:T(2,128)}, f32[2,256]{1,0:T(2,128)S(1)}, u32[]{:S(2)}) copy-start(f32[2,256]{1,0:T(2,128)S(1)} %get-tuple-element.119) | copy-start | bytes 6148
  17.2 72.3 %copy-start.47 = (f32[2,256]{1,0:T(2,128)}, f32[2,256]{1,0:T(2,128)S(1)}, u32[]{:S(2)}) copy-start(f32[2,256]{1,0:T(2,128)S(1)} %get-tuple-element.120) | copy-start | bytes 6148
  92.4 84.6 %copy-start.5 = (bf16[2,256,12,64]{1,3,2,0:T(8,128)(2,1)}, bf16[2,256,12,64]{1,3,2,0:T(8,128)(2,1)S(1)}, u32[]{:S(2)}) copy-start(bf16[2,256,12,64]{1,3,2,0:T(8,128)(2,1)S(1)} %get-tuple-element.112) | copy-start | bytes 2359300
  92.4 84.5 %copy-start.7 = (bf16[2,256,12,64]{1,3,2,0:T(8,128)(2,1)}, bf16[2,256,12,64]{1,3,2,0:T(8,128)(2,1)S(1)}, u32[]{:S(2)}) copy-start(bf16[2,256,12,64]{1,3,2,0:T(8,128)(2,1)S(1)} %get-tuple-element.113) | copy-start | bytes 2359300
  92.4 84.5 %copy-start.11 = (bf16[2,256,12,64]{1,3,2,0:T(8,128)(2,1)}, bf16[2,256,12,64]{1,3,2,0:T(8,128)(2,1)S(1)}, u32[]{:S(2)}) copy-start(bf16[2,256,12,64]{1,3,2,0:T(8,128)(2,1)S(1)} %get-tuple-element.115) | copy-start | bytes 2359300
  92.4 84.5 %copy-start.14 = (bf16[2,256,12,64]{1,3,2,0:T(8,128)(2,1)}, bf16[2,256,12,64]{1,3,2,0:T(8,128)(2,1)S(1)}, u32[]{:S(2)}) copy-start(bf16[2,256,12,64]{1,3,2,0:T(8,128)(2,1)S(1)} %get-tuple-element.116) | copy-start | bytes 2359300
  92.5 6.4 copy-start.74
  92.5 6.6 copy-start.75
  92.5 6.9 copy-start.76
  92.5 7.1 copy-start.77
  94.4 82.1 %copy-start.64 = (bf16[2,16]{1,0:T(2,128)(2,1)S(1)}, bf16[2,16]{1,0:T(2,128)(2,1)}, u32[]{:S(2)}) copy-start(bf16[2,16]{1,0:T(2,128)(2,1)} %get-tuple-element.122) | copy-start | bytes 196
  96.9 116.2 %all-gather.12.cloned.1.call-start = ((), (), s32[]{:S(2)}) async-start(), calls=%async_computation.5 | async-start | bytes 1216512 | tf_op jit(solution)/shard_map/all_gather | solution.py:69
  97.6 180.9 %all-gather.14.cloned.1.call-start = ((), (), s32[]{:S(2)}) async-start(), calls=%async_computation.6 | async-start | bytes 4866048 | tf_op jit(solution)/shard_map/all_gather | solution.py:70
  98.2 245.7 %all-gather.16.cloned.1.call-start = ((), (), s32[]{:S(2)}) async-start(), calls=%async_computation.7 | async-start | bytes 4866048 | tf_op jit(solution)/shard_map/all_gather | solution.py:71
  98.8 340.9 %all-gather.20.cloned.1.call-start = ((), (), s32[]{:S(2)}) async-start(), calls=%async_computation.12 | async-start | bytes 3594240 | tf_op jit(solution)/shard_map/all_gather | solution.py:228
  142.6 223.5 %copy-start.49 = (f32[768]{0:T(1024)}, f32[768]{0:T(1024)S(1)}, u32[]{:S(2)}) copy-start(f32[768]{0:T(1024)S(1)} %convert_element_type.191) | copy-start | bytes 9220
  145.0 34.5 %copy-start.40 = (pred[256,256]{0,1:T(8,128)(4,1)}, pred[256,256]{0,1:T(8,128)(4,1)S(1)}, u32[]{:S(2)}) copy-start(pred[256,256]{0,1:T(8,128)(4,1)S(1)} %iota_compare_fusion) | copy-start | bytes 196612
  189.5 23.6 %copy-start.63 = (f32[768]{0:T(1024)S(1)}, f32[768]{0:T(1024)}, u32[]{:S(2)}) copy-start(f32[768]{0:T(1024)} %convert_element_type.190) | copy-start | bytes 9220
  213.1 65.5 %copy-start.52 = (f32[3072]{0:T(1024)S(1)}, f32[3072]{0:T(1024)}, u32[]{:S(2)}) copy-start(f32[3072]{0:T(1024)} %convert_element_type.194) | copy-start | bytes 36868
  213.1 65.5 %copy-start.60 = (f32[768]{0:T(1024)S(1)}, f32[768]{0:T(1024)}, u32[]{:S(2)}) copy-start(f32[768]{0:T(1024)} %convert_element_type.192) | copy-start | bytes 9220
  215.7 150.5 %copy-start.17 = (f32[512,768]{1,0:T(8,128)}, f32[512,768]{1,0:T(8,128)S(1)}, u32[]{:S(2)}) copy-start(f32[512,768]{1,0:T(8,128)S(1)} %get-tuple-element.128) | copy-start | bytes 4718596
  215.7 150.4 %copy-start.43 = (f32[512]{0:T(512)}, f32[512]{0:T(512)S(1)}, u32[]{:S(2)}) copy-start(f32[512]{0:T(512)S(1)} %broadcast_multiply_fusion.5) | copy-start | bytes 6148
  216.1 150.1 %copy-start.54 = (f32[512]{0:T(512)}, f32[512]{0:T(512)S(1)}, u32[]{:S(2)}) copy-start(f32[512]{0:T(512)S(1)} %add_rsqrt_fusion.1) | copy-start | bytes 6148
  216.1 127.8 %copy-start.62 = (f32[768]{0:T(1024)S(1)}, f32[768]{0:T(1024)}, u32[]{:S(2)}) copy-start(f32[768]{0:T(1024)} %convert_element_type.196) | copy-start | bytes 9220
  343.9 6.4 copy-start.23
  343.9 6.4 copy-start.51
  352.5 10.0 %slice-start = ((s8[4718592]{0:T(1024)(128)(4,1)}), s8[4194304]{0:T(1024)(128)(4,1)S(1)}, s32[]{:S(2)}) async-start(s8[4718592]{0:T(1024)(128)(4,1)} %bitcast.143), calls=%async_computation.15 | async-start | bytes 8388608
  353.8 8.8 copy-start.24
  353.8 8.8 slice-start.1
  379.7 166.9 %reduce-scatter.13.cloned.1.call-start = ((), (), s32[]{:S(2)}) async-start(), calls=%async_computation.13 | async-start | bytes 3981312
  385.4 7.6 copy-start.32
  385.4 7.6 copy-start.37
  385.4 7.6 copy-start.39
  468.8 145.3 %reduce-scatter.7.cloned.1.call-start = ((), (), s32[]{:S(2)}) async-start(), calls=%async_computation.8 | async-start | bytes 1327104 | tf_op jit(solution)/shard_map/reduce_scatter | solution.py:259
  473.1 238.9 %reduce-scatter.9.cloned.1.call-start = ((), (), s32[]{:S(2)}) async-start(), calls=%async_computation.9 | async-start | bytes 5308416 | tf_op jit(solution)/shard_map/reduce_scatter | solution.py:271
  480.0 330.6 %reduce-scatter.11.cloned.1.call-start = ((), (), s32[]{:S(2)}) async-start(), calls=%async_computation.10 | async-start | bytes 5308416 | tf_op jit(solution)/shard_map/reduce_scatter | solution.py:277
  488.2 322.4 %copy-start.79 = (u32[32]{0:T(128)S(1)}, u32[32]{0:T(128)}, u32[]{:S(2)}) copy-start(u32[32]{0:T(128)} %constant.140) | copy-start | bytes 388
  488.2 324.3 %copy-start.53 = (bf16[768]{0:T(1024)(128)(2,1)S(1)}, bf16[768]{0:T(1024)(128)(2,1)}, u32[]{:S(2)}) copy-start(bf16[768]{0:T(1024)(128)(2,1)} %get-tuple-element.99) | copy-start | bytes 4612
  488.2 324.3 %copy-start.56 = (bf16[768]{0:T(1024)(128)(2,1)S(1)}, bf16[768]{0:T(1024)(128)(2,1)}, u32[]{:S(2)}) copy-start(bf16[768]{0:T(1024)(128)(2,1)} %get-tuple-element.97) | copy-start | bytes 4612
  488.2 324.3 %copy-start.57 = (bf16[768]{0:T(1024)(128)(2,1)S(1)}, bf16[768]{0:T(1024)(128)(2,1)}, u32[]{:S(2)}) copy-start(bf16[768]{0:T(1024)(128)(2,1)} %get-tuple-element.114) | copy-start | bytes 4612
  488.2 324.4 %copy-start.58 = (bf16[768]{0:T(1024)(128)(2,1)S(1)}, bf16[768]{0:T(1024)(128)(2,1)}, u32[]{:S(2)}) copy-start(bf16[768]{0:T(1024)(128)(2,1)} %get-tuple-element.67) | copy-start | bytes 4612
  488.2 324.4 %copy-start.59 = (bf16[3072]{0:T(1024)(128)(2,1)S(1)}, bf16[3072]{0:T(1024)(128)(2,1)}, u32[]{:S(2)}) copy-start(bf16[3072]{0:T(1024)(128)(2,1)} %get-tuple-element.135) | copy-start | bytes 18436
  488.2 324.4 %copy-start.65 = (bf16[768]{0:T(1024)(128)(2,1)S(1)}, bf16[768]{0:T(1024)(128)(2,1)}, u32[]{:S(2)}) copy-start(bf16[768]{0:T(1024)(128)(2,1)} %get-tuple-element.65) | copy-start | bytes 4612
  488.2 324.4 %copy-start.66 = (bf16[768]{0:T(1024)(128)(2,1)S(1)}, bf16[768]{0:T(1024)(128)(2,1)}, u32[]{:S(2)}) copy-start(bf16[768]{0:T(1024)(128)(2,1)} %get-tuple-element.70) | copy-start | bytes 4612
  488.3 376.7 %all-reduce.20.cloned.1.call-start = ((), (), s32[]{:S(2)}) async-start(), calls=%async_computation.14 | async-start | bytes 3833856 | tf_op jit(solution)/shard_map/psum | solution.py:291
  865.0 6.1 copy-start.29
  (47 other events, 116.9 us)
Sparse Core Ops, SparseCore 0:
  11.0 62.8 all-gather.9
  97.0 60.1 all-gather.17
  160.2 52.8 all-gather.11
  215.9 62.6 all-gather.13
  281.4 62.4 all-gather.15
  379.9 59.7 all-gather.19
  468.9 77.7 reduce-scatter.12
  550.6 63.5 reduce-scatter.6
  617.8 94.1 reduce-scatter.8
  715.5 94.9 reduce-scatter.10
  813.8 49.0 all-reduce.19
where the time goes:
time: 888 us; the launch traced here: 879 us
  waiting for transfers between devices  549 us (62%)
  blocking collectives  113 us (13%)
  matrix products  111 us (12%)
  local copies, waits for them, and re-layouts  60.7 us (7%)
  other arithmetic  28.8 us (3%)
  between operations  16.8 us (2%)
    reduce_scatter x1, waiting for transfers between devices, body(): lax.psum_scatter(w_down_grad.astype(jnp.bfloat16), 'fsdp', scatter_dimens...  98.5 us
    reduce_scatter x1, waiting for transfers between devices, body(): lax.psum_scatter(w_up_grad.astype(jnp.bfloat16), 'fsdp', scatter_dimensio...  97.9 us
    unnamed x2, blocking collectives  75.6 us
    reduce_scatter x1, waiting for transfers between devices, body(): lax.psum_scatter(w_out_grad.astype(jnp.bfloat16), 'fsdp', scatter_dimensi...  65.4 us
    all_gather x1, waiting for transfers between devices, body(): lax.all_gather(w_up, ('group', 'fsdp'), axis=0, tiled=True)  62.5 us
    unnamed x12, waiting for transfers between devices  60.9 us
    all_gather x1, waiting for transfers between devices, body(): lax.all_gather(w_qkv, ('group', 'fsdp'), axis=0, tiled=True)  56.7 us
    all_gather x1, waiting for transfers between devices, body(): lax.all_gather(w_down, ('group', 'fsdp'), axis=0, tiled=True)  45.3 us
  transfers between devices with their start and end apart: 11, of which 9 were waited for; matrix products, arithmetic and copies ran while one was open for 11% of the time, Pallas kernels for 0%

commit v1 on v0

v1 whole, which is shorter than its diff:
```python
import math

import jax
import jax.numpy as jnp
from jax import lax
from jax.experimental import pallas as pl
from jax.experimental.pallas import tpu as pltpu
from jax.sharding import PartitionSpec as P

D = 768
H = 12
HD = 64
SEG = 256
HORIZON = 2560
PAIRS = H // 2
LANES = 2 * HD
EPS = 1e-05

f32 = jnp.float32
bf16 = jnp.bfloat16

B_OUT, GAIN1, BIAS1, B_DOWN, GAIN2, BIAS2, B_UP = range(7)
OUT_AT = D + LANES


def exchange(x, axis, *bits):
    size, offset = lax.axis_size(axis), sum(1 << b for b in bits)
    return lax.ppermute(x, axis, [(i, i ^ offset) for i in range(size)])


def axis_bits(axis):
    return [(axis, b) for b in range(lax.axis_size(axis).bit_length() - 1)]


def tie(x, *others):
    return lax.optimization_barrier((x,) + others)[0]


def trade(pieces):
    size = lax.axis_size("fsdp")
    far = [pieces[0]]
    for m in range(1, size // 2):
        far.append(lax.ppermute(pieces[m], "fsdp", [(i, i ^ (2 * m)) for i in range(size)]))
    return far, exchange(jnp.concatenate([x[1:] for x in far], axis=0), "fsdp", 0)


def near_steps(first_low):
    low, high = axis_bits("fsdp")[:1], axis_bits("group")[1:]
    return low + high if first_low else high + low


def moved(masks, axis, bit):
    step = (1 << bit) * (lax.axis_size("fsdp") if axis == "group" else 1)
    return tuple(m ^ step for m in masks)


def gather_stages(shard):
    lin = lax.axis_index("group") * lax.axis_size("fsdp") + lax.axis_index("fsdp")
    rows, columns = shard.shape
    if rows % 8:
        whole = lax.all_gather(shard, ("group", "fsdp"), axis=0, tiled=True)
        merged = rows
        while merged % 8:
            merged *= 2
        blocks = whole.reshape(-1, merged, columns)
        yield []
        return [[(blocks, tuple(range(blocks.shape[0])))]], jnp.zeros_like(lin)
    blocks, masks = shard[None], (0,)
    for axis, bit in reversed(axis_bits("fsdp")[1:]):
        (other,) = yield [(blocks, axis, bit)]
        blocks = jnp.concatenate([blocks, other], axis=0)
        masks = masks + moved(masks, axis, bit)
    half = columns // 2
    sides = [(blocks[:, :, :half], masks), (blocks[:, :, half:], masks)]
    steps = [near_steps(True), near_steps(False)]
    for n in range(len(steps[0]) - 1):
        others = yield [(b,) + st[n] for (b, _), st in zip(sides, steps)]
        sides = [
            (jnp.concatenate([b, o], axis=0), m + moved(m, *st[n]))
            for (b, m), st, o in zip(sides, steps, others)
        ]
    core = ("group", 0)
    others = yield [(b,) + st[-1] for (b, _), st in zip(sides, steps)] + [
        (b,) + core for b, _ in sides
    ]
    parts = []
    for (b, m), st, o, c in zip(sides, steps, others, others[2:]):
        parts.append([(b, m), (o, moved(m, *st[-1])), (c, moved(m, *core))])
    lasts = yield [(part[1][0],) + core for part in parts]
    for part, last in zip(parts, lasts):
        part.append((last, moved(part[1][1], *core)))
    return parts, lin


class Pipeline:
    def __init__(self):
        self.running = {}
        self.finished = {}
        self.started = ()

    def add(self, name, stages):
        self.running[name] = (stages, None)

    def slot(self, *others, only=None):
        names = [n for n in self.running if only is None or n in only]
        arrived = [x for n in names for x in self.running[n][1] or ()]
        if arrived:
            arrived = lax.optimization_barrier(tuple(arrived) + others)[: len(arrived)]
        at, requests = 0, []
        for n in names:
            stages, results = self.running.pop(n)
            count = len(results or ())
            mine, at = arrived[at : at + count], at + count
            try:
                wanted = next(stages) if results is None else stages.send(mine)
            except StopIteration as done:
                self.finished[n] = done.value
            else:
                self.running[n] = (stages, ())
                requests += [(n, w) for w in wanted]
        operands = tuple(w[0] for _, w in requests)
        if operands and others:
            operands = lax.optimization_barrier(operands + others)[: len(operands)]
        self.started = operands
        for x, (n, (_, axis, *bits)) in zip(operands, requests):
            stages, results = self.running[n]
            self.running[n] = (stages, results + (exchange(x, axis, *bits),))

    def finish(self, name, *others, only=None):
        while name not in self.finished:
            self.slot(*others, only=only)
        return self.finished[name]


VMEM = pl.BlockSpec(memory_space=pltpu.VMEM)
SMEM = pl.BlockSpec(memory_space=pltpu.SMEM)


COSTS = {
    "assemble": 1.5, "project": 5.4, "mix_segments": 1.1, "intra_forward": 5.9, "inter_forward": 5.5,
    "expand": 9.5, "contract": 10.5, "back_to_heads": 11.8, "intra_backward": 10.3,
    "inter_backward": 4.6, "input_grad": 4.0, "weight_grad": 4.0,
}
FLOPS_PER_US = 1.4e9


def call(kernel, name, outs, in_specs, scratch=(), mib=12):
    return pl.pallas_call(
        kernel,
        out_shape=outs,
        in_specs=in_specs,
        out_specs=jax.tree.map(lambda _: VMEM, outs),
        scratch_shapes=scratch,
        compiler_params=pltpu.CompilerParams(vmem_limit_bytes=mib * 1024 * 1024),
        cost_estimate=pl.CostEstimate(
            flops=int(COSTS[name] * FLOPS_PER_US), transcendentals=0, bytes_accessed=0
        ),
        name=name,
    )


def shape_of(shape, dtype):
    return jax.ShapeDtypeStruct(shape, dtype)


def dot(a, b):
    return lax.dot_general(a, b, (((1,), (0,)), ((), ())), preferred_element_type=f32)


def dot_nt(a, b):
    return lax.dot_general(a, b, (((1,), (1,)), ((), ())), preferred_element_type=f32)


def dot_tn(a, b):
    return lax.dot_general(a, b, (((0,), (0,)), ((), ())), preferred_element_type=f32)


def loop(count, body):
    def step(i, carry):
        body(i)
        return carry

    lax.fori_loop(0, count, step, 0)


def rows_at(i):
    return pl.ds(pl.multiple_of(i * SEG, SEG), SEG)


def lanes_at(p):
    return pl.ds(pl.multiple_of(p * LANES, LANES), LANES)


def head_masks(rows):
    lane = lax.broadcasted_iota(jnp.int32, (rows, LANES), 1)
    first = (lane < HD).astype(f32)
    return first.astype(bf16), (1.0 - first).astype(bf16)


def diagonal():
    row = lax.broadcasted_iota(jnp.int32, (LANES, LANES), 0)
    lane = lax.broadcasted_iota(jnp.int32, (LANES, LANES), 1)
    return (row < HD) == (lane < HD)


def head_ones():
    return jnp.where(diagonal(), 1.0, 0.0).astype(bf16)


def split_state(packed):
    same = diagonal()
    cos_part = jnp.where(same, packed, 0.0)
    sin_part = pltpu.roll(jnp.where(same, 0.0, packed), HD, 1)
    return cos_part.astype(bf16), sin_part.astype(bf16)


def state_scratch(fsdp):
    return [pltpu.VMEM((D, LANES), f32), pltpu.VMEM((8 * max(2 * PAIRS, fsdp), LANES), f32)]


def piece_shapes(fsdp, segs):
    return (shape_of((2, segs, D // fsdp + 8, LANES), bf16),) * (fsdp // 2)


def norm_row(n, fsdp):
    per = max(16, fsdp) // fsdp
    return 8 * (n // per) + n % per


def store_states(s, own, left_ref, right_ref, weight_ref, cos_ref, sin_ref, state_scr, norm_scr, out_refs):
    fsdp = 2 * len(out_refs)
    chunk = D // fsdp
    same = diagonal()
    rows = rows_at(s)
    cos, sin = cos_ref[rows, :], sin_ref[rows, :]

    def pair(p):
        lanes = lanes_at(p)
        a = left_ref[rows, lanes]
        b = right_ref[rows, lanes].astype(f32)
        both = jnp.concatenate(
            [(b * cos).astype(bf16), (pltpu.roll(b, HD, 1) * sin).astype(bf16)], axis=1
        )
        product = dot_tn(a, both)
        state_scr[lanes, :] = jnp.where(same, product[:, :LANES], product[:, LANES:])
        wide = a.astype(f32)
        if weight_ref is not None:
            wide = wide * weight_ref[rows, lanes]
        for n, wave in ((p, cos), (PAIRS + p, sin)):
            norm_scr[pl.ds(norm_row(n, fsdp), 1), :] = jnp.sum(wide * wave, axis=0, keepdims=True)

    loop(PAIRS, pair)
    for r in range(fsdp):
        j = own ^ r
        at = pl.ds(pl.multiple_of(chunk * j, 8), chunk)
        norms = pl.ds(pl.multiple_of(8 * j, 8), 8)
        out_refs[r // 2][r % 2, s, 0:chunk, :] = state_scr[at, :].astype(bf16)
        out_refs[r // 2][r % 2, s, chunk : chunk + 8, :] = norm_scr[norms, :].astype(bf16)


def load_states(s, own, far_refs, near_ref, state_scr, norm_scr):
    fsdp = 2 * len(far_refs)
    chunk = D // fsdp
    for r in range(fsdp):
        j = own ^ r
        at = pl.ds(pl.multiple_of(chunk * j, 8), chunk)
        norms = pl.ds(pl.multiple_of(8 * j, 8), 8)
        ref, place = (near_ref, r // 2) if r % 2 else (far_refs[r // 2], 0)
        state_scr[at, :] = ref[place, s, 0:chunk, :].astype(f32)
        norm_scr[norms, :] = ref[place, s, chunk : chunk + 8, :].astype(f32)


def pair_state(p, state_scr, norm_scr, fsdp):
    cos_part, sin_part = split_state(state_scr[lanes_at(p), :])
    norm_cos = norm_scr[pl.ds(norm_row(p, fsdp), 1), :]
    norm_sin = norm_scr[pl.ds(norm_row(PAIRS + p, fsdp), 1), :]
    return cos_part, sin_part, norm_cos, norm_sin


def assemble(parts, lin):
    arrays = [blocks for part in parts for blocks, _ in part]
    places = jnp.concatenate(
        [jnp.array(masks, jnp.int32) for part in parts for _, masks in part]
    ) ^ lin.astype(jnp.int32)
    rows = arrays[0].shape[1]
    count = sum(len(masks) for _, masks in parts[0])
    width = sum(part[0][0].shape[2] for part in parts)
    lefts, left = [], 0
    for part in parts:
        lefts += [left] * len(part)
        left += part[0][0].shape[2]

    def kernel(places_ref, *refs):
        out_ref = refs[-1]
        first = 0
        for ref, at in zip(refs[:-1], lefts):
            number, _, columns = ref.shape

            def place(i, ref=ref, at=at, columns=columns, first=first):
                out_ref[places_ref[first + i], :, at : at + columns] = ref[i]

            loop(number, place)
            first += number

    whole = call(
        kernel, "assemble", shape_of((count, rows, width), bf16), [SMEM] + [VMEM] * len(arrays)
    )(places, *arrays)
    return whole.reshape(count * rows, width)


def project(ids, tokens, w_kv, cos, sin, fsdp):
    rows = tokens.shape[0]
    segs = rows // SEG

    def kernel(ids_ref, tok_ref, w_ref, cos_ref, sin_ref, k_ref, v_ref, *refs):
        inc_refs, (state_scr, norm_scr) = refs[:-2], refs[-2:]
        norm_scr[...] = jnp.zeros_like(norm_scr)

        def segment(s):
            at = rows_at(s)
            x = tok_ref[at, :]
            k_ref[at, :] = jnp.maximum(dot(x, w_ref[:, :D]), 0.0).astype(bf16)
            v_ref[at, :] = dot(x, w_ref[:, D:]).astype(bf16)
            store_states(s, ids_ref[2], k_ref, v_ref, None, cos_ref, sin_ref, state_scr, norm_scr,
                         inc_refs)

        loop(segs, segment)

    act = shape_of((rows, D), bf16)
    k, v, *pieces = call(
        kernel,
        "project",
        (act, act) + piece_shapes(fsdp, segs),
        [SMEM] + [VMEM] * 4,
        state_scratch(fsdp),
    )(ids, tokens, w_kv, cos, sin)
    return k, v, pieces


def mix_segments(spread, far, near):
    fsdp = 2 * len(far)
    _, segs, height, _ = near.shape

    def kernel(spread_ref, *refs):
        far_refs, near_ref, out_refs = refs[: fsdp // 2], refs[fsdp // 2], refs[fsdp // 2 + 1 :]
        for t in range(height // 8):
            at = slice(8 * t, 8 * t + 8)
            stacked = []
            for r in range(fsdp):
                ref, place = (near_ref, r // 2) if r % 2 else (far_refs[r // 2], 0)
                stacked += [ref[place, s, at, :].astype(f32) for s in range(segs)]
            mixed = dot(spread_ref[...], jnp.concatenate(stacked, axis=0).astype(bf16))
            for c in range(fsdp * segs):
                r, s = c // segs, c % segs
                out_refs[r // 2][r % 2, s, at, :] = mixed[8 * c : 8 * c + 8, :].astype(bf16)

    return call(
        kernel, "mix_segments", piece_shapes(fsdp, segs), [VMEM] * (fsdp // 2 + 2)
    )(spread, *far, near)


def intra_forward(tokens, w_q, k, v, wave):
    rows = tokens.shape[0]

    def kernel(tok_ref, w_ref, k_ref, v_ref, wave_ref, q_ref, num_ref, den_ref):
        masks = head_masks(SEG)

        def segment(s):
            at = rows_at(s)
            q_ref[at, :] = jnp.maximum(dot(tok_ref[at, :], w_ref[:, :D]), 0.0).astype(bf16)

            def pair(p):
                lanes = lanes_at(p)
                qs, ks, vs = q_ref[at, lanes], k_ref[at, lanes], v_ref[at, lanes]
                weights, values = [], []
                for m in masks:
                    weights.append((dot_nt(qs, ks * m) * wave_ref[...]).astype(bf16))
                    values.append(jnp.concatenate([vs * m, m], axis=1))
                both = dot(jnp.concatenate(weights, axis=1), jnp.concatenate(values, axis=0))
                num_ref[at, lanes] = both[:, :LANES]
                den_ref[at, lanes] = both[:, LANES:]

            loop(PAIRS, pair)

        loop(rows // SEG, segment)

    wide = shape_of((rows, D), f32)
    return call(
        kernel, "intra_forward", (shape_of((rows, D), bf16), wide, wide), [VMEM] * 5
    )(tokens, w_q, k, v, wave)


def inter_forward(ids, q, num, den, cos, sin, far, near):
    rows = q.shape[0]
    fsdp = 2 * len(far)

    def kernel(ids_ref, q_ref, num_ref, den_ref, cos_ref, sin_ref, *refs):
        far_refs, near_ref = refs[: fsdp // 2], refs[fsdp // 2]
        att_ref, rden_ref, state_scr, norm_scr = refs[fsdp // 2 + 1 :]
        ones = head_ones()
        twice = jnp.concatenate([ones, ones], axis=0)

        def segment(s):
            at = rows_at(s)
            load_states(s, ids_ref[2], far_refs, near_ref, state_scr, norm_scr)

            def pair(p):
                lanes = lanes_at(p)
                cos_part, sin_part, norm_cos, norm_sin = pair_state(p, state_scr, norm_scr, fsdp)
                qs = q_ref[at, lanes].astype(f32)
                q_cos = (qs * cos_ref[at, :]).astype(bf16)
                q_sin = (qs * sin_ref[at, :]).astype(bf16)
                carried = dot(
                    jnp.concatenate([q_cos, q_sin], axis=1),
                    jnp.concatenate([cos_part, sin_part], axis=0),
                )
                along = q_cos.astype(f32) * norm_cos + q_sin.astype(f32) * norm_sin
                high = along.astype(bf16)
                rest = (along - high.astype(f32)).astype(bf16)
                weight = dot(jnp.concatenate([high, rest], axis=1), twice)
                inverse = 1.0 / (den_ref[at, lanes] + weight + 1.0)
                att_ref[at, lanes] = ((num_ref[at, lanes] + carried) * inverse).astype(bf16)
                rden_ref[at, lanes] = inverse

            loop(PAIRS, pair)

        loop(rows // SEG, segment)

    return call(
        kernel,
        "inter_forward",
        (shape_of((rows, D), bf16), shape_of((rows, D), f32)),
        [SMEM] + [VMEM] * (6 + fsdp // 2),
        state_scratch(fsdp),
    )(ids, q, num, den, cos, sin, *far, near)


def standardize(resid):
    centred = resid - jnp.mean(resid, axis=1, keepdims=True)
    inv = lax.rsqrt(jnp.mean(centred * centred, axis=1, keepdims=True) + EPS)
    return centred * inv, inv


def standardize_back(d_hat, hat, inv):
    return inv * (
        d_hat
        - jnp.mean(d_hat, axis=1, keepdims=True)
        - hat * jnp.mean(d_hat * hat, axis=1, keepdims=True)
    )


def expand(att, tokens, w_out, w_up, small):
    rows = att.shape[0]
    ff = w_up.shape[1]

    def kernel(att_ref, tok_ref, out_w_ref, up_ref, small_ref, hat_ref, inv_ref, low_ref, gelu_ref,
               slope_ref):
        def block(i):
            at = rows_at(i)
            mixed = dot(att_ref[at, :], out_w_ref[:, OUT_AT : OUT_AT + D])
            hat, inv = standardize(
                tok_ref[at, :].astype(f32) + mixed + small_ref[B_OUT : B_OUT + 1, :]
            )
            hat_ref[at, :] = hat
            inv_ref[at, :] = jnp.broadcast_to(inv, (SEG, LANES))
            low_ref[at, :] = (
                hat * small_ref[GAIN1 : GAIN1 + 1, :] + small_ref[BIAS1 : BIAS1 + 1, :]
            ).astype(bf16)

            def part(m):
                for c in range(3):
                    columns = pl.ds(pl.multiple_of(m * D + 256 * c, 256), 256)
                    bias = small_ref[pl.ds(B_UP + m, 1), 256 * c : 256 * (c + 1)]
                    upper = dot(low_ref[at, :], up_ref[:, columns]) + bias
                    cdf = 0.5 + 0.5 * lax.erf(upper * math.sqrt(0.5))
                    pdf = jnp.exp(-0.5 * upper * upper) * (1.0 / math.sqrt(2.0 * math.pi))
                    gelu_ref[at, columns] = (upper * cdf).astype(bf16)
                    slope_ref[at, columns] = (cdf + upper * pdf).astype(bf16)

            loop(ff // D, part)

        loop(rows // SEG, block)

    return call(
        kernel,
        "expand",
        (
            shape_of((rows, D), f32),
            shape_of((rows, LANES), f32),
            shape_of((rows, D), bf16),
            shape_of((rows, ff), bf16),
            shape_of((rows, ff), bf16),
        ),
        [VMEM] * 5,
    )(att, tokens, w_out, w_up, small)


def contract(ids, gelu, slope, hat1, cotangent, w_down, small):
    rows, ff = gelu.shape

    def kernel(ids_ref, gelu_ref, slope_ref, hat1_ref, cot_ref, w_ref, small_ref,
               out_ref, dres_ref, dlow_ref, dup_ref, dlow_half_ref, dup_half_ref, sums_ref):
        sums_ref[...] = jnp.zeros_like(sums_ref)

        def block(i):
            at = rows_at(i)
            normed = hat1_ref[at, :] * small_ref[GAIN1 : GAIN1 + 1, :]
            normed += small_ref[BIAS1 : BIAS1 + 1, :]
            resid = normed + dot(gelu_ref[at, :], w_ref[...]) + small_ref[B_DOWN : B_DOWN + 1, :]
            hat, inv = standardize(resid)
            gain = small_ref[GAIN2 : GAIN2 + 1, :]
            out_ref[at, :] = (hat * gain + small_ref[BIAS2 : BIAS2 + 1, :]).astype(bf16)
            cot = cot_ref[at, :].astype(f32)
            sums_ref[GAIN2 : GAIN2 + 1, :] += jnp.sum(cot * hat, axis=0, keepdims=True)
            sums_ref[BIAS2 : BIAS2 + 1, :] += jnp.sum(cot, axis=0, keepdims=True)
            d_res = standardize_back(cot * gain, hat, inv)
            dres_ref[at, :] = d_res
            d_low = d_res.astype(bf16)
            dlow_ref[at, :] = d_low
            sums_ref[B_DOWN : B_DOWN + 1, :] += jnp.sum(d_low.astype(f32), axis=0, keepdims=True)

            def part(m):
                for c in range(3):
                    columns = pl.ds(pl.multiple_of(m * D + 256 * c, 256), 256)
                    d_up = dot_nt(dlow_ref[at, :], w_ref[columns, :])
                    d_up = (d_up * slope_ref[at, columns].astype(f32)).astype(bf16)
                    dup_ref[at, columns] = d_up
                    sums_ref[pl.ds(B_UP + m, 1), 256 * c : 256 * (c + 1)] += jnp.sum(
                        d_up.astype(f32), axis=0, keepdims=True
                    )

            loop(ff // D, part)
            theirs = 1 - ids_ref[0]
            dlow_half_ref[at, :] = dlow_ref[
                at, pl.ds(pl.multiple_of(theirs * (D // 2), 128), D // 2)
            ]
            dup_half_ref[at, :] = dup_ref[
                at, pl.ds(pl.multiple_of(theirs * (ff // 2), 128), ff // 2)
            ]

        loop(rows // SEG, block)

    return call(
        kernel,
        "contract",
        (
            shape_of((rows, D), bf16),
            shape_of((rows, D), f32),
            shape_of((rows, D), bf16),
            shape_of((rows, ff), bf16),
            shape_of((rows, D // 2), bf16),
            shape_of((rows, ff // 2), bf16),
            shape_of((16, D), f32),
        ),
        [SMEM] + [VMEM] * 6,
    )(ids, gelu, slope, hat1, cotangent, w_down, small)


def back_to_heads(ids, d_upper, d_res2, hat1, inv1, rden, att, q, cos, sin, w_out, w_up, small,
                  sums, fsdp):
    rows, ff = d_upper.shape
    segs = rows // SEG

    def kernel(ids_ref, dup_ref, dres_ref, hat_ref, inv_ref, rden_ref, att_ref, q_ref, cos_ref,
               sin_ref, out_w_ref, up_ref, small_ref, sums_in_ref,
               dres1_ref, dmix_ref, dmix_half_ref, dnum_ref, dden_ref, sums_ref, *refs):
        inc_refs, (state_scr, norm_scr) = refs[:-2], refs[-2:]
        sums_ref[...] = sums_in_ref[...]
        norm_scr[...] = jnp.zeros_like(norm_scr)
        ones = head_ones()
        twice = jnp.concatenate([ones, ones], axis=0)

        def block(i):
            at = rows_at(i)
            d_normed = dres_ref[at, :] + dot_nt(dup_ref[at, :], up_ref[...])
            hat = hat_ref[at, :]
            sums_ref[GAIN1 : GAIN1 + 1, :] += jnp.sum(d_normed * hat, axis=0, keepdims=True)
            sums_ref[BIAS1 : BIAS1 + 1, :] += jnp.sum(d_normed, axis=0, keepdims=True)
            d_res = standardize_back(
                d_normed * small_ref[GAIN1 : GAIN1 + 1, :], hat, inv_ref[at, 0:1]
            )
            dres1_ref[at, :] = d_res
            d_mix = d_res.astype(bf16)
            dmix_ref[at, :] = d_mix
            sums_ref[B_OUT : B_OUT + 1, :] += jnp.sum(d_mix.astype(f32), axis=0, keepdims=True)
            d_att = dot_nt(d_mix, out_w_ref[:, OUT_AT : OUT_AT + D])
            inverse = rden_ref[at, :]
            dnum_ref[at, :] = (d_att * inverse).astype(bf16)
            along = d_att * att_ref[at, :].astype(f32)
            for p in range(PAIRS):
                lanes = slice(LANES * p, LANES * (p + 1))
                high = along[:, lanes].astype(bf16)
                rest = (along[:, lanes] - high.astype(f32)).astype(bf16)
                total = dot(jnp.concatenate([high, rest], axis=1), twice)
                dden_ref[at, lanes] = -total * inverse[:, lanes]
            theirs = 1 - ids_ref[0]
            dmix_half_ref[at, :] = dmix_ref[
                at, pl.ds(pl.multiple_of(theirs * (D // 2), 128), D // 2)
            ]
            store_states(i, ids_ref[2], q_ref, dnum_ref, dden_ref, cos_ref, sin_ref, state_scr,
                         norm_scr, inc_refs)

        loop(segs, block)

    return call(
        kernel,
        "back_to_heads",
        (
            shape_of((rows, D), f32),
            shape_of((rows, D), bf16),
            shape_of((rows, D // 2), bf16),
            shape_of((rows, D), bf16),
            shape_of((rows, D), f32),
            shape_of((16, D), f32),
        )
        + piece_shapes(fsdp, segs),
        [SMEM] + [VMEM] * 13,
        state_scratch(fsdp),
    )(ids, d_upper, d_res2, hat1, inv1, rden, att, q, cos, sin, w_out, w_up, small, sums)


def intra_backward(ids, q, k, v, d_num, d_den, cos, sin, wave, wave_t, far, near):
    rows = q.shape[0]
    fsdp = 2 * len(far)

    def kernel(ids_ref, q_ref, k_ref, v_ref, dnum_ref, dden_ref, cos_ref, sin_ref, wave_ref,
               wave_t_ref, *refs):
        far_refs, near_ref = refs[: fsdp // 2], refs[fsdp // 2]
        dq_ref, dq_half_ref, dk_ref, dv_ref, state_scr, norm_scr = refs[fsdp // 2 + 1 :]
        masks = head_masks(SEG)
        lane = lax.broadcasted_iota(jnp.int32, (SEG, LANES), 1) % HD
        picks = [jnp.where(lane < 2, m.astype(f32), 0.0).astype(bf16) for m in masks]

        def segment(s):
            at = rows_at(s)
            load_states(s, ids_ref[2], far_refs, near_ref, state_scr, norm_scr)
            cosine, sine = cos_ref[at, :], sin_ref[at, :]

            def pair(p):
                lanes = lanes_at(p)
                qs, ks, vs = q_ref[at, lanes], k_ref[at, lanes], v_ref[at, lanes]
                dn, dd = dnum_ref[at, lanes], dden_ref[at, lanes]
                high = dd.astype(bf16).astype(f32)
                spread = jnp.where(lane == 0, high, jnp.where(lane == 1, dd - high, 0.0))
                grads = jnp.concatenate([dn, spread.astype(bf16)], axis=1)
                w_ts, d_ss, d_ts, khs, qhs, dns = [], [], [], [], [], []
                for m, pick in zip(masks, picks):
                    kh = ks * m
                    values = jnp.concatenate([vs * m, pick], axis=1)
                    w_ts.append((dot_nt(kh, qs) * wave_t_ref[...]).astype(bf16))
                    d_ss.append((dot_nt(grads, values) * wave_ref[...]).astype(bf16))
                    d_ts.append((dot_nt(values, grads) * wave_t_ref[...]).astype(bf16))
                    khs.append(kh)
                    qhs.append(qs * m)
                    dns.append(dn * m)

                def both(left, right):
                    return dot(jnp.concatenate(left, axis=1), jnp.concatenate(right, axis=0))

                dk_ref[at, lanes] = both(d_ts, qhs)
                dv_ref[at, lanes] = both(w_ts, dns)
                d_q = both(d_ss, khs)
                cos_part, sin_part, norm_cos, norm_sin = pair_state(p, state_scr, norm_scr, fsdp)
                d_q += cosine * (dot_nt(dn, cos_part) + dd * norm_cos)
                d_q += sine * (dot_nt(dn, sin_part) + dd * norm_sin)
                dq_ref[at, lanes] = jnp.where(qs.astype(f32) > 0.0, d_q, 0.0).astype(bf16)

            loop(PAIRS, pair)
            theirs = 1 - ids_ref[0]
            dq_half_ref[at, :] = dq_ref[at, pl.ds(pl.multiple_of(theirs * (D // 2), 128), D // 2)]

        loop(rows // SEG, segment)

    return call(
        kernel,
        "intra_backward",
        (
            shape_of((rows, D), bf16),
            shape_of((rows, D // 2), bf16),
            shape_of((rows, D), f32),
            shape_of((rows, D), f32),
        ),
        [SMEM] + [VMEM] * (10 + fsdp // 2),
        state_scratch(fsdp),
    )(ids, q, k, v, d_num, d_den, cos, sin, wave, wave_t, *far, near)


def inter_backward(ids, k, v, d_k, d_v, cos, sin, far, near):
    rows = k.shape[0]
    fsdp = 2 * len(far)

    def kernel(ids_ref, k_ref, v_ref, dk_ref, dv_ref, cos_ref, sin_ref, *refs):
        far_refs, near_ref = refs[: fsdp // 2], refs[fsdp // 2]
        out_ref, state_scr, norm_scr = refs[fsdp // 2 + 1 :]
        core = ids_ref[0]

        def segment(s):
            at = rows_at(s)
            load_states(s, ids_ref[2], far_refs, near_ref, state_scr, norm_scr)
            cosine, sine = cos_ref[at, :], sin_ref[at, :]

            def pair(p):
                lanes = lanes_at(p)
                cos_part, sin_part, norm_cos, norm_sin = pair_state(p, state_scr, norm_scr, fsdp)
                ks = k_ref[at, lanes].astype(f32)
                vs = v_ref[at, lanes]
                d_k = dk_ref[at, lanes]
                d_k += cosine * (dot_nt(vs, cos_part) + norm_cos)
                d_k += sine * (dot_nt(vs, sin_part) + norm_sin)
                feats = jnp.concatenate(
                    [(ks * cosine).astype(bf16), (ks * sine).astype(bf16)], axis=1
                )
                d_v = dv_ref[at, lanes]
                d_v += dot(feats, jnp.concatenate([cos_part, sin_part], axis=0))
                out_ref[core, at, lanes] = jnp.where(ks > 0.0, d_k, 0.0).astype(bf16)
                out_ref[1 - core, at, lanes] = d_v.astype(bf16)

            loop(PAIRS, pair)

        loop(rows // SEG, segment)

    return call(
        kernel,
        "inter_backward",
        shape_of((2, rows, D), bf16),
        [SMEM] + [VMEM] * (7 + fsdp // 2),
        state_scratch(fsdp),
    )(ids, k, v, d_k, d_v, cos, sin, *far, near)


def input_grad(ids, d_q, d_kv, d_res1, w_q, w_kv):
    rows = d_q.shape[0]

    def kernel(ids_ref, dq_ref, dkv_ref, dres_ref, w_q_ref, w_kv_ref, out_ref):
        core = ids_ref[0]

        def block(i):
            at = rows_at(i)
            total = dres_ref[at, :] + dot_nt(dq_ref[at, :], w_q_ref[:, :D])
            total += dot_nt(dkv_ref[core, at, :], w_kv_ref[:, :D])
            total += dot_nt(dkv_ref[1 - core, at, :], w_kv_ref[:, D:])
            out_ref[at, :] = total

        loop(rows // SEG, block)

    return call(
        kernel, "input_grad", shape_of((rows, D), f32), [SMEM] + [VMEM] * 5
    )(ids, d_q, d_kv, d_res1, w_q, w_kv)


def reversed_bits(index, bits):
    total = 0
    for b in range(bits):
        total = total + (((index >> b) & 1) << (bits - 1 - b))
    return total


def weight_grad(ids, products, fsdp, splits, own_half=True, sums=None):
    height = products[0][0].shape[1]
    widths = [product[3].shape[1] for product in products]
    block = height // fsdp
    bits = fsdp.bit_length() - 1
    share = block // len(splits)
    group = block if block % 128 == 0 else height
    extra = [] if sums is None else [sums]

    def kernel(ids_ref, *refs):
        ins, out_refs = refs[: 4 * len(products)], refs[4 * len(products) + len(extra) :]

        def part(i):
            columns = pl.ds(pl.multiple_of(i * group, 128), group)

            def store(total, left):
                right = left + total.shape[1]
                for j in range(group // block):
                    place = reversed_bits((i * (group // block) + j) ^ ids_ref[2], bits)
                    for n, (split, out_ref) in enumerate(zip(splits, out_refs)):
                        strip = share // split
                        for h in range(split):
                            row = block * j + share * n + strip * h
                            half = h ^ ids_ref[1] if split > 1 else 0
                            out_ref[half, place, :, left:right] = total[
                                row : row + strip, :
                            ].astype(bf16)

            left = 0
            for n, width in enumerate(widths):
                a0_ref, a1_ref, b0_ref, b1_ref = ins[4 * n : 4 * n + 4]
                first = pl.multiple_of(ids_ref[0] * width, 128) if own_half else 0
                total = dot_tn(a0_ref[:, columns], b0_ref[:, pl.ds(first, width)])
                store(total + dot_tn(a1_ref[:, columns], b1_ref[...]), left)
                left += width
            if extra:
                tall = jnp.concatenate(
                    [refs[4 * len(products)][...], jnp.zeros((LANES - 16, height), f32)], axis=0
                )
                store(tall.T, left)

        loop(height // group, part)

    width = sum(widths) + LANES * len(extra)
    return call(
        kernel,
        "weight_grad",
        tuple(shape_of((n, fsdp, share // n, width), bf16) for n in splits),
        [SMEM] + [VMEM] * (4 * len(products) + len(extra)),
    )(ids, *(x for product in products for x in product), *extra)


def add_low(a, b):
    return (a.astype(f32) + b.astype(f32)).astype(bf16)


def halving_stages(keep, send):
    for axis, bit in axis_bits("fsdp"):
        (received,) = yield [(send, axis, bit)]
        half = keep.shape[0] // 2
        if half == 0:
            return add_low(keep[0], received[0])
        keep, send = add_low(keep[:half], received[:half]), add_low(keep[half:], received[half:])


def reduce_stages(x, core):
    half = x.shape[1] // 2
    x = yield from halving_stages(x[0, :half], x[0, half:])
    bits = axis_bits("group")[1:]
    for axis, bit in bits[:-1]:
        (received,) = yield [(x, axis, bit)]
        x = add_low(x, received)
    if not bits:
        return (yield from core_stages(x, core))
    axis, bit = bits[-1]
    above, beside, across = yield [(x, axis, bit), (x, axis, 0), (x, axis, bit, 0)]
    mine = x.astype(f32) + above.astype(f32)
    theirs = beside.astype(f32) + across.astype(f32)
    return ordered(mine, theirs, core == 0, -1)


def share_stages(x, core, chip):
    axis, bit = axis_bits("group")[1]
    half = x.shape[1] // 2
    (received,) = yield [(x[1], axis, bit)]
    keep = add_low(x[0, :half], received[:half])
    x = yield from halving_stages(keep, add_low(x[0, half:], received[half:]))
    above, beside, across = yield [(x, axis, bit), (x, axis, 0), (x, axis, bit, 0)]
    mine = ordered(x, above, chip == 0, 0)
    theirs = ordered(beside, across, chip == 0, 0)
    return ordered(mine, theirs, core == 0, -1).astype(f32)


def ordered(x, other, first, axis):
    return jnp.concatenate([jnp.where(first, x, other), jnp.where(first, other, x)], axis=axis)


def core_stages(x, core):
    (other,) = yield [(x, "group", 0)]
    return ordered(x, other, core == 0, -1).astype(f32)


def ancestor_matrix(parents):
    count = parents.shape[0]
    columns = jnp.arange(count, dtype=jnp.int32)
    step = (parents[:, None] == columns[None, :]).astype(f32)
    same = (columns[:, None] == columns[None, :]).astype(f32)
    reached = step + same
    for _ in range(4):
        reached = (jnp.dot(reached, reached, preferred_element_type=f32) > 0.0).astype(f32)
    return reached - same


def spread_rows(matrix):
    count = matrix.shape[0]
    row = jnp.arange(8 * count, dtype=jnp.int32)
    pick = (row[:, None] // 8 == jnp.arange(count, dtype=jnp.int32)[None, :]).astype(f32)
    wide = jnp.dot(jnp.dot(pick, matrix), pick.T)
    return jnp.where(row[:, None] % 8 == row[None, :] % 8, wide, 0.0).astype(bf16)


def waves(local, segs):
    depth = jnp.sum(local[:segs], axis=1)
    angle = (depth[:, None] * SEG + jnp.arange(SEG, dtype=f32)[None, :]) * (
        math.pi / (2.0 * HORIZON)
    )
    angle = jnp.broadcast_to(angle.reshape(segs * SEG, 1), (segs * SEG, LANES))
    return jnp.cos(angle), jnp.sin(angle)


def gap_wave():
    position = jnp.arange(SEG, dtype=jnp.int32)
    gap = position[:, None] - position[None, :]
    wave = jnp.cos(gap.astype(f32) * (math.pi / (2.0 * HORIZON)))
    return jnp.where(gap >= 0, wave, 0.0), jnp.where(gap <= 0, wave, 0.0)


def vector_columns(vectors, wide):
    rows = vectors[0].shape[0]
    columns = jnp.concatenate([jnp.stack(vectors, axis=1), wide.reshape(-1, rows).T], axis=1)
    return jnp.pad(columns, ((0, 0), (0, LANES - columns.shape[1])))


def vector_rows(columns, rows, longer):
    turned = columns[:, :16].T.astype(f32)
    wide = turned[B_UP : B_UP + longer].reshape(longer, -1, rows)
    wide = jnp.swapaxes(wide, 0, 1).reshape(longer, D)
    return jnp.concatenate([turned[:B_UP], wide, turned[B_UP + longer :]], axis=0)


def wide_by_block(sums, fsdp, longer):
    wide = sums[B_UP : B_UP + longer].reshape(fsdp, longer, D // fsdp)
    wide = jnp.swapaxes(wide, 0, 1).reshape(longer, D)
    return jnp.concatenate([sums[:B_UP], wide, sums[B_UP + longer :]], axis=0)


def body(
    tokens, cotangent, parent_seg, w_qkv, w_out, b_out, norm1_gain, norm1_bias, w_up, b_up,
    w_down, b_down, norm2_gain, norm2_bias,
):
    fsdp = lax.axis_size("fsdp")
    chips = lax.axis_size("group") // 2
    own = lax.axis_index("fsdp")
    group = lax.axis_index("group")
    core, chip = group % 2, group // 2
    rows = tokens.shape[0]
    segs = rows // SEG
    ff = w_up.shape[1]
    ids = jnp.stack([core, chip, own]).astype(jnp.int32)

    ancestry = ancestor_matrix(parent_seg[0])
    count = parent_seg.shape[1]
    place = jnp.arange(count, dtype=jnp.int32)
    there = (own ^ (place // segs)) * segs + place % segs
    select = (there[:, None] == place[None, :]).astype(f32)
    local = jnp.dot(jnp.dot(select, ancestry), select.T)
    from_ancestors, from_descendants = spread_rows(local), spread_rows(local.T)
    cos, sin = waves(local, segs)
    wave, wave_t = gap_wave()

    pipe = Pipeline()
    pipe.add("kv", gather_stages(w_qkv[:, D:]))
    pipe.slot()
    columns = vector_columns(
        (b_out, norm1_gain, norm1_bias, b_down, norm2_gain, norm2_bias), b_up
    )
    pipe.add("qo", gather_stages(jnp.concatenate([w_qkv[:, :D], columns, w_out, columns], axis=1)))
    pipe.add("up", gather_stages(w_up))
    pipe.add("down", gather_stages(w_down))
    pipe.slot(only=("kv",))
    pipe.slot(*pipe.started, only=("qo",))
    pipe.slot(only=("kv",))
    pipe.slot(*pipe.started, only=("qo",))
    pipe.slot(*pipe.started, only=("up",))
    pipe.slot(only=("kv",))
    pipe.slot(*pipe.started, only=("qo",))
    w_kv = assemble(*pipe.finish("kv", only=("kv",)))
    tables = (from_ancestors, from_descendants, wave, wave_t)
    k, v, increments = project(ids, tie(tokens, *tables), w_kv, cos, sin, fsdp)
    far, near = trade(increments)
    pipe.slot(k, only=("qo", "up"))
    pipe.slot(*pipe.started, only=("down",))
    pipe.slot(near, only=("qo",))
    pipe.slot(*pipe.started, only=("up",))
    w_qo = assemble(*pipe.finish("qo", only=("qo",)))
    q, num, den = intra_forward(tokens, w_qo, k, v, wave)
    pipe.slot(q, only=("up", "down"))
    mixed = mix_segments(from_ancestors, far, tie(near, q))
    path = trade(mixed)
    tokens_other = exchange(tie(tokens, q), "group", 0)
    small = vector_rows(tie(w_qo, mixed[0])[:, D:OUT_AT], w_qkv.shape[0], ff // D)
    pipe.slot(path[1], only=("up", "down"))
    att, rden = inter_forward(ids, q, num, den, cos, sin, *path)
    pipe.slot(att, only=("down",))
    att_other = exchange(att, "group", 0)
    w_up_full = assemble(*pipe.finish("up", only=("up",)))
    hat1, inv1, low1, gelu, slope = expand(att, tokens, w_qo, w_up_full, small)
    w_down_full = assemble(*pipe.finish("down", low1, only=("down",)))
    gelu_other = exchange(gelu, "group", 0)
    low1_other = exchange(low1, "group", 0)
    output, d_res2, d_lower, d_upper, d_lower_half, d_upper_half, sums = contract(
        ids, gelu, slope, hat1, cotangent, w_down_full, small
    )
    d_lower_other = exchange(d_lower_half, "group", 0)
    d_upper_other = exchange(d_upper_half, "group", 0)
    d_res1, d_mixed, d_mixed_half, d_num, d_den, sums, *back = back_to_heads(
        ids, d_upper, d_res2, hat1, inv1, rden, att, q, cos, sin, w_qo, w_up_full, small, sums, fsdp
    )
    d_mixed_other = exchange(d_mixed_half, "group", 0)
    far, near = trade(back)
    grads = Pipeline()
    two = chips == 2

    def reduction(part):
        return share_stages(part, core, chip) if two else reduce_stages(part, core)

    split = 2 if two else 1
    (down_part,) = weight_grad(
        ids, [(gelu, gelu_other, tie(d_lower, d_num), d_lower_other)], fsdp, [split]
    )
    grads.add("down", reduction(down_part))
    grads.slot()
    (up_part,) = weight_grad(
        ids, [(low1, low1_other, tie(d_upper, *grads.started), d_upper_other)], fsdp, [1]
    )
    grads.add("up", reduce_stages(up_part, core))
    grads.slot(only=("up",))
    mixed = mix_segments(from_descendants, far, tie(near, *grads.started))
    back = trade(mixed)
    d_q, d_q_half, d_k, d_v = intra_backward(
        ids, tie(q, mixed[0]), k, v, d_num, d_den, cos, sin, wave, wave_t, *path
    )
    d_q_other = exchange(d_q_half, "group", 0)
    grads.slot(d_q)
    (outq_part,) = weight_grad(
        ids,
        [
            (tie(att, *grads.started), att_other, d_mixed, d_mixed_other),
            (tokens, tokens_other, d_q, d_q_other),
        ],
        fsdp, [split], sums=wide_by_block(sums, fsdp, ff // D),
    )
    grads.add("outq", reduction(outq_part))
    grads.slot(only=("outq",))
    d_kv = inter_backward(ids, tie(k, *grads.started), v, d_k, d_v, cos, sin, *back)
    d_kv_other = exchange(d_kv[1], "group", 0)
    grads.slot(d_kv)
    tokens_grad = input_grad(ids, d_q, tie(d_kv, *grads.started), d_res1, w_qo, w_kv)
    kv_parts = weight_grad(
        ids, [(tokens, tokens_other, tie(d_kv[0], tokens_grad), d_kv_other)], fsdp,
        [2, 1] if two else [1], False,
    )
    grads.add("kv0", reduction(kv_parts[0]))
    for part in kv_parts[1:]:
        grads.add("kv1", reduce_stages(part, core))
    while grads.running:
        grads.slot(kv_parts[0])
    done = grads.finished
    kv_grad = jnp.concatenate([done[n] for n in ("kv0", "kv1") if n in done], axis=0)
    ours, others = jnp.split(done["outq"], 2, axis=1)
    half = D // 2
    sums = ours[:, D : D + 16] + others[:, D : D + 16]
    return (
        output,
        tokens_grad,
        jnp.concatenate([ours[:, half:D], others[:, half:D], kv_grad], axis=1),
        jnp.concatenate([ours[:, :half], others[:, :half]], axis=1),
        sums[:, B_OUT],
        sums[:, GAIN1],
        sums[:, BIAS1],
        done["up"],
        sums[:, B_UP : B_UP + ff // D].T.reshape(-1),
        done["down"],
        sums[:, B_DOWN],
        sums[:, GAIN2],
        sums[:, BIAS2],
    )


def solution(mesh):
    both = ("group", "fsdp")
    matrix, vector = P(both, None), P(both)
    in_specs = (
        matrix, matrix, P("group", None), matrix, matrix, vector, vector, vector, matrix, vector,
        matrix, vector, vector, vector,
    )
    rows, line = P("fsdp", None), P("fsdp")
    out_specs = (
        matrix, matrix, rows, rows, line, line, line, rows, line, rows, line, line, line,
    )
    return jax.shard_map(body, mesh=mesh, in_specs=in_specs, out_specs=out_specs, check_vma=False)
```

time: 888 us -> 339 us (0.38)
  waiting for transfers between devices: 549 us -> 106 us
  blocking collectives: 113 us -> 0 us
  matrix products: 111 us -> 3.1 us
  starting transfers between devices: 0.44 us -> 90.7 us
  Pallas kernels: 0 us -> 82.8 us
  local copies, waits for them, and re-layouts: 60.7 us -> 38.5 us
  between operations: 16.8 us -> 2.18 us
  other arithmetic: 28.8 us -> 14.6 us
    reduce_scatter x3 -> x0, waiting for transfers between devices: 262 us -> none  [the longest x1 98.5 us: body(): lax.psum_scatter(w_down_grad.astype(jnp.bfloat16), 'fsdp', scatter_dimens...]
    all_gather x6 -> x0, waiting for transfers between devices: 226 us -> none  [the longest x1 62.5 us: body(): lax.all_gather(w_up, ('group', 'fsdp'), axis=0, tiled=True)]
    dot_general x49 -> x5, matrix products: 111 us -> 3.1 us  [the longest x2 1.44 us: spread_rows(): wide = jnp.dot(jnp.dot(pick, matrix), pick.T)]
    ppermute x0 -> x98, waiting for transfers between devices: none -> 106 us  [the longest x86 91.2 us: exchange(): return lax.ppermute(x, axis, [(i, i ^ offset) for i in range(size)])]
    ppermute x0 -> x98, starting transfers between devices: none -> 90.7 us  [the longest x86 73 us: exchange(): return lax.ppermute(x, axis, [(i, i ^ offset) for i in range(size)])]
    pallas_call x0 -> x19, Pallas kernels: none -> 82.8 us  [the longest x4 15.4 us: weight_grad(): call(kernel, 'weight_grad', tuple((shape_of((n, fsdp, share // n, width),...]
    unnamed x2 -> x0, blocking collectives: 75.6 us -> none
    unnamed x12 -> x0, waiting for transfers between devices: 60.9 us -> none
  transfers between devices with their start and end apart: 11 -> 98, of which waited for: 9 -> 36; matrix products, arithmetic and copies ran while one was open for 11% -> 11% of each run, Pallas kernels for 0% -> 24%
where the time goes in v1:
time: 339 us; the launch traced here: 338 us
  waiting for transfers between devices  106 us (31%)
  starting transfers between devices  90.7 us (27%)
  Pallas kernels  82.8 us (24%)
  local copies, waits for them, and re-layouts  38.5 us (11%)
  other arithmetic  14.6 us (4%)
    ppermute x86, waiting for transfers between devices, exchange(): return lax.ppermute(x, axis, [(i, i ^ offset) for i in range(size)])  91.2 us
    ppermute x86, starting transfers between devices, exchange(): return lax.ppermute(x, axis, [(i, i ^ offset) for i in range(size)])  73 us
    ppermute x12, starting transfers between devices, trade(): lax.ppermute(pieces[m], 'fsdp', [(i, i ^ 2 * m) for i in range(size)])  17.7 us
    pallas_call x4, Pallas kernels, weight_grad(): call(kernel, 'weight_grad', tuple((shape_of((n, fsdp, share // n, width),...  15.4 us
    ppermute x12, waiting for transfers between devices, trade(): lax.ppermute(pieces[m], 'fsdp', [(i, i ^ 2 * m) for i in range(size)])  14.7 us
    unnamed x142, local copies, waits for them, and re-layouts  13.3 us
    pallas_call x1, Pallas kernels, back_to_heads(): call(kernel, 'back_to_heads', (shape_of((rows, D), f32), shape_of((rows,...  10.7 us
    pallas_call x1, Pallas kernels, contract(): call(kernel, 'contract', (shape_of((rows, D), bf16), shape_of((rows, D),...  10.7 us
  transfers between devices with their start and end apart: 98, of which 36 were waited for; matrix products, arithmetic and copies ran while one was open for 11% of the time, Pallas kernels for 24%

profile of v1, /device:TPU:0, one launch (start us, length us, event | category | flops | bytes accessed | tf_op | source)
XLA Modules:
  0.0 337.8 jit_solution(17822133511837643756)
XLA Ops:
  1.5 4.0 %collective-permute-start = (bf16[1,24,1536]{2,1,0:T(8,128)(2,1)S(1)}, bf16[1,24,1536]{2,1,0:T(8,128)(2,1)S(1)}, u32[]{:S(2)}, u32[]{:S(2)}) collective-permute-start(bf16[1,24,1536]{2,1,0:T(8,128)(2,1)S(1)} %slice_bitcast_fusion.13), channel_id=1, source_target_pairs={{0,4},{1,5},{2,6},{3,7},{4,0},{5,1},{6,2},{7,3},{8,12},{9,13},{10,... | collective-permute-start | bytes 221192 | tf_op jit(solution)/shard_map/ppermute | solution.py:28
  18.3 2.9 collective-permute-done.2
  26.1 5.0 %collective-permute-done.1 = bf16[1,24,1792]{2,1,0:T(8,128)(2,1)S(1)} collective-permute-done((bf16[1,24,1792]{2,1,0:T(8,128)(2,1)S(1)}, bf16[1,24,1792]{2,1,0:T(8,128)(2,1)S(1)}, u32[]{:S(2)}, u32[]{:S(2)}) %collective-permute-start.1) | collective-permute-done | bytes 86048 | tf_op jit(solution)/shard_map/ppermute | solution.py:28
  34.5 4.5 %collective-permute-done.3 = bf16[2,24,1792]{2,1,0:T(8,128)(2,1)S(1)} collective-permute-done((bf16[2,24,1792]{2,1,0:T(8,128)(2,1)S(1)}, bf16[2,24,1792]{2,1,0:T(8,128)(2,1)S(1)}, u32[]{:S(2)}, u32[]{:S(2)}) %collective-permute-start.3) | collective-permute-done | bytes 172064 | tf_op jit(solution)/shard_map/ppermute | solution.py:28
  45.6 5.1 %project.1 = (bf16[512,768]{1,0:T(8,128)(2,1)S(1)}, bf16[512,768]{1,0:T(8,128)(2,1)S(1)}, bf16[2,2,104,128]{3,2,1,0:T(8,128)(2,1)S(1)}, bf16[2,2,104,128]{3,2,1,...) custom-call(s32[3]{0:T(128)S(1)} %pad_add_fusion.ids_ref, ...), custom_call_target="tpu_custom_call" | custom-call | flops 7560000000 | tf_op jit(solution)/shard_map/project/pallas_call | solution.py:330
  55.7 7.0 %collective-permute-done.20.refs_2_ = bf16[2,2,104,128]{3,2,1,0:T(8,128)(2,1)S(1)} collective-permute-done((bf16[2,2,104,128]{3,2,1,0:T(8,128)(2,1)S(1)}, bf16[2,2,104,128]{3,2,1,0:T(8,128)(2,1)S(1)}, u32[]{:S(2)}, u32[]{:S(2)}) %collective-permute-start.20) | collective-permute-done | bytes 106528 | tf_op jit(solution)/shard_map/ppermute | solution.py:43
  67.0 4.0 %collective-permute-done.22.refs_4_ = bf16[4,2,104,128]{3,2,1,0:T(8,128)(2,1)S(1)} collective-permute-done((bf16[4,2,104,128]{3,2,1,0:T(8,128)(2,1)S(1)}, bf16[4,2,104,128]{3,2,1,0:T(8,128)(2,1)S(1)}, u32[]{:S(2)}, u32[]{:S(2)}) %collective-permute-start.22) | collective-permute-done | bytes 213024 | tf_op jit(solution)/shard_map/ppermute | solution.py:28
  71.0 2.0 collective-permute-start.29
  73.0 2.2 collective-permute-start.30
  76.3 3.8 %collective-permute-done.29 = bf16[2,24,3072]{2,1,0:T(8,128)(2,1)S(1)} collective-permute-done((bf16[2,24,3072]{2,1,0:T(8,128)(2,1)S(1)}, bf16[2,24,3072]{2,1,0:T(8,128)(2,1)S(1)}, u32[]{:S(2)}, u32[]{:S(2)}) %collective-permute-start.29) | collective-permute-done | bytes 294944 | tf_op jit(solution)/shard_map/ppermute | solution.py:28
  80.2 1.8 collective-permute-start.31
  83.2 5.9 %intra_forward.1 = (bf16[512,768]{1,0:T(8,128)(2,1)S(1)}, f32[512,768]{1,0:T(8,128)S(1)}, f32[512,768]{1,0:T(8,128)S(1)}) custom-call(bf16[512,768]{1,0:T(8,128)(2,1)S(1)} %copy-done.25, bf16[768,1792]{1,0:T(8,128)(2,1)S(1)} %bitcast.110, bf16[512,768]{1,0:T(8,128)(2,1)S(1)} %get-tuple-element.323.k_ref, bf16[512,768]{1,0:T(8,128)(2,1)S(1)} %get-tuple-element.239.v_ref, ...), custom_call_target="tpu_custom_call" | custom-call | flops 8259999744 | tf_op jit(solution)/shard_map/intra_forward/pallas_call | solution.py:388
  91.2 3.2 collective-permute-start.26
  95.4 2.1 collective-permute-start.34
  103.5 5.6 %collective-permute-done.33 = bf16[2,96,768]{2,1,0:T(8,128)(2,1)S(1)} collective-permute-done((bf16[2,96,768]{2,1,0:T(8,128)(2,1)S(1)}, bf16[2,96,768]{2,1,0:T(8,128)(2,1)S(1)}, u32[]{:S(2)}, u32[]{:S(2)}) %collective-permute-start.33) | collective-permute-done | bytes 294944 | tf_op jit(solution)/shard_map/ppermute | solution.py:28
  109.8 2.2 collective-permute-start.28
  113.9 1.7 copy.92
  115.7 1.7 copy.93
  117.4 1.9 copy.91
  123.2 2.4 collective-permute-start.41
  129.0 4.4 %inter_forward.1 = (bf16[512,768]{1,0:T(8,128)(2,1)S(1)}, f32[512,768]{1,0:T(8,128)S(1)}) custom-call(s32[3]{0:T(128)S(1)} %pad_add_fusion.ids_ref, bf16[512,768]{1,0:T(8,128)(2,1)S(1)} %copy-done.55, f32[512,768]{1,0:T(8,128)S(1)} %copy-done.51, f32[512,768]{1,0:T(8,128)S(1)} %copy-done.53, f32[512,128]{1,0:T(8,128)S(1)} %copy-done.4, ...), custom_call_target="tpu_custom_call" | custom-call | flops 7699999744 | tf_op jit(solution)/shard_map/inter_forward/pallas_call | solution.py:429
  137.0 7.4 %expand.1 = (f32[512,768]{1,0:T(8,128)S(1)}, f32[512,128]{1,0:T(8,128)S(1)}, bf16[512,768]{1,0:T(8,128)(2,1)S(1)}, bf16[512,3072]{1,0:T(8,128)(2,1)S(1)}, bf16[512,3072]{1,0:T(8,128)(2,1)S(1)}) custom-call(bf16[512,768]{1,0:T(8,128)(2,1)S(1)} %get-tuple-element.317.att_ref.refs_0_, bf16[512,768]{1,0:T(8,128)(2,1)S(1)} %copy-done.26, ...), custom_call_target="tpu_custom_call" | custom-call | flops 13299999744 | tf_op jit(solution)/shard_map/expand/pallas_call | solution.py:484
  145.3 3.6 %collective-permute-done.42.refs_1_ = bf16[8,96,384]{2,1,0:T(8,128)(2,1)S(1)} collective-permute-done((bf16[8,96,384]{2,1,0:T(8,128)(2,1)S(1)}, bf16[8,96,384]{2,1,0:T(8,128)(2,1)S(1)}, u32[]{:S(2)}, u32[]{:S(2)}) %collective-permute-start.42) | collective-permute-done | bytes 589856 | tf_op jit(solution)/shard_map/ppermute | solution.py:28
  154.0 10.7 %contract.1 = (bf16[512,768]{1,0:T(8,128)(2,1)}, f32[512,768]{1,0:T(8,128)S(1)}, bf16[512,768]{1,0:T(8,128)(2,1)S(1)}, bf16[512,3072]{1,0:T(8,128)(2,1)S(1)}, bf...) custom-call(s32[3]{0:T(128)S(1)} %pad_add_fusion.ids_ref, ...), custom_call_target="tpu_custom_call" | custom-call | flops 14700000256 | tf_op jit(solution)/shard_map/contract/pallas_call | solution.py:543
  165.3 10.7 %back_to_heads.1 = (f32[512,768]{1,0:T(8,128)S(1)}, bf16[512,768]{1,0:T(8,128)(2,1)S(1)}, bf16[512,384]{1,0:T(8,128)(2,1)S(1)}, bf16[512,768]{1,0:T(8,128)(2,1)S...) custom-call(s32[3]{0:T(128)S(1)} %pad_add_fusion.ids_ref, ...), custom_call_target="tpu_custom_call" | custom-call | flops 16519999488 | tf_op jit(solution)/shard_map/back_to_heads/pallas_call | solution.py:605
  188.5 2.1 collective-permute-start.50
  191.4 3.8 %collective-permute-done.50.refs_3_ = bf16[2,2,104,128]{3,2,1,0:T(8,128)(2,1)S(1)} collective-permute-done((bf16[2,2,104,128]{3,2,1,0:T(8,128)(2,1)}, bf16[2,2,104,128]{3,2,1,0:T(8,128)(2,1)S(1)}, u32[]{:S(2)}, u32[]{:S(2)}) %collective-permute-start.50) | collective-permute-done | bytes 106528 | tf_op jit(solution)/shard_map/ppermute | solution.py:43
  198.0 7.0 %weight_grad.4 = bf16[2,8,192,384]{3,2,1,0:T(8,128)(2,1)S(1)} custom-call(s32[3]{0:T(128)S(1)} %pad_add_fusion.ids_ref, bf16[512,3072]{1,0:T(8,128)(2,1)S(1)} %get-tuple-element.272.gelu_ref.refs_0_, bf16[512,3072]{1,0:T(8,128)(2,1)} %collective-permute-done.53.refs_1_, bf16[512,768]{1,0:T(8,128)(2,1)S(1)} %copy-done.43, ...), custom_call_target="tpu_custom_call" | custom-call | flops 5600000000 | tf_op jit(solution)/shard_map/weight_grad/pallas_call | solution.py:802
  206.2 4.1 %weight_grad.5 = bf16[1,8,96,1536]{3,2,1,0:T(8,128)(2,1)S(1)} custom-call(s32[3]{0:T(128)S(1)} %pad_add_fusion.ids_ref, bf16[512,768]{1,0:T(8,128)(2,1)S(1)} %copy-done.31, bf16[512,768]{1,0:T(8,128)(2,1)S(1)} %collective-permute-done.52.refs_1_, bf16[512,3072]{1,0:T(8,128)(2,1)S(1)} %copy-done.39, bf16[512,1536]{1,0:T(8,128)(2,1)} %collective-permute-done.55.refs_3_), custom_call_target="tpu_custom_call" | custom-call | flops 5600000000 | tf_op jit(solution)/shard_map/weight_grad/pallas_call | solution.py:802
  212.6 2.2 collective-permute-start.63
  215.9 9.4 %intra_backward.1 = (bf16[512,768]{1,0:T(8,128)(2,1)S(1)}, bf16[512,384]{1,0:T(8,128)(2,1)S(1)}, f32[512,768]{1,0:T(8,128)S(1)}, f32[512,768]{1,0:T(8,128)S(1)}) custom-call(s32[3]{0:T(128)S(1)} %pad_add_fusion.ids_ref, bf16[512,768]{1,0:T(8,128)(2,1)S(1)} %copy-done.56, bf16[512,768]{1,0:T(8,128)(2,1)S(1)} %copy-done.47, bf16[512,768]{1,0:T(8,128)(2,1)S(1)} %copy-done.49, ...), custom_call_target="tpu_custom_call" | custom-call | flops 14419999744 | tf_op jit(solution)/shard_map/intra_backward/pallas_call | solution.py:674
  226.2 10.4 %collective-permute-done.57 = bf16[4,96,1536]{2,1,0:T(8,128)(2,1)S(1)} collective-permute-done((bf16[4,96,1536]{2,1,0:T(8,128)(2,1)S(1)}, bf16[4,96,1536]{2,1,0:T(8,128)(2,1)S(1)}, u32[]{:S(2)}, u32[]{:S(2)}) %collective-permute-start.57) | collective-permute-done | bytes 1179680 | tf_op jit(solution)/shard_map/ppermute | solution.py:28
  238.6 2.4 weight_grad.6
  244.4 4.1 %inter_backward.1.dkv_ref = bf16[2,512,768]{2,1,0:T(8,128)(2,1)S(1)} custom-call(s32[3]{0:T(128)S(1)} %pad_add_fusion.ids_ref, bf16[512,768]{1,0:T(8,128)(2,1)S(1)} %copy-done.47, bf16[512,768]{1,0:T(8,128)(2,1)S(1)} %copy-done.49, f32[512,768]{1,0:T(8,128)S(1)} %get-tuple-element.324.dk_ref, f32[512,768]{1,0:T(8,128)S(1)} %get-tuple-element.325.dv_ref, ...), custom_call_target="tpu_custom_call" | custom-call | flops 6440000000 | tf_op jit(solution)/shard_map/inter_backward/pallas_call | solution.py:722
  248.7 8.5 %collective-permute-done.66 = bf16[4,192,384]{2,1,0:T(8,128)(2,1)S(1)} collective-permute-done((bf16[4,192,384]{2,1,0:T(8,128)(2,1)S(1)}, bf16[4,192,384]{2,1,0:T(8,128)(2,1)S(1)}, u32[]{:S(2)}, u32[]{:S(2)}) %collective-permute-start.66) | collective-permute-done | bytes 589856 | tf_op jit(solution)/shard_map/ppermute | solution.py:28
  263.0 4.2 %input_grad.1 = f32[512,768]{1,0:T(8,128)} custom-call(s32[3]{0:T(128)S(1)} %pad_add_fusion.ids_ref, bf16[512,768]{1,0:T(8,128)(2,1)S(1)} %get-tuple-element.312.refs_6_.dq_ref, bf16[2,512,768]{2,1,0:T(8,128)(2,1)S(1)} %inter_backward.1.dkv_ref, f32[512,768]{1,0:T(8,128)S(1)} %copy-done.41, bf16[768,1792]{1,0:T(8,128)(2,1)S(1)} %bitcast.114, ...), custom_call_target="tpu_custom_call" | custom-call | flops 5600000000 | tf_op jit(solution)/shard_map/input_grad/pallas_call | solution.py:746
  267.2 2.0 weight_grad.7
  270.7 3.6 %collective-permute-done.69 = bf16[2,192,384]{2,1,0:T(8,128)(2,1)S(1)} collective-permute-done((bf16[2,192,384]{2,1,0:T(8,128)(2,1)S(1)}, bf16[2,192,384]{2,1,0:T(8,128)(2,1)S(1)}, u32[]{:S(2)}, u32[]{:S(2)}) %collective-permute-start.69) | collective-permute-done | bytes 294944 | tf_op jit(solution)/shard_map/ppermute | solution.py:28
  274.3 2.4 collective-permute-done.70
  277.1 2.4 collective-permute-start.73
  281.6 3.2 collective-permute-done.73
  289.1 4.4 %collective-permute-done.76 = bf16[96,1536]{1,0:T(8,128)(2,1)S(1)} collective-permute-done((bf16[96,1536]{1,0:T(8,128)(2,1)S(1)}, bf16[96,1536]{1,0:T(8,128)(2,1)S(1)}, u32[]{:S(2)}, u32[]{:S(2)}) %collective-permute-start.76) | collective-permute-done | bytes 294944 | tf_op jit(solution)/shard_map/ppermute | solution.py:28
  293.4 5.4 %collective-permute-done.78 = bf16[8,24,768]{2,1,0:T(8,128)(2,1)S(1)} collective-permute-done((bf16[8,24,768]{2,1,0:T(8,128)(2,1)}, bf16[8,24,768]{2,1,0:T(8,128)(2,1)S(1)}, u32[]{:S(2)}, u32[]{:S(2)}) %collective-permute-start.78) | collective-permute-done | bytes 294944 | tf_op jit(solution)/shard_map/ppermute | solution.py:28
  304.4 5.1 %collective-permute-done.83 = bf16[1,48,896]{2,1,0:T(8,128)(2,1)S(1)} collective-permute-done((bf16[1,48,896]{2,1,0:T(8,128)(2,1)S(1)}, bf16[1,48,896]{2,1,0:T(8,128)(2,1)S(1)}, u32[]{:S(2)}, u32[]{:S(2)}) %collective-permute-start.83) | collective-permute-done | bytes 86048 | tf_op jit(solution)/shard_map/ppermute | solution.py:28
  310.6 4.2 %collective-permute-done.85 = bf16[2,48,768]{2,1,0:T(8,128)(2,1)S(1)} collective-permute-done((bf16[2,48,768]{2,1,0:T(8,128)(2,1)S(1)}, bf16[2,48,768]{2,1,0:T(8,128)(2,1)S(1)}, u32[]{:S(2)}, u32[]{:S(2)}) %collective-permute-start.85) | collective-permute-done | bytes 147488 | tf_op jit(solution)/shard_map/ppermute | solution.py:28
  317.4 3.0 collective-permute-start.90
  322.5 1.7 collective-permute-done.90
  334.3 1.8 collective-permute-done.95
  (439 shorter events, 132.3 us)
Async XLA Ops:
  1.5 14.3 %collective-permute-start = (bf16[1,24,1536]{2,1,0:T(8,128)(2,1)S(1)}, bf16[1,24,1536]{2,1,0:T(8,128)(2,1)S(1)}, u32[]{:S(2)}, u32[]{:S(2)}) collective-permute-start(bf16[1,24,1536]{2,1,0:T(8,128)(2,1)S(1)} %slice_bitcast_fusion.13), channel_id=1, source_target_pairs={{0,4},{1,5},{2,6},{3,7},{4,0},{5,1},{6,2},{7,3},{8,12},{9,13},{10,... | collective-permute-start | bytes 221192 | tf_op jit(solution)/shard_map/ppermute | solution.py:28
  21.3 9.8 %collective-permute-start.4 = (bf16[4,24,768]{2,1,0:T(8,128)(2,1)S(1)}, bf16[4,24,768]{2,1,0:T(8,128)(2,1)S(1)}, u32[]{:S(2)}, u32[]{:S(2)}) collective-permute-start(bf16[4,24,768]{2,1,0:T(8,128)(2,1)S(1)} %get-tuple-element.442), channel_id=1, source_target_pairs={{0,1},{1,0},{2,3},{3,2},{4,5},{5,4},{6,7},{7,6},{8,9},{9,8},{10,11... | collective-permute-start | bytes 442376 | tf_op jit(solution)/shard_map/ppermute | solution.py:28
  39.0 15.0 %collective-permute-start.6 = (bf16[1,24,3072]{2,1,0:T(8,128)(2,1)S(1)}, bf16[1,24,3072]{2,1,0:T(8,128)(2,1)S(1)}, u32[]{:S(2)}, u32[]{:S(2)}) collective-permute-start(bf16[1,24,3072]{2,1,0:T(8,128)(2,1)S(1)} %bitcast.118), channel_id=1, source_target_pairs={{0,4},{1,5},{2,6},{3,7},{4,0},{5,1},{6,2},{7,3},{8,12},{9,13},{10,... | collective-permute-start | bytes 442376 | tf_op jit(solution)/shard_map/ppermute | solution.py:28
  41.9 13.2 %collective-permute-start.7 = (bf16[4,24,896]{2,1,0:T(8,128)(2,1)S(1)}, bf16[4,24,896]{2,1,0:T(8,128)(2,1)S(1)}, u32[]{:S(2)}, u32[]{:S(2)}) collective-permute-start(bf16[4,24,896]{2,1,0:T(8,128)(2,1)S(1)} %get-tuple-element.210), channel_id=1, source_target_pairs={{0,1},{1,0},{2,3},{3,2},{4,5},{5,4},{6,7},{7,6},{8,9},{9,8},{10,11... | collective-permute-start | bytes 516104 | tf_op jit(solution)/shard_map/ppermute | solution.py:28
  43.5 11.7 %collective-permute-start.8 = (bf16[4,24,896]{2,1,0:T(8,128)(2,1)S(1)}, bf16[4,24,896]{2,1,0:T(8,128)(2,1)S(1)}, u32[]{:S(2)}, u32[]{:S(2)}) collective-permute-start(bf16[4,24,896]{2,1,0:T(8,128)(2,1)S(1)} %get-tuple-element.211), channel_id=1, source_target_pairs={{0,16},{8,24},{16,0},{24,8},{1,17},{9,25},{17,1},{25,9},{2,18},{10... | collective-permute-start | bytes 516104 | tf_op jit(solution)/shard_map/ppermute | solution.py:28
  52.3 10.4 %collective-permute-start.20 = (bf16[2,2,104,128]{3,2,1,0:T(8,128)(2,1)S(1)}, bf16[2,2,104,128]{3,2,1,0:T(8,128)(2,1)S(1)}, u32[]{:S(2)}, u32[]{:S(2)}) collective-permute-start(bf16[2,2,104,128]{3,2,1,0:T(8,128)(2,1)S(1)} %get-tuple-element.229), channel_id=1, source_target_pairs={{0,4},{1,5},{2,6},{3,7},{4,0},{5,1},{6,2},{7,3},{8,12},{9,13},{10,... | collective-permute-start | bytes 319496 | tf_op jit(solution)/shard_map/ppermute | solution.py:43
  65.3 10.4 %collective-permute-start.16 = (bf16[8,24,896]{2,1,0:T(8,128)(2,1)S(1)}, bf16[8,24,896]{2,1,0:T(8,128)(2,1)S(1)}, u32[]{:S(2)}, u32[]{:S(2)}) collective-permute-start(bf16[8,24,896]{2,1,0:T(8,128)(2,1)S(1)} %get-tuple-element.226.refs_4_), channel_id=1, source_target_pairs={{0,1},{1,0},{2,3},{3,2},{4,5},{5,4},{6,7},{7,6},{8,9},{9,8},{10,11... | collective-permute-start | bytes 1032200 | tf_op jit(solution)/shard_map/ppermute | solution.py:28
  73.0 16.1 %collective-permute-start.30 = (bf16[1,96,768]{2,1,0:T(8,128)(2,1)S(1)}, bf16[1,96,768]{2,1,0:T(8,128)(2,1)S(1)}, u32[]{:S(2)}, u32[]{:S(2)}) collective-permute-start(bf16[1,96,768]{2,1,0:T(8,128)(2,1)S(1)} %bitcast.122), channel_id=1, source_target_pairs={{0,4},{1,5},{2,6},{3,7},{4,0},{5,1},{6,2},{7,3},{8,12},{9,13},{10,... | collective-permute-start | bytes 442376 | tf_op jit(solution)/shard_map/ppermute | solution.py:28
  95.4 26.4 %collective-permute-start.34 = (bf16[8,24,1536]{2,1,0:T(8,128)(2,1)S(1)}, bf16[8,24,1536]{2,1,0:T(8,128)(2,1)S(1)}, u32[]{:S(2)}, u32[]{:S(2)}) collective-permute-start(bf16[8,24,1536]{2,1,0:T(8,128)(2,1)S(1)} %pad_maximum_fusion.2.refs_0_), channel_id=1, source_target_pairs={{0,16},{8,24},{16,0},{24,8},{1,17},{9,25},{17,1},{25,9},{2,18},{10... | collective-permute-start | bytes 1769480 | tf_op jit(solution)/shard_map/ppermute | solution.py:28
  97.5 24.3 %collective-permute-start.35 = (bf16[8,24,1536]{2,1,0:T(8,128)(2,1)S(1)}, bf16[8,24,1536]{2,1,0:T(8,128)(2,1)S(1)}, u32[]{:S(2)}, u32[]{:S(2)}) collective-permute-start(bf16[8,24,1536]{2,1,0:T(8,128)(2,1)S(1)} %pad_maximum_fusion.3.refs_4_), channel_id=1, source_target_pairs={{0,1},{1,0},{2,3},{3,2},{4,5},{5,4},{6,7},{7,6},{8,9},{9,8},{10,11... | collective-permute-start | bytes 1769480 | tf_op jit(solution)/shard_map/ppermute | solution.py:28
  98.0 23.9 %collective-permute-start.36 = (bf16[8,24,1536]{2,1,0:T(8,128)(2,1)S(1)}, bf16[8,24,1536]{2,1,0:T(8,128)(2,1)S(1)}, u32[]{:S(2)}, u32[]{:S(2)}) collective-permute-start(bf16[8,24,1536]{2,1,0:T(8,128)(2,1)S(1)} %pad_maximum_fusion.2.refs_0_), channel_id=1, source_target_pairs={{0,8},{8,0},{16,24},{24,16},{1,9},{9,1},{17,25},{25,17},{2,10},{10... | collective-permute-start | bytes 1769480 | tf_op jit(solution)/shard_map/ppermute | solution.py:28
  99.5 22.4 %collective-permute-start.37 = (bf16[8,24,1536]{2,1,0:T(8,128)(2,1)S(1)}, bf16[8,24,1536]{2,1,0:T(8,128)(2,1)S(1)}, u32[]{:S(2)}, u32[]{:S(2)}) collective-permute-start(bf16[8,24,1536]{2,1,0:T(8,128)(2,1)S(1)} %pad_maximum_fusion.3.refs_4_), channel_id=1, source_target_pairs={{0,8},{8,0},{16,24},{24,16},{1,9},{9,1},{17,25},{25,17},{2,10},{10... | collective-permute-start | bytes 1769480 | tf_op jit(solution)/shard_map/ppermute | solution.py:28
  109.8 12.0 %collective-permute-start.28 = (bf16[4,2,104,128]{3,2,1,0:T(8,128)(2,1)}, bf16[4,2,104,128]{3,2,1,0:T(8,128)(2,1)}, u32[]{:S(2)}, u32[]{:S(2)}) collective-permute-start(bf16[4,2,104,128]{3,2,1,0:T(8,128)(2,1)} %pad_maximum_fusion.19), channel_id=1, source_target_pairs={{0,1},{1,0},{2,3},{3,2},{4,5},{5,4},{6,7},{7,6},{8,9},{9,8},{10,11... | collective-permute-start | bytes 638984 | tf_op jit(solution)/shard_map/ppermute | solution.py:28
  123.1 10.3 %collective-permute-start.40 = (bf16[4,96,384]{2,1,0:T(8,128)(2,1)S(1)}, bf16[4,96,384]{2,1,0:T(8,128)(2,1)S(1)}, u32[]{:S(2)}, u32[]{:S(2)}) collective-permute-start(bf16[4,96,384]{2,1,0:T(8,128)(2,1)S(1)} %get-tuple-element.275), channel_id=1, source_target_pairs={{0,1},{1,0},{2,3},{3,2},{4,5},{5,4},{6,7},{7,6},{8,9},{9,8},{10,11... | collective-permute-start | bytes 884744 | tf_op jit(solution)/shard_map/ppermute | solution.py:28
  123.2 10.2 %collective-permute-start.41 = (bf16[4,96,384]{2,1,0:T(8,128)(2,1)S(1)}, bf16[4,96,384]{2,1,0:T(8,128)(2,1)S(1)}, u32[]{:S(2)}, u32[]{:S(2)}) collective-permute-start(bf16[4,96,384]{2,1,0:T(8,128)(2,1)S(1)} %get-tuple-element.276), channel_id=1, source_target_pairs={{0,16},{8,24},{16,0},{24,8},{1,17},{9,25},{17,1},{25,9},{2,18},{10... | collective-permute-start | bytes 884744 | tf_op jit(solution)/shard_map/ppermute | solution.py:28
  125.6 9.6 %collective-permute-start.38 = (bf16[8,24,1536]{2,1,0:T(8,128)(2,1)S(1)}, bf16[8,24,1536]{2,1,0:T(8,128)(2,1)S(1)}, u32[]{:S(2)}, u32[]{:S(2)}) collective-permute-start(bf16[8,24,1536]{2,1,0:T(8,128)(2,1)S(1)} %collective-permute-done.34.refs_1_), channel_id=1, source_target_pairs={{0,8},{8,0},{16,24},{24,16},{1,9},{9,1},{17,25},{25,17},{2,10},{10... | collective-permute-start | bytes 1769480 | tf_op jit(solution)/shard_map/ppermute | solution.py:28
  125.6 10.1 %collective-permute-start.39 = (bf16[8,24,1536]{2,1,0:T(8,128)(2,1)S(1)}, bf16[8,24,1536]{2,1,0:T(8,128)(2,1)S(1)}, u32[]{:S(2)}, u32[]{:S(2)}) collective-permute-start(bf16[8,24,1536]{2,1,0:T(8,128)(2,1)S(1)} %collective-permute-done.35.refs_5_), channel_id=1, source_target_pairs={{0,8},{8,0},{16,24},{24,16},{1,9},{9,1},{17,25},{25,17},{2,10},{10... | collective-permute-start | bytes 1769480 | tf_op jit(solution)/shard_map/ppermute | solution.py:28
  133.6 15.3 %collective-permute-start.42 = (bf16[8,96,384]{2,1,0:T(8,128)(2,1)S(1)}, bf16[8,96,384]{2,1,0:T(8,128)(2,1)S(1)}, u32[]{:S(2)}, u32[]{:S(2)}) collective-permute-start(bf16[8,96,384]{2,1,0:T(8,128)(2,1)S(1)} %pad_maximum_fusion.5.refs_0_), channel_id=1, source_target_pairs={{0,16},{8,24},{16,0},{24,8},{1,17},{9,25},{17,1},{25,9},{2,18},{10... | collective-permute-start | bytes 1769480 | tf_op jit(solution)/shard_map/ppermute | solution.py:28
  133.8 15.1 %collective-permute-start.43 = (bf16[8,96,384]{2,1,0:T(8,128)(2,1)S(1)}, bf16[8,96,384]{2,1,0:T(8,128)(2,1)S(1)}, u32[]{:S(2)}, u32[]{:S(2)}) collective-permute-start(bf16[8,96,384]{2,1,0:T(8,128)(2,1)S(1)} %pad_maximum_fusion.6.refs_4_), channel_id=1, source_target_pairs={{0,1},{1,0},{2,3},{3,2},{4,5},{5,4},{6,7},{7,6},{8,9},{9,8},{10,11... | collective-permute-start | bytes 1769480 | tf_op jit(solution)/shard_map/ppermute | solution.py:28
  135.2 13.7 %collective-permute-start.44 = (bf16[8,96,384]{2,1,0:T(8,128)(2,1)S(1)}, bf16[8,96,384]{2,1,0:T(8,128)(2,1)S(1)}, u32[]{:S(2)}, u32[]{:S(2)}) collective-permute-start(bf16[8,96,384]{2,1,0:T(8,128)(2,1)S(1)} %pad_maximum_fusion.5.refs_0_), channel_id=1, source_target_pairs={{0,8},{8,0},{16,24},{24,16},{1,9},{9,1},{17,25},{25,17},{2,10},{10... | collective-permute-start | bytes 1769480 | tf_op jit(solution)/shard_map/ppermute | solution.py:28
  135.2 13.7 %collective-permute-start.45 = (bf16[8,96,384]{2,1,0:T(8,128)(2,1)S(1)}, bf16[8,96,384]{2,1,0:T(8,128)(2,1)S(1)}, u32[]{:S(2)}, u32[]{:S(2)}) collective-permute-start(bf16[8,96,384]{2,1,0:T(8,128)(2,1)S(1)} %pad_maximum_fusion.6.refs_4_), channel_id=1, source_target_pairs={{0,8},{8,0},{16,24},{24,16},{1,9},{9,1},{17,25},{25,17},{2,10},{10... | collective-permute-start | bytes 1769480 | tf_op jit(solution)/shard_map/ppermute | solution.py:28
  149.5 47.3 %collective-permute-start.53 = (bf16[512,3072]{1,0:T(8,128)(2,1)S(1)}, bf16[512,3072]{1,0:T(8,128)(2,1)}, u32[]{:S(2)}, u32[]{:S(2)}) collective-permute-start(bf16[512,3072]{1,0:T(8,128)(2,1)S(1)} %get-tuple-element.272.gelu_ref.refs_0_), channel_id=1, source_target_pairs={{0,8},{8,0},{16,24},{24,16},{1,9},{9,1},{17,25},{25,17},{2,10},{10... | collective-permute-start | bytes 9437192 | tf_op jit(solution)/shard_map/ppermute | solution.py:28
  164.7 32.1 %collective-permute-start.54 = (bf16[512,384]{1,0:T(8,128)(2,1)}, bf16[512,384]{1,0:T(8,128)(2,1)}, u32[]{:S(2)}, u32[]{:S(2)}) collective-permute-start(bf16[512,384]{1,0:T(8,128)(2,1)} %get-tuple-element.305), channel_id=1, source_target_pairs={{0,8},{8,0},{16,24},{24,16},{1,9},{9,1},{17,25},{25,17},{2,10},{10... | collective-permute-start | bytes 1179656 | tf_op jit(solution)/shard_map/ppermute | solution.py:28
  164.9 40.9 %collective-permute-start.55 = (bf16[512,1536]{1,0:T(8,128)(2,1)}, bf16[512,1536]{1,0:T(8,128)(2,1)}, u32[]{:S(2)}, u32[]{:S(2)}) collective-permute-start(bf16[512,1536]{1,0:T(8,128)(2,1)} %get-tuple-element.307), channel_id=1, source_target_pairs={{0,8},{8,0},{16,24},{24,16},{1,9},{9,1},{17,25},{25,17},{2,10},{10... | collective-permute-start | bytes 4718600 | tf_op jit(solution)/shard_map/ppermute | solution.py:28
  191.3 14.5 %collective-permute-start.52 = (bf16[512,768]{1,0:T(8,128)(2,1)}, bf16[512,768]{1,0:T(8,128)(2,1)S(1)}, u32[]{:S(2)}, u32[]{:S(2)}) collective-permute-start(bf16[512,768]{1,0:T(8,128)(2,1)} %copy-done.30), channel_id=1, source_target_pairs={{0,8},{8,0},{16,24},{24,16},{1,9},{9,1},{17,25},{25,17},{2,10},{10... | collective-permute-start | bytes 2359304 | tf_op jit(solution)/shard_map/ppermute | solution.py:28
  195.3 15.8 %collective-permute-start.51 = (bf16[4,2,104,128]{3,2,1,0:T(8,128)(2,1)S(1)}, bf16[4,2,104,128]{3,2,1,0:T(8,128)(2,1)S(1)}, u32[]{:S(2)}, u32[]{:S(2)}) collective-permute-start(bf16[4,2,104,128]{3,2,1,0:T(8,128)(2,1)S(1)} %pad_maximum_fusion.20), channel_id=1, source_target_pairs={{0,1},{1,0},{2,3},{3,2},{4,5},{5,4},{6,7},{7,6},{8,9},{9,8},{10,11... | collective-permute-start | bytes 638984 | tf_op jit(solution)/shard_map/ppermute | solution.py:28
  205.2 31.4 %collective-permute-start.56 = (bf16[8,192,384]{2,1,0:T(8,128)(2,1)S(1)}, bf16[8,192,384]{2,1,0:T(8,128)(2,1)S(1)}, u32[]{:S(2)}, u32[]{:S(2)}) collective-permute-start(bf16[8,192,384]{2,1,0:T(8,128)(2,1)S(1)} %slice_bitcast_fusion.1), channel_id=1, source_target_pairs={{0,16},{8,24},{16,0},{24,8},{1,17},{9,25},{17,1},{25,9},{2,18},{10... | collective-permute-start | bytes 3538952 | tf_op jit(solution)/shard_map/ppermute | solution.py:28
  210.5 26.1 %collective-permute-start.57 = (bf16[4,96,1536]{2,1,0:T(8,128)(2,1)S(1)}, bf16[4,96,1536]{2,1,0:T(8,128)(2,1)S(1)}, u32[]{:S(2)}, u32[]{:S(2)}) collective-permute-start(bf16[4,96,1536]{2,1,0:T(8,128)(2,1)S(1)} %slice_bitcast_fusion), channel_id=1, source_target_pairs={{0,1},{1,0},{2,3},{3,2},{4,5},{5,4},{6,7},{7,6},{8,9},{9,8},{10,11... | collective-permute-start | bytes 3538952 | tf_op jit(solution)/shard_map/ppermute | solution.py:28
  211.4 14.0 %collective-permute-start.62 = (bf16[2,2,104,128]{3,2,1,0:T(8,128)(2,1)S(1)}, bf16[2,2,104,128]{3,2,1,0:T(8,128)(2,1)S(1)}, u32[]{:S(2)}, u32[]{:S(2)}) collective-permute-start(bf16[2,2,104,128]{3,2,1,0:T(8,128)(2,1)S(1)} %get-tuple-element.326), channel_id=1, source_target_pairs={{0,2},{1,3},{2,0},{3,1},{4,6},{5,7},{6,4},{7,5},{8,10},{9,11},{10,... | collective-permute-start | bytes 319496 | tf_op jit(solution)/shard_map/ppermute | solution.py:43
  212.6 12.9 %collective-permute-start.63 = (bf16[2,2,104,128]{3,2,1,0:T(8,128)(2,1)S(1)}, bf16[2,2,104,128]{3,2,1,0:T(8,128)(2,1)S(1)}, u32[]{:S(2)}, u32[]{:S(2)}) collective-permute-start(bf16[2,2,104,128]{3,2,1,0:T(8,128)(2,1)S(1)} %get-tuple-element.327), channel_id=1, source_target_pairs={{0,4},{1,5},{2,6},{3,7},{4,0},{5,1},{6,2},{7,3},{8,12},{9,13},{10,... | collective-permute-start | bytes 319496 | tf_op jit(solution)/shard_map/ppermute | solution.py:43
  214.8 11.3 %collective-permute-start.64 = (bf16[2,2,104,128]{3,2,1,0:T(8,128)(2,1)S(1)}, bf16[2,2,104,128]{3,2,1,0:T(8,128)(2,1)S(1)}, u32[]{:S(2)}, u32[]{:S(2)}) collective-permute-start(bf16[2,2,104,128]{3,2,1,0:T(8,128)(2,1)S(1)} %get-tuple-element.328), channel_id=1, source_target_pairs={{0,6},{1,7},{2,4},{3,5},{4,2},{5,3},{6,0},{7,1},{8,14},{9,15},{10,... | collective-permute-start | bytes 319496 | tf_op jit(solution)/shard_map/ppermute | solution.py:43
  225.4 12.4 %collective-permute-start.60 = (bf16[512,768]{1,0:T(8,128)(2,1)S(1)}, bf16[512,768]{1,0:T(8,128)(2,1)S(1)}, u32[]{:S(2)}, u32[]{:S(2)}) collective-permute-start(bf16[512,768]{1,0:T(8,128)(2,1)S(1)} %copy-done.27), channel_id=1, source_target_pairs={{0,8},{8,0},{16,24},{24,16},{1,9},{9,1},{17,25},{25,17},{2,10},{10... | collective-permute-start | bytes 2359304 | tf_op jit(solution)/shard_map/ppermute | solution.py:28
  225.5 12.3 %collective-permute-start.58 = (bf16[512,768]{1,0:T(8,128)(2,1)S(1)}, bf16[512,768]{1,0:T(8,128)(2,1)S(1)}, u32[]{:S(2)}, u32[]{:S(2)}) collective-permute-start(bf16[512,768]{1,0:T(8,128)(2,1)S(1)} %copy-done.29), channel_id=1, source_target_pairs={{0,8},{8,0},{16,24},{24,16},{1,9},{9,1},{17,25},{25,17},{2,10},{10... | collective-permute-start | bytes 2359304 | tf_op jit(solution)/shard_map/ppermute | solution.py:28
  226.1 11.7 %collective-permute-start.59 = (bf16[512,384]{1,0:T(8,128)(2,1)S(1)}, bf16[512,384]{1,0:T(8,128)(2,1)S(1)}, u32[]{:S(2)}, u32[]{:S(2)}) collective-permute-start(bf16[512,384]{1,0:T(8,128)(2,1)S(1)} %copy-done.33), channel_id=1, source_target_pairs={{0,8},{8,0},{16,24},{24,16},{1,9},{9,1},{17,25},{25,17},{2,10},{10... | collective-permute-start | bytes 1179656 | tf_op jit(solution)/shard_map/ppermute | solution.py:28
  241.1 17.6 %collective-permute-start.68 = (bf16[8,48,896]{2,1,0:T(8,128)(2,1)S(1)}, bf16[8,48,896]{2,1,0:T(8,128)(2,1)S(1)}, u32[]{:S(2)}, u32[]{:S(2)}) collective-permute-start(bf16[8,48,896]{2,1,0:T(8,128)(2,1)S(1)} %slice_bitcast_fusion.4), channel_id=1, source_target_pairs={{0,16},{8,24},{16,0},{24,8},{1,17},{9,25},{17,1},{25,9},{2,18},{10... | collective-permute-start | bytes 2064392 | tf_op jit(solution)/shard_map/ppermute | solution.py:28
  242.0 15.2 %collective-permute-start.66 = (bf16[4,192,384]{2,1,0:T(8,128)(2,1)S(1)}, bf16[4,192,384]{2,1,0:T(8,128)(2,1)S(1)}, u32[]{:S(2)}, u32[]{:S(2)}) collective-permute-start(bf16[4,192,384]{2,1,0:T(8,128)(2,1)S(1)} %get-tuple-element.315), channel_id=1, source_target_pairs={{0,1},{1,0},{2,3},{3,2},{4,5},{5,4},{6,7},{7,6},{8,9},{9,8},{10,11... | collective-permute-start | bytes 1769480 | tf_op jit(solution)/shard_map/ppermute | solution.py:28
  243.5 14.9 %collective-permute-start.67 = (bf16[2,96,1536]{2,1,0:T(8,128)(2,1)S(1)}, bf16[2,96,1536]{2,1,0:T(8,128)(2,1)S(1)}, u32[]{:S(2)}, u32[]{:S(2)}) collective-permute-start(bf16[2,96,1536]{2,1,0:T(8,128)(2,1)S(1)} %get-tuple-element.316), channel_id=1, source_target_pairs={{0,2},{1,3},{2,0},{3,1},{4,6},{5,7},{6,4},{7,5},{8,10},{9,11},{10,... | collective-permute-start | bytes 1769480 | tf_op jit(solution)/shard_map/ppermute | solution.py:28
  248.6 18.7 %collective-permute-start.72 = (bf16[512,768]{1,0:T(8,128)(2,1)S(1)}, bf16[512,768]{1,0:T(8,128)(2,1)S(1)}, u32[]{:S(2)}, u32[]{:S(2)}) collective-permute-start(bf16[512,768]{1,0:T(8,128)(2,1)S(1)} %get-tuple-element.405), channel_id=1, source_target_pairs={{0,8},{8,0},{16,24},{24,16},{1,9},{9,1},{17,25},{25,17},{2,10},{10... | collective-permute-start | bytes 2359304 | tf_op jit(solution)/shard_map/ppermute | solution.py:28
  259.1 17.6 %collective-permute-start.71 = (bf16[4,48,896]{2,1,0:T(8,128)(2,1)S(1)}, bf16[4,48,896]{2,1,0:T(8,128)(2,1)S(1)}, u32[]{:S(2)}, u32[]{:S(2)}) collective-permute-start(bf16[4,48,896]{2,1,0:T(8,128)(2,1)S(1)} %get-tuple-element.334), channel_id=1, source_target_pairs={{0,1},{1,0},{2,3},{3,2},{4,5},{5,4},{6,7},{7,6},{8,9},{9,8},{10,11... | collective-permute-start | bytes 1032200 | tf_op jit(solution)/shard_map/ppermute | solution.py:28
  260.7 13.6 %collective-permute-start.69 = (bf16[2,192,384]{2,1,0:T(8,128)(2,1)S(1)}, bf16[2,192,384]{2,1,0:T(8,128)(2,1)S(1)}, u32[]{:S(2)}, u32[]{:S(2)}) collective-permute-start(bf16[2,192,384]{2,1,0:T(8,128)(2,1)S(1)} %get-tuple-element.332), channel_id=1, source_target_pairs={{0,2},{1,3},{2,0},{3,1},{4,6},{5,7},{6,4},{7,5},{8,10},{9,11},{10,... | collective-permute-start | bytes 884744 | tf_op jit(solution)/shard_map/ppermute | solution.py:28
  261.6 15.1 %collective-permute-start.70 = (bf16[1,96,1536]{2,1,0:T(8,128)(2,1)S(1)}, bf16[1,96,1536]{2,1,0:T(8,128)(2,1)S(1)}, u32[]{:S(2)}, u32[]{:S(2)}) collective-permute-start(bf16[1,96,1536]{2,1,0:T(8,128)(2,1)S(1)} %add_convert_fusion.3), channel_id=1, source_target_pairs={{0,4},{1,5},{2,6},{3,7},{4,0},{5,1},{6,2},{7,3},{8,12},{9,13},{10,... | collective-permute-start | bytes 884744 | tf_op jit(solution)/shard_map/ppermute | solution.py:28
  279.4 9.6 %collective-permute-start.74 = (bf16[96,1536]{1,0:T(8,128)(2,1)S(1)}, bf16[96,1536]{1,0:T(8,128)(2,1)S(1)}, u32[]{:S(2)}, u32[]{:S(2)}) collective-permute-start(bf16[96,1536]{1,0:T(8,128)(2,1)S(1)} %fusion.19), channel_id=1, source_target_pairs={{0,16},{8,24},{16,0},{24,8},{1,17},{9,25},{17,1},{25,9},{2,18},{10... | collective-permute-start | bytes 884744 | tf_op jit(solution)/shard_map/ppermute | solution.py:28
  280.3 13.1 %collective-permute-start.76 = (bf16[96,1536]{1,0:T(8,128)(2,1)S(1)}, bf16[96,1536]{1,0:T(8,128)(2,1)S(1)}, u32[]{:S(2)}, u32[]{:S(2)}) collective-permute-start(bf16[96,1536]{1,0:T(8,128)(2,1)S(1)} %fusion.19), channel_id=1, source_target_pairs={{0,24},{8,16},{16,8},{24,0},{1,25},{9,17},{17,9},{25,1},{2,26},{10... | collective-permute-start | bytes 884744 | tf_op jit(solution)/shard_map/ppermute | solution.py:28
  284.8 14.0 %collective-permute-start.78 = (bf16[8,24,768]{2,1,0:T(8,128)(2,1)}, bf16[8,24,768]{2,1,0:T(8,128)(2,1)S(1)}, u32[]{:S(2)}, u32[]{:S(2)}) collective-permute-start(bf16[8,24,768]{2,1,0:T(8,128)(2,1)} %slice_bitcast_fusion.12), channel_id=1, source_target_pairs={{0,16},{8,24},{16,0},{24,8},{1,17},{9,25},{17,1},{25,9},{2,18},{10... | collective-permute-start | bytes 884744 | tf_op jit(solution)/shard_map/ppermute | solution.py:28
  286.3 12.5 %collective-permute-start.79 = (bf16[4,48,768]{2,1,0:T(8,128)(2,1)}, bf16[4,48,768]{2,1,0:T(8,128)(2,1)S(1)}, u32[]{:S(2)}, u32[]{:S(2)}) collective-permute-start(bf16[4,48,768]{2,1,0:T(8,128)(2,1)} %slice_bitcast_fusion.11), channel_id=1, source_target_pairs={{0,1},{1,0},{2,3},{3,2},{4,5},{5,4},{6,7},{7,6},{8,9},{9,8},{10,11... | collective-permute-start | bytes 884744 | tf_op jit(solution)/shard_map/ppermute | solution.py:28
  300.1 10.5 %collective-permute-start.80 = (bf16[192,384]{1,0:T(8,128)(2,1)S(1)}, bf16[192,384]{1,0:T(8,128)(2,1)S(1)}, u32[]{:S(2)}, u32[]{:S(2)}) collective-permute-start(bf16[192,384]{1,0:T(8,128)(2,1)S(1)} %fusion.28), channel_id=1, source_target_pairs={{0,16},{8,24},{16,0},{24,8},{1,17},{9,25},{17,1},{25,9},{2,18},{10... | collective-permute-start | bytes 442376 | tf_op jit(solution)/shard_map/ppermute | solution.py:28
  300.9 9.6 %collective-permute-start.81 = (bf16[192,384]{1,0:T(8,128)(2,1)S(1)}, bf16[192,384]{1,0:T(8,128)(2,1)S(1)}, u32[]{:S(2)}, u32[]{:S(2)}) collective-permute-start(bf16[192,384]{1,0:T(8,128)(2,1)S(1)} %fusion.28), channel_id=1, source_target_pairs={{0,8},{8,0},{16,24},{24,16},{1,9},{9,1},{17,25},{25,17},{2,10},{10... | collective-permute-start | bytes 442376 | tf_op jit(solution)/shard_map/ppermute | solution.py:28
  301.0 9.6 %collective-permute-start.82 = (bf16[192,384]{1,0:T(8,128)(2,1)S(1)}, bf16[192,384]{1,0:T(8,128)(2,1)S(1)}, u32[]{:S(2)}, u32[]{:S(2)}) collective-permute-start(bf16[192,384]{1,0:T(8,128)(2,1)S(1)} %fusion.28), channel_id=1, source_target_pairs={{0,24},{8,16},{16,8},{24,0},{1,25},{9,17},{17,9},{25,1},{2,26},{10... | collective-permute-start | bytes 442376 | tf_op jit(solution)/shard_map/ppermute | solution.py:28
  (120 other events, 920.3 us)

commit v2 on v1

--- a/solution.py
+++ b/solution.py
@@ -36,12 +36,15 @@
     return lax.optimization_barrier((x,) + others)[0]
 
 
-def trade(pieces):
-    size = lax.axis_size("fsdp")
-    far = [pieces[0]]
-    for m in range(1, size // 2):
-        far.append(lax.ppermute(pieces[m], "fsdp", [(i, i ^ (2 * m)) for i in range(size)]))
-    return far, exchange(jnp.concatenate([x[1:] for x in far], axis=0), "fsdp", 0)
+def trade_stages(pieces):
+    bits = axis_bits("fsdp")[1:]
+    requests = []
+    for m in range(1, len(pieces)):
+        requests.append((pieces[m], "fsdp") + tuple(b for n, (_, b) in enumerate(bits) if m >> n & 1))
+    arrived = yield requests
+    far = [pieces[0]] + list(arrived)
+    (near,) = yield [(jnp.concatenate([x[1:] for x in far], axis=0), "fsdp", 0)]
+    return far, near
 
 
 def near_steps(first_low):
@@ -54,7 +57,7 @@
     return tuple(m ^ step for m in masks)
 
 
-def gather_stages(shard):
+def gather_stages(shard, early=False):
     lin = lax.axis_index("group") * lax.axis_size("fsdp") + lax.axis_index("fsdp")
     rows, columns = shard.shape
     if rows % 8:
@@ -80,33 +83,46 @@
             for (b, m), st, o in zip(sides, steps, others)
         ]
     core = ("group", 0)
-    others = yield [(b,) + st[-1] for (b, _), st in zip(sides, steps)] + [
-        (b,) + core for b, _ in sides
+    others = yield [(b,) + st[-1] for (b, _), st in zip(sides, steps)] + (
+        [(b,) + core for b, _ in sides] if early else []
+    )
+    parts = []
+    if early:
+        lasts = yield [(o,) + core for o in others[:2]]
+        for n, ((b, m), st) in enumerate(zip(sides, steps)):
+            there = moved(m, *st[-1])
+            parts.append([
+                (b, m), (others[n], there), (others[n + 2], moved(m, *core)),
+                (lasts[n], moved(there, *core)),
+            ])
+        return parts, lin
+    sides = [
+        (jnp.concatenate([b, o], axis=0), m + moved(m, *st[-1]))
+        for (b, m), st, o in zip(sides, steps, others)
     ]
-    parts = []
-    for (b, m), st, o, c in zip(sides, steps, others, others[2:]):
-        parts.append([(b, m), (o, moved(m, *st[-1])), (c, moved(m, *core))])
-    lasts = yield [(part[1][0],) + core for part in parts]
-    for part, last in zip(parts, lasts):
-        part.append((last, moved(part[1][1], *core)))
-    return parts, lin
+    lasts = yield [(b,) + core for b, _ in sides]
+    return [[(b, m), (last, moved(m, *core))] for (b, m), last in zip(sides, lasts)], lin
 
 
 class Pipeline:
     def __init__(self):
         self.running = {}
+        self.waiting = {}
         self.finished = {}
         self.started = ()
 
     def add(self, name, stages):
         self.running[name] = (stages, None)
 
-    def slot(self, *others, only=None):
-        names = [n for n in self.running if only is None or n in only]
+    def names(self, only):
+        return [n for n in self.running if only is None or n in only]
+
+    def arrive(self, *others, only=None):
+        names = [n for n in self.names(only) if n not in self.waiting]
         arrived = [x for n in names for x in self.running[n][1] or ()]
         if arrived:
             arrived = lax.optimization_barrier(tuple(arrived) + others)[: len(arrived)]
-        at, requests = 0, []
+        at, ready = 0, ()
         for n in names:
             stages, results = self.running.pop(n)
             count = len(results or ())
@@ -117,14 +133,24 @@
                 self.finished[n] = done.value
             else:
                 self.running[n] = (stages, ())
-                requests += [(n, w) for w in wanted]
+                self.waiting[n] = wanted
+                ready += tuple(w[0] for w in wanted)
+        self.started = ready or self.started
+
+    def slot(self, *others, only=None):
+        self.arrive(*others, only=only)
+        requests = [(n, w) for n in self.names(only) for w in self.waiting.pop(n)]
         operands = tuple(w[0] for _, w in requests)
         if operands and others:
             operands = lax.optimization_barrier(operands + others)[: len(operands)]
-        self.started = operands
+        self.started = operands or self.started
         for x, (n, (_, axis, *bits)) in zip(operands, requests):
             stages, results = self.running[n]
             self.running[n] = (stages, results + (exchange(x, axis, *bits),))
+
+    def read(self, name, *others):
+        self.arrive(*others, only=(name,))
+        return self.finished[name]
 
     def finish(self, name, *others, only=None):
         while name not in self.finished:
@@ -139,12 +165,12 @@
 COSTS = {
     "assemble": 1.5, "project": 5.4, "mix_segments": 1.1, "intra_forward": 5.9, "inter_forward": 5.5,
     "expand": 9.5, "contract": 10.5, "back_to_heads": 11.8, "intra_backward": 10.3,
-    "inter_backward": 4.6, "input_grad": 4.0, "weight_grad": 4.0,
+    "inter_backward": 4.6, "input_grad": 4.0, "weight_grad": 4.0, "vector_rows": 1.5,
 }
-FLOPS_PER_US = 1.4e9
-
-
-def call(kernel, name, outs, in_specs, scratch=(), mib=12):
+FLOPS_PER_US = 6.0e8
+
+
+def call(kernel, name, outs, in_specs, scratch=(), mib=8):
     return pl.pallas_call(
         kernel,
         out_shape=outs,
@@ -566,6 +592,14 @@
                dres1_ref, dmix_ref, dmix_half_ref, dnum_ref, dden_ref, sums_ref, *refs):
         inc_refs, (state_scr, norm_scr) = refs[:-2], refs[-2:]
         sums_ref[...] = sums_in_ref[...]
+        share = D // fsdp
+        for j in range(fsdp):
+            for c in range(ff // D):
+                at = (j * (ff // D) + c) * share
+                m, lane = B_UP + at // D, at % D
+                sums_ref[B_UP + c : B_UP + c + 1, share * j : share * (j + 1)] = sums_in_ref[
+                    m : m + 1, lane : lane + share
+                ]
         norm_scr[...] = jnp.zeros_like(norm_scr)
         ones = head_ones()
         twice = jnp.concatenate([ones, ones], axis=0)
@@ -811,8 +845,13 @@
     return (a.astype(f32) + b.astype(f32)).astype(bf16)
 
 
-def halving_stages(keep, send):
-    for axis, bit in axis_bits("fsdp"):
+def core_stage(x):
+    (other,) = yield [(x, "group", 0)]
+    return other
+
+
+def halving_stages(keep, send, bits):
+    for axis, bit in bits:
         (received,) = yield [(send, axis, bit)]
         half = keep.shape[0] // 2
         if half == 0:
@@ -820,41 +859,39 @@
         keep, send = add_low(keep[:half], received[:half]), add_low(keep[half:], received[half:])
 
 
-def reduce_stages(x, core):
+def reduce_stages(x, core, large=False):
     half = x.shape[1] // 2
-    x = yield from halving_stages(x[0, :half], x[0, half:])
-    bits = axis_bits("group")[1:]
-    for axis, bit in bits[:-1]:
+    bits = axis_bits("fsdp")
+    keep, send = x[0, :half], x[0, half:]
+    if large and half > 1:
+        quarter = half // 2
+        axis, bit = bits.pop(0)
+        (received,) = yield [(send[quarter:], axis, bit)]
+        after = add_low(keep[quarter:], received)
+        (received,) = yield [(tie(send[:quarter], after), axis, bit)]
+        keep, send = add_low(keep[:quarter], received), after
+    x = yield from halving_stages(keep, send, bits)
+    for axis, bit in axis_bits("group")[1:]:
         (received,) = yield [(x, axis, bit)]
         x = add_low(x, received)
-    if not bits:
-        return (yield from core_stages(x, core))
-    axis, bit = bits[-1]
-    above, beside, across = yield [(x, axis, bit), (x, axis, 0), (x, axis, bit, 0)]
-    mine = x.astype(f32) + above.astype(f32)
-    theirs = beside.astype(f32) + across.astype(f32)
-    return ordered(mine, theirs, core == 0, -1)
+    other = yield from core_stage(x)
+    return ordered(x, other, core == 0, -1).astype(f32)
 
 
 def share_stages(x, core, chip):
     axis, bit = axis_bits("group")[1]
     half = x.shape[1] // 2
     (received,) = yield [(x[1], axis, bit)]
-    keep = add_low(x[0, :half], received[:half])
-    x = yield from halving_stages(keep, add_low(x[0, half:], received[half:]))
-    above, beside, across = yield [(x, axis, bit), (x, axis, 0), (x, axis, bit, 0)]
-    mine = ordered(x, above, chip == 0, 0)
-    theirs = ordered(beside, across, chip == 0, 0)
-    return ordered(mine, theirs, core == 0, -1).astype(f32)
+    keep, send = add_low(x[0, :half], received[:half]), add_low(x[0, half:], received[half:])
+    x = yield from halving_stages(keep, send, axis_bits("fsdp"))
+    (other,) = yield [(x, axis, bit)]
+    x = ordered(x, other, chip == 0, 0)
+    other = yield from core_stage(x)
+    return ordered(x, other, core == 0, -1).astype(f32)
 
 
 def ordered(x, other, first, axis):
     return jnp.concatenate([jnp.where(first, x, other), jnp.where(first, other, x)], axis=axis)
-
-
-def core_stages(x, core):
-    (other,) = yield [(x, "group", 0)]
-    return ordered(x, other, core == 0, -1).astype(f32)
 
 
 def ancestor_matrix(parents):
@@ -885,30 +922,35 @@
     return jnp.cos(angle), jnp.sin(angle)
 
 
-def gap_wave():
-    position = jnp.arange(SEG, dtype=jnp.int32)
+def gap_wave(position):
     gap = position[:, None] - position[None, :]
     wave = jnp.cos(gap.astype(f32) * (math.pi / (2.0 * HORIZON)))
     return jnp.where(gap >= 0, wave, 0.0), jnp.where(gap <= 0, wave, 0.0)
 
 
-def vector_columns(vectors, wide):
-    rows = vectors[0].shape[0]
-    columns = jnp.concatenate([jnp.stack(vectors, axis=1), wide.reshape(-1, rows).T], axis=1)
-    return jnp.pad(columns, ((0, 0), (0, LANES - columns.shape[1])))
-
-
-def vector_rows(columns, rows, longer):
-    turned = columns[:, :16].T.astype(f32)
-    wide = turned[B_UP : B_UP + longer].reshape(longer, -1, rows)
-    wide = jnp.swapaxes(wide, 0, 1).reshape(longer, D)
-    return jnp.concatenate([turned[:B_UP], wide, turned[B_UP + longer :]], axis=0)
-
-
-def wide_by_block(sums, fsdp, longer):
-    wide = sums[B_UP : B_UP + longer].reshape(fsdp, longer, D // fsdp)
-    wide = jnp.swapaxes(wide, 0, 1).reshape(longer, D)
-    return jnp.concatenate([sums[:B_UP], wide, sums[B_UP + longer :]], axis=0)
+def vector_columns(vectors):
+    return jnp.pad(jnp.stack(vectors), ((0, LANES - len(vectors)), (0, 0))).T
+
+
+def wide_row(shard, rows):
+    return jnp.pad(shard[None], ((0, rows - 1), (0, LANES - shard.shape[0])))
+
+
+def vector_rows(weight, rows, share, longer):
+    per = D // share
+
+    def kernel(w_ref, out_ref):
+        out_ref[...] = jnp.zeros_like(out_ref)
+        turned = w_ref[:, D:OUT_AT].astype(f32).T
+        out_ref[:B_UP, :] = turned[:B_UP, :]
+        for block in range(longer * per):
+            m, lane = B_UP + block // per, share * (block % per)
+            first = rows * block // 8 * 8
+            tile = w_ref[first : first + 8, OUT_AT + D :].astype(f32)
+            row = rows * block - first
+            out_ref[m : m + 1, lane : lane + share] = tile[row : row + 1, :share]
+
+    return call(kernel, "vector_rows", shape_of((16, D), f32), [VMEM])(weight)
 
 
 def body(
@@ -925,7 +967,15 @@
     ff = w_up.shape[1]
     ids = jnp.stack([core, chip, own]).astype(jnp.int32)
 
-    ancestry = ancestor_matrix(parent_seg[0])
+    pipe = Pipeline()
+    pipe.add("kv", gather_stages(w_qkv[:, D:], True))
+    pipe.add("tokens", core_stage(tokens))
+    pipe.slot()
+    pipe.slot(only=("kv",))
+    begun = pipe.started[0]
+    tokens_other = pipe.read("tokens", begun)
+
+    ancestry = ancestor_matrix(tie(parent_seg[0], begun))
     count = parent_seg.shape[1]
     place = jnp.arange(count, dtype=jnp.int32)
     there = (own ^ (place // segs)) * segs + place % segs
@@ -933,59 +983,70 @@
     local = jnp.dot(jnp.dot(select, ancestry), select.T)
     from_ancestors, from_descendants = spread_rows(local), spread_rows(local.T)
     cos, sin = waves(local, segs)
-    wave, wave_t = gap_wave()
-
-    pipe = Pipeline()
-    pipe.add("kv", gather_stages(w_qkv[:, D:]))
-    pipe.slot()
-    columns = vector_columns(
-        (b_out, norm1_gain, norm1_bias, b_down, norm2_gain, norm2_bias), b_up
-    )
-    pipe.add("qo", gather_stages(jnp.concatenate([w_qkv[:, :D], columns, w_out, columns], axis=1)))
+    wave, wave_t = gap_wave(tie(jnp.arange(SEG, dtype=jnp.int32), begun))
+    shard_rows = w_qkv.shape[0]
+    columns = vector_columns((b_out, norm1_gain, norm1_bias, b_down, norm2_gain, norm2_bias))
+    pipe.add("qo", gather_stages(tie(
+        jnp.concatenate([w_qkv[:, :D], columns, w_out, wide_row(b_up, shard_rows)], axis=1), begun
+    )))
     pipe.add("up", gather_stages(w_up))
     pipe.add("down", gather_stages(w_down))
-    pipe.slot(only=("kv",))
-    pipe.slot(*pipe.started, only=("qo",))
-    pipe.slot(only=("kv",))
-    pipe.slot(*pipe.started, only=("qo",))
+    pipe.slot(only=("kv", "qo"))
+    pipe.slot(only=("kv", "qo"))
+    pipe.slot(only=("kv", "qo"))
     pipe.slot(*pipe.started, only=("up",))
-    pipe.slot(only=("kv",))
-    pipe.slot(*pipe.started, only=("qo",))
     w_kv = assemble(*pipe.finish("kv", only=("kv",)))
     tables = (from_ancestors, from_descendants, wave, wave_t)
-    k, v, increments = project(ids, tie(tokens, *tables), w_kv, cos, sin, fsdp)
-    far, near = trade(increments)
-    pipe.slot(k, only=("qo", "up"))
+    k, v, increments = project(ids, tie(tokens, tokens_other, *tables), w_kv, cos, sin, fsdp)
+    pipe.arrive(k, only=("qo", "up"))
+    pipe.add("state", trade_stages(increments))
+    pipe.slot(*pipe.started, only=("state", "qo"))
+    pipe.slot(only=("state", "qo"))
+    pipe.slot(*pipe.started, only=("up",))
     pipe.slot(*pipe.started, only=("down",))
-    pipe.slot(near, only=("qo",))
-    pipe.slot(*pipe.started, only=("up",))
     w_qo = assemble(*pipe.finish("qo", only=("qo",)))
-    q, num, den = intra_forward(tokens, w_qo, k, v, wave)
-    pipe.slot(q, only=("up", "down"))
-    mixed = mix_segments(from_ancestors, far, tie(near, q))
-    path = trade(mixed)
-    tokens_other = exchange(tie(tokens, q), "group", 0)
-    small = vector_rows(tie(w_qo, mixed[0])[:, D:OUT_AT], w_qkv.shape[0], ff // D)
-    pipe.slot(path[1], only=("up", "down"))
+    pipe.slot(w_qo, only=("up",))
+    pipe.slot(*pipe.started, only=("down",))
+    q, num, den = intra_forward(tie(tokens, *pipe.started), w_qo, k, v, wave)
+    far, near = pipe.finish("state", q, only=("state",))
+    mixed = mix_segments(from_ancestors, far, near)
+    pipe.arrive(q, only=("up", "down"))
+    pipe.add("path", trade_stages(mixed))
+    pipe.slot(*pipe.started, only=("path", "up"))
+    small = vector_rows(tie(w_qo, *pipe.started), shard_rows, b_up.shape[0], ff // D)
+    pipe.slot(small, only=("path", "up", "down"))
+    path = pipe.finish("path", *pipe.started, only=("path",))
     att, rden = inter_forward(ids, q, num, den, cos, sin, *path)
-    pipe.slot(att, only=("down",))
-    att_other = exchange(att, "group", 0)
-    w_up_full = assemble(*pipe.finish("up", only=("up",)))
-    hat1, inv1, low1, gelu, slope = expand(att, tokens, w_qo, w_up_full, small)
-    w_down_full = assemble(*pipe.finish("down", low1, only=("down",)))
-    gelu_other = exchange(gelu, "group", 0)
-    low1_other = exchange(low1, "group", 0)
+    pipe.add("att", core_stage(att))
+    pipe.slot(att, only=("down", "att"))
+    w_up_full = assemble(*pipe.finish("up", att, only=("up",)))
+    att_other = pipe.read("att", w_up_full)
+    hat1, inv1, low1, gelu, slope = expand(
+        tie(att, att_other, *pipe.started), tokens, w_qo, w_up_full, small
+    )
+    pipe.slot(low1, only=("down",))
+    w_down_full = assemble(*pipe.finish("down", only=("down",)))
+    pipe.add("gelu", core_stage(gelu))
+    pipe.add("low1", core_stage(low1))
+    pipe.slot(w_down_full, only=("gelu", "low1"))
     output, d_res2, d_lower, d_upper, d_lower_half, d_upper_half, sums = contract(
         ids, gelu, slope, hat1, cotangent, w_down_full, small
     )
-    d_lower_other = exchange(d_lower_half, "group", 0)
-    d_upper_other = exchange(d_upper_half, "group", 0)
+    low1_other = pipe.read("low1", sums)
+    gelu_other = pipe.read("gelu", sums)
+    grads = Pipeline()
+    grads.add("d_lower", core_stage(d_lower_half))
+    grads.add("d_upper", core_stage(d_upper_half))
+    grads.slot(low1_other, gelu_other)
     d_res1, d_mixed, d_mixed_half, d_num, d_den, sums, *back = back_to_heads(
-        ids, d_upper, d_res2, hat1, inv1, rden, att, q, cos, sin, w_qo, w_up_full, small, sums, fsdp
-    )
-    d_mixed_other = exchange(d_mixed_half, "group", 0)
-    far, near = trade(back)
-    grads = Pipeline()
+        ids, tie(d_upper, *grads.started), d_res2, hat1, inv1, rden, att, q, cos, sin, w_qo,
+        w_up_full, small, sums, fsdp,
+    )
+    d_lower_other = grads.read("d_lower", d_num)
+    d_upper_other = grads.read("d_upper", d_num)
+    grads.add("state", trade_stages(back))
+    grads.add("d_mixed", core_stage(d_mixed_half))
+    grads.slot(d_lower_other, d_upper_other)
     two = chips == 2
 
     def reduction(part):
@@ -993,45 +1054,62 @@
 
     split = 2 if two else 1
     (down_part,) = weight_grad(
-        ids, [(gelu, gelu_other, tie(d_lower, d_num), d_lower_other)], fsdp, [split]
-    )
+        ids, [(gelu, gelu_other, tie(d_lower, *grads.started), d_lower_other)], fsdp, [split]
+    )
+    d_mixed_other = grads.read("d_mixed", down_part)
     grads.add("down", reduction(down_part))
-    grads.slot()
+    grads.slot(d_mixed_other, only=("state", "down"))
     (up_part,) = weight_grad(
         ids, [(low1, low1_other, tie(d_upper, *grads.started), d_upper_other)], fsdp, [1]
     )
-    grads.add("up", reduce_stages(up_part, core))
-    grads.slot(only=("up",))
+    far, near = grads.finish("state", up_part, only=("state",))
+    grads.add("up", reduce_stages(up_part, core, True))
+    grads.slot(near, only=("up",))
     mixed = mix_segments(from_descendants, far, tie(near, *grads.started))
-    back = trade(mixed)
+    grads.add("path", trade_stages(mixed))
+    grads.slot(only=("path",))
     d_q, d_q_half, d_k, d_v = intra_backward(
-        ids, tie(q, mixed[0]), k, v, d_num, d_den, cos, sin, wave, wave_t, *path
-    )
-    d_q_other = exchange(d_q_half, "group", 0)
-    grads.slot(d_q)
+        ids, tie(q, *grads.started), k, v, d_num, d_den, cos, sin, wave, wave_t, *path
+    )
+    grads.add("d_q", core_stage(d_q_half))
+    grads.slot(d_q, only=("path", "d_q"))
+    grads.slot(*grads.started, only=("up",))
+    d_q_other = grads.read("d_q", *grads.started)
     (outq_part,) = weight_grad(
         ids,
         [
-            (tie(att, *grads.started), att_other, d_mixed, d_mixed_other),
+            (att, att_other, d_mixed, d_mixed_other),
             (tokens, tokens_other, d_q, d_q_other),
         ],
-        fsdp, [split], sums=wide_by_block(sums, fsdp, ff // D),
+        fsdp, [split], sums=sums,
     )
     grads.add("outq", reduction(outq_part))
-    grads.slot(only=("outq",))
-    d_kv = inter_backward(ids, tie(k, *grads.started), v, d_k, d_v, cos, sin, *back)
-    d_kv_other = exchange(d_kv[1], "group", 0)
-    grads.slot(d_kv)
-    tokens_grad = input_grad(ids, d_q, tie(d_kv, *grads.started), d_res1, w_qo, w_kv)
+    grads.arrive(outq_part, only=("down",))
+    grads.slot(*grads.started, only=("outq",))
+    back = grads.finish("path", *grads.started, only=("path",))
+    d_kv = inter_backward(ids, k, v, d_k, d_v, cos, sin, *back)
+    grads.add("d_kv", core_stage(d_kv[1]))
+    grads.slot(only=("d_kv",))
+    d_kv_other = grads.read("d_kv")
     kv_parts = weight_grad(
-        ids, [(tokens, tokens_other, tie(d_kv[0], tokens_grad), d_kv_other)], fsdp,
-        [2, 1] if two else [1], False,
+        ids, [(tokens, tokens_other, d_kv[0], d_kv_other)], fsdp, [2, 1] if two else [1], False,
     )
     grads.add("kv0", reduction(kv_parts[0]))
     for part in kv_parts[1:]:
         grads.add("kv1", reduce_stages(part, core))
+    kv = ("kv0", "kv1")
+    grads.slot(only=kv)
+    grads.slot(*kv_parts, only=("up",))
+    tokens_grad = input_grad(ids, d_q, tie(d_kv, *grads.started), d_res1, w_qo, w_kv)
+    grads.slot(tokens_grad, only=kv)
+    grads.slot(*grads.started, only=("down",))
+    grads.slot(*grads.started, only=("outq",))
+    grads.slot(*grads.started, only=kv)
+    grads.slot(*grads.started, only=kv)
+    grads.slot(*grads.started, only=("up", "down"))
+    grads.slot(*grads.started, only=kv)
     while grads.running:
-        grads.slot(kv_parts[0])
+        grads.slot(*grads.started)
     done = grads.finished
     kv_grad = jnp.concatenate([done[n] for n in ("kv0", "kv1") if n in done], axis=0)
     ours, others = jnp.split(done["outq"], 2, axis=1)

time: 339 us -> 285 us (0.84)
  local copies, waits for them, and re-layouts: 38.5 us -> 7.5 us
  waiting for transfers between devices: 106 us -> 95.8 us
  Pallas kernels: 82.8 us -> 78.4 us
  starting transfers between devices: 90.7 us -> 86.5 us
    ppermute x12 -> x0, starting transfers between devices: 17.7 us -> none  [trade(): lax.ppermute(pieces[m], 'fsdp', [(i, i ^ 2 * m) for i in range(size)])]
    ppermute x12 -> x0, waiting for transfers between devices: 14.7 us -> none  [trade(): lax.ppermute(pieces[m], 'fsdp', [(i, i ^ 2 * m) for i in range(size)])]
    ppermute x86 -> x88, starting transfers between devices: 73 us -> 86.5 us  [exchange(): return lax.ppermute(x, axis, [(i, i ^ offset) for i in range(size)])]
    unnamed x142 -> x18, local copies, waits for them, and re-layouts: 13.3 us -> 2.4 us
    reshape x7 -> x0, local copies, waits for them, and re-layouts: 8.38 us -> none  [the longest x2 2.72 us: wide_by_block(): wide = sums[B_UP:B_UP + longer].reshape(fsdp, longer, D // fsdp)]
    slice x22 -> x17, local copies, waits for them, and re-layouts: 6.69 us -> 0.18 us  [the longest x1 0.09 us: reduce_stages(): received, = (yield [(tie(send[:quarter], after), axis, bit)])]
    ppermute x86 -> x88, waiting for transfers between devices: 91.2 us -> 95.8 us  [exchange(): return lax.ppermute(x, axis, [(i, i ^ offset) for i in range(size)])]
    another operation x6 -> x2, local copies, waits for them, and re-layouts: 4.48 us -> 0.86 us  [vector_columns(): return jnp.pad(jnp.stack(vectors), ((0, LANES - len(vectors)), (0, 0))).T]
  transfers between devices with their start and end apart: 98 -> 88, of which waited for: 36 -> 41; matrix products, arithmetic and copies ran while one was open for 11% -> 4% of each run, Pallas kernels for 24% -> 26%
where the time goes in v2:
time: 285 us
  waiting for transfers between devices  95.8 us (34%)
  starting transfers between devices  86.5 us (30%)
  Pallas kernels  78.4 us (28%)
  other arithmetic  12.2 us (4%)
  local copies, waits for them, and re-layouts  7.5 us (3%)
    ppermute x88, waiting for transfers between devices, exchange(): return lax.ppermute(x, axis, [(i, i ^ offset) for i in range(size)])  95.8 us
    ppermute x88, starting transfers between devices, exchange(): return lax.ppermute(x, axis, [(i, i ^ offset) for i in range(size)])  86.5 us
    pallas_call x4, Pallas kernels, weight_grad(): call(kernel, 'weight_grad', tuple((shape_of((n, fsdp, share // n, width),...  13 us
    pallas_call x1, Pallas kernels, back_to_heads(): call(kernel, 'back_to_heads', (shape_of((rows, D), f32), shape_of((rows,...  10.2 us
    pallas_call x1, Pallas kernels, contract(): call(kernel, 'contract', (shape_of((rows, D), bf16), shape_of((rows, D),...  10.1 us
    pallas_call x1, Pallas kernels, intra_backward(): call(kernel, 'intra_backward', (shape_of((rows, D), bf16), shape_of((rows...  8.89 us
    pallas_call x1, Pallas kernels, expand(): call(kernel, 'expand', (shape_of((rows, D), f32), shape_of((rows, LANES),...  7.47 us
    pallas_call x1, Pallas kernels, intra_forward(): call(kernel, 'intra_forward', (shape_of((rows, D), bf16), wide, wide), [V...  5.87 us
  transfers between devices with their start and end apart: 88, of which 41 were waited for; matrix products, arithmetic and copies ran while one was open for 4% of the time, Pallas kernels for 26%

profile of v2, /device:TPU:0, one launch (start us, length us, event | category | flops | bytes accessed | tf_op | source)
XLA Modules:
  0.0 284.7 jit_solution(12495514423053393981)
XLA Ops:
  1.5 4.0 %collective-permute-start = (bf16[1,24,1536]{2,1,0:T(8,128)(2,1)S(1)}, bf16[1,24,1536]{2,1,0:T(8,128)(2,1)S(1)}, u32[]{:S(2)}, u32[]{:S(2)}) collective-permute-start(bf16[1,24,1536]{2,1,0:T(8,128)(2,1)S(1)} %slice_bitcast_fusion.14), channel_id=1, source_target_pairs={{0,4},{1,5},{2,6},{3,7},{4,0},{5,1},{6,2},{7,3},{8,12},{9,13},{10,... | collective-permute-start | bytes 221192 | tf_op jit(solution)/shard_map/ppermute | solution.py:28
  13.0 3.2 %collective-permute-start.4 = (bf16[1,24,1792]{2,1,0:T(8,128)(2,1)S(1)}, bf16[1,24,1792]{2,1,0:T(8,128)(2,1)S(1)}, u32[]{:S(2)}, u32[]{:S(2)}) collective-permute-start(bf16[1,24,1792]{2,1,0:T(8,128)(2,1)S(1)} %bitcast.113), channel_id=1, source_target_pairs={{0,4},{1,5},{2,6},{3,7},{4,0},{5,1},{6,2},{7,3},{8,12},{9,13},{10,... | collective-permute-start | bytes 258056 | tf_op jit(solution)/shard_map/ppermute | solution.py:28
  25.9 2.7 collective-permute-done.9
  30.9 3.9 %collective-permute-done.6.refs_5_ = bf16[8,24,768]{2,1,0:T(8,128)(2,1)S(1)} collective-permute-done((bf16[8,24,768]{2,1,0:T(8,128)(2,1)S(1)}, bf16[8,24,768]{2,1,0:T(8,128)(2,1)S(1)}, u32[]{:S(2)}, u32[]{:S(2)}) %collective-permute-start.6) | collective-permute-done | bytes 294944 | tf_op jit(solution)/shard_map/ppermute | solution.py:28
  36.5 2.4 collective-permute-start.12
  40.4 5.1 %project.1 = (bf16[512,768]{1,0:T(8,128)(2,1)S(1)}, bf16[512,768]{1,0:T(8,128)(2,1)S(1)}, bf16[2,2,104,128]{3,2,1,0:T(8,128)(2,1)S(1)}, bf16[2,2,104,128]{3,2,1,...) custom-call(s32[3]{0:T(128)S(1)} %pad_add_fusion.ids_ref, ...), custom_call_target="tpu_custom_call" | custom-call | flops 3240000000 | tf_op jit(solution)/shard_map/project/pallas_call | solution.py:356
  49.1 2.7 collective-permute-start.19
  53.7 5.3 %collective-permute-done.19.refs_2_ = bf16[2,2,104,128]{3,2,1,0:T(8,128)(2,1)S(1)} collective-permute-done((bf16[2,2,104,128]{3,2,1,0:T(8,128)(2,1)S(1)}, bf16[2,2,104,128]{3,2,1,0:T(8,128)(2,1)S(1)}, u32[]{:S(2)}, u32[]{:S(2)}) %collective-permute-start.19) | collective-permute-done | bytes 106528 | tf_op jit(solution)/shard_map/ppermute | solution.py:28
  59.9 1.8 collective-permute-start.22
  64.3 7.8 %collective-permute-done.22 = bf16[2,24,3072]{2,1,0:T(8,128)(2,1)S(1)} collective-permute-done((bf16[2,24,3072]{2,1,0:T(8,128)(2,1)S(1)}, bf16[2,24,3072]{2,1,0:T(8,128)(2,1)S(1)}, u32[]{:S(2)}, u32[]{:S(2)}) %collective-permute-start.22) | collective-permute-done | bytes 294944 | tf_op jit(solution)/shard_map/ppermute | solution.py:28
  74.5 5.9 %intra_forward.1 = (bf16[512,768]{1,0:T(8,128)(2,1)S(1)}, f32[512,768]{1,0:T(8,128)S(1)}, f32[512,768]{1,0:T(8,128)S(1)}) custom-call(bf16[512,768]{1,0:T(8,128)(2,1)S(1)} %copy-done.1, bf16[768,1792]{1,0:T(8,128)(2,1)S(1)} %bitcast.103, bf16[512,768]{1,0:T(8,128)(2,1)S(1)} %get-tuple-element.239.k_ref, bf16[512,768]{1,0:T(8,128)(2,1)S(1)} %get-tuple-element.267.v_ref, ...), custom_call_target="tpu_custom_call" | custom-call | flops 3540000000 | tf_op jit(solution)/shard_map/intra_forward/pallas_call | solution.py:414
  85.0 2.0 collective-permute-start.32
  87.0 1.7 collective-permute-start.33
  88.9 2.1 collective-permute-done.31.refs_1_
  91.0 3.1 %collective-permute-done.32.refs_2_ = bf16[2,2,104,128]{3,2,1,0:T(8,128)(2,1)S(1)} collective-permute-done((bf16[2,2,104,128]{3,2,1,0:T(8,128)(2,1)S(1)}, bf16[2,2,104,128]{3,2,1,0:T(8,128)(2,1)S(1)}, u32[]{:S(2)}, u32[]{:S(2)}) %collective-permute-start.32) | collective-permute-done | bytes 106528 | tf_op jit(solution)/shard_map/ppermute | solution.py:28
  95.9 2.0 collective-permute-start.34
  99.9 3.8 %collective-permute-done.34.refs_4_ = bf16[4,2,104,128]{3,2,1,0:T(8,128)(2,1)S(1)} collective-permute-done((bf16[4,2,104,128]{3,2,1,0:T(8,128)(2,1)S(1)}, bf16[4,2,104,128]{3,2,1,0:T(8,128)(2,1)S(1)}, u32[]{:S(2)}, u32[]{:S(2)}) %collective-permute-start.34) | collective-permute-done | bytes 213024 | tf_op jit(solution)/shard_map/ppermute | solution.py:28
  103.7 4.0 %inter_forward.1 = (bf16[512,768]{1,0:T(8,128)(2,1)S(1)}, f32[512,768]{1,0:T(8,128)S(1)}) custom-call(s32[3]{0:T(128)S(1)} %pad_add_fusion.ids_ref, bf16[512,768]{1,0:T(8,128)(2,1)S(1)} %get-tuple-element.358.q_ref, f32[512,768]{1,0:T(8,128)S(1)} %get-tuple-element.269.num_ref, f32[512,768]{1,0:T(8,128)S(1)} %get-tuple-element.270.den_ref, ...), custom_call_target="tpu_custom_call" | custom-call | flops 3300000000 | tf_op jit(solution)/shard_map/inter_forward/pallas_call | solution.py:455
  111.8 7.5 %expand.1 = (f32[512,768]{1,0:T(8,128)S(1)}, f32[512,128]{1,0:T(8,128)S(1)}, bf16[512,768]{1,0:T(8,128)(2,1)S(1)}, bf16[512,3072]{1,0:T(8,128)(2,1)S(1)}, bf16[512,3072]{1,0:T(8,128)(2,1)S(1)}) custom-call(bf16[512,768]{1,0:T(8,128)(2,1)S(1)} %get-tuple-element.305.att_ref.refs_0_, bf16[512,768]{1,0:T(8,128)(2,1)S(1)} %copy-done.1, ...), custom_call_target="tpu_custom_call" | custom-call | flops 5699999744 | tf_op jit(solution)/shard_map/expand/pallas_call | solution.py:510
  119.3 5.3 %collective-permute-done.40 = bf16[8,96,384]{2,1,0:T(8,128)(2,1)S(1)} collective-permute-done((bf16[8,96,384]{2,1,0:T(8,128)(2,1)S(1)}, bf16[8,96,384]{2,1,0:T(8,128)(2,1)S(1)}, u32[]{:S(2)}, u32[]{:S(2)}) %collective-permute-start.40) | collective-permute-done | bytes 589856 | tf_op jit(solution)/shard_map/ppermute | solution.py:28
  126.6 2.3 collective-permute-done.42.refs_1_
  129.0 1.7 collective-permute-done.43.refs_3_
  132.6 10.1 %contract.1 = (bf16[512,768]{1,0:T(8,128)(2,1)}, f32[512,768]{1,0:T(8,128)S(1)}, bf16[512,768]{1,0:T(8,128)(2,1)S(1)}, bf16[512,3072]{1,0:T(8,128)(2,1)S(1)}, bf...) custom-call(s32[3]{0:T(128)S(1)} %pad_add_fusion.ids_ref, ...), custom_call_target="tpu_custom_call" | custom-call | flops 6300000256 | tf_op jit(solution)/shard_map/contract/pallas_call | solution.py:569
  144.6 10.2 %back_to_heads.1 = (f32[512,768]{1,0:T(8,128)S(1)}, bf16[512,768]{1,0:T(8,128)(2,1)S(1)}, bf16[512,384]{1,0:T(8,128)(2,1)S(1)}, bf16[512,768]{1,0:T(8,128)(2,1)S...) custom-call(s32[3]{0:T(128)S(1)} %pad_add_fusion.ids_ref, ...), custom_call_target="tpu_custom_call" | custom-call | flops 7080000000 | tf_op jit(solution)/shard_map/back_to_heads/pallas_call | solution.py:639
  156.8 2.5 collective-permute-start.50
  159.3 5.5 %weight_grad.4 = bf16[2,8,192,384]{3,2,1,0:T(8,128)(2,1)S(1)} custom-call(s32[3]{0:T(128)S(1)} %pad_add_fusion.ids_ref, bf16[512,3072]{1,0:T(8,128)(2,1)S(1)} %get-tuple-element.323.gelu_ref.refs_0_, bf16[512,3072]{1,0:T(8,128)(2,1)S(1)} %collective-permute-done.45.refs_1_, bf16[512,768]{1,0:T(8,128)(2,1)S(1)} %get-tuple-element.344.refs_2_, ...), custom_call_target="tpu_custom_call" | custom-call | flops 2400000000 | tf_op jit(solution)/shard_map/weight_grad/pallas_call | solution.py:836
  164.9 2.0 collective-permute-done.49.refs_2_
  169.4 3.2 %weight_grad.5 = bf16[1,8,96,1536]{3,2,1,0:T(8,128)(2,1)S(1)} custom-call(s32[3]{0:T(128)S(1)} %pad_add_fusion.ids_ref, bf16[512,768]{1,0:T(8,128)(2,1)S(1)} %get-tuple-element.320.refs_0_, bf16[512,768]{1,0:T(8,128)(2,1)S(1)} %collective-permute-done.44.refs_1_, bf16[512,3072]{1,0:T(8,128)(2,1)S(1)} %get-tuple-element.351.dup_ref.refs_2_, ...), custom_call_target="tpu_custom_call" | custom-call | flops 2400000000 | tf_op jit(solution)/shard_map/weight_grad/pallas_call | solution.py:836
  173.2 2.5 collective-permute-start.53
  176.1 2.0 collective-permute-start.55
  179.5 8.9 %intra_backward.1 = (bf16[512,768]{1,0:T(8,128)(2,1)S(1)}, bf16[512,384]{1,0:T(8,128)(2,1)S(1)}, f32[512,768]{1,0:T(8,128)S(1)}, f32[512,768]{1,0:T(8,128)S(1)}) custom-call(s32[3]{0:T(128)S(1)} %pad_add_fusion.ids_ref, bf16[512,768]{1,0:T(8,128)(2,1)S(1)} %get-tuple-element.358.q_ref, bf16[512,768]{1,0:T(8,128)(2,1)S(1)} %get-tuple-element.239.k_ref, ...), custom_call_target="tpu_custom_call" | custom-call | flops 6179999744 | tf_op jit(solution)/shard_map/intra_backward/pallas_call | solution.py:708
  189.3 4.1 %collective-permute-done.58 = bf16[2,96,1536]{2,1,0:T(8,128)(2,1)S(1)} collective-permute-done((bf16[2,96,1536]{2,1,0:T(8,128)(2,1)S(1)}, bf16[2,96,1536]{2,1,0:T(8,128)(2,1)S(1)}, u32[]{:S(2)}, u32[]{:S(2)}) %collective-permute-start.58) | collective-permute-done | bytes 589856 | tf_op jit(solution)/shard_map/ppermute | solution.py:28
  193.6 2.4 weight_grad.6
  196.4 4.1 %inter_backward.1.dkv_ref = bf16[2,512,768]{2,1,0:T(8,128)(2,1)S(1)} custom-call(s32[3]{0:T(128)S(1)} %pad_add_fusion.ids_ref, bf16[512,768]{1,0:T(8,128)(2,1)S(1)} %get-tuple-element.239.k_ref, bf16[512,768]{1,0:T(8,128)(2,1)S(1)} %get-tuple-element.267.v_ref, f32[512,768]{1,0:T(8,128)S(1)} %get-tuple-element.361.dk_ref, ...), custom_call_target="tpu_custom_call" | custom-call | flops 2760000000 | tf_op jit(solution)/shard_map/inter_backward/pallas_call | solution.py:756
  203.0 2.0 weight_grad.7
  209.3 7.6 %collective-permute-done.71 = bf16[2,96,1536]{2,1,0:T(8,128)(2,1)S(1)} collective-permute-done((bf16[2,96,1536]{2,1,0:T(8,128)(2,1)S(1)}, bf16[2,96,1536]{2,1,0:T(8,128)(2,1)S(1)}, u32[]{:S(2)}, u32[]{:S(2)}) %collective-permute-start.71) | collective-permute-done | bytes 589856 | tf_op jit(solution)/shard_map/ppermute | solution.py:28
  216.9 4.2 %input_grad.1 = f32[512,768]{1,0:T(8,128)} custom-call(s32[3]{0:T(128)S(1)} %pad_add_fusion.ids_ref, bf16[512,768]{1,0:T(8,128)(2,1)S(1)} %get-tuple-element.360.refs_6_.dq_ref, bf16[2,512,768]{2,1,0:T(8,128)(2,1)S(1)} %inter_backward.1.dkv_ref, f32[512,768]{1,0:T(8,128)S(1)} %get-tuple-element.383.dres_ref, bf16[768,1792]{1,0:T(8,128)(2,1)S(1)} %bitcast.107, ...), custom_call_target="tpu_custom_call" | custom-call | flops 2400000000 | tf_op jit(solution)/shard_map/input_grad/pallas_call | solution.py:780
  226.1 2.7 collective-permute-done.61
  234.5 2.5 collective-permute-done.70
  237.6 1.9 collective-permute-start.75
  239.5 2.8 collective-permute-done.65
  245.1 2.0 collective-permute-start.76
  249.2 5.0 %collective-permute-done.72 = bf16[2,192,384]{2,1,0:T(8,128)(2,1)S(1)} collective-permute-done((bf16[2,192,384]{2,1,0:T(8,128)(2,1)S(1)}, bf16[2,192,384]{2,1,0:T(8,128)(2,1)S(1)}, u32[]{:S(2)}, u32[]{:S(2)}) %collective-permute-start.72) | collective-permute-done | bytes 294944 | tf_op jit(solution)/shard_map/ppermute | solution.py:28
  254.2 3.0 %collective-permute-done.73 = bf16[1,96,1536]{2,1,0:T(8,128)(2,1)} collective-permute-done((bf16[1,96,1536]{2,1,0:T(8,128)(2,1)S(1)}, bf16[1,96,1536]{2,1,0:T(8,128)(2,1)}, u32[]{:S(2)}, u32[]{:S(2)}) %collective-permute-start.73) | collective-permute-done | bytes 294944 | tf_op jit(solution)/shard_map/ppermute | solution.py:28
  259.8 2.6 collective-permute-start.79
  263.6 3.8 %collective-permute-done.79 = bf16[1,192,384]{2,1,0:T(8,128)(2,1)S(1)} collective-permute-done((bf16[1,192,384]{2,1,0:T(8,128)(2,1)S(1)}, bf16[1,192,384]{2,1,0:T(8,128)(2,1)S(1)}, u32[]{:S(2)}, u32[]{:S(2)}) %collective-permute-start.79) | collective-permute-done | bytes 147488 | tf_op jit(solution)/shard_map/ppermute | solution.py:28
  269.1 5.8 %collective-permute-done.82 = bf16[1,48,896]{2,1,0:T(8,128)(2,1)S(1)} collective-permute-done((bf16[1,48,896]{2,1,0:T(8,128)(2,1)S(1)}, bf16[1,48,896]{2,1,0:T(8,128)(2,1)S(1)}, u32[]{:S(2)}, u32[]{:S(2)}) %collective-permute-start.82) | collective-permute-done | bytes 86048 | tf_op jit(solution)/shard_map/ppermute | solution.py:28
  277.6 2.1 collective-permute-done.85
  (284 shorter events, 97.4 us)
Async XLA Ops:
  1.5 7.9 %collective-permute-start = (bf16[1,24,1536]{2,1,0:T(8,128)(2,1)S(1)}, bf16[1,24,1536]{2,1,0:T(8,128)(2,1)S(1)}, u32[]{:S(2)}, u32[]{:S(2)}) collective-permute-start(bf16[1,24,1536]{2,1,0:T(8,128)(2,1)S(1)} %slice_bitcast_fusion.14), channel_id=1, source_target_pairs={{0,4},{1,5},{2,6},{3,7},{4,0},{5,1},{6,2},{7,3},{8,12},{9,13},{10,... | collective-permute-start | bytes 221192 | tf_op jit(solution)/shard_map/ppermute | solution.py:28
  5.6 30.9 %collective-permute-start.13 = (bf16[512,768]{1,0:T(8,128)(2,1)}, bf16[512,768]{1,0:T(8,128)(2,1)S(1)}, u32[]{:S(2)}, u32[]{:S(2)}) collective-permute-start(bf16[512,768]{1,0:T(8,128)(2,1)} %refs_0_.1), channel_id=1, source_target_pairs={{0,8},{8,0},{16,24},{24,16},{1,9},{9,1},{17,25},{25,17},{2,10},{10... | collective-permute-start | bytes 2359304 | tf_op jit(solution)/shard_map/ppermute | solution.py:28
  25.3 9.5 %collective-permute-start.7 = (bf16[8,24,768]{2,1,0:T(8,128)(2,1)S(1)}, bf16[8,24,768]{2,1,0:T(8,128)(2,1)S(1)}, u32[]{:S(2)}, u32[]{:S(2)}) collective-permute-start(bf16[8,24,768]{2,1,0:T(8,128)(2,1)S(1)} %pad_maximum_fusion.17.refs_0_), channel_id=1, source_target_pairs={{0,8},{8,0},{16,24},{24,16},{1,9},{9,1},{17,25},{25,17},{2,10},{10... | collective-permute-start | bytes 884744 | tf_op jit(solution)/shard_map/ppermute | solution.py:28
  25.3 9.5 %collective-permute-start.6 = (bf16[8,24,768]{2,1,0:T(8,128)(2,1)S(1)}, bf16[8,24,768]{2,1,0:T(8,128)(2,1)S(1)}, u32[]{:S(2)}, u32[]{:S(2)}) collective-permute-start(bf16[8,24,768]{2,1,0:T(8,128)(2,1)S(1)} %pad_maximum_fusion.18.refs_4_), channel_id=1, source_target_pairs={{0,1},{1,0},{2,3},{3,2},{4,5},{5,4},{6,7},{7,6},{8,9},{9,8},{10,11... | collective-permute-start | bytes 884744 | tf_op jit(solution)/shard_map/ppermute | solution.py:28
  35.4 10.4 %collective-permute-start.10 = (bf16[4,24,896]{2,1,0:T(8,128)(2,1)S(1)}, bf16[4,24,896]{2,1,0:T(8,128)(2,1)S(1)}, u32[]{:S(2)}, u32[]{:S(2)}) collective-permute-start(bf16[4,24,896]{2,1,0:T(8,128)(2,1)S(1)} %get-tuple-element.470), channel_id=1, source_target_pairs={{0,1},{1,0},{2,3},{3,2},{4,5},{5,4},{6,7},{7,6},{8,9},{9,8},{10,11... | collective-permute-start | bytes 516104 | tf_op jit(solution)/shard_map/ppermute | solution.py:28
  36.0 9.8 %collective-permute-start.11 = (bf16[4,24,896]{2,1,0:T(8,128)(2,1)S(1)}, bf16[4,24,896]{2,1,0:T(8,128)(2,1)S(1)}, u32[]{:S(2)}, u32[]{:S(2)}) collective-permute-start(bf16[4,24,896]{2,1,0:T(8,128)(2,1)S(1)} %get-tuple-element.469), channel_id=1, source_target_pairs={{0,16},{8,24},{16,0},{24,8},{1,17},{9,25},{17,1},{25,9},{2,18},{10... | collective-permute-start | bytes 516104 | tf_op jit(solution)/shard_map/ppermute | solution.py:28
  36.5 9.3 %collective-permute-start.12 = (bf16[1,24,3072]{2,1,0:T(8,128)(2,1)S(1)}, bf16[1,24,3072]{2,1,0:T(8,128)(2,1)S(1)}, u32[]{:S(2)}, u32[]{:S(2)}) collective-permute-start(bf16[1,24,3072]{2,1,0:T(8,128)(2,1)S(1)} %bitcast.116), channel_id=1, source_target_pairs={{0,4},{1,5},{2,6},{3,7},{4,0},{5,1},{6,2},{7,3},{8,12},{9,13},{10,... | collective-permute-start | bytes 442376 | tf_op jit(solution)/shard_map/ppermute | solution.py:28
  45.9 13.1 %collective-permute-start.16 = (bf16[8,24,896]{2,1,0:T(8,128)(2,1)S(1)}, bf16[8,24,896]{2,1,0:T(8,128)(2,1)S(1)}, u32[]{:S(2)}, u32[]{:S(2)}) collective-permute-start(bf16[8,24,896]{2,1,0:T(8,128)(2,1)S(1)} %get-tuple-element.246), channel_id=1, source_target_pairs={{0,16},{8,24},{16,0},{24,8},{1,17},{9,25},{17,1},{25,9},{2,18},{10... | collective-permute-start | bytes 1032200 | tf_op jit(solution)/shard_map/ppermute | solution.py:28
  47.5 11.5 %collective-permute-start.17 = (bf16[8,24,896]{2,1,0:T(8,128)(2,1)S(1)}, bf16[8,24,896]{2,1,0:T(8,128)(2,1)S(1)}, u32[]{:S(2)}, u32[]{:S(2)}) collective-permute-start(bf16[8,24,896]{2,1,0:T(8,128)(2,1)S(1)} %get-tuple-element.247), channel_id=1, source_target_pairs={{0,1},{1,0},{2,3},{3,2},{4,5},{5,4},{6,7},{7,6},{8,9},{9,8},{10,11... | collective-permute-start | bytes 1032200 | tf_op jit(solution)/shard_map/ppermute | solution.py:28
  49.1 9.9 %collective-permute-start.19 = (bf16[2,2,104,128]{3,2,1,0:T(8,128)(2,1)S(1)}, bf16[2,2,104,128]{3,2,1,0:T(8,128)(2,1)S(1)}, u32[]{:S(2)}, u32[]{:S(2)}) collective-permute-start(bf16[2,2,104,128]{3,2,1,0:T(8,128)(2,1)S(1)} %get-tuple-element.249), channel_id=1, source_target_pairs={{0,4},{1,5},{2,6},{3,7},{4,0},{5,1},{6,2},{7,3},{8,12},{9,13},{10,... | collective-permute-start | bytes 319496 | tf_op jit(solution)/shard_map/ppermute | solution.py:28
  59.9 12.2 %collective-permute-start.22 = (bf16[2,24,3072]{2,1,0:T(8,128)(2,1)S(1)}, bf16[2,24,3072]{2,1,0:T(8,128)(2,1)S(1)}, u32[]{:S(2)}, u32[]{:S(2)}) collective-permute-start(bf16[2,24,3072]{2,1,0:T(8,128)(2,1)S(1)} %pad_maximum_fusion.19), channel_id=1, source_target_pairs={{0,2},{1,3},{2,0},{3,1},{4,6},{5,7},{6,4},{7,5},{8,10},{9,11},{10,... | collective-permute-start | bytes 884744 | tf_op jit(solution)/shard_map/ppermute | solution.py:28
  61.7 18.8 %collective-permute-start.25 = (bf16[4,2,104,128]{3,2,1,0:T(8,128)(2,1)S(1)}, bf16[4,2,104,128]{3,2,1,0:T(8,128)(2,1)S(1)}, u32[]{:S(2)}, u32[]{:S(2)}) collective-permute-start(bf16[4,2,104,128]{3,2,1,0:T(8,128)(2,1)S(1)} %pad_maximum_fusion.23), channel_id=1, source_target_pairs={{0,1},{1,0},{2,3},{3,2},{4,5},{5,4},{6,7},{7,6},{8,9},{9,8},{10,11... | collective-permute-start | bytes 638984 | tf_op jit(solution)/shard_map/ppermute | solution.py:28
  62.2 11.1 %collective-permute-start.21 = (bf16[1,96,768]{2,1,0:T(8,128)(2,1)S(1)}, bf16[1,96,768]{2,1,0:T(8,128)(2,1)S(1)}, u32[]{:S(2)}, u32[]{:S(2)}) collective-permute-start(bf16[1,96,768]{2,1,0:T(8,128)(2,1)S(1)} %bitcast.119), channel_id=1, source_target_pairs={{0,4},{1,5},{2,6},{3,7},{4,0},{5,1},{6,2},{7,3},{8,12},{9,13},{10,... | collective-permute-start | bytes 442376 | tf_op jit(solution)/shard_map/ppermute | solution.py:28
  72.2 8.5 %collective-permute-start.26 = (bf16[4,24,1536]{2,1,0:T(8,128)(2,1)S(1)}, bf16[4,24,1536]{2,1,0:T(8,128)(2,1)S(1)}, u32[]{:S(2)}, u32[]{:S(2)}) collective-permute-start(bf16[4,24,1536]{2,1,0:T(8,128)(2,1)S(1)} %get-tuple-element.262), channel_id=1, source_target_pairs={{0,1},{1,0},{2,3},{3,2},{4,5},{5,4},{6,7},{7,6},{8,9},{9,8},{10,11... | collective-permute-start | bytes 884744 | tf_op jit(solution)/shard_map/ppermute | solution.py:28
  72.8 7.9 %collective-permute-start.27 = (bf16[4,24,1536]{2,1,0:T(8,128)(2,1)S(1)}, bf16[4,24,1536]{2,1,0:T(8,128)(2,1)S(1)}, u32[]{:S(2)}, u32[]{:S(2)}) collective-permute-start(bf16[4,24,1536]{2,1,0:T(8,128)(2,1)S(1)} %get-tuple-element.263), channel_id=1, source_target_pairs={{0,16},{8,24},{16,0},{24,8},{1,17},{9,25},{17,1},{25,9},{2,18},{10... | collective-permute-start | bytes 884744 | tf_op jit(solution)/shard_map/ppermute | solution.py:28
  81.3 14.0 %collective-permute-start.29 = (bf16[8,24,1536]{2,1,0:T(8,128)(2,1)S(1)}, bf16[8,24,1536]{2,1,0:T(8,128)(2,1)S(1)}, u32[]{:S(2)}, u32[]{:S(2)}) collective-permute-start(bf16[8,24,1536]{2,1,0:T(8,128)(2,1)S(1)} %pad_maximum_fusion.8), channel_id=1, source_target_pairs={{0,16},{8,24},{16,0},{24,8},{1,17},{9,25},{17,1},{25,9},{2,18},{10... | collective-permute-start | bytes 1769480 | tf_op jit(solution)/shard_map/ppermute | solution.py:28
  82.9 12.7 %collective-permute-start.30 = (bf16[8,24,1536]{2,1,0:T(8,128)(2,1)S(1)}, bf16[8,24,1536]{2,1,0:T(8,128)(2,1)S(1)}, u32[]{:S(2)}, u32[]{:S(2)}) collective-permute-start(bf16[8,24,1536]{2,1,0:T(8,128)(2,1)S(1)} %pad_maximum_fusion.9), channel_id=1, source_target_pairs={{0,1},{1,0},{2,3},{3,2},{4,5},{5,4},{6,7},{7,6},{8,9},{9,8},{10,11... | collective-permute-start | bytes 1769480 | tf_op jit(solution)/shard_map/ppermute | solution.py:28
  85.0 9.0 %collective-permute-start.32 = (bf16[2,2,104,128]{3,2,1,0:T(8,128)(2,1)S(1)}, bf16[2,2,104,128]{3,2,1,0:T(8,128)(2,1)S(1)}, u32[]{:S(2)}, u32[]{:S(2)}) collective-permute-start(bf16[2,2,104,128]{3,2,1,0:T(8,128)(2,1)S(1)} %get-tuple-element.282), channel_id=1, source_target_pairs={{0,4},{1,5},{2,6},{3,7},{4,0},{5,1},{6,2},{7,3},{8,12},{9,13},{10,... | collective-permute-start | bytes 319496 | tf_op jit(solution)/shard_map/ppermute | solution.py:28
  97.8 9.9 %collective-permute-start.35 = (bf16[4,96,384]{2,1,0:T(8,128)(2,1)S(1)}, bf16[4,96,384]{2,1,0:T(8,128)(2,1)S(1)}, u32[]{:S(2)}, u32[]{:S(2)}) collective-permute-start(bf16[4,96,384]{2,1,0:T(8,128)(2,1)S(1)} %get-tuple-element.291), channel_id=1, source_target_pairs={{0,1},{1,0},{2,3},{3,2},{4,5},{5,4},{6,7},{7,6},{8,9},{9,8},{10,11... | collective-permute-start | bytes 884744 | tf_op jit(solution)/shard_map/ppermute | solution.py:28
  98.0 9.7 %collective-permute-start.36 = (bf16[4,96,384]{2,1,0:T(8,128)(2,1)S(1)}, bf16[4,96,384]{2,1,0:T(8,128)(2,1)S(1)}, u32[]{:S(2)}, u32[]{:S(2)}) collective-permute-start(bf16[4,96,384]{2,1,0:T(8,128)(2,1)S(1)} %get-tuple-element.292), channel_id=1, source_target_pairs={{0,16},{8,24},{16,0},{24,8},{1,17},{9,25},{17,1},{25,9},{2,18},{10... | collective-permute-start | bytes 884744 | tf_op jit(solution)/shard_map/ppermute | solution.py:28
  99.4 11.2 %collective-permute-start.38 = (bf16[16,24,1536]{2,1,0:T(8,128)(2,1)S(1)}, bf16[16,24,1536]{2,1,0:T(8,128)(2,1)S(1)}, u32[]{:S(2)}, u32[]{:S(2)}) collective-permute-start(bf16[16,24,1536]{2,1,0:T(8,128)(2,1)S(1)} %pad_maximum_fusion.refs_0_), channel_id=1, source_target_pairs={{0,8},{8,0},{16,24},{24,16},{1,9},{9,1},{17,25},{25,17},{2,10},{10... | collective-permute-start | bytes 3538952 | tf_op jit(solution)/shard_map/ppermute | solution.py:28
  99.4 11.2 %collective-permute-start.39 = (bf16[16,24,1536]{2,1,0:T(8,128)(2,1)S(1)}, bf16[16,24,1536]{2,1,0:T(8,128)(2,1)S(1)}, u32[]{:S(2)}, u32[]{:S(2)}) collective-permute-start(bf16[16,24,1536]{2,1,0:T(8,128)(2,1)S(1)} %pad_maximum_fusion.1.refs_2_), channel_id=1, source_target_pairs={{0,8},{8,0},{16,24},{24,16},{1,9},{9,1},{17,25},{25,17},{2,10},{10... | collective-permute-start | bytes 3538952 | tf_op jit(solution)/shard_map/ppermute | solution.py:28
  108.8 15.7 %collective-permute-start.40 = (bf16[8,96,384]{2,1,0:T(8,128)(2,1)S(1)}, bf16[8,96,384]{2,1,0:T(8,128)(2,1)S(1)}, u32[]{:S(2)}, u32[]{:S(2)}) collective-permute-start(bf16[8,96,384]{2,1,0:T(8,128)(2,1)S(1)} %pad_maximum_fusion.11), channel_id=1, source_target_pairs={{0,16},{8,24},{16,0},{24,8},{1,17},{9,25},{17,1},{25,9},{2,18},{10... | collective-permute-start | bytes 1769480 | tf_op jit(solution)/shard_map/ppermute | solution.py:28
  110.3 15.5 %collective-permute-start.41 = (bf16[8,96,384]{2,1,0:T(8,128)(2,1)S(1)}, bf16[8,96,384]{2,1,0:T(8,128)(2,1)S(1)}, u32[]{:S(2)}, u32[]{:S(2)}) collective-permute-start(bf16[8,96,384]{2,1,0:T(8,128)(2,1)S(1)} %pad_maximum_fusion.12), channel_id=1, source_target_pairs={{0,1},{1,0},{2,3},{3,2},{4,5},{5,4},{6,7},{7,6},{8,9},{9,8},{10,11... | collective-permute-start | bytes 1769480 | tf_op jit(solution)/shard_map/ppermute | solution.py:28
  132.0 10.6 %collective-permute-start.45 = (bf16[512,3072]{1,0:T(8,128)(2,1)S(1)}, bf16[512,3072]{1,0:T(8,128)(2,1)S(1)}, u32[]{:S(2)}, u32[]{:S(2)}) collective-permute-start(bf16[512,3072]{1,0:T(8,128)(2,1)S(1)} %get-tuple-element.323.gelu_ref.refs_0_), channel_id=1, source_target_pairs={{0,8},{8,0},{16,24},{24,16},{1,9},{9,1},{17,25},{25,17},{2,10},{10... | collective-permute-start | bytes 9437192 | tf_op jit(solution)/shard_map/ppermute | solution.py:28
  132.2 10.4 %collective-permute-start.44 = (bf16[512,768]{1,0:T(8,128)(2,1)S(1)}, bf16[512,768]{1,0:T(8,128)(2,1)S(1)}, u32[]{:S(2)}, u32[]{:S(2)}) collective-permute-start(bf16[512,768]{1,0:T(8,128)(2,1)S(1)} %get-tuple-element.320.refs_0_), channel_id=1, source_target_pairs={{0,8},{8,0},{16,24},{24,16},{1,9},{9,1},{17,25},{25,17},{2,10},{10... | collective-permute-start | bytes 2359304 | tf_op jit(solution)/shard_map/ppermute | solution.py:28
  142.6 12.2 %collective-permute-start.47 = (bf16[512,1536]{1,0:T(8,128)(2,1)S(1)}, bf16[512,1536]{1,0:T(8,128)(2,1)S(1)}, u32[]{:S(2)}, u32[]{:S(2)}) collective-permute-start(bf16[512,1536]{1,0:T(8,128)(2,1)S(1)} %get-tuple-element.326), channel_id=1, source_target_pairs={{0,8},{8,0},{16,24},{24,16},{1,9},{9,1},{17,25},{25,17},{2,10},{10... | collective-permute-start | bytes 4718600 | tf_op jit(solution)/shard_map/ppermute | solution.py:28
  142.8 12.0 %collective-permute-start.46 = (bf16[512,384]{1,0:T(8,128)(2,1)S(1)}, bf16[512,384]{1,0:T(8,128)(2,1)S(1)}, u32[]{:S(2)}, u32[]{:S(2)}) collective-permute-start(bf16[512,384]{1,0:T(8,128)(2,1)S(1)} %get-tuple-element.325), channel_id=1, source_target_pairs={{0,8},{8,0},{16,24},{24,16},{1,9},{9,1},{17,25},{25,17},{2,10},{10... | collective-permute-start | bytes 1179656 | tf_op jit(solution)/shard_map/ppermute | solution.py:28
  154.8 10.1 %collective-permute-start.48 = (bf16[2,2,104,128]{3,2,1,0:T(8,128)(2,1)S(1)}, bf16[2,2,104,128]{3,2,1,0:T(8,128)(2,1)S(1)}, u32[]{:S(2)}, u32[]{:S(2)}) collective-permute-start(bf16[2,2,104,128]{3,2,1,0:T(8,128)(2,1)S(1)} %get-tuple-element.339), channel_id=1, source_target_pairs={{0,2},{1,3},{2,0},{3,1},{4,6},{5,7},{6,4},{7,5},{8,10},{9,11},{10,... | collective-permute-start | bytes 319496 | tf_op jit(solution)/shard_map/ppermute | solution.py:28
  155.8 11.1 %collective-permute-start.49 = (bf16[2,2,104,128]{3,2,1,0:T(8,128)(2,1)S(1)}, bf16[2,2,104,128]{3,2,1,0:T(8,128)(2,1)S(1)}, u32[]{:S(2)}, u32[]{:S(2)}) collective-permute-start(bf16[2,2,104,128]{3,2,1,0:T(8,128)(2,1)S(1)} %get-tuple-element.340), channel_id=1, source_target_pairs={{0,4},{1,5},{2,6},{3,7},{4,0},{5,1},{6,2},{7,3},{8,12},{9,13},{10,... | collective-permute-start | bytes 319496 | tf_op jit(solution)/shard_map/ppermute | solution.py:28
  156.8 10.2 %collective-permute-start.50 = (bf16[2,2,104,128]{3,2,1,0:T(8,128)(2,1)S(1)}, bf16[2,2,104,128]{3,2,1,0:T(8,128)(2,1)S(1)}, u32[]{:S(2)}, u32[]{:S(2)}) collective-permute-start(bf16[2,2,104,128]{3,2,1,0:T(8,128)(2,1)S(1)} %get-tuple-element.341), channel_id=1, source_target_pairs={{0,6},{1,7},{2,4},{3,5},{4,2},{5,3},{6,0},{7,1},{8,14},{9,15},{10,... | collective-permute-start | bytes 319496 | tf_op jit(solution)/shard_map/ppermute | solution.py:28
  168.3 27.8 %collective-permute-start.59 = (bf16[8,192,384]{2,1,0:T(8,128)(2,1)S(1)}, bf16[8,192,384]{2,1,0:T(8,128)(2,1)S(1)}, u32[]{:S(2)}, u32[]{:S(2)}) collective-permute-start(bf16[8,192,384]{2,1,0:T(8,128)(2,1)S(1)} %slice_bitcast_fusion), channel_id=1, source_target_pairs={{0,16},{8,24},{16,0},{24,8},{1,17},{9,25},{17,1},{25,9},{2,18},{10... | collective-permute-start | bytes 3538952 | tf_op jit(solution)/shard_map/ppermute | solution.py:28
  173.2 15.2 %collective-permute-start.53 = (bf16[2,2,104,128]{3,2,1,0:T(8,128)(2,1)S(1)}, bf16[2,2,104,128]{3,2,1,0:T(8,128)(2,1)S(1)}, u32[]{:S(2)}, u32[]{:S(2)}) collective-permute-start(bf16[2,2,104,128]{3,2,1,0:T(8,128)(2,1)S(1)} %get-tuple-element.355), channel_id=1, source_target_pairs={{0,2},{1,3},{2,0},{3,1},{4,6},{5,7},{6,4},{7,5},{8,10},{9,11},{10,... | collective-permute-start | bytes 319496 | tf_op jit(solution)/shard_map/ppermute | solution.py:28
  175.7 12.7 %collective-permute-start.54 = (bf16[2,2,104,128]{3,2,1,0:T(8,128)(2,1)S(1)}, bf16[2,2,104,128]{3,2,1,0:T(8,128)(2,1)S(1)}, u32[]{:S(2)}, u32[]{:S(2)}) collective-permute-start(bf16[2,2,104,128]{3,2,1,0:T(8,128)(2,1)S(1)} %get-tuple-element.356), channel_id=1, source_target_pairs={{0,4},{1,5},{2,6},{3,7},{4,0},{5,1},{6,2},{7,3},{8,12},{9,13},{10,... | collective-permute-start | bytes 319496 | tf_op jit(solution)/shard_map/ppermute | solution.py:28
  176.1 12.3 %collective-permute-start.55 = (bf16[2,2,104,128]{3,2,1,0:T(8,128)(2,1)S(1)}, bf16[2,2,104,128]{3,2,1,0:T(8,128)(2,1)S(1)}, u32[]{:S(2)}, u32[]{:S(2)}) collective-permute-start(bf16[2,2,104,128]{3,2,1,0:T(8,128)(2,1)S(1)} %get-tuple-element.357), channel_id=1, source_target_pairs={{0,6},{1,7},{2,4},{3,5},{4,2},{5,3},{6,0},{7,1},{8,14},{9,15},{10,... | collective-permute-start | bytes 319496 | tf_op jit(solution)/shard_map/ppermute | solution.py:28
  178.2 15.2 %collective-permute-start.58 = (bf16[2,96,1536]{2,1,0:T(8,128)(2,1)S(1)}, bf16[2,96,1536]{2,1,0:T(8,128)(2,1)S(1)}, u32[]{:S(2)}, u32[]{:S(2)}) collective-permute-start(bf16[2,96,1536]{2,1,0:T(8,128)(2,1)S(1)} %get-tuple-element.353), channel_id=1, source_target_pairs={{0,1},{1,0},{2,3},{3,2},{4,5},{5,4},{6,7},{7,6},{8,9},{9,8},{10,11... | collective-permute-start | bytes 1769480 | tf_op jit(solution)/shard_map/ppermute | solution.py:28
  200.7 16.2 %collective-permute-start.71 = (bf16[2,96,1536]{2,1,0:T(8,128)(2,1)S(1)}, bf16[2,96,1536]{2,1,0:T(8,128)(2,1)S(1)}, u32[]{:S(2)}, u32[]{:S(2)}) collective-permute-start(bf16[2,96,1536]{2,1,0:T(8,128)(2,1)S(1)} %get-tuple-element.373), channel_id=1, source_target_pairs={{0,1},{1,0},{2,3},{3,2},{4,5},{5,4},{6,7},{7,6},{8,9},{9,8},{10,11... | collective-permute-start | bytes 1769480 | tf_op jit(solution)/shard_map/ppermute | solution.py:28
  205.0 16.1 %collective-permute-start.62 = (bf16[8,24,768]{2,1,0:T(8,128)(2,1)S(1)}, bf16[8,24,768]{2,1,0:T(8,128)(2,1)S(1)}, u32[]{:S(2)}, u32[]{:S(2)}) collective-permute-start(bf16[8,24,768]{2,1,0:T(8,128)(2,1)S(1)} %slice_bitcast_fusion.13), channel_id=1, source_target_pairs={{0,16},{8,24},{16,0},{24,8},{1,17},{9,25},{17,1},{25,9},{2,18},{10... | collective-permute-start | bytes 884744 | tf_op jit(solution)/shard_map/ppermute | solution.py:28
  206.3 16.5 %collective-permute-start.63 = (bf16[4,48,768]{2,1,0:T(8,128)(2,1)S(1)}, bf16[4,48,768]{2,1,0:T(8,128)(2,1)S(1)}, u32[]{:S(2)}, u32[]{:S(2)}) collective-permute-start(bf16[4,48,768]{2,1,0:T(8,128)(2,1)S(1)} %slice_bitcast_fusion.12), channel_id=1, source_target_pairs={{0,1},{1,0},{2,3},{3,2},{4,5},{5,4},{6,7},{7,6},{8,9},{9,8},{10,11... | collective-permute-start | bytes 884744 | tf_op jit(solution)/shard_map/ppermute | solution.py:28
  207.0 21.8 %collective-permute-start.61 = (bf16[8,48,896]{2,1,0:T(8,128)(2,1)S(1)}, bf16[8,48,896]{2,1,0:T(8,128)(2,1)S(1)}, u32[]{:S(2)}, u32[]{:S(2)}) collective-permute-start(bf16[8,48,896]{2,1,0:T(8,128)(2,1)S(1)} %slice_bitcast_fusion.3), channel_id=1, source_target_pairs={{0,16},{8,24},{16,0},{24,8},{1,17},{9,25},{17,1},{25,9},{2,18},{10... | collective-permute-start | bytes 2064392 | tf_op jit(solution)/shard_map/ppermute | solution.py:28
  208.5 31.0 %collective-permute-start.66 = (bf16[2,96,1536]{2,1,0:T(8,128)(2,1)S(1)}, bf16[2,96,1536]{2,1,0:T(8,128)(2,1)S(1)}, u32[]{:S(2)}, u32[]{:S(2)}) collective-permute-start(bf16[2,96,1536]{2,1,0:T(8,128)(2,1)S(1)} %fusion.3), channel_id=1, source_target_pairs={{0,2},{1,3},{2,0},{3,1},{4,6},{5,7},{6,4},{7,5},{8,10},{9,11},{10,... | collective-permute-start | bytes 1769480 | tf_op jit(solution)/shard_map/ppermute | solution.py:28
  225.1 17.2 %collective-permute-start.65 = (bf16[4,192,384]{2,1,0:T(8,128)(2,1)S(1)}, bf16[4,192,384]{2,1,0:T(8,128)(2,1)S(1)}, u32[]{:S(2)}, u32[]{:S(2)}) collective-permute-start(bf16[4,192,384]{2,1,0:T(8,128)(2,1)S(1)} %get-tuple-element.388), channel_id=1, source_target_pairs={{0,1},{1,0},{2,3},{3,2},{4,5},{5,4},{6,7},{7,6},{8,9},{9,8},{10,11... | collective-permute-start | bytes 1769480 | tf_op jit(solution)/shard_map/ppermute | solution.py:28
  232.3 16.1 %collective-permute-start.64 = (bf16[4,48,896]{2,1,0:T(8,128)(2,1)S(1)}, bf16[4,48,896]{2,1,0:T(8,128)(2,1)S(1)}, u32[]{:S(2)}, u32[]{:S(2)}) collective-permute-start(bf16[4,48,896]{2,1,0:T(8,128)(2,1)S(1)} %get-tuple-element.390), channel_id=1, source_target_pairs={{0,1},{1,0},{2,3},{3,2},{4,5},{5,4},{6,7},{7,6},{8,9},{9,8},{10,11... | collective-permute-start | bytes 1032200 | tf_op jit(solution)/shard_map/ppermute | solution.py:28
  237.1 7.9 %collective-permute-start.74 = (bf16[1,24,768]{2,1,0:T(8,128)(2,1)S(1)}, bf16[1,24,768]{2,1,0:T(8,128)(2,1)S(1)}, u32[]{:S(2)}, u32[]{:S(2)}) collective-permute-start(bf16[1,24,768]{2,1,0:T(8,128)(2,1)S(1)} %add_convert_fusion.22), channel_id=1, source_target_pairs={{0,4},{1,5},{2,6},{3,7},{4,0},{5,1},{6,2},{7,3},{8,12},{9,13},{10,... | collective-permute-start | bytes 110600 | tf_op jit(solution)/shard_map/ppermute | solution.py:28
  242.6 11.6 %collective-permute-start.72 = (bf16[2,192,384]{2,1,0:T(8,128)(2,1)S(1)}, bf16[2,192,384]{2,1,0:T(8,128)(2,1)S(1)}, u32[]{:S(2)}, u32[]{:S(2)}) collective-permute-start(bf16[2,192,384]{2,1,0:T(8,128)(2,1)S(1)} %get-tuple-element.402), channel_id=1, source_target_pairs={{0,2},{1,3},{2,0},{3,1},{4,6},{5,7},{6,4},{7,5},{8,10},{9,11},{10,... | collective-permute-start | bytes 884744 | tf_op jit(solution)/shard_map/ppermute | solution.py:28
  243.8 13.4 %collective-permute-start.73 = (bf16[1,96,1536]{2,1,0:T(8,128)(2,1)S(1)}, bf16[1,96,1536]{2,1,0:T(8,128)(2,1)}, u32[]{:S(2)}, u32[]{:S(2)}) collective-permute-start(bf16[1,96,1536]{2,1,0:T(8,128)(2,1)S(1)} %add_convert_fusion.4), channel_id=1, source_target_pairs={{0,4},{1,5},{2,6},{3,7},{4,0},{5,1},{6,2},{7,3},{8,12},{9,13},{10,... | collective-permute-start | bytes 884744 | tf_op jit(solution)/shard_map/ppermute | solution.py:28
  258.4 9.0 %collective-permute-start.80 = (bf16[96,1536]{1,0:T(8,128)(2,1)S(1)}, bf16[96,1536]{1,0:T(8,128)(2,1)S(1)}, u32[]{:S(2)}, u32[]{:S(2)}) collective-permute-start(bf16[96,1536]{1,0:T(8,128)(2,1)S(1)} %fusion.17), channel_id=1, source_target_pairs={{0,16},{8,24},{16,0},{24,8},{1,17},{9,25},{17,1},{25,9},{2,18},{10... | collective-permute-start | bytes 884744 | tf_op jit(solution)/shard_map/ppermute | solution.py:28
  259.3 8.2 %collective-permute-start.78 = (bf16[2,48,896]{2,1,0:T(8,128)(2,1)S(1)}, bf16[2,48,896]{2,1,0:T(8,128)(2,1)S(1)}, u32[]{:S(2)}, u32[]{:S(2)}) collective-permute-start(bf16[2,48,896]{2,1,0:T(8,128)(2,1)S(1)} %get-tuple-element.412), channel_id=1, source_target_pairs={{0,2},{1,3},{2,0},{3,1},{4,6},{5,7},{6,4},{7,5},{8,10},{9,11},{10,... | collective-permute-start | bytes 516104 | tf_op jit(solution)/shard_map/ppermute | solution.py:28
  (48 other events, 264.5 us)

commit v3 on v2

--- a/solution.py
+++ b/solution.py
@@ -162,15 +162,12 @@
 SMEM = pl.BlockSpec(memory_space=pltpu.SMEM)
 
 
-COSTS = {
-    "assemble": 1.5, "project": 5.4, "mix_segments": 1.1, "intra_forward": 5.9, "inter_forward": 5.5,
-    "expand": 9.5, "contract": 10.5, "back_to_heads": 11.8, "intra_backward": 10.3,
-    "inter_backward": 4.6, "input_grad": 4.0, "weight_grad": 4.0, "vector_rows": 1.5,
-}
+COSTS = {"assemble": 1.5, "project": 5.4, "mix_segments": 1.1, "intra_forward": 5.9, "inter_forward": 5.5, "expand": 2.85, "contract": 6.0, "turn": 22.5, "back_to_heads": 11.8, "intra_backward": 10.3, "inter_backward": 4.6, "input_grad": 4.0, "vector_rows": 1.5, "down": 6.0, "up": 1.2, "outq": 2.4, "kv": 3.36}
+TAIL = ('kv0+kv1', 'up', 'grad', 'down', 'outq', 'kv1', 'kv0', 'kv1', 'up', 'outq', 'kv0', 'outq', 'down', 'kv0', 'up', 'kv1', 'outq', 'kv0', 'down', 'kv1', 'outq', 'kv0', 'kv1')
 FLOPS_PER_US = 6.0e8
 
 
-def call(kernel, name, outs, in_specs, scratch=(), mib=8):
+def call(kernel, name, outs, in_specs, scratch=(), cost=None, mib=8):
     return pl.pallas_call(
         kernel,
         out_shape=outs,
@@ -179,7 +176,7 @@
         scratch_shapes=scratch,
         compiler_params=pltpu.CompilerParams(vmem_limit_bytes=mib * 1024 * 1024),
         cost_estimate=pl.CostEstimate(
-            flops=int(COSTS[name] * FLOPS_PER_US), transcendentals=0, bytes_accessed=0
+            flops=int((cost or COSTS[name]) * FLOPS_PER_US), transcendentals=0, bytes_accessed=0
         ),
         name=name,
     )
@@ -521,11 +518,11 @@
     )(att, tokens, w_out, w_up, small)
 
 
-def contract(ids, gelu, slope, hat1, cotangent, w_down, small):
+def contract(ids, gelu, hat1, cotangent, w_down, small):
     rows, ff = gelu.shape
 
-    def kernel(ids_ref, gelu_ref, slope_ref, hat1_ref, cot_ref, w_ref, small_ref,
-               out_ref, dres_ref, dlow_ref, dup_ref, dlow_half_ref, dup_half_ref, sums_ref):
+    def kernel(ids_ref, gelu_ref, hat1_ref, cot_ref, w_ref, small_ref,
+               out_ref, dres_ref, dlow_ref, dlow_half_ref, sums_ref):
         sums_ref[...] = jnp.zeros_like(sums_ref)
 
         def block(i):
@@ -544,6 +541,35 @@
             d_low = d_res.astype(bf16)
             dlow_ref[at, :] = d_low
             sums_ref[B_DOWN : B_DOWN + 1, :] += jnp.sum(d_low.astype(f32), axis=0, keepdims=True)
+            theirs = 1 - ids_ref[0]
+            dlow_half_ref[at, :] = dlow_ref[
+                at, pl.ds(pl.multiple_of(theirs * (D // 2), 128), D // 2)
+            ]
+
+        loop(rows // SEG, block)
+
+    return call(
+        kernel,
+        "contract",
+        (
+            shape_of((rows, D), bf16),
+            shape_of((rows, D), f32),
+            shape_of((rows, D), bf16),
+            shape_of((rows, D // 2), bf16),
+            shape_of((16, D), f32),
+        ),
+        [SMEM] + [VMEM] * 5,
+    )(ids, gelu, hat1, cotangent, w_down, small)
+
+
+def turn(ids, d_lower, slope, w_down, sums):
+    rows, ff = slope.shape
+
+    def kernel(ids_ref, dlow_ref, slope_ref, w_ref, sums_in_ref, dup_ref, dup_half_ref, sums_ref):
+        sums_ref[...] = sums_in_ref[...]
+
+        def block(i):
+            at = rows_at(i)
 
             def part(m):
                 for c in range(3):
@@ -557,9 +583,6 @@
 
             loop(ff // D, part)
             theirs = 1 - ids_ref[0]
-            dlow_half_ref[at, :] = dlow_ref[
-                at, pl.ds(pl.multiple_of(theirs * (D // 2), 128), D // 2)
-            ]
             dup_half_ref[at, :] = dup_ref[
                 at, pl.ds(pl.multiple_of(theirs * (ff // 2), 128), ff // 2)
             ]
@@ -568,18 +591,12 @@
 
     return call(
         kernel,
-        "contract",
+        "turn",
         (
-            shape_of((rows, D), bf16),
-            shape_of((rows, D), f32),
-            shape_of((rows, D), bf16),
-            shape_of((rows, ff), bf16),
-            shape_of((rows, D // 2), bf16),
-            shape_of((rows, ff // 2), bf16),
-            shape_of((16, D), f32),
+            shape_of((rows, ff), bf16), shape_of((rows, ff // 2), bf16), shape_of((16, D), f32),
         ),
-        [SMEM] + [VMEM] * 6,
-    )(ids, gelu, slope, hat1, cotangent, w_down, small)
+        [SMEM] + [VMEM] * 4,
+    )(ids, d_lower, slope, w_down, sums)
 
 
 def back_to_heads(ids, d_upper, d_res2, hat1, inv1, rden, att, q, cos, sin, w_out, w_up, small,
@@ -789,7 +806,7 @@
     return total
 
 
-def weight_grad(ids, products, fsdp, splits, own_half=True, sums=None):
+def weight_grad(ids, products, fsdp, splits, key, own_half=True, sums=None):
     height = products[0][0].shape[1]
     widths = [product[3].shape[1] for product in products]
     block = height // fsdp
@@ -838,6 +855,7 @@
         "weight_grad",
         tuple(shape_of((n, fsdp, share // n, width), bf16) for n in splits),
         [SMEM] + [VMEM] * (4 * len(products) + len(extra)),
+        cost=COSTS[key],
     )(ids, *(x for product in products for x in product), *extra)
 
 
@@ -869,7 +887,8 @@
         (received,) = yield [(send[quarter:], axis, bit)]
         after = add_low(keep[quarter:], received)
         (received,) = yield [(tie(send[:quarter], after), axis, bit)]
-        keep, send = add_low(keep[:quarter], received), after
+        keep = add_low(keep[:quarter], received)
+        send = tie(after, keep)
     x = yield from halving_stages(keep, send, bits)
     for axis, bit in axis_bits("group")[1:]:
         (received,) = yield [(x, axis, bit)]
@@ -968,7 +987,7 @@
     ids = jnp.stack([core, chip, own]).astype(jnp.int32)
 
     pipe = Pipeline()
-    pipe.add("kv", gather_stages(w_qkv[:, D:], True))
+    pipe.add("kv", gather_stages(w_qkv[:, D:]))
     pipe.add("tokens", core_stage(tokens))
     pipe.slot()
     pipe.slot(only=("kv",))
@@ -991,22 +1010,25 @@
     )))
     pipe.add("up", gather_stages(w_up))
     pipe.add("down", gather_stages(w_down))
-    pipe.slot(only=("kv", "qo"))
-    pipe.slot(only=("kv", "qo"))
+    pipe.slot(only=("kv",))
+    pipe.slot(*pipe.started, only=("qo",))
+    pipe.slot(only=("kv",))
+    pipe.slot(*pipe.started, only=("qo",))
+    pipe.slot(*pipe.started, only=("up",))
     pipe.slot(only=("kv", "qo"))
     pipe.slot(*pipe.started, only=("up",))
     w_kv = assemble(*pipe.finish("kv", only=("kv",)))
     tables = (from_ancestors, from_descendants, wave, wave_t)
-    k, v, increments = project(ids, tie(tokens, tokens_other, *tables), w_kv, cos, sin, fsdp)
-    pipe.arrive(k, only=("qo", "up"))
+    k, v, increments = project(
+        ids, tie(tokens, tokens_other, *tables, *pipe.started), w_kv, cos, sin, fsdp
+    )
+    pipe.arrive(k, only=("qo",))
     pipe.add("state", trade_stages(increments))
     pipe.slot(*pipe.started, only=("state", "qo"))
     pipe.slot(only=("state", "qo"))
     pipe.slot(*pipe.started, only=("up",))
-    pipe.slot(*pipe.started, only=("down",))
     w_qo = assemble(*pipe.finish("qo", only=("qo",)))
-    pipe.slot(w_qo, only=("up",))
-    pipe.slot(*pipe.started, only=("down",))
+    pipe.slot(w_qo, only=("down",))
     q, num, den = intra_forward(tie(tokens, *pipe.started), w_qo, k, v, wave)
     far, near = pipe.finish("state", q, only=("state",))
     mixed = mix_segments(from_ancestors, far, near)
@@ -1014,65 +1036,79 @@
     pipe.add("path", trade_stages(mixed))
     pipe.slot(*pipe.started, only=("path", "up"))
     small = vector_rows(tie(w_qo, *pipe.started), shard_rows, b_up.shape[0], ff // D)
-    pipe.slot(small, only=("path", "up", "down"))
-    path = pipe.finish("path", *pipe.started, only=("path",))
-    att, rden = inter_forward(ids, q, num, den, cos, sin, *path)
+    pipe.slot(small, only=("path", "down"))
+    pipe.slot(*pipe.started, only=("up",))
+    w_up_full = assemble(*pipe.finish("up", only=("up",)))
+    path = pipe.finish("path", w_up_full, only=("path",))
+    pipe.slot(path[1], only=("down",))
+    att, rden = inter_forward(ids, tie(q, *pipe.started), num, den, cos, sin, *path)
+    pipe.slot(att, only=("down",))
     pipe.add("att", core_stage(att))
-    pipe.slot(att, only=("down", "att"))
-    w_up_full = assemble(*pipe.finish("up", att, only=("up",)))
-    att_other = pipe.read("att", w_up_full)
+    pipe.slot(*pipe.started, only=("att",))
+    att_other = pipe.read("att", *pipe.started)
     hat1, inv1, low1, gelu, slope = expand(
-        tie(att, att_other, *pipe.started), tokens, w_qo, w_up_full, small
+        tie(att, *pipe.started), tokens, w_qo, w_up_full, small
     )
     pipe.slot(low1, only=("down",))
     w_down_full = assemble(*pipe.finish("down", only=("down",)))
     pipe.add("gelu", core_stage(gelu))
     pipe.add("low1", core_stage(low1))
     pipe.slot(w_down_full, only=("gelu", "low1"))
-    output, d_res2, d_lower, d_upper, d_lower_half, d_upper_half, sums = contract(
-        ids, gelu, slope, hat1, cotangent, w_down_full, small
-    )
-    low1_other = pipe.read("low1", sums)
-    gelu_other = pipe.read("gelu", sums)
+    output, d_res2, d_lower, d_lower_half, sums = contract(
+        ids, gelu, hat1, cotangent, w_down_full, small
+    )
+    low1_other = pipe.read("low1", d_lower)
+    gelu_other = pipe.read("gelu", d_lower)
     grads = Pipeline()
     grads.add("d_lower", core_stage(d_lower_half))
+    grads.slot(low1_other, gelu_other)
+    d_upper, d_upper_half, sums = turn(
+        ids, tie(d_lower, *grads.started), slope, w_down_full, sums
+    )
+    d_lower_other = grads.read("d_lower", d_upper)
     grads.add("d_upper", core_stage(d_upper_half))
-    grads.slot(low1_other, gelu_other)
+    grads.slot(d_lower_other, only=("d_upper",))
+    two = chips == 2
+
+    def reduction(part):
+        return share_stages(part, core, chip) if two else reduce_stages(part, core)
+
+    split = 2 if two else 1
+    (down_part,) = weight_grad(
+        ids, [(gelu, gelu_other, tie(d_lower, *grads.started), d_lower_other)], fsdp, [split],
+        "down",
+    )
+    d_upper_other = grads.read("d_upper", down_part)
+    grads.add("down", reduction(down_part))
+    grads.slot(d_upper_other, only=("down",))
+    (up_part,) = weight_grad(
+        ids, [(low1, low1_other, tie(d_upper, *grads.started), d_upper_other)], fsdp, [1], "up",
+    )
+    grads.add("up", reduce_stages(up_part, core, True))
+    grads.slot(only=("up",))
     d_res1, d_mixed, d_mixed_half, d_num, d_den, sums, *back = back_to_heads(
         ids, tie(d_upper, *grads.started), d_res2, hat1, inv1, rden, att, q, cos, sin, w_qo,
         w_up_full, small, sums, fsdp,
     )
-    d_lower_other = grads.read("d_lower", d_num)
-    d_upper_other = grads.read("d_upper", d_num)
     grads.add("state", trade_stages(back))
+    grads.slot(only=("state",))
+    grads.slot(d_num, only=("up",))
+    grads.slot(*grads.started, only=("state",))
     grads.add("d_mixed", core_stage(d_mixed_half))
-    grads.slot(d_lower_other, d_upper_other)
-    two = chips == 2
-
-    def reduction(part):
-        return share_stages(part, core, chip) if two else reduce_stages(part, core)
-
-    split = 2 if two else 1
-    (down_part,) = weight_grad(
-        ids, [(gelu, gelu_other, tie(d_lower, *grads.started), d_lower_other)], fsdp, [split]
-    )
-    d_mixed_other = grads.read("d_mixed", down_part)
-    grads.add("down", reduction(down_part))
-    grads.slot(d_mixed_other, only=("state", "down"))
-    (up_part,) = weight_grad(
-        ids, [(low1, low1_other, tie(d_upper, *grads.started), d_upper_other)], fsdp, [1]
-    )
-    far, near = grads.finish("state", up_part, only=("state",))
-    grads.add("up", reduce_stages(up_part, core, True))
-    grads.slot(near, only=("up",))
-    mixed = mix_segments(from_descendants, far, tie(near, *grads.started))
+    grads.slot(*grads.started, only=("d_mixed",))
+    grads.slot(*grads.started, only=("down",))
+    d_mixed_other = grads.read("d_mixed", *grads.started)
+    far, near = grads.finish("state", d_mixed_other, only=("state",))
+    mixed = mix_segments(from_descendants, far, near)
+    grads.arrive(*mixed, only=("up",))
     grads.add("path", trade_stages(mixed))
-    grads.slot(only=("path",))
+    grads.slot(*grads.started, only=("path",))
     d_q, d_q_half, d_k, d_v = intra_backward(
         ids, tie(q, *grads.started), k, v, d_num, d_den, cos, sin, wave, wave_t, *path
     )
     grads.add("d_q", core_stage(d_q_half))
-    grads.slot(d_q, only=("path", "d_q"))
+    grads.arrive(d_q, only=("down",))
+    grads.slot(*grads.started, only=("path", "d_q"))
     grads.slot(*grads.started, only=("up",))
     d_q_other = grads.read("d_q", *grads.started)
     (outq_part,) = weight_grad(
@@ -1081,33 +1117,30 @@
             (att, att_other, d_mixed, d_mixed_other),
             (tokens, tokens_other, d_q, d_q_other),
         ],
-        fsdp, [split], sums=sums,
+        fsdp, [split], "outq", sums=sums,
     )
     grads.add("outq", reduction(outq_part))
-    grads.arrive(outq_part, only=("down",))
-    grads.slot(*grads.started, only=("outq",))
+    grads.slot(only=("outq",))
     back = grads.finish("path", *grads.started, only=("path",))
     d_kv = inter_backward(ids, k, v, d_k, d_v, cos, sin, *back)
     grads.add("d_kv", core_stage(d_kv[1]))
     grads.slot(only=("d_kv",))
-    d_kv_other = grads.read("d_kv")
+    grads.slot(*grads.started, only=("down",))
+    grads.arrive(*grads.started, only=("up",))
+    d_kv_other = grads.read("d_kv", *grads.started)
     kv_parts = weight_grad(
-        ids, [(tokens, tokens_other, d_kv[0], d_kv_other)], fsdp, [2, 1] if two else [1], False,
+        ids, [(tokens, tokens_other, d_kv[0], d_kv_other)], fsdp, [2, 1] if two else [1], "kv",
+        False,
     )
     grads.add("kv0", reduction(kv_parts[0]))
     for part in kv_parts[1:]:
         grads.add("kv1", reduce_stages(part, core))
-    kv = ("kv0", "kv1")
-    grads.slot(only=kv)
-    grads.slot(*kv_parts, only=("up",))
-    tokens_grad = input_grad(ids, d_q, tie(d_kv, *grads.started), d_res1, w_qo, w_kv)
-    grads.slot(tokens_grad, only=kv)
-    grads.slot(*grads.started, only=("down",))
-    grads.slot(*grads.started, only=("outq",))
-    grads.slot(*grads.started, only=kv)
-    grads.slot(*grads.started, only=kv)
-    grads.slot(*grads.started, only=("up", "down"))
-    grads.slot(*grads.started, only=kv)
+    for step in TAIL:
+        if step == "grad":
+            tokens_grad = input_grad(ids, d_q, tie(d_kv, *grads.started), d_res1, w_qo, w_kv)
+            grads.started = (tokens_grad,)
+        elif grads.names(step.split("+")):
+            grads.slot(*grads.started, only=step.split("+"))
     while grads.running:
         grads.slot(*grads.started)
     done = grads.finished

time: 285 us -> 280 us (0.982)
  waiting for transfers between devices: 95.8 us -> 85 us
  other arithmetic: 12.2 us -> 17.6 us
  starting transfers between devices: 86.5 us -> 81.9 us
    ppermute x88 -> x86, waiting for transfers between devices: 95.8 us -> 85 us  [exchange(): return lax.ppermute(x, axis, [(i, i ^ offset) for i in range(size)])]
    pallas_call x0 -> x1, Pallas kernels: none -> 5.03 us  [turn(): call(kernel, 'turn', (shape_of((rows, ff), bf16), shape_of((rows, ff // 2...]
    pallas_call x1, Pallas kernels: 10.1 us -> 5.32 us  [contract(): call(kernel, 'contract', (shape_of((rows, D), bf16), shape_of((rows, D),...]
    ppermute x88 -> x86, starting transfers between devices: 86.5 us -> 81.9 us  [exchange(): return lax.ppermute(x, axis, [(i, i ^ offset) for i in range(size)])]
    convert_element_type x21, other arithmetic: 2.69 us -> 6.17 us  [add_low(): return (a.astype(f32) + b.astype(f32)).astype(bf16)]
  transfers between devices with their start and end apart: 88 -> 86, of which waited for: 41 -> 40; matrix products, arithmetic and copies ran while one was open for 4% -> 7% of each run, Pallas kernels for 26% -> 27%
where the time goes in v3:
time: 280 us; the launch traced here: 279 us
  waiting for transfers between devices  85 us (30%)
  starting transfers between devices  81.9 us (29%)
  Pallas kernels  79.2 us (28%)
  other arithmetic  17.6 us (6%)
  local copies, waits for them, and re-layouts  10 us (4%)
  matrix products  3.7 us (1%)
    ppermute x86, waiting for transfers between devices, exchange(): return lax.ppermute(x, axis, [(i, i ^ offset) for i in range(size)])  85 us
    ppermute x86, starting transfers between devices, exchange(): return lax.ppermute(x, axis, [(i, i ^ offset) for i in range(size)])  81.9 us
    pallas_call x4, Pallas kernels, weight_grad(): call(kernel, 'weight_grad', tuple((shape_of((n, fsdp, share // n, width),...  14 us
    pallas_call x1, Pallas kernels, back_to_heads(): call(kernel, 'back_to_heads', (shape_of((rows, D), f32), shape_of((rows,...  9.92 us
    pallas_call x1, Pallas kernels, intra_backward(): call(kernel, 'intra_backward', (shape_of((rows, D), bf16), shape_of((rows...  8.77 us
    pallas_call x1, Pallas kernels, expand(): call(kernel, 'expand', (shape_of((rows, D), f32), shape_of((rows, LANES),...  7.46 us
    convert_element_type x21, other arithmetic, add_low(): return (a.astype(f32) + b.astype(f32)).astype(bf16)  6.17 us
    pallas_call x1, Pallas kernels, intra_forward(): call(kernel, 'intra_forward', (shape_of((rows, D), bf16), wide, wide), [V...  5.87 us
  transfers between devices with their start and end apart: 86, of which 40 were waited for; matrix products, arithmetic and copies ran while one was open for 7% of the time, Pallas kernels for 27%

profile of v3, /device:TPU:0, one launch (start us, length us, event | category | flops | bytes accessed | tf_op | source)
XLA Modules:
  0.0 279.2 jit_solution(16985057203707557376)
XLA Ops:
  1.5 4.0 %collective-permute-start = (bf16[1,24,1536]{2,1,0:T(8,128)(2,1)S(1)}, bf16[1,24,1536]{2,1,0:T(8,128)(2,1)S(1)}, u32[]{:S(2)}, u32[]{:S(2)}) collective-permute-start(bf16[1,24,1536]{2,1,0:T(8,128)(2,1)S(1)} %slice_bitcast_fusion.14), channel_id=1, source_target_pairs={{0,4},{1,5},{2,6},{3,7},{4,0},{5,1},{6,2},{7,3},{8,12},{9,13},{10,... | collective-permute-start | bytes 221192 | tf_op jit(solution)/shard_map/ppermute | solution.py:28
  12.4 1.8 fusion.24
  19.3 2.2 collective-permute-start.2
  27.4 3.0 %collective-permute-start.11 = (bf16[1,24,3072]{2,1,0:T(8,128)(2,1)}, bf16[1,24,3072]{2,1,0:T(8,128)(2,1)S(1)}, u32[]{:S(2)}, u32[]{:S(2)}) collective-permute-start(bf16[1,24,3072]{2,1,0:T(8,128)(2,1)} %bitcast.15), channel_id=1, source_target_pairs={{0,4},{1,5},{2,6},{3,7},{4,0},{5,1},{6,2},{7,3},{8,12},{9,13},{10,... | collective-permute-start | bytes 442376 | tf_op jit(solution)/shard_map/ppermute | solution.py:28
  32.8 2.6 collective-permute-done.11
  38.4 5.1 %project.1 = (bf16[512,768]{1,0:T(8,128)(2,1)S(1)}, bf16[512,768]{1,0:T(8,128)(2,1)S(1)}, bf16[2,2,104,128]{3,2,1,0:T(8,128)(2,1)S(1)}, bf16[2,2,104,128]{3,2,1,...) custom-call(s32[3]{0:T(128)S(1)} %pad_add_fusion.ids_ref, ...), custom_call_target="tpu_custom_call" | custom-call | flops 3240000000 | tf_op jit(solution)/shard_map/project/pallas_call | solution.py:353
  46.0 3.1 %collective-permute-start.17 = (bf16[2,2,104,128]{3,2,1,0:T(8,128)(2,1)S(1)}, bf16[2,2,104,128]{3,2,1,0:T(8,128)(2,1)S(1)}, u32[]{:S(2)}, u32[]{:S(2)}) collective-permute-start(bf16[2,2,104,128]{3,2,1,0:T(8,128)(2,1)S(1)} %get-tuple-element.254), channel_id=1, source_target_pairs={{0,4},{1,5},{2,6},{3,7},{4,0},{5,1},{6,2},{7,3},{8,12},{9,13},{10,... | collective-permute-start | bytes 319496 | tf_op jit(solution)/shard_map/ppermute | solution.py:28
  50.4 4.5 %collective-permute-done.16.refs_1_ = bf16[2,2,104,128]{3,2,1,0:T(8,128)(2,1)S(1)} collective-permute-done((bf16[2,2,104,128]{3,2,1,0:T(8,128)(2,1)S(1)}, bf16[2,2,104,128]{3,2,1,0:T(8,128)(2,1)S(1)}, u32[]{:S(2)}, u32[]{:S(2)}) %collective-permute-start.16) | collective-permute-done | bytes 106528 | tf_op jit(solution)/shard_map/ppermute | solution.py:28
  56.9 1.7 collective-permute-start.25
  59.4 2.3 collective-permute-done.21
  65.9 5.9 %intra_forward.1 = (bf16[512,768]{1,0:T(8,128)(2,1)S(1)}, f32[512,768]{1,0:T(8,128)S(1)}, f32[512,768]{1,0:T(8,128)S(1)}) custom-call(bf16[512,768]{1,0:T(8,128)(2,1)S(1)} %copy-done.6, bf16[768,1792]{1,0:T(8,128)(2,1)S(1)} %bitcast.103, bf16[512,768]{1,0:T(8,128)(2,1)S(1)} %get-tuple-element.245.k_ref, bf16[512,768]{1,0:T(8,128)(2,1)S(1)} %get-tuple-element.262.v_ref, ...), custom_call_target="tpu_custom_call" | custom-call | flops 3540000000 | tf_op jit(solution)/shard_map/intra_forward/pallas_call | solution.py:411
  77.4 2.3 collective-permute-start.28
  79.8 1.8 collective-permute-done.26.refs_1_
  81.6 3.0 %collective-permute-done.27.refs_2_ = bf16[2,2,104,128]{3,2,1,0:T(8,128)(2,1)S(1)} collective-permute-done((bf16[2,2,104,128]{3,2,1,0:T(8,128)(2,1)S(1)}, bf16[2,2,104,128]{3,2,1,0:T(8,128)(2,1)S(1)}, u32[]{:S(2)}, u32[]{:S(2)}) %collective-permute-start.27) | collective-permute-done | bytes 106528 | tf_op jit(solution)/shard_map/ppermute | solution.py:28
  86.6 1.8 collective-permute-start.29
  91.8 3.5 %collective-permute-done.30.refs_4_ = bf16[4,2,104,128]{3,2,1,0:T(8,128)(2,1)S(1)} collective-permute-done((bf16[4,2,104,128]{3,2,1,0:T(8,128)(2,1)S(1)}, bf16[4,2,104,128]{3,2,1,0:T(8,128)(2,1)S(1)}, u32[]{:S(2)}, u32[]{:S(2)}) %collective-permute-start.30) | collective-permute-done | bytes 213024 | tf_op jit(solution)/shard_map/ppermute | solution.py:28
  97.8 4.0 %inter_forward.1 = (bf16[512,768]{1,0:T(8,128)(2,1)S(1)}, f32[512,768]{1,0:T(8,128)S(1)}) custom-call(s32[3]{0:T(128)S(1)} %pad_add_fusion.ids_ref, bf16[512,768]{1,0:T(8,128)(2,1)S(1)} %get-tuple-element.370.q_ref, f32[512,768]{1,0:T(8,128)S(1)} %get-tuple-element.301.num_ref, f32[512,768]{1,0:T(8,128)S(1)} %get-tuple-element.302.den_ref, ...), custom_call_target="tpu_custom_call" | custom-call | flops 3300000000 | tf_op jit(solution)/shard_map/inter_forward/pallas_call | solution.py:452
  101.8 2.2 collective-permute-done.35
  106.0 1.7 collective-permute-start.38
  107.7 7.5 %expand.1 = (f32[512,768]{1,0:T(8,128)S(1)}, f32[512,128]{1,0:T(8,128)S(1)}, bf16[512,768]{1,0:T(8,128)(2,1)S(1)}, bf16[512,3072]{1,0:T(8,128)(2,1)S(1)}, bf16[512,3072]{1,0:T(8,128)(2,1)S(1)}) custom-call(bf16[512,768]{1,0:T(8,128)(2,1)S(1)} %get-tuple-element.309.att_ref.refs_0_, bf16[512,768]{1,0:T(8,128)(2,1)S(1)} %copy-done.6, ...), custom_call_target="tpu_custom_call" | custom-call | flops 1710000000 | tf_op jit(solution)/shard_map/expand/pallas_call | solution.py:507
  115.1 4.1 %collective-permute-done.37 = bf16[8,96,384]{2,1,0:T(8,128)(2,1)S(1)} collective-permute-done((bf16[8,96,384]{2,1,0:T(8,128)(2,1)S(1)}, bf16[8,96,384]{2,1,0:T(8,128)(2,1)S(1)}, u32[]{:S(2)}, u32[]{:S(2)}) %collective-permute-start.37) | collective-permute-done | bytes 589856 | tf_op jit(solution)/shard_map/ppermute | solution.py:28
  120.4 2.3 collective-permute-done.39.refs_1_
  122.8 1.7 collective-permute-done.40.refs_3_
  126.3 5.3 %contract.1 = (bf16[512,768]{1,0:T(8,128)(2,1)}, f32[512,768]{1,0:T(8,128)S(1)}, bf16[512,768]{1,0:T(8,128)(2,1)S(1)}, bf16[512,384]{1,0:T(8,128)(2,1)S(1)}, f32[16,768]{1,0:T(8,128)S(1)}) custom-call(s32[3]{0:T(128)S(1)} %pad_add_fusion.ids_ref, bf16[512,3072]{1,0:T(8,128)(2,1)S(1)} %get-tuple-element.324.gelu_ref.refs_0_, ...), custom_call_target="tpu_custom_call" | custom-call | flops 3600000000 | tf_op jit(solution)/shard_map/contract/pallas_call | solution.py:551
  132.7 5.0 %turn.1 = (bf16[512,3072]{1,0:T(8,128)(2,1)S(1)}, bf16[512,1536]{1,0:T(8,128)(2,1)S(1)}, f32[16,768]{1,0:T(8,128)S(1)}) custom-call(s32[3]{0:T(128)S(1)} %pad_add_fusion.ids_ref, bf16[512,768]{1,0:T(8,128)(2,1)S(1)} %get-tuple-element.334.dlow_ref.refs_2_, bf16[512,3072]{1,0:T(8,128)(2,1)S(1)} %get-tuple-element.328.slope_ref, ...), custom_call_target="tpu_custom_call" | custom-call | flops 13500000256 | tf_op jit(solution)/shard_map/turn/pallas_call | solution.py:592
  138.2 5.7 %weight_grad.4 = bf16[2,8,192,384]{3,2,1,0:T(8,128)(2,1)S(1)} custom-call(s32[3]{0:T(128)S(1)} %pad_add_fusion.ids_ref, bf16[512,3072]{1,0:T(8,128)(2,1)S(1)} %get-tuple-element.324.gelu_ref.refs_0_, bf16[512,3072]{1,0:T(8,128)(2,1)S(1)} %collective-permute-done.42.refs_1_, bf16[512,768]{1,0:T(8,128)(2,1)S(1)} %get-tuple-element.334.dlow_ref.refs_2_, ...), custom_call_target="tpu_custom_call" | custom-call | flops 3600000000 | tf_op jit(solution)/shard_map/weight_grad/pallas_call | solution.py:853
  144.1 3.2 %weight_grad.5 = bf16[1,8,96,1536]{3,2,1,0:T(8,128)(2,1)S(1)} custom-call(s32[3]{0:T(128)S(1)} %pad_add_fusion.ids_ref, bf16[512,768]{1,0:T(8,128)(2,1)S(1)} %get-tuple-element.322.refs_0_, bf16[512,768]{1,0:T(8,128)(2,1)S(1)} %collective-permute-done.41.refs_1_, bf16[512,3072]{1,0:T(8,128)(2,1)S(1)} %get-tuple-element.338.refs_2_.dup_ref, ...), custom_call_target="tpu_custom_call" | custom-call | flops 720000000 | tf_op jit(solution)/shard_map/weight_grad/pallas_call | solution.py:853
  149.4 9.9 %back_to_heads.1 = (f32[512,768]{1,0:T(8,128)S(1)}, bf16[512,768]{1,0:T(8,128)(2,1)S(1)}, bf16[512,384]{1,0:T(8,128)(2,1)S(1)}, bf16[512,768]{1,0:T(8,128)(2,1)S...) custom-call(s32[3]{0:T(128)S(1)} %pad_add_fusion.ids_ref, ...), custom_call_target="tpu_custom_call" | custom-call | flops 7080000000 | tf_op jit(solution)/shard_map/back_to_heads/pallas_call | solution.py:656
  161.7 2.2 collective-permute-start.47
  166.3 4.9 %collective-permute-done.46.refs_2_ = bf16[2,2,104,128]{3,2,1,0:T(8,128)(2,1)S(1)} collective-permute-done((bf16[2,2,104,128]{3,2,1,0:T(8,128)(2,1)S(1)}, bf16[2,2,104,128]{3,2,1,0:T(8,128)(2,1)S(1)}, u32[]{:S(2)}, u32[]{:S(2)}) %collective-permute-start.46) | collective-permute-done | bytes 106528 | tf_op jit(solution)/shard_map/ppermute | solution.py:28
  173.4 3.2 %collective-permute-done.51 = bf16[8,192,384]{2,1,0:T(8,128)(2,1)S(1)} collective-permute-done((bf16[8,192,384]{2,1,0:T(8,128)(2,1)S(1)}, bf16[8,192,384]{2,1,0:T(8,128)(2,1)S(1)}, u32[]{:S(2)}, u32[]{:S(2)}) %collective-permute-start.51) | collective-permute-done | bytes 1179680 | tf_op jit(solution)/shard_map/ppermute | solution.py:28
  177.5 8.1 %collective-permute-done.49.refs_4_ = bf16[4,2,104,128]{3,2,1,0:T(8,128)(2,1)S(1)} collective-permute-done((bf16[4,2,104,128]{3,2,1,0:T(8,128)(2,1)S(1)}, bf16[4,2,104,128]{3,2,1,0:T(8,128)(2,1)S(1)}, u32[]{:S(2)}, u32[]{:S(2)}) %collective-permute-start.49) | collective-permute-done | bytes 213024 | tf_op jit(solution)/shard_map/ppermute | solution.py:28
  187.1 2.0 collective-permute-start.54
  189.2 2.2 collective-permute-start.55
  191.3 8.8 %intra_backward.1 = (bf16[512,768]{1,0:T(8,128)(2,1)S(1)}, bf16[512,384]{1,0:T(8,128)(2,1)S(1)}, f32[512,768]{1,0:T(8,128)S(1)}, f32[512,768]{1,0:T(8,128)S(1)}) custom-call(s32[3]{0:T(128)S(1)} %pad_add_fusion.ids_ref, bf16[512,768]{1,0:T(8,128)(2,1)S(1)} %get-tuple-element.370.q_ref, bf16[512,768]{1,0:T(8,128)(2,1)S(1)} %get-tuple-element.245.k_ref, ...), custom_call_target="tpu_custom_call" | custom-call | flops 6179999744 | tf_op jit(solution)/shard_map/intra_backward/pallas_call | solution.py:725
  203.0 2.4 weight_grad.6
  206.4 2.5 collective-permute-done.57.refs_4_
  208.9 4.1 %inter_backward.1.dkv_ref = bf16[2,512,768]{2,1,0:T(8,128)(2,1)S(1)} custom-call(s32[3]{0:T(128)S(1)} %pad_add_fusion.ids_ref, bf16[512,768]{1,0:T(8,128)(2,1)S(1)} %get-tuple-element.245.k_ref, bf16[512,768]{1,0:T(8,128)(2,1)S(1)} %get-tuple-element.262.v_ref, f32[512,768]{1,0:T(8,128)S(1)} %get-tuple-element.373.dk_ref, ...), custom_call_target="tpu_custom_call" | custom-call | flops 2760000000 | tf_op jit(solution)/shard_map/inter_backward/pallas_call | solution.py:773
  216.1 2.4 collective-permute-done.60
  221.9 2.7 weight_grad.7
  227.1 4.2 %input_grad.1 = f32[512,768]{1,0:T(8,128)} custom-call(s32[3]{0:T(128)S(1)} %pad_add_fusion.ids_ref, bf16[512,768]{1,0:T(8,128)(2,1)S(1)} %copy-done.8, bf16[2,512,768]{2,1,0:T(8,128)(2,1)S(1)} %copy-done.3, f32[512,768]{1,0:T(8,128)S(1)} %copy-done.10, bf16[768,1792]{1,0:T(8,128)(2,1)S(1)} %bitcast.107, bf16[768,1536]{1,0:T(8,128)(2,1)S(1)} %bitcast.111), custom_call_target="tpu_custom_call" | custom-call | flops 2400000000 | tf_op jit(solution)/shard_map/input_grad/pallas_call | solution.py:797
  231.3 2.7 collective-permute-start.75
  235.3 3.8 %collective-permute-done.68 = bf16[8,24,768]{2,1,0:T(8,128)(2,1)S(1)} collective-permute-done((bf16[8,24,768]{2,1,0:T(8,128)(2,1)S(1)}, bf16[8,24,768]{2,1,0:T(8,128)(2,1)S(1)}, u32[]{:S(2)}, u32[]{:S(2)}) %collective-permute-start.68) | collective-permute-done | bytes 294944 | tf_op jit(solution)/shard_map/ppermute | solution.py:28
  240.7 9.3 %collective-permute-done.67 = bf16[2,48,768]{2,1,0:T(8,128)(2,1)S(1)} collective-permute-done((bf16[2,48,768]{2,1,0:T(8,128)(2,1)S(1)}, bf16[2,48,768]{2,1,0:T(8,128)(2,1)S(1)}, u32[]{:S(2)}, u32[]{:S(2)}) %collective-permute-start.67) | collective-permute-done | bytes 147488 | tf_op jit(solution)/shard_map/ppermute | solution.py:28
  251.4 2.3 collective-permute-start.69
  253.8 4.6 %collective-permute-done.69 = bf16[2,48,896]{2,1,0:T(8,128)(2,1)S(1)} collective-permute-done((bf16[2,48,896]{2,1,0:T(8,128)(2,1)S(1)}, bf16[2,48,896]{2,1,0:T(8,128)(2,1)S(1)}, u32[]{:S(2)}, u32[]{:S(2)}) %collective-permute-start.69) | collective-permute-done | bytes 172064 | tf_op jit(solution)/shard_map/ppermute | solution.py:28
  259.9 3.0 %collective-permute-start.78 = (bf16[192,384]{1,0:T(8,128)(2,1)S(1)}, bf16[192,384]{1,0:T(8,128)(2,1)S(1)}, u32[]{:S(2)}, u32[]{:S(2)}) collective-permute-start(bf16[192,384]{1,0:T(8,128)(2,1)S(1)} %fusion.27), channel_id=1, source_target_pairs={{0,16},{8,24},{16,0},{24,8},{1,17},{9,25},{17,1},{25,9},{2,18},{10... | collective-permute-start | bytes 442376 | tf_op jit(solution)/shard_map/ppermute | solution.py:28
  265.4 2.4 collective-permute-done.79
  (313 shorter events, 98.6 us)
Async XLA Ops:
  1.5 7.9 %collective-permute-start = (bf16[1,24,1536]{2,1,0:T(8,128)(2,1)S(1)}, bf16[1,24,1536]{2,1,0:T(8,128)(2,1)S(1)}, u32[]{:S(2)}, u32[]{:S(2)}) collective-permute-start(bf16[1,24,1536]{2,1,0:T(8,128)(2,1)S(1)} %slice_bitcast_fusion.14), channel_id=1, source_target_pairs={{0,4},{1,5},{2,6},{3,7},{4,0},{5,1},{6,2},{7,3},{8,12},{9,13},{10,... | collective-permute-start | bytes 221192 | tf_op jit(solution)/shard_map/ppermute | solution.py:28
  5.6 31.2 %collective-permute-start.10 = (bf16[512,768]{1,0:T(8,128)(2,1)}, bf16[512,768]{1,0:T(8,128)(2,1)S(1)}, u32[]{:S(2)}, u32[]{:S(2)}) collective-permute-start(bf16[512,768]{1,0:T(8,128)(2,1)} %refs_0_.1), channel_id=1, source_target_pairs={{0,8},{8,0},{16,24},{24,16},{1,9},{9,1},{17,25},{25,17},{2,10},{10... | collective-permute-start | bytes 2359304 | tf_op jit(solution)/shard_map/ppermute | solution.py:28
  21.9 8.8 %collective-permute-start.6 = (bf16[8,24,768]{2,1,0:T(8,128)(2,1)S(1)}, bf16[8,24,768]{2,1,0:T(8,128)(2,1)S(1)}, u32[]{:S(2)}, u32[]{:S(2)}) collective-permute-start(bf16[8,24,768]{2,1,0:T(8,128)(2,1)S(1)} %pad_maximum_fusion.20), channel_id=1, source_target_pairs={{0,1},{1,0},{2,3},{3,2},{4,5},{5,4},{6,7},{7,6},{8,9},{9,8},{10,11... | collective-permute-start | bytes 884744 | tf_op jit(solution)/shard_map/ppermute | solution.py:28
  22.6 8.2 %collective-permute-start.5 = (bf16[8,24,768]{2,1,0:T(8,128)(2,1)S(1)}, bf16[8,24,768]{2,1,0:T(8,128)(2,1)S(1)}, u32[]{:S(2)}, u32[]{:S(2)}) collective-permute-start(bf16[8,24,768]{2,1,0:T(8,128)(2,1)S(1)} %pad_maximum_fusion.19), channel_id=1, source_target_pairs={{0,16},{8,24},{16,0},{24,8},{1,17},{9,25},{17,1},{25,9},{2,18},{10... | collective-permute-start | bytes 884744 | tf_op jit(solution)/shard_map/ppermute | solution.py:28
  27.4 7.9 %collective-permute-start.11 = (bf16[1,24,3072]{2,1,0:T(8,128)(2,1)}, bf16[1,24,3072]{2,1,0:T(8,128)(2,1)S(1)}, u32[]{:S(2)}, u32[]{:S(2)}) collective-permute-start(bf16[1,24,3072]{2,1,0:T(8,128)(2,1)} %bitcast.15), channel_id=1, source_target_pairs={{0,4},{1,5},{2,6},{3,7},{4,0},{5,1},{6,2},{7,3},{8,12},{9,13},{10,... | collective-permute-start | bytes 442376 | tf_op jit(solution)/shard_map/ppermute | solution.py:28
  31.6 11.8 %collective-permute-start.8 = (bf16[4,24,896]{2,1,0:T(8,128)(2,1)S(1)}, bf16[4,24,896]{2,1,0:T(8,128)(2,1)S(1)}, u32[]{:S(2)}, u32[]{:S(2)}) collective-permute-start(bf16[4,24,896]{2,1,0:T(8,128)(2,1)S(1)} %get-tuple-element.478), channel_id=1, source_target_pairs={{0,1},{1,0},{2,3},{3,2},{4,5},{5,4},{6,7},{7,6},{8,9},{9,8},{10,11... | collective-permute-start | bytes 516104 | tf_op jit(solution)/shard_map/ppermute | solution.py:28
  35.3 8.1 %collective-permute-start.9 = (bf16[4,24,896]{2,1,0:T(8,128)(2,1)S(1)}, bf16[4,24,896]{2,1,0:T(8,128)(2,1)S(1)}, u32[]{:S(2)}, u32[]{:S(2)}) collective-permute-start(bf16[4,24,896]{2,1,0:T(8,128)(2,1)S(1)} %get-tuple-element.477), channel_id=1, source_target_pairs={{0,16},{8,24},{16,0},{24,8},{1,17},{9,25},{17,1},{25,9},{2,18},{10... | collective-permute-start | bytes 516104 | tf_op jit(solution)/shard_map/ppermute | solution.py:28
  43.6 13.2 %collective-permute-start.14 = (bf16[8,24,896]{2,1,0:T(8,128)(2,1)S(1)}, bf16[8,24,896]{2,1,0:T(8,128)(2,1)S(1)}, u32[]{:S(2)}, u32[]{:S(2)}) collective-permute-start(bf16[8,24,896]{2,1,0:T(8,128)(2,1)S(1)} %get-tuple-element.251), channel_id=1, source_target_pairs={{0,16},{8,24},{16,0},{24,8},{1,17},{9,25},{17,1},{25,9},{2,18},{10... | collective-permute-start | bytes 1032200 | tf_op jit(solution)/shard_map/ppermute | solution.py:28
  45.2 11.6 %collective-permute-start.15 = (bf16[8,24,896]{2,1,0:T(8,128)(2,1)S(1)}, bf16[8,24,896]{2,1,0:T(8,128)(2,1)S(1)}, u32[]{:S(2)}, u32[]{:S(2)}) collective-permute-start(bf16[8,24,896]{2,1,0:T(8,128)(2,1)S(1)} %get-tuple-element.252), channel_id=1, source_target_pairs={{0,1},{1,0},{2,3},{3,2},{4,5},{5,4},{6,7},{7,6},{8,9},{9,8},{10,11... | collective-permute-start | bytes 1032200 | tf_op jit(solution)/shard_map/ppermute | solution.py:28
  46.0 8.9 %collective-permute-start.16 = (bf16[2,2,104,128]{3,2,1,0:T(8,128)(2,1)S(1)}, bf16[2,2,104,128]{3,2,1,0:T(8,128)(2,1)S(1)}, u32[]{:S(2)}, u32[]{:S(2)}) collective-permute-start(bf16[2,2,104,128]{3,2,1,0:T(8,128)(2,1)S(1)} %get-tuple-element.253), channel_id=1, source_target_pairs={{0,2},{1,3},{2,0},{3,1},{4,6},{5,7},{6,4},{7,5},{8,10},{9,11},{10,... | collective-permute-start | bytes 319496 | tf_op jit(solution)/shard_map/ppermute | solution.py:28
  46.0 9.5 %collective-permute-start.17 = (bf16[2,2,104,128]{3,2,1,0:T(8,128)(2,1)S(1)}, bf16[2,2,104,128]{3,2,1,0:T(8,128)(2,1)S(1)}, u32[]{:S(2)}, u32[]{:S(2)}) collective-permute-start(bf16[2,2,104,128]{3,2,1,0:T(8,128)(2,1)S(1)} %get-tuple-element.254), channel_id=1, source_target_pairs={{0,4},{1,5},{2,6},{3,7},{4,0},{5,1},{6,2},{7,3},{8,12},{9,13},{10,... | collective-permute-start | bytes 319496 | tf_op jit(solution)/shard_map/ppermute | solution.py:28
  56.9 14.9 %collective-permute-start.25 = (bf16[4,2,104,128]{3,2,1,0:T(8,128)(2,1)S(1)}, bf16[4,2,104,128]{3,2,1,0:T(8,128)(2,1)S(1)}, u32[]{:S(2)}, u32[]{:S(2)}) collective-permute-start(bf16[4,2,104,128]{3,2,1,0:T(8,128)(2,1)S(1)} %pad_maximum_fusion.25), channel_id=1, source_target_pairs={{0,1},{1,0},{2,3},{3,2},{4,5},{5,4},{6,7},{7,6},{8,9},{9,8},{10,11... | collective-permute-start | bytes 638984 | tf_op jit(solution)/shard_map/ppermute | solution.py:28
  62.7 9.4 %collective-permute-start.22 = (bf16[4,24,1536]{2,1,0:T(8,128)(2,1)S(1)}, bf16[4,24,1536]{2,1,0:T(8,128)(2,1)S(1)}, u32[]{:S(2)}, u32[]{:S(2)}) collective-permute-start(bf16[4,24,1536]{2,1,0:T(8,128)(2,1)S(1)} %get-tuple-element.269), channel_id=1, source_target_pairs={{0,1},{1,0},{2,3},{3,2},{4,5},{5,4},{6,7},{7,6},{8,9},{9,8},{10,11... | collective-permute-start | bytes 884744 | tf_op jit(solution)/shard_map/ppermute | solution.py:28
  63.6 8.5 %collective-permute-start.23 = (bf16[4,24,1536]{2,1,0:T(8,128)(2,1)S(1)}, bf16[4,24,1536]{2,1,0:T(8,128)(2,1)S(1)}, u32[]{:S(2)}, u32[]{:S(2)}) collective-permute-start(bf16[4,24,1536]{2,1,0:T(8,128)(2,1)S(1)} %get-tuple-element.270), channel_id=1, source_target_pairs={{0,16},{8,24},{16,0},{24,8},{1,17},{9,25},{17,1},{25,9},{2,18},{10... | collective-permute-start | bytes 884744 | tf_op jit(solution)/shard_map/ppermute | solution.py:28
  72.7 12.1 %collective-permute-start.31 = (bf16[8,24,1536]{2,1,0:T(8,128)(2,1)S(1)}, bf16[8,24,1536]{2,1,0:T(8,128)(2,1)S(1)}, u32[]{:S(2)}, u32[]{:S(2)}) collective-permute-start(bf16[8,24,1536]{2,1,0:T(8,128)(2,1)S(1)} %pad_maximum_fusion.10), channel_id=1, source_target_pairs={{0,16},{8,24},{16,0},{24,8},{1,17},{9,25},{17,1},{25,9},{2,18},{10... | collective-permute-start | bytes 1769480 | tf_op jit(solution)/shard_map/ppermute | solution.py:28
  74.1 11.6 %collective-permute-start.32 = (bf16[8,24,1536]{2,1,0:T(8,128)(2,1)S(1)}, bf16[8,24,1536]{2,1,0:T(8,128)(2,1)S(1)}, u32[]{:S(2)}, u32[]{:S(2)}) collective-permute-start(bf16[8,24,1536]{2,1,0:T(8,128)(2,1)S(1)} %pad_maximum_fusion.11), channel_id=1, source_target_pairs={{0,1},{1,0},{2,3},{3,2},{4,5},{5,4},{6,7},{7,6},{8,9},{9,8},{10,11... | collective-permute-start | bytes 1769480 | tf_op jit(solution)/shard_map/ppermute | solution.py:28
  76.3 8.4 %collective-permute-start.27 = (bf16[2,2,104,128]{3,2,1,0:T(8,128)(2,1)S(1)}, bf16[2,2,104,128]{3,2,1,0:T(8,128)(2,1)S(1)}, u32[]{:S(2)}, u32[]{:S(2)}) collective-permute-start(bf16[2,2,104,128]{3,2,1,0:T(8,128)(2,1)S(1)} %get-tuple-element.280), channel_id=1, source_target_pairs={{0,4},{1,5},{2,6},{3,7},{4,0},{5,1},{6,2},{7,3},{8,12},{9,13},{10,... | collective-permute-start | bytes 319496 | tf_op jit(solution)/shard_map/ppermute | solution.py:28
  86.6 9.0 %collective-permute-start.29 = (bf16[2,96,768]{2,1,0:T(8,128)(2,1)S(1)}, bf16[2,96,768]{2,1,0:T(8,128)(2,1)S(1)}, u32[]{:S(2)}, u32[]{:S(2)}) collective-permute-start(bf16[2,96,768]{2,1,0:T(8,128)(2,1)S(1)} %pad_maximum_fusion.22), channel_id=1, source_target_pairs={{0,2},{1,3},{2,0},{3,1},{4,6},{5,7},{6,4},{7,5},{8,10},{9,11},{10,... | collective-permute-start | bytes 884744 | tf_op jit(solution)/shard_map/ppermute | solution.py:28
  95.7 8.3 %collective-permute-start.35 = (bf16[4,96,384]{2,1,0:T(8,128)(2,1)S(1)}, bf16[4,96,384]{2,1,0:T(8,128)(2,1)S(1)}, u32[]{:S(2)}, u32[]{:S(2)}) collective-permute-start(bf16[4,96,384]{2,1,0:T(8,128)(2,1)S(1)} %get-tuple-element.298), channel_id=1, source_target_pairs={{0,1},{1,0},{2,3},{3,2},{4,5},{5,4},{6,7},{7,6},{8,9},{9,8},{10,11... | collective-permute-start | bytes 884744 | tf_op jit(solution)/shard_map/ppermute | solution.py:28
  97.3 8.2 %collective-permute-start.36 = (bf16[4,96,384]{2,1,0:T(8,128)(2,1)S(1)}, bf16[4,96,384]{2,1,0:T(8,128)(2,1)S(1)}, u32[]{:S(2)}, u32[]{:S(2)}) collective-permute-start(bf16[4,96,384]{2,1,0:T(8,128)(2,1)S(1)} %get-tuple-element.299), channel_id=1, source_target_pairs={{0,16},{8,24},{16,0},{24,8},{1,17},{9,25},{17,1},{25,9},{2,18},{10... | collective-permute-start | bytes 884744 | tf_op jit(solution)/shard_map/ppermute | solution.py:28
  105.6 13.7 %collective-permute-start.37 = (bf16[8,96,384]{2,1,0:T(8,128)(2,1)S(1)}, bf16[8,96,384]{2,1,0:T(8,128)(2,1)S(1)}, u32[]{:S(2)}, u32[]{:S(2)}) collective-permute-start(bf16[8,96,384]{2,1,0:T(8,128)(2,1)S(1)} %pad_maximum_fusion.13), channel_id=1, source_target_pairs={{0,16},{8,24},{16,0},{24,8},{1,17},{9,25},{17,1},{25,9},{2,18},{10... | collective-permute-start | bytes 1769480 | tf_op jit(solution)/shard_map/ppermute | solution.py:28
  106.0 13.5 %collective-permute-start.38 = (bf16[8,96,384]{2,1,0:T(8,128)(2,1)S(1)}, bf16[8,96,384]{2,1,0:T(8,128)(2,1)S(1)}, u32[]{:S(2)}, u32[]{:S(2)}) collective-permute-start(bf16[8,96,384]{2,1,0:T(8,128)(2,1)S(1)} %pad_maximum_fusion.14), channel_id=1, source_target_pairs={{0,1},{1,0},{2,3},{3,2},{4,5},{5,4},{6,7},{7,6},{8,9},{9,8},{10,11... | collective-permute-start | bytes 1769480 | tf_op jit(solution)/shard_map/ppermute | solution.py:28
  147.4 16.5 %collective-permute-start.48 = (bf16[2,96,1536]{2,1,0:T(8,128)(2,1)S(1)}, bf16[2,96,1536]{2,1,0:T(8,128)(2,1)S(1)}, u32[]{:S(2)}, u32[]{:S(2)}) collective-permute-start(bf16[2,96,1536]{2,1,0:T(8,128)(2,1)S(1)} %get-tuple-element.450), channel_id=1, source_target_pairs={{0,1},{1,0},{2,3},{3,2},{4,5},{5,4},{6,7},{7,6},{8,9},{9,8},{10,11... | collective-permute-start | bytes 1769480 | tf_op jit(solution)/shard_map/ppermute | solution.py:28
  148.9 27.7 %collective-permute-start.51 = (bf16[8,192,384]{2,1,0:T(8,128)(2,1)S(1)}, bf16[8,192,384]{2,1,0:T(8,128)(2,1)S(1)}, u32[]{:S(2)}, u32[]{:S(2)}) collective-permute-start(bf16[8,192,384]{2,1,0:T(8,128)(2,1)S(1)} %slice_bitcast_fusion), channel_id=1, source_target_pairs={{0,16},{8,24},{16,0},{24,8},{1,17},{9,25},{17,1},{25,9},{2,18},{10... | collective-permute-start | bytes 3538952 | tf_op jit(solution)/shard_map/ppermute | solution.py:28
  160.6 10.7 %collective-permute-start.46 = (bf16[2,2,104,128]{3,2,1,0:T(8,128)(2,1)S(1)}, bf16[2,2,104,128]{3,2,1,0:T(8,128)(2,1)S(1)}, u32[]{:S(2)}, u32[]{:S(2)}) collective-permute-start(bf16[2,2,104,128]{3,2,1,0:T(8,128)(2,1)S(1)} %get-tuple-element.345), channel_id=1, source_target_pairs={{0,4},{1,5},{2,6},{3,7},{4,0},{5,1},{6,2},{7,3},{8,12},{9,13},{10,... | collective-permute-start | bytes 319496 | tf_op jit(solution)/shard_map/ppermute | solution.py:28
  161.7 9.5 %collective-permute-start.47 = (bf16[2,2,104,128]{3,2,1,0:T(8,128)(2,1)S(1)}, bf16[2,2,104,128]{3,2,1,0:T(8,128)(2,1)S(1)}, u32[]{:S(2)}, u32[]{:S(2)}) collective-permute-start(bf16[2,2,104,128]{3,2,1,0:T(8,128)(2,1)S(1)} %get-tuple-element.346), channel_id=1, source_target_pairs={{0,6},{1,7},{2,4},{3,5},{4,2},{5,3},{6,0},{7,1},{8,14},{9,15},{10,... | collective-permute-start | bytes 319496 | tf_op jit(solution)/shard_map/ppermute | solution.py:28
  164.8 21.1 %collective-permute-start.52 = (bf16[2,96,1536]{2,1,0:T(8,128)(2,1)S(1)}, bf16[2,96,1536]{2,1,0:T(8,128)(2,1)S(1)}, u32[]{:S(2)}, u32[]{:S(2)}) collective-permute-start(bf16[2,96,1536]{2,1,0:T(8,128)(2,1)S(1)} %get-tuple-element.350), channel_id=1, source_target_pairs={{0,1},{1,0},{2,3},{3,2},{4,5},{5,4},{6,7},{7,6},{8,9},{9,8},{10,11... | collective-permute-start | bytes 1769480 | tf_op jit(solution)/shard_map/ppermute | solution.py:28
  171.4 29.8 %collective-permute-start.58 = (bf16[512,768]{1,0:T(8,128)(2,1)S(1)}, bf16[512,768]{1,0:T(8,128)(2,1)S(1)}, u32[]{:S(2)}, u32[]{:S(2)}) collective-permute-start(bf16[512,768]{1,0:T(8,128)(2,1)S(1)} %get-tuple-element.309.att_ref.refs_0_), channel_id=1, source_target_pairs={{0,8},{8,0},{16,24},{24,16},{1,9},{9,1},{17,25},{25,17},{2,10},{10... | collective-permute-start | bytes 2359304 | tf_op jit(solution)/shard_map/ppermute | solution.py:28
  171.9 13.7 %collective-permute-start.49 = (bf16[4,2,104,128]{3,2,1,0:T(8,128)(2,1)S(1)}, bf16[4,2,104,128]{3,2,1,0:T(8,128)(2,1)S(1)}, u32[]{:S(2)}, u32[]{:S(2)}) collective-permute-start(bf16[4,2,104,128]{3,2,1,0:T(8,128)(2,1)S(1)} %pad_maximum_fusion.27), channel_id=1, source_target_pairs={{0,1},{1,0},{2,3},{3,2},{4,5},{5,4},{6,7},{7,6},{8,9},{9,8},{10,11... | collective-permute-start | bytes 638984 | tf_op jit(solution)/shard_map/ppermute | solution.py:28
  176.9 23.2 %collective-permute-start.56 = (bf16[4,192,384]{2,1,0:T(8,128)(2,1)S(1)}, bf16[4,192,384]{2,1,0:T(8,128)(2,1)S(1)}, u32[]{:S(2)}, u32[]{:S(2)}) collective-permute-start(bf16[4,192,384]{2,1,0:T(8,128)(2,1)S(1)} %get-tuple-element.358), channel_id=1, source_target_pairs={{0,1},{1,0},{2,3},{3,2},{4,5},{5,4},{6,7},{7,6},{8,9},{9,8},{10,11... | collective-permute-start | bytes 1769480 | tf_op jit(solution)/shard_map/ppermute | solution.py:28
  186.9 14.2 %collective-permute-start.53 = (bf16[2,2,104,128]{3,2,1,0:T(8,128)(2,1)S(1)}, bf16[2,2,104,128]{3,2,1,0:T(8,128)(2,1)S(1)}, u32[]{:S(2)}, u32[]{:S(2)}) collective-permute-start(bf16[2,2,104,128]{3,2,1,0:T(8,128)(2,1)S(1)} %get-tuple-element.367), channel_id=1, source_target_pairs={{0,2},{1,3},{2,0},{3,1},{4,6},{5,7},{6,4},{7,5},{8,10},{9,11},{10,... | collective-permute-start | bytes 319496 | tf_op jit(solution)/shard_map/ppermute | solution.py:28
  187.1 14.0 %collective-permute-start.54 = (bf16[2,2,104,128]{3,2,1,0:T(8,128)(2,1)S(1)}, bf16[2,2,104,128]{3,2,1,0:T(8,128)(2,1)S(1)}, u32[]{:S(2)}, u32[]{:S(2)}) collective-permute-start(bf16[2,2,104,128]{3,2,1,0:T(8,128)(2,1)S(1)} %get-tuple-element.368), channel_id=1, source_target_pairs={{0,4},{1,5},{2,6},{3,7},{4,0},{5,1},{6,2},{7,3},{8,12},{9,13},{10,... | collective-permute-start | bytes 319496 | tf_op jit(solution)/shard_map/ppermute | solution.py:28
  189.2 11.9 %collective-permute-start.55 = (bf16[2,2,104,128]{3,2,1,0:T(8,128)(2,1)S(1)}, bf16[2,2,104,128]{3,2,1,0:T(8,128)(2,1)S(1)}, u32[]{:S(2)}, u32[]{:S(2)}) collective-permute-start(bf16[2,2,104,128]{3,2,1,0:T(8,128)(2,1)S(1)} %get-tuple-element.369), channel_id=1, source_target_pairs={{0,6},{1,7},{2,4},{3,5},{4,2},{5,3},{6,0},{7,1},{8,14},{9,15},{10,... | collective-permute-start | bytes 319496 | tf_op jit(solution)/shard_map/ppermute | solution.py:28
  202.8 15.7 %collective-permute-start.60 = (bf16[2,96,1536]{2,1,0:T(8,128)(2,1)}, bf16[2,96,1536]{2,1,0:T(8,128)(2,1)}, u32[]{:S(2)}, u32[]{:S(2)}) collective-permute-start(bf16[2,96,1536]{2,1,0:T(8,128)(2,1)} %fusion.3), channel_id=1, source_target_pairs={{0,2},{1,3},{2,0},{3,1},{4,6},{5,7},{6,4},{7,5},{8,10},{9,11},{10,... | collective-permute-start | bytes 1769480 | tf_op jit(solution)/shard_map/ppermute | solution.py:28
  214.7 19.4 %collective-permute-start.62 = (bf16[8,48,896]{2,1,0:T(8,128)(2,1)}, bf16[8,48,896]{2,1,0:T(8,128)(2,1)S(1)}, u32[]{:S(2)}, u32[]{:S(2)}) collective-permute-start(bf16[8,48,896]{2,1,0:T(8,128)(2,1)} %slice_bitcast_fusion.3), channel_id=1, source_target_pairs={{0,16},{8,24},{16,0},{24,8},{1,17},{9,25},{17,1},{25,9},{2,18},{10... | collective-permute-start | bytes 2064392 | tf_op jit(solution)/shard_map/ppermute | solution.py:28
  216.1 15.2 %collective-permute-start.63 = (bf16[2,192,384]{2,1,0:T(8,128)(2,1)}, bf16[2,192,384]{2,1,0:T(8,128)(2,1)S(1)}, u32[]{:S(2)}, u32[]{:S(2)}) collective-permute-start(bf16[2,192,384]{2,1,0:T(8,128)(2,1)} %get-tuple-element.388), channel_id=1, source_target_pairs={{0,2},{1,3},{2,0},{3,1},{4,6},{5,7},{6,4},{7,5},{8,10},{9,11},{10,... | collective-permute-start | bytes 884744 | tf_op jit(solution)/shard_map/ppermute | solution.py:28
  224.7 10.2 %collective-permute-start.66 = (bf16[4,48,768]{2,1,0:T(8,128)(2,1)S(1)}, bf16[4,48,768]{2,1,0:T(8,128)(2,1)S(1)}, u32[]{:S(2)}, u32[]{:S(2)}) collective-permute-start(bf16[4,48,768]{2,1,0:T(8,128)(2,1)S(1)} %slice_bitcast_fusion.12), channel_id=1, source_target_pairs={{0,1},{1,0},{2,3},{3,2},{4,5},{5,4},{6,7},{7,6},{8,9},{9,8},{10,11... | collective-permute-start | bytes 884744 | tf_op jit(solution)/shard_map/ppermute | solution.py:28
  225.3 13.7 %collective-permute-start.68 = (bf16[8,24,768]{2,1,0:T(8,128)(2,1)S(1)}, bf16[8,24,768]{2,1,0:T(8,128)(2,1)S(1)}, u32[]{:S(2)}, u32[]{:S(2)}) collective-permute-start(bf16[8,24,768]{2,1,0:T(8,128)(2,1)S(1)} %slice_bitcast_fusion.13), channel_id=1, source_target_pairs={{0,16},{8,24},{16,0},{24,8},{1,17},{9,25},{17,1},{25,9},{2,18},{10... | collective-permute-start | bytes 884744 | tf_op jit(solution)/shard_map/ppermute | solution.py:28
  226.8 23.3 %collective-permute-start.65 = (bf16[1,96,1536]{2,1,0:T(8,128)(2,1)S(1)}, bf16[1,96,1536]{2,1,0:T(8,128)(2,1)S(1)}, u32[]{:S(2)}, u32[]{:S(2)}) collective-permute-start(bf16[1,96,1536]{2,1,0:T(8,128)(2,1)S(1)} %add_convert_fusion.4), channel_id=1, source_target_pairs={{0,4},{1,5},{2,6},{3,7},{4,0},{5,1},{6,2},{7,3},{8,12},{9,13},{10,... | collective-permute-start | bytes 884744 | tf_op jit(solution)/shard_map/ppermute | solution.py:28
  231.3 28.5 %collective-permute-start.75 = (bf16[1,192,384]{2,1,0:T(8,128)(2,1)S(1)}, bf16[1,192,384]{2,1,0:T(8,128)(2,1)S(1)}, u32[]{:S(2)}, u32[]{:S(2)}) collective-permute-start(bf16[1,192,384]{2,1,0:T(8,128)(2,1)S(1)} %add_convert_fusion.10), channel_id=1, source_target_pairs={{0,4},{1,5},{2,6},{3,7},{4,0},{5,1},{6,2},{7,3},{8,12},{9,13},{10,... | collective-permute-start | bytes 442376 | tf_op jit(solution)/shard_map/ppermute | solution.py:28
  234.2 17.0 %collective-permute-start.64 = (bf16[4,48,896]{2,1,0:T(8,128)(2,1)S(1)}, bf16[4,48,896]{2,1,0:T(8,128)(2,1)S(1)}, u32[]{:S(2)}, u32[]{:S(2)}) collective-permute-start(bf16[4,48,896]{2,1,0:T(8,128)(2,1)S(1)} %get-tuple-element.401), channel_id=1, source_target_pairs={{0,1},{1,0},{2,3},{3,2},{4,5},{5,4},{6,7},{7,6},{8,9},{9,8},{10,11... | collective-permute-start | bytes 1032200 | tf_op jit(solution)/shard_map/ppermute | solution.py:28
  235.0 15.0 %collective-permute-start.67 = (bf16[2,48,768]{2,1,0:T(8,128)(2,1)S(1)}, bf16[2,48,768]{2,1,0:T(8,128)(2,1)S(1)}, u32[]{:S(2)}, u32[]{:S(2)}) collective-permute-start(bf16[2,48,768]{2,1,0:T(8,128)(2,1)S(1)} %get-tuple-element.403), channel_id=1, source_target_pairs={{0,2},{1,3},{2,0},{3,1},{4,6},{5,7},{6,4},{7,5},{8,10},{9,11},{10,... | collective-permute-start | bytes 442376 | tf_op jit(solution)/shard_map/ppermute | solution.py:28
  239.1 14.5 %collective-permute-start.70 = (bf16[4,24,768]{2,1,0:T(8,128)(2,1)S(1)}, bf16[4,24,768]{2,1,0:T(8,128)(2,1)S(1)}, u32[]{:S(2)}, u32[]{:S(2)}) collective-permute-start(bf16[4,24,768]{2,1,0:T(8,128)(2,1)S(1)} %get-tuple-element.405), channel_id=1, source_target_pairs={{0,1},{1,0},{2,3},{3,2},{4,5},{5,4},{6,7},{7,6},{8,9},{9,8},{10,11... | collective-permute-start | bytes 442376 | tf_op jit(solution)/shard_map/ppermute | solution.py:28
  250.0 13.2 %collective-permute-start.72 = (bf16[1,48,768]{2,1,0:T(8,128)(2,1)S(1)}, bf16[1,48,768]{2,1,0:T(8,128)(2,1)S(1)}, u32[]{:S(2)}, u32[]{:S(2)}) collective-permute-start(bf16[1,48,768]{2,1,0:T(8,128)(2,1)S(1)} %add_convert_fusion.19), channel_id=1, source_target_pairs={{0,4},{1,5},{2,6},{3,7},{4,0},{5,1},{6,2},{7,3},{8,12},{9,13},{10,... | collective-permute-start | bytes 221192 | tf_op jit(solution)/shard_map/ppermute | solution.py:28
  251.2 11.8 %collective-permute-start.73 = (bf16[96,1536]{1,0:T(8,128)(2,1)S(1)}, bf16[96,1536]{1,0:T(8,128)(2,1)S(1)}, u32[]{:S(2)}, u32[]{:S(2)}) collective-permute-start(bf16[96,1536]{1,0:T(8,128)(2,1)S(1)} %fusion.17), channel_id=1, source_target_pairs={{0,16},{8,24},{16,0},{24,8},{1,17},{9,25},{17,1},{25,9},{2,18},{10... | collective-permute-start | bytes 884744 | tf_op jit(solution)/shard_map/ppermute | solution.py:28
  253.7 9.2 %collective-permute-start.74 = (bf16[2,24,768]{2,1,0:T(8,128)(2,1)S(1)}, bf16[2,24,768]{2,1,0:T(8,128)(2,1)S(1)}, u32[]{:S(2)}, u32[]{:S(2)}) collective-permute-start(bf16[2,24,768]{2,1,0:T(8,128)(2,1)S(1)} %get-tuple-element.413), channel_id=1, source_target_pairs={{0,2},{1,3},{2,0},{3,1},{4,6},{5,7},{6,4},{7,5},{8,10},{9,11},{10,... | collective-permute-start | bytes 221192 | tf_op jit(solution)/shard_map/ppermute | solution.py:28
  259.9 8.1 %collective-permute-start.78 = (bf16[192,384]{1,0:T(8,128)(2,1)S(1)}, bf16[192,384]{1,0:T(8,128)(2,1)S(1)}, u32[]{:S(2)}, u32[]{:S(2)}) collective-permute-start(bf16[192,384]{1,0:T(8,128)(2,1)S(1)} %fusion.27), channel_id=1, source_target_pairs={{0,16},{8,24},{16,0},{24,8},{1,17},{9,25},{17,1},{25,9},{2,18},{10... | collective-permute-start | bytes 442376 | tf_op jit(solution)/shard_map/ppermute | solution.py:28
  263.1 10.2 %collective-permute-start.80 = (bf16[96,1536]{1,0:T(8,128)(2,1)S(1)}, bf16[96,1536]{1,0:T(8,128)(2,1)S(1)}, u32[]{:S(2)}, u32[]{:S(2)}) collective-permute-start(bf16[96,1536]{1,0:T(8,128)(2,1)S(1)} %add_convert_fusion), channel_id=1, source_target_pairs={{0,8},{8,0},{16,24},{24,16},{1,9},{9,1},{17,25},{25,17},{2,10},{10... | collective-permute-start | bytes 884744 | tf_op jit(solution)/shard_map/ppermute | solution.py:28
  (61 other events, 324.4 us)

commit v4 on v3

--- a/solution.py
+++ b/solution.py
@@ -162,12 +162,12 @@
 SMEM = pl.BlockSpec(memory_space=pltpu.SMEM)
 
 
-COSTS = {"assemble": 1.5, "project": 5.4, "mix_segments": 1.1, "intra_forward": 5.9, "inter_forward": 5.5, "expand": 2.85, "contract": 6.0, "turn": 22.5, "back_to_heads": 11.8, "intra_backward": 10.3, "inter_backward": 4.6, "input_grad": 4.0, "vector_rows": 1.5, "down": 6.0, "up": 1.2, "outq": 2.4, "kv": 3.36}
-TAIL = ('kv0+kv1', 'up', 'grad', 'down', 'outq', 'kv1', 'kv0', 'kv1', 'up', 'outq', 'kv0', 'outq', 'down', 'kv0', 'up', 'kv1', 'outq', 'kv0', 'down', 'kv1', 'outq', 'kv0', 'kv1')
+COSTS = {"assemble": 1.5, "project": 10.8, "mix_segments": 1.1, "intra_forward": 5.9, "inter_forward": 16.5, "expand": 0.285, "contract": 6.0, "turn": 22.5, "back_to_heads": 11.8, "intra_backward": 10.3, "inter_backward": 4.6, "input_grad": 4.0, "vector_rows": 1.5, "down": 6.0, "up": 1.2, "outq": 3.36, "kv": 3.36}
+TAIL = ('kv0+kv1', 'up', 'grad', 'down', 'outq', 'kv1', 'kv0', 'kv1', 'up', 'outq', 'kv0', 'down', 'outq', 'kv0', 'kv1', 'up', 'outq', 'kv1', 'kv0', 'down', 'outq', 'close', 'kv0', 'kv1', 'outq', 'close', 'kv0', 'kv1')
 FLOPS_PER_US = 6.0e8
 
 
-def call(kernel, name, outs, in_specs, scratch=(), cost=None, mib=8):
+def call(kernel, name, outs, in_specs, scratch=(), cost=None, mib=5):
     return pl.pallas_call(
         kernel,
         out_shape=outs,
@@ -881,14 +881,16 @@
     half = x.shape[1] // 2
     bits = axis_bits("fsdp")
     keep, send = x[0, :half], x[0, half:]
-    if large and half > 1:
-        quarter = half // 2
+    if large and half >= 4:
         axis, bit = bits.pop(0)
-        (received,) = yield [(send[quarter:], axis, bit)]
-        after = add_low(keep[quarter:], received)
-        (received,) = yield [(tie(send[:quarter], after), axis, bit)]
-        keep = add_low(keep[:quarter], received)
-        send = tie(after, keep)
+        middle, first = half // 2, half // 4
+        (received,) = yield [(send[first:], axis, bit)]
+        after = add_low(keep[middle:], received[middle - first :])
+        beside = add_low(keep[first:middle], received[: middle - first])
+        rest, after = lax.optimization_barrier((send[:first], after))
+        (received,) = yield [(rest, axis, bit)]
+        keep = jnp.concatenate([add_low(keep[:first], received), beside], axis=0)
+        send, keep = lax.optimization_barrier((after, keep))
     x = yield from halving_stages(keep, send, bits)
     for axis, bit in axis_bits("group")[1:]:
         (received,) = yield [(x, axis, bit)]
@@ -1042,12 +1044,12 @@
     path = pipe.finish("path", w_up_full, only=("path",))
     pipe.slot(path[1], only=("down",))
     att, rden = inter_forward(ids, tie(q, *pipe.started), num, den, cos, sin, *path)
+    pipe.add("att", core_stage(att))
+    pipe.slot(only=("att",))
     pipe.slot(att, only=("down",))
-    pipe.add("att", core_stage(att))
-    pipe.slot(*pipe.started, only=("att",))
     att_other = pipe.read("att", *pipe.started)
     hat1, inv1, low1, gelu, slope = expand(
-        tie(att, *pipe.started), tokens, w_qo, w_up_full, small
+        tie(att, att_other, *pipe.started), tokens, w_qo, w_up_full, small
     )
     pipe.slot(low1, only=("down",))
     w_down_full = assemble(*pipe.finish("down", only=("down",)))
@@ -1092,24 +1094,24 @@
     )
     grads.add("state", trade_stages(back))
     grads.slot(only=("state",))
-    grads.slot(d_num, only=("up",))
-    grads.slot(*grads.started, only=("state",))
+    grads.slot(d_num, only=("state",))
     grads.add("d_mixed", core_stage(d_mixed_half))
     grads.slot(*grads.started, only=("d_mixed",))
+    grads.slot(*grads.started, only=("up",))
     grads.slot(*grads.started, only=("down",))
     d_mixed_other = grads.read("d_mixed", *grads.started)
     far, near = grads.finish("state", d_mixed_other, only=("state",))
     mixed = mix_segments(from_descendants, far, near)
-    grads.arrive(*mixed, only=("up",))
     grads.add("path", trade_stages(mixed))
-    grads.slot(*grads.started, only=("path",))
+    grads.slot(only=("path",))
     d_q, d_q_half, d_k, d_v = intra_backward(
         ids, tie(q, *grads.started), k, v, d_num, d_den, cos, sin, wave, wave_t, *path
     )
     grads.add("d_q", core_stage(d_q_half))
-    grads.arrive(d_q, only=("down",))
+    grads.arrive(d_q, only=("up",))
     grads.slot(*grads.started, only=("path", "d_q"))
     grads.slot(*grads.started, only=("up",))
+    grads.arrive(*grads.started, only=("down",))
     d_q_other = grads.read("d_q", *grads.started)
     (outq_part,) = weight_grad(
         ids,
@@ -1135,33 +1137,45 @@
     grads.add("kv0", reduction(kv_parts[0]))
     for part in kv_parts[1:]:
         grads.add("kv1", reduce_stages(part, core))
+    half = D // 2
+    closed = ()
+
+    def close(outq):
+        ours, others = jnp.split(outq, 2, axis=1)
+        sums = ours[:, D : D + 16] + others[:, D : D + 16]
+        q_grad = jnp.concatenate([ours[:, half:D], others[:, half:D]], axis=1)
+        out_grad = jnp.concatenate([ours[:, :half], others[:, :half]], axis=1)
+        return q_grad, out_grad, sums.T, sums[:, B_UP : B_UP + ff // D].T.reshape(-1)
+
     for step in TAIL:
         if step == "grad":
             tokens_grad = input_grad(ids, d_q, tie(d_kv, *grads.started), d_res1, w_qo, w_kv)
             grads.started = (tokens_grad,)
+        elif step == "close":
+            if not closed and "outq" in grads.finished:
+                closed = close(grads.finished["outq"])
+                grads.started += closed
         elif grads.names(step.split("+")):
             grads.slot(*grads.started, only=step.split("+"))
     while grads.running:
         grads.slot(*grads.started)
     done = grads.finished
+    q_grad, out_grad, sums, b_up_grad = closed or close(done["outq"])
     kv_grad = jnp.concatenate([done[n] for n in ("kv0", "kv1") if n in done], axis=0)
-    ours, others = jnp.split(done["outq"], 2, axis=1)
-    half = D // 2
-    sums = ours[:, D : D + 16] + others[:, D : D + 16]
     return (
         output,
         tokens_grad,
-        jnp.concatenate([ours[:, half:D], others[:, half:D], kv_grad], axis=1),
-        jnp.concatenate([ours[:, :half], others[:, :half]], axis=1),
-        sums[:, B_OUT],
-        sums[:, GAIN1],
-        sums[:, BIAS1],
+        jnp.concatenate([q_grad, kv_grad], axis=1),
+        out_grad,
+        sums[B_OUT],
+        sums[GAIN1],
+        sums[BIAS1],
         done["up"],
-        sums[:, B_UP : B_UP + ff // D].T.reshape(-1),
+        b_up_grad,
         done["down"],
-        sums[:, B_DOWN],
-        sums[:, GAIN2],
-        sums[:, BIAS2],
+        sums[B_DOWN],
+        sums[GAIN2],
+        sums[BIAS2],
     )
 
 

time: 280 us -> 270 us (0.964)
  waiting for transfers between devices: 85 us -> 72.2 us
  starting transfers between devices: 81.9 us -> 84.9 us
    ppermute x86, waiting for transfers between devices: 85 us -> 72.2 us  [exchange(): return lax.ppermute(x, axis, [(i, i ^ offset) for i in range(size)])]
    ppermute x86, starting transfers between devices: 81.9 us -> 84.9 us  [exchange(): return lax.ppermute(x, axis, [(i, i ^ offset) for i in range(size)])]
  transfers between devices with their start and end apart: 86 -> 86, of which waited for: 40 -> 40; matrix products, arithmetic and copies ran while one was open for 7% -> 9% of each run, Pallas kernels for 27% -> 28%
where the time goes in v4:
time: 270 us; the launch traced here: 269 us
  starting transfers between devices  84.9 us (31%)
  Pallas kernels  79.2 us (29%)
  waiting for transfers between devices  72.2 us (27%)
  other arithmetic  17.6 us (7%)
  local copies, waits for them, and re-layouts  10 us (4%)
  matrix products  3.7 us (1%)
    ppermute x86, starting transfers between devices, exchange(): return lax.ppermute(x, axis, [(i, i ^ offset) for i in range(size)])  84.9 us
    ppermute x86, waiting for transfers between devices, exchange(): return lax.ppermute(x, axis, [(i, i ^ offset) for i in range(size)])  72.2 us
    pallas_call x4, Pallas kernels, weight_grad(): call(kernel, 'weight_grad', tuple((shape_of((n, fsdp, share // n, width),...  14 us
    pallas_call x1, Pallas kernels, back_to_heads(): call(kernel, 'back_to_heads', (shape_of((rows, D), f32), shape_of((rows,...  9.94 us
    pallas_call x1, Pallas kernels, intra_backward(): call(kernel, 'intra_backward', (shape_of((rows, D), bf16), shape_of((rows...  8.77 us
    pallas_call x1, Pallas kernels, expand(): call(kernel, 'expand', (shape_of((rows, D), f32), shape_of((rows, LANES),...  7.47 us
    pallas_call x1, Pallas kernels, intra_forward(): call(kernel, 'intra_forward', (shape_of((rows, D), bf16), wide, wide), [V...  5.87 us
  transfers between devices with their start and end apart: 86, of which 40 were waited for; matrix products, arithmetic and copies ran while one was open for 9% of the time, Pallas kernels for 28%

profile of v4, /device:TPU:0, one launch (start us, length us, event | category | flops | bytes accessed | tf_op | source)
XLA Modules:
  0.0 269.4 jit_solution(12949965264664943252)
XLA Ops:
  1.5 4.0 %collective-permute-start = (bf16[1,24,1536]{2,1,0:T(8,128)(2,1)S(1)}, bf16[1,24,1536]{2,1,0:T(8,128)(2,1)S(1)}, u32[]{:S(2)}, u32[]{:S(2)}) collective-permute-start(bf16[1,24,1536]{2,1,0:T(8,128)(2,1)S(1)} %slice_bitcast_fusion.15), channel_id=1, source_target_pairs={{0,4},{1,5},{2,6},{3,7},{4,0},{5,1},{6,2},{7,3},{8,12},{9,13},{10,... | collective-permute-start | bytes 221192 | tf_op jit(solution)/shard_map/ppermute | solution.py:28
  12.4 1.8 fusion.25
  19.3 2.3 collective-permute-start.2
  27.4 3.0 %collective-permute-start.11 = (bf16[1,24,3072]{2,1,0:T(8,128)(2,1)}, bf16[1,24,3072]{2,1,0:T(8,128)(2,1)S(1)}, u32[]{:S(2)}, u32[]{:S(2)}) collective-permute-start(bf16[1,24,3072]{2,1,0:T(8,128)(2,1)} %bitcast.15), channel_id=1, source_target_pairs={{0,4},{1,5},{2,6},{3,7},{4,0},{5,1},{6,2},{7,3},{8,12},{9,13},{10,... | collective-permute-start | bytes 442376 | tf_op jit(solution)/shard_map/ppermute | solution.py:28
  32.7 2.6 collective-permute-done.11
  38.4 5.1 %project.1 = (bf16[512,768]{1,0:T(8,128)(2,1)S(1)}, bf16[512,768]{1,0:T(8,128)(2,1)S(1)}, bf16[2,2,104,128]{3,2,1,0:T(8,128)(2,1)S(1)}, bf16[2,2,104,128]{3,2,1,...) custom-call(s32[3]{0:T(128)S(1)} %pad_add_fusion.ids_ref, ...), custom_call_target="tpu_custom_call" | custom-call | flops 6480000000 | tf_op jit(solution)/shard_map/project/pallas_call | solution.py:353
  46.0 3.1 %collective-permute-start.17 = (bf16[2,2,104,128]{3,2,1,0:T(8,128)(2,1)S(1)}, bf16[2,2,104,128]{3,2,1,0:T(8,128)(2,1)S(1)}, u32[]{:S(2)}, u32[]{:S(2)}) collective-permute-start(bf16[2,2,104,128]{3,2,1,0:T(8,128)(2,1)S(1)} %get-tuple-element.252), channel_id=1, source_target_pairs={{0,4},{1,5},{2,6},{3,7},{4,0},{5,1},{6,2},{7,3},{8,12},{9,13},{10,... | collective-permute-start | bytes 319496 | tf_op jit(solution)/shard_map/ppermute | solution.py:28
  50.4 4.5 %collective-permute-done.16.refs_1_ = bf16[2,2,104,128]{3,2,1,0:T(8,128)(2,1)S(1)} collective-permute-done((bf16[2,2,104,128]{3,2,1,0:T(8,128)(2,1)S(1)}, bf16[2,2,104,128]{3,2,1,0:T(8,128)(2,1)S(1)}, u32[]{:S(2)}, u32[]{:S(2)}) %collective-permute-start.16) | collective-permute-done | bytes 106528 | tf_op jit(solution)/shard_map/ppermute | solution.py:28
  58.3 3.3 %collective-permute-done.21 = bf16[2,24,3072]{2,1,0:T(8,128)(2,1)S(1)} collective-permute-done((bf16[2,24,3072]{2,1,0:T(8,128)(2,1)S(1)}, bf16[2,24,3072]{2,1,0:T(8,128)(2,1)S(1)}, u32[]{:S(2)}, u32[]{:S(2)}) %collective-permute-start.21) | collective-permute-done | bytes 294944 | tf_op jit(solution)/shard_map/ppermute | solution.py:28
  65.9 5.9 %intra_forward.1 = (bf16[512,768]{1,0:T(8,128)(2,1)S(1)}, f32[512,768]{1,0:T(8,128)S(1)}, f32[512,768]{1,0:T(8,128)S(1)}) custom-call(bf16[512,768]{1,0:T(8,128)(2,1)S(1)} %copy-done.8, bf16[768,1792]{1,0:T(8,128)(2,1)S(1)} %bitcast.109, bf16[512,768]{1,0:T(8,128)(2,1)S(1)} %get-tuple-element.243.k_ref, bf16[512,768]{1,0:T(8,128)(2,1)S(1)} %get-tuple-element.260.v_ref, ...), custom_call_target="tpu_custom_call" | custom-call | flops 3540000000 | tf_op jit(solution)/shard_map/intra_forward/pallas_call | solution.py:411
  77.3 2.3 collective-permute-start.28
  79.8 1.8 collective-permute-done.26.refs_1_
  81.6 3.0 %collective-permute-done.27.refs_2_ = bf16[2,2,104,128]{3,2,1,0:T(8,128)(2,1)S(1)} collective-permute-done((bf16[2,2,104,128]{3,2,1,0:T(8,128)(2,1)S(1)}, bf16[2,2,104,128]{3,2,1,0:T(8,128)(2,1)S(1)}, u32[]{:S(2)}, u32[]{:S(2)}) %collective-permute-start.27) | collective-permute-done | bytes 106528 | tf_op jit(solution)/shard_map/ppermute | solution.py:28
  86.6 1.8 collective-permute-start.29
  91.8 3.5 %collective-permute-done.30.refs_4_ = bf16[4,2,104,128]{3,2,1,0:T(8,128)(2,1)S(1)} collective-permute-done((bf16[4,2,104,128]{3,2,1,0:T(8,128)(2,1)S(1)}, bf16[4,2,104,128]{3,2,1,0:T(8,128)(2,1)S(1)}, u32[]{:S(2)}, u32[]{:S(2)}) %collective-permute-start.30) | collective-permute-done | bytes 213024 | tf_op jit(solution)/shard_map/ppermute | solution.py:28
  97.8 4.0 %inter_forward.1 = (bf16[512,768]{1,0:T(8,128)(2,1)S(1)}, f32[512,768]{1,0:T(8,128)S(1)}) custom-call(s32[3]{0:T(128)S(1)} %pad_add_fusion.ids_ref, bf16[512,768]{1,0:T(8,128)(2,1)S(1)} %get-tuple-element.362.q_ref, f32[512,768]{1,0:T(8,128)S(1)} %get-tuple-element.299.num_ref, f32[512,768]{1,0:T(8,128)S(1)} %get-tuple-element.300.den_ref, ...), custom_call_target="tpu_custom_call" | custom-call | flops 9900000256 | tf_op jit(solution)/shard_map/inter_forward/pallas_call | solution.py:452
  101.9 2.1 collective-permute-done.36
  106.0 1.7 collective-permute-start.39
  107.7 7.5 %expand.1 = (f32[512,768]{1,0:T(8,128)S(1)}, f32[512,128]{1,0:T(8,128)S(1)}, bf16[512,768]{1,0:T(8,128)(2,1)S(1)}, bf16[512,3072]{1,0:T(8,128)(2,1)S(1)}, bf16[512,3072]{1,0:T(8,128)(2,1)S(1)}) custom-call(bf16[512,768]{1,0:T(8,128)(2,1)S(1)} %get-tuple-element.307.att_ref.refs_0_, bf16[512,768]{1,0:T(8,128)(2,1)S(1)} %copy-done.8, ...), custom_call_target="tpu_custom_call" | custom-call | flops 171000000 | tf_op jit(solution)/shard_map/expand/pallas_call | solution.py:507
  115.2 4.1 %collective-permute-done.38 = bf16[8,96,384]{2,1,0:T(8,128)(2,1)S(1)} collective-permute-done((bf16[8,96,384]{2,1,0:T(8,128)(2,1)S(1)}, bf16[8,96,384]{2,1,0:T(8,128)(2,1)S(1)}, u32[]{:S(2)}, u32[]{:S(2)}) %collective-permute-start.38) | collective-permute-done | bytes 589856 | tf_op jit(solution)/shard_map/ppermute | solution.py:28
  120.4 2.3 collective-permute-done.40.refs_1_
  122.8 1.7 collective-permute-done.41.refs_3_
  126.3 5.3 %contract.1 = (bf16[512,768]{1,0:T(8,128)(2,1)}, f32[512,768]{1,0:T(8,128)S(1)}, bf16[512,768]{1,0:T(8,128)(2,1)S(1)}, bf16[512,384]{1,0:T(8,128)(2,1)S(1)}, f32[16,768]{1,0:T(8,128)S(1)}) custom-call(s32[3]{0:T(128)S(1)} %pad_add_fusion.ids_ref, bf16[512,3072]{1,0:T(8,128)(2,1)S(1)} %get-tuple-element.322.gelu_ref.refs_0_, ...), custom_call_target="tpu_custom_call" | custom-call | flops 3600000000 | tf_op jit(solution)/shard_map/contract/pallas_call | solution.py:551
  132.7 5.0 %turn.1 = (bf16[512,3072]{1,0:T(8,128)(2,1)S(1)}, bf16[512,1536]{1,0:T(8,128)(2,1)S(1)}, f32[16,768]{1,0:T(8,128)S(1)}) custom-call(s32[3]{0:T(128)S(1)} %pad_add_fusion.ids_ref, bf16[512,768]{1,0:T(8,128)(2,1)S(1)} %get-tuple-element.332.dlow_ref.refs_2_, bf16[512,3072]{1,0:T(8,128)(2,1)S(1)} %get-tuple-element.326.slope_ref, ...), custom_call_target="tpu_custom_call" | custom-call | flops 13500000256 | tf_op jit(solution)/shard_map/turn/pallas_call | solution.py:592
  138.2 5.7 %weight_grad.4 = bf16[2,8,192,384]{3,2,1,0:T(8,128)(2,1)S(1)} custom-call(s32[3]{0:T(128)S(1)} %pad_add_fusion.ids_ref, bf16[512,3072]{1,0:T(8,128)(2,1)S(1)} %get-tuple-element.322.gelu_ref.refs_0_, bf16[512,3072]{1,0:T(8,128)(2,1)S(1)} %collective-permute-done.43.refs_1_, bf16[512,768]{1,0:T(8,128)(2,1)S(1)} %get-tuple-element.332.dlow_ref.refs_2_, ...), custom_call_target="tpu_custom_call" | custom-call | flops 3600000000 | tf_op jit(solution)/shard_map/weight_grad/pallas_call | solution.py:853
  144.0 3.2 %weight_grad.5 = bf16[1,8,96,1536]{3,2,1,0:T(8,128)(2,1)S(1)} custom-call(s32[3]{0:T(128)S(1)} %pad_add_fusion.ids_ref, bf16[512,768]{1,0:T(8,128)(2,1)S(1)} %get-tuple-element.320.refs_0_, bf16[512,768]{1,0:T(8,128)(2,1)S(1)} %collective-permute-done.42.refs_1_, bf16[512,3072]{1,0:T(8,128)(2,1)S(1)} %get-tuple-element.336.refs_2_.dup_ref, ...), custom_call_target="tpu_custom_call" | custom-call | flops 720000000 | tf_op jit(solution)/shard_map/weight_grad/pallas_call | solution.py:853
  149.4 9.9 %back_to_heads.1 = (f32[512,768]{1,0:T(8,128)S(1)}, bf16[512,768]{1,0:T(8,128)(2,1)S(1)}, bf16[512,384]{1,0:T(8,128)(2,1)S(1)}, bf16[512,768]{1,0:T(8,128)(2,1)S...) custom-call(s32[3]{0:T(128)S(1)} %pad_add_fusion.ids_ref, ...), custom_call_target="tpu_custom_call" | custom-call | flops 7080000000 | tf_op jit(solution)/shard_map/back_to_heads/pallas_call | solution.py:656
  161.6 2.1 collective-permute-start.48
  164.7 6.4 %collective-permute-done.47.refs_2_ = bf16[2,2,104,128]{3,2,1,0:T(8,128)(2,1)S(1)} collective-permute-done((bf16[2,2,104,128]{3,2,1,0:T(8,128)(2,1)S(1)}, bf16[2,2,104,128]{3,2,1,0:T(8,128)(2,1)S(1)}, u32[]{:S(2)}, u32[]{:S(2)}) %collective-permute-start.47) | collective-permute-done | bytes 106528 | tf_op jit(solution)/shard_map/ppermute | solution.py:28
  174.3 2.3 collective-permute-done.51
  177.7 3.2 %collective-permute-start.53 = (bf16[2,2,104,128]{3,2,1,0:T(8,128)(2,1)S(1)}, bf16[2,2,104,128]{3,2,1,0:T(8,128)(2,1)S(1)}, u32[]{:S(2)}, u32[]{:S(2)}) collective-permute-start(bf16[2,2,104,128]{3,2,1,0:T(8,128)(2,1)S(1)} %get-tuple-element.359), channel_id=1, source_target_pairs={{0,2},{1,3},{2,0},{3,1},{4,6},{5,7},{6,4},{7,5},{8,10},{9,11},{10,... | collective-permute-start | bytes 319496 | tf_op jit(solution)/shard_map/ppermute | solution.py:28
  180.9 2.4 collective-permute-start.55
  183.3 1.7 collective-permute-start.59
  185.0 8.8 %intra_backward.1 = (bf16[512,768]{1,0:T(8,128)(2,1)S(1)}, bf16[512,384]{1,0:T(8,128)(2,1)S(1)}, f32[512,768]{1,0:T(8,128)S(1)}, f32[512,768]{1,0:T(8,128)S(1)}) custom-call(s32[3]{0:T(128)S(1)} %pad_add_fusion.ids_ref, bf16[512,768]{1,0:T(8,128)(2,1)S(1)} %get-tuple-element.362.q_ref, bf16[512,768]{1,0:T(8,128)(2,1)S(1)} %get-tuple-element.243.k_ref, ...), custom_call_target="tpu_custom_call" | custom-call | flops 6179999744 | tf_op jit(solution)/shard_map/intra_backward/pallas_call | solution.py:725
  197.5 2.4 weight_grad.6
  201.0 1.8 collective-permute-done.57.refs_4_
  202.8 4.1 %inter_backward.1.dkv_ref = bf16[2,512,768]{2,1,0:T(8,128)(2,1)S(1)} custom-call(s32[3]{0:T(128)S(1)} %pad_add_fusion.ids_ref, bf16[512,768]{1,0:T(8,128)(2,1)S(1)} %get-tuple-element.243.k_ref, bf16[512,768]{1,0:T(8,128)(2,1)S(1)} %get-tuple-element.260.v_ref, f32[512,768]{1,0:T(8,128)S(1)} %get-tuple-element.365.dk_ref, ...), custom_call_target="tpu_custom_call" | custom-call | flops 2760000000 | tf_op jit(solution)/shard_map/inter_backward/pallas_call | solution.py:773
  214.6 2.7 %weight_grad.7 = (bf16[2,8,24,768]{3,2,1,0:T(8,128)(2,1)S(1)}, bf16[1,8,48,768]{3,2,1,0:T(8,128)(2,1)S(1)}) custom-call(s32[3]{0:T(128)S(1)} %pad_add_fusion.ids_ref, bf16[512,768]{1,0:T(8,128)(2,1)S(1)} %copy-done.8, bf16[512,768]{1,0:T(8,128)(2,1)S(1)} %copy-done.17, bf16[512,768]{1,0:T(8,128)(2,1)S(1)} %copy-done.9, ...), custom_call_target="tpu_custom_call" | custom-call | flops 2016000000 | tf_op jit(solution)/shard_map/weight_grad/pallas_call | solution.py:853
  218.6 1.9 collective-permute-start.68
  220.8 4.2 %input_grad.1 = f32[512,768]{1,0:T(8,128)} custom-call(s32[3]{0:T(128)S(1)} %pad_add_fusion.ids_ref, bf16[512,768]{1,0:T(8,128)(2,1)S(1)} %copy-done.11, bf16[2,512,768]{2,1,0:T(8,128)(2,1)S(1)} %copy-done.3, f32[512,768]{1,0:T(8,128)S(1)} %copy-done.5, bf16[768,1792]{1,0:T(8,128)(2,1)S(1)} %bitcast.113, bf16[768,1536]{1,0:T(8,128)(2,1)S(1)} %bitcast.117), custom_call_target="tpu_custom_call" | custom-call | flops 2400000000 | tf_op jit(solution)/shard_map/input_grad/pallas_call | solution.py:797
  225.0 1.8 collective-permute-start.70
  227.1 1.7 collective-permute-start.64
  230.0 2.9 %collective-permute-done.68 = bf16[8,24,768]{2,1,0:T(8,128)(2,1)S(1)} collective-permute-done((bf16[8,24,768]{2,1,0:T(8,128)(2,1)S(1)}, bf16[8,24,768]{2,1,0:T(8,128)(2,1)S(1)}, u32[]{:S(2)}, u32[]{:S(2)}) %collective-permute-start.68) | collective-permute-done | bytes 294944 | tf_op jit(solution)/shard_map/ppermute | solution.py:28
  233.4 8.2 %collective-permute-done.67 = bf16[2,48,768]{2,1,0:T(8,128)(2,1)S(1)} collective-permute-done((bf16[2,48,768]{2,1,0:T(8,128)(2,1)S(1)}, bf16[2,48,768]{2,1,0:T(8,128)(2,1)S(1)}, u32[]{:S(2)}, u32[]{:S(2)}) %collective-permute-start.67) | collective-permute-done | bytes 147488 | tf_op jit(solution)/shard_map/ppermute | solution.py:28
  244.0 2.0 collective-permute-start.69
  247.4 3.5 %collective-permute-done.69 = bf16[2,48,896]{2,1,0:T(8,128)(2,1)S(1)} collective-permute-done((bf16[2,48,896]{2,1,0:T(8,128)(2,1)S(1)}, bf16[2,48,896]{2,1,0:T(8,128)(2,1)S(1)}, u32[]{:S(2)}, u32[]{:S(2)}) %collective-permute-start.69) | collective-permute-done | bytes 172064 | tf_op jit(solution)/shard_map/ppermute | solution.py:28
  250.9 1.9 collective-permute-start.72
  255.5 1.8 collective-permute-done.72
  (315 shorter events, 99.5 us)
Async XLA Ops:
  1.5 7.9 %collective-permute-start = (bf16[1,24,1536]{2,1,0:T(8,128)(2,1)S(1)}, bf16[1,24,1536]{2,1,0:T(8,128)(2,1)S(1)}, u32[]{:S(2)}, u32[]{:S(2)}) collective-permute-start(bf16[1,24,1536]{2,1,0:T(8,128)(2,1)S(1)} %slice_bitcast_fusion.15), channel_id=1, source_target_pairs={{0,4},{1,5},{2,6},{3,7},{4,0},{5,1},{6,2},{7,3},{8,12},{9,13},{10,... | collective-permute-start | bytes 221192 | tf_op jit(solution)/shard_map/ppermute | solution.py:28
  5.6 31.2 %collective-permute-start.10 = (bf16[512,768]{1,0:T(8,128)(2,1)}, bf16[512,768]{1,0:T(8,128)(2,1)S(1)}, u32[]{:S(2)}, u32[]{:S(2)}) collective-permute-start(bf16[512,768]{1,0:T(8,128)(2,1)} %refs_0_.1), channel_id=1, source_target_pairs={{0,8},{8,0},{16,24},{24,16},{1,9},{9,1},{17,25},{25,17},{2,10},{10... | collective-permute-start | bytes 2359304 | tf_op jit(solution)/shard_map/ppermute | solution.py:28
  22.0 8.8 %collective-permute-start.6 = (bf16[8,24,768]{2,1,0:T(8,128)(2,1)S(1)}, bf16[8,24,768]{2,1,0:T(8,128)(2,1)S(1)}, u32[]{:S(2)}, u32[]{:S(2)}) collective-permute-start(bf16[8,24,768]{2,1,0:T(8,128)(2,1)S(1)} %pad_maximum_fusion.21), channel_id=1, source_target_pairs={{0,1},{1,0},{2,3},{3,2},{4,5},{5,4},{6,7},{7,6},{8,9},{9,8},{10,11... | collective-permute-start | bytes 884744 | tf_op jit(solution)/shard_map/ppermute | solution.py:28
  23.5 7.2 %collective-permute-start.5 = (bf16[8,24,768]{2,1,0:T(8,128)(2,1)S(1)}, bf16[8,24,768]{2,1,0:T(8,128)(2,1)S(1)}, u32[]{:S(2)}, u32[]{:S(2)}) collective-permute-start(bf16[8,24,768]{2,1,0:T(8,128)(2,1)S(1)} %pad_maximum_fusion.20), channel_id=1, source_target_pairs={{0,16},{8,24},{16,0},{24,8},{1,17},{9,25},{17,1},{25,9},{2,18},{10... | collective-permute-start | bytes 884744 | tf_op jit(solution)/shard_map/ppermute | solution.py:28
  27.4 7.9 %collective-permute-start.11 = (bf16[1,24,3072]{2,1,0:T(8,128)(2,1)}, bf16[1,24,3072]{2,1,0:T(8,128)(2,1)S(1)}, u32[]{:S(2)}, u32[]{:S(2)}) collective-permute-start(bf16[1,24,3072]{2,1,0:T(8,128)(2,1)} %bitcast.15), channel_id=1, source_target_pairs={{0,4},{1,5},{2,6},{3,7},{4,0},{5,1},{6,2},{7,3},{8,12},{9,13},{10,... | collective-permute-start | bytes 442376 | tf_op jit(solution)/shard_map/ppermute | solution.py:28
  31.5 12.0 %collective-permute-start.9 = (bf16[4,24,896]{2,1,0:T(8,128)(2,1)S(1)}, bf16[4,24,896]{2,1,0:T(8,128)(2,1)S(1)}, u32[]{:S(2)}, u32[]{:S(2)}) collective-permute-start(bf16[4,24,896]{2,1,0:T(8,128)(2,1)S(1)} %get-tuple-element.473), channel_id=1, source_target_pairs={{0,16},{8,24},{16,0},{24,8},{1,17},{9,25},{17,1},{25,9},{2,18},{10... | collective-permute-start | bytes 516104 | tf_op jit(solution)/shard_map/ppermute | solution.py:28
  35.3 8.2 %collective-permute-start.8 = (bf16[4,24,896]{2,1,0:T(8,128)(2,1)S(1)}, bf16[4,24,896]{2,1,0:T(8,128)(2,1)S(1)}, u32[]{:S(2)}, u32[]{:S(2)}) collective-permute-start(bf16[4,24,896]{2,1,0:T(8,128)(2,1)S(1)} %get-tuple-element.474), channel_id=1, source_target_pairs={{0,1},{1,0},{2,3},{3,2},{4,5},{5,4},{6,7},{7,6},{8,9},{9,8},{10,11... | collective-permute-start | bytes 516104 | tf_op jit(solution)/shard_map/ppermute | solution.py:28
  43.6 13.2 %collective-permute-start.14 = (bf16[8,24,896]{2,1,0:T(8,128)(2,1)S(1)}, bf16[8,24,896]{2,1,0:T(8,128)(2,1)S(1)}, u32[]{:S(2)}, u32[]{:S(2)}) collective-permute-start(bf16[8,24,896]{2,1,0:T(8,128)(2,1)S(1)} %get-tuple-element.249), channel_id=1, source_target_pairs={{0,16},{8,24},{16,0},{24,8},{1,17},{9,25},{17,1},{25,9},{2,18},{10... | collective-permute-start | bytes 1032200 | tf_op jit(solution)/shard_map/ppermute | solution.py:28
  44.5 12.3 %collective-permute-start.15 = (bf16[8,24,896]{2,1,0:T(8,128)(2,1)S(1)}, bf16[8,24,896]{2,1,0:T(8,128)(2,1)S(1)}, u32[]{:S(2)}, u32[]{:S(2)}) collective-permute-start(bf16[8,24,896]{2,1,0:T(8,128)(2,1)S(1)} %get-tuple-element.250), channel_id=1, source_target_pairs={{0,1},{1,0},{2,3},{3,2},{4,5},{5,4},{6,7},{7,6},{8,9},{9,8},{10,11... | collective-permute-start | bytes 1032200 | tf_op jit(solution)/shard_map/ppermute | solution.py:28
  46.0 8.9 %collective-permute-start.16 = (bf16[2,2,104,128]{3,2,1,0:T(8,128)(2,1)S(1)}, bf16[2,2,104,128]{3,2,1,0:T(8,128)(2,1)S(1)}, u32[]{:S(2)}, u32[]{:S(2)}) collective-permute-start(bf16[2,2,104,128]{3,2,1,0:T(8,128)(2,1)S(1)} %get-tuple-element.251), channel_id=1, source_target_pairs={{0,2},{1,3},{2,0},{3,1},{4,6},{5,7},{6,4},{7,5},{8,10},{9,11},{10,... | collective-permute-start | bytes 319496 | tf_op jit(solution)/shard_map/ppermute | solution.py:28
  46.0 9.5 %collective-permute-start.17 = (bf16[2,2,104,128]{3,2,1,0:T(8,128)(2,1)S(1)}, bf16[2,2,104,128]{3,2,1,0:T(8,128)(2,1)S(1)}, u32[]{:S(2)}, u32[]{:S(2)}) collective-permute-start(bf16[2,2,104,128]{3,2,1,0:T(8,128)(2,1)S(1)} %get-tuple-element.252), channel_id=1, source_target_pairs={{0,4},{1,5},{2,6},{3,7},{4,0},{5,1},{6,2},{7,3},{8,12},{9,13},{10,... | collective-permute-start | bytes 319496 | tf_op jit(solution)/shard_map/ppermute | solution.py:28
  49.1 7.7 %collective-permute-start.18 = (bf16[2,2,104,128]{3,2,1,0:T(8,128)(2,1)S(1)}, bf16[2,2,104,128]{3,2,1,0:T(8,128)(2,1)S(1)}, u32[]{:S(2)}, u32[]{:S(2)}) collective-permute-start(bf16[2,2,104,128]{3,2,1,0:T(8,128)(2,1)S(1)} %get-tuple-element.253), channel_id=1, source_target_pairs={{0,6},{1,7},{2,4},{3,5},{4,2},{5,3},{6,0},{7,1},{8,14},{9,15},{10,... | collective-permute-start | bytes 319496 | tf_op jit(solution)/shard_map/ppermute | solution.py:28
  56.8 14.9 %collective-permute-start.25 = (bf16[4,2,104,128]{3,2,1,0:T(8,128)(2,1)S(1)}, bf16[4,2,104,128]{3,2,1,0:T(8,128)(2,1)S(1)}, u32[]{:S(2)}, u32[]{:S(2)}) collective-permute-start(bf16[4,2,104,128]{3,2,1,0:T(8,128)(2,1)S(1)} %pad_maximum_fusion.27), channel_id=1, source_target_pairs={{0,1},{1,0},{2,3},{3,2},{4,5},{5,4},{6,7},{7,6},{8,9},{9,8},{10,11... | collective-permute-start | bytes 638984 | tf_op jit(solution)/shard_map/ppermute | solution.py:28
  62.7 9.4 %collective-permute-start.22 = (bf16[4,24,1536]{2,1,0:T(8,128)(2,1)S(1)}, bf16[4,24,1536]{2,1,0:T(8,128)(2,1)S(1)}, u32[]{:S(2)}, u32[]{:S(2)}) collective-permute-start(bf16[4,24,1536]{2,1,0:T(8,128)(2,1)S(1)} %get-tuple-element.267), channel_id=1, source_target_pairs={{0,1},{1,0},{2,3},{3,2},{4,5},{5,4},{6,7},{7,6},{8,9},{9,8},{10,11... | collective-permute-start | bytes 884744 | tf_op jit(solution)/shard_map/ppermute | solution.py:28
  63.5 8.6 %collective-permute-start.23 = (bf16[4,24,1536]{2,1,0:T(8,128)(2,1)S(1)}, bf16[4,24,1536]{2,1,0:T(8,128)(2,1)S(1)}, u32[]{:S(2)}, u32[]{:S(2)}) collective-permute-start(bf16[4,24,1536]{2,1,0:T(8,128)(2,1)S(1)} %get-tuple-element.268), channel_id=1, source_target_pairs={{0,16},{8,24},{16,0},{24,8},{1,17},{9,25},{17,1},{25,9},{2,18},{10... | collective-permute-start | bytes 884744 | tf_op jit(solution)/shard_map/ppermute | solution.py:28
  72.7 12.2 %collective-permute-start.31 = (bf16[8,24,1536]{2,1,0:T(8,128)(2,1)S(1)}, bf16[8,24,1536]{2,1,0:T(8,128)(2,1)S(1)}, u32[]{:S(2)}, u32[]{:S(2)}) collective-permute-start(bf16[8,24,1536]{2,1,0:T(8,128)(2,1)S(1)} %pad_maximum_fusion.10), channel_id=1, source_target_pairs={{0,16},{8,24},{16,0},{24,8},{1,17},{9,25},{17,1},{25,9},{2,18},{10... | collective-permute-start | bytes 1769480 | tf_op jit(solution)/shard_map/ppermute | solution.py:28
  74.0 11.7 %collective-permute-start.32 = (bf16[8,24,1536]{2,1,0:T(8,128)(2,1)S(1)}, bf16[8,24,1536]{2,1,0:T(8,128)(2,1)S(1)}, u32[]{:S(2)}, u32[]{:S(2)}) collective-permute-start(bf16[8,24,1536]{2,1,0:T(8,128)(2,1)S(1)} %pad_maximum_fusion.11), channel_id=1, source_target_pairs={{0,1},{1,0},{2,3},{3,2},{4,5},{5,4},{6,7},{7,6},{8,9},{9,8},{10,11... | collective-permute-start | bytes 1769480 | tf_op jit(solution)/shard_map/ppermute | solution.py:28
  76.3 8.4 %collective-permute-start.27 = (bf16[2,2,104,128]{3,2,1,0:T(8,128)(2,1)S(1)}, bf16[2,2,104,128]{3,2,1,0:T(8,128)(2,1)S(1)}, u32[]{:S(2)}, u32[]{:S(2)}) collective-permute-start(bf16[2,2,104,128]{3,2,1,0:T(8,128)(2,1)S(1)} %get-tuple-element.278), channel_id=1, source_target_pairs={{0,4},{1,5},{2,6},{3,7},{4,0},{5,1},{6,2},{7,3},{8,12},{9,13},{10,... | collective-permute-start | bytes 319496 | tf_op jit(solution)/shard_map/ppermute | solution.py:28
  77.3 7.3 %collective-permute-start.28 = (bf16[2,2,104,128]{3,2,1,0:T(8,128)(2,1)S(1)}, bf16[2,2,104,128]{3,2,1,0:T(8,128)(2,1)S(1)}, u32[]{:S(2)}, u32[]{:S(2)}) collective-permute-start(bf16[2,2,104,128]{3,2,1,0:T(8,128)(2,1)S(1)} %get-tuple-element.279), channel_id=1, source_target_pairs={{0,6},{1,7},{2,4},{3,5},{4,2},{5,3},{6,0},{7,1},{8,14},{9,15},{10,... | collective-permute-start | bytes 319496 | tf_op jit(solution)/shard_map/ppermute | solution.py:28
  86.6 9.0 %collective-permute-start.29 = (bf16[2,96,768]{2,1,0:T(8,128)(2,1)S(1)}, bf16[2,96,768]{2,1,0:T(8,128)(2,1)S(1)}, u32[]{:S(2)}, u32[]{:S(2)}) collective-permute-start(bf16[2,96,768]{2,1,0:T(8,128)(2,1)S(1)} %pad_maximum_fusion.23), channel_id=1, source_target_pairs={{0,2},{1,3},{2,0},{3,1},{4,6},{5,7},{6,4},{7,5},{8,10},{9,11},{10,... | collective-permute-start | bytes 884744 | tf_op jit(solution)/shard_map/ppermute | solution.py:28
  95.7 8.2 %collective-permute-start.36 = (bf16[4,96,384]{2,1,0:T(8,128)(2,1)S(1)}, bf16[4,96,384]{2,1,0:T(8,128)(2,1)S(1)}, u32[]{:S(2)}, u32[]{:S(2)}) collective-permute-start(bf16[4,96,384]{2,1,0:T(8,128)(2,1)S(1)} %get-tuple-element.296), channel_id=1, source_target_pairs={{0,1},{1,0},{2,3},{3,2},{4,5},{5,4},{6,7},{7,6},{8,9},{9,8},{10,11... | collective-permute-start | bytes 884744 | tf_op jit(solution)/shard_map/ppermute | solution.py:28
  97.2 8.2 %collective-permute-start.37 = (bf16[4,96,384]{2,1,0:T(8,128)(2,1)S(1)}, bf16[4,96,384]{2,1,0:T(8,128)(2,1)S(1)}, u32[]{:S(2)}, u32[]{:S(2)}) collective-permute-start(bf16[4,96,384]{2,1,0:T(8,128)(2,1)S(1)} %get-tuple-element.297), channel_id=1, source_target_pairs={{0,16},{8,24},{16,0},{24,8},{1,17},{9,25},{17,1},{25,9},{2,18},{10... | collective-permute-start | bytes 884744 | tf_op jit(solution)/shard_map/ppermute | solution.py:28
  105.6 13.7 %collective-permute-start.38 = (bf16[8,96,384]{2,1,0:T(8,128)(2,1)S(1)}, bf16[8,96,384]{2,1,0:T(8,128)(2,1)S(1)}, u32[]{:S(2)}, u32[]{:S(2)}) collective-permute-start(bf16[8,96,384]{2,1,0:T(8,128)(2,1)S(1)} %pad_maximum_fusion.13), channel_id=1, source_target_pairs={{0,16},{8,24},{16,0},{24,8},{1,17},{9,25},{17,1},{25,9},{2,18},{10... | collective-permute-start | bytes 1769480 | tf_op jit(solution)/shard_map/ppermute | solution.py:28
  106.0 13.5 %collective-permute-start.39 = (bf16[8,96,384]{2,1,0:T(8,128)(2,1)S(1)}, bf16[8,96,384]{2,1,0:T(8,128)(2,1)S(1)}, u32[]{:S(2)}, u32[]{:S(2)}) collective-permute-start(bf16[8,96,384]{2,1,0:T(8,128)(2,1)S(1)} %pad_maximum_fusion.14), channel_id=1, source_target_pairs={{0,1},{1,0},{2,3},{3,2},{4,5},{5,4},{6,7},{7,6},{8,9},{9,8},{10,11... | collective-permute-start | bytes 1769480 | tf_op jit(solution)/shard_map/ppermute | solution.py:28
  147.3 25.5 %collective-permute-start.52 = (bf16[3,96,1536]{2,1,0:T(8,128)(2,1)S(1)}, bf16[3,96,1536]{2,1,0:T(8,128)(2,1)S(1)}, u32[]{:S(2)}, u32[]{:S(2)}) collective-permute-start(bf16[3,96,1536]{2,1,0:T(8,128)(2,1)S(1)} %slice_bitcast_fusion.1), channel_id=1, source_target_pairs={{0,1},{1,0},{2,3},{3,2},{4,5},{5,4},{6,7},{7,6},{8,9},{9,8},{10,11... | collective-permute-start | bytes 2654216 | tf_op jit(solution)/shard_map/ppermute | solution.py:28
  148.8 27.8 %collective-permute-start.51 = (bf16[8,192,384]{2,1,0:T(8,128)(2,1)S(1)}, bf16[8,192,384]{2,1,0:T(8,128)(2,1)S(1)}, u32[]{:S(2)}, u32[]{:S(2)}) collective-permute-start(bf16[8,192,384]{2,1,0:T(8,128)(2,1)S(1)} %slice_bitcast_fusion), channel_id=1, source_target_pairs={{0,16},{8,24},{16,0},{24,8},{1,17},{9,25},{17,1},{25,9},{2,18},{10... | collective-permute-start | bytes 3538952 | tf_op jit(solution)/shard_map/ppermute | solution.py:28
  160.6 10.5 %collective-permute-start.47 = (bf16[2,2,104,128]{3,2,1,0:T(8,128)(2,1)S(1)}, bf16[2,2,104,128]{3,2,1,0:T(8,128)(2,1)S(1)}, u32[]{:S(2)}, u32[]{:S(2)}) collective-permute-start(bf16[2,2,104,128]{3,2,1,0:T(8,128)(2,1)S(1)} %get-tuple-element.343), channel_id=1, source_target_pairs={{0,4},{1,5},{2,6},{3,7},{4,0},{5,1},{6,2},{7,3},{8,12},{9,13},{10,... | collective-permute-start | bytes 319496 | tf_op jit(solution)/shard_map/ppermute | solution.py:28
  161.6 9.5 %collective-permute-start.48 = (bf16[2,2,104,128]{3,2,1,0:T(8,128)(2,1)S(1)}, bf16[2,2,104,128]{3,2,1,0:T(8,128)(2,1)S(1)}, u32[]{:S(2)}, u32[]{:S(2)}) collective-permute-start(bf16[2,2,104,128]{3,2,1,0:T(8,128)(2,1)S(1)} %get-tuple-element.344), channel_id=1, source_target_pairs={{0,6},{1,7},{2,4},{3,5},{4,2},{5,3},{6,0},{7,1},{8,14},{9,15},{10,... | collective-permute-start | bytes 319496 | tf_op jit(solution)/shard_map/ppermute | solution.py:28
  173.7 20.1 %collective-permute-start.56 = (bf16[1,96,1536]{2,1,0:T(8,128)(2,1)S(1)}, bf16[1,96,1536]{2,1,0:T(8,128)(2,1)S(1)}, u32[]{:S(2)}, u32[]{:S(2)}) collective-permute-start(bf16[1,96,1536]{2,1,0:T(8,128)(2,1)S(1)} %slice_bitcast_fusion.12), channel_id=1, source_target_pairs={{0,1},{1,0},{2,3},{3,2},{4,5},{5,4},{6,7},{7,6},{8,9},{9,8},{10,11... | collective-permute-start | bytes 884744 | tf_op jit(solution)/shard_map/ppermute | solution.py:28
  177.7 17.2 %collective-permute-start.53 = (bf16[2,2,104,128]{3,2,1,0:T(8,128)(2,1)S(1)}, bf16[2,2,104,128]{3,2,1,0:T(8,128)(2,1)S(1)}, u32[]{:S(2)}, u32[]{:S(2)}) collective-permute-start(bf16[2,2,104,128]{3,2,1,0:T(8,128)(2,1)S(1)} %get-tuple-element.359), channel_id=1, source_target_pairs={{0,2},{1,3},{2,0},{3,1},{4,6},{5,7},{6,4},{7,5},{8,10},{9,11},{10,... | collective-permute-start | bytes 319496 | tf_op jit(solution)/shard_map/ppermute | solution.py:28
  180.9 14.0 %collective-permute-start.54 = (bf16[2,2,104,128]{3,2,1,0:T(8,128)(2,1)S(1)}, bf16[2,2,104,128]{3,2,1,0:T(8,128)(2,1)S(1)}, u32[]{:S(2)}, u32[]{:S(2)}) collective-permute-start(bf16[2,2,104,128]{3,2,1,0:T(8,128)(2,1)S(1)} %get-tuple-element.360), channel_id=1, source_target_pairs={{0,4},{1,5},{2,6},{3,7},{4,0},{5,1},{6,2},{7,3},{8,12},{9,13},{10,... | collective-permute-start | bytes 319496 | tf_op jit(solution)/shard_map/ppermute | solution.py:28
  180.9 14.0 %collective-permute-start.55 = (bf16[2,2,104,128]{3,2,1,0:T(8,128)(2,1)S(1)}, bf16[2,2,104,128]{3,2,1,0:T(8,128)(2,1)S(1)}, u32[]{:S(2)}, u32[]{:S(2)}) collective-permute-start(bf16[2,2,104,128]{3,2,1,0:T(8,128)(2,1)S(1)} %get-tuple-element.361), channel_id=1, source_target_pairs={{0,6},{1,7},{2,4},{3,5},{4,2},{5,3},{6,0},{7,1},{8,14},{9,15},{10,... | collective-permute-start | bytes 319496 | tf_op jit(solution)/shard_map/ppermute | solution.py:28
  183.3 13.2 %collective-permute-start.59 = (bf16[4,192,384]{2,1,0:T(8,128)(2,1)S(1)}, bf16[4,192,384]{2,1,0:T(8,128)(2,1)S(1)}, u32[]{:S(2)}, u32[]{:S(2)}) collective-permute-start(bf16[4,192,384]{2,1,0:T(8,128)(2,1)S(1)} %get-tuple-element.356), channel_id=1, source_target_pairs={{0,1},{1,0},{2,3},{3,2},{4,5},{5,4},{6,7},{7,6},{8,9},{9,8},{10,11... | collective-permute-start | bytes 1769480 | tf_op jit(solution)/shard_map/ppermute | solution.py:28
  195.1 7.7 %collective-permute-start.57 = (bf16[4,2,104,128]{3,2,1,0:T(8,128)(2,1)S(1)}, bf16[4,2,104,128]{3,2,1,0:T(8,128)(2,1)S(1)}, u32[]{:S(2)}, u32[]{:S(2)}) collective-permute-start(bf16[4,2,104,128]{3,2,1,0:T(8,128)(2,1)S(1)} %pad_maximum_fusion.30), channel_id=1, source_target_pairs={{0,1},{1,0},{2,3},{3,2},{4,5},{5,4},{6,7},{7,6},{8,9},{9,8},{10,11... | collective-permute-start | bytes 638984 | tf_op jit(solution)/shard_map/ppermute | solution.py:28
  195.5 15.7 %collective-permute-start.60 = (bf16[2,96,1536]{2,1,0:T(8,128)(2,1)}, bf16[2,96,1536]{2,1,0:T(8,128)(2,1)}, u32[]{:S(2)}, u32[]{:S(2)}) collective-permute-start(bf16[2,96,1536]{2,1,0:T(8,128)(2,1)} %fusion.1), channel_id=1, source_target_pairs={{0,2},{1,3},{2,0},{3,1},{4,6},{5,7},{6,4},{7,5},{8,10},{9,11},{10,... | collective-permute-start | bytes 1769480 | tf_op jit(solution)/shard_map/ppermute | solution.py:28
  208.5 18.4 %collective-permute-start.62 = (bf16[8,48,896]{2,1,0:T(8,128)(2,1)}, bf16[8,48,896]{2,1,0:T(8,128)(2,1)S(1)}, u32[]{:S(2)}, u32[]{:S(2)}) collective-permute-start(bf16[8,48,896]{2,1,0:T(8,128)(2,1)} %slice_bitcast_fusion.4), channel_id=1, source_target_pairs={{0,16},{8,24},{16,0},{24,8},{1,17},{9,25},{17,1},{25,9},{2,18},{10... | collective-permute-start | bytes 2064392 | tf_op jit(solution)/shard_map/ppermute | solution.py:28
  208.9 16.1 %collective-permute-start.63 = (bf16[2,192,384]{2,1,0:T(8,128)(2,1)}, bf16[2,192,384]{2,1,0:T(8,128)(2,1)S(1)}, u32[]{:S(2)}, u32[]{:S(2)}) collective-permute-start(bf16[2,192,384]{2,1,0:T(8,128)(2,1)} %get-tuple-element.384), channel_id=1, source_target_pairs={{0,2},{1,3},{2,0},{3,1},{4,6},{5,7},{6,4},{7,5},{8,10},{9,11},{10,... | collective-permute-start | bytes 884744 | tf_op jit(solution)/shard_map/ppermute | solution.py:28
  217.4 24.3 %collective-permute-start.65 = (bf16[1,96,1536]{2,1,0:T(8,128)(2,1)S(1)}, bf16[1,96,1536]{2,1,0:T(8,128)(2,1)S(1)}, u32[]{:S(2)}, u32[]{:S(2)}) collective-permute-start(bf16[1,96,1536]{2,1,0:T(8,128)(2,1)S(1)} %add_convert_fusion.4), channel_id=1, source_target_pairs={{0,4},{1,5},{2,6},{3,7},{4,0},{5,1},{6,2},{7,3},{8,12},{9,13},{10,... | collective-permute-start | bytes 884744 | tf_op jit(solution)/shard_map/ppermute | solution.py:28
  218.6 14.3 %collective-permute-start.68 = (bf16[8,24,768]{2,1,0:T(8,128)(2,1)S(1)}, bf16[8,24,768]{2,1,0:T(8,128)(2,1)S(1)}, u32[]{:S(2)}, u32[]{:S(2)}) collective-permute-start(bf16[8,24,768]{2,1,0:T(8,128)(2,1)S(1)} %slice_bitcast_fusion.14), channel_id=1, source_target_pairs={{0,16},{8,24},{16,0},{24,8},{1,17},{9,25},{17,1},{25,9},{2,18},{10... | collective-permute-start | bytes 884744 | tf_op jit(solution)/shard_map/ppermute | solution.py:28
  220.5 8.4 %collective-permute-start.66 = (bf16[4,48,768]{2,1,0:T(8,128)(2,1)S(1)}, bf16[4,48,768]{2,1,0:T(8,128)(2,1)S(1)}, u32[]{:S(2)}, u32[]{:S(2)}) collective-permute-start(bf16[4,48,768]{2,1,0:T(8,128)(2,1)S(1)} %slice_bitcast_fusion.13), channel_id=1, source_target_pairs={{0,1},{1,0},{2,3},{3,2},{4,5},{5,4},{6,7},{7,6},{8,9},{9,8},{10,11... | collective-permute-start | bytes 884744 | tf_op jit(solution)/shard_map/ppermute | solution.py:28
  225.0 21.2 %collective-permute-start.70 = (bf16[1,192,384]{2,1,0:T(8,128)(2,1)S(1)}, bf16[1,192,384]{2,1,0:T(8,128)(2,1)S(1)}, u32[]{:S(2)}, u32[]{:S(2)}) collective-permute-start(bf16[1,192,384]{2,1,0:T(8,128)(2,1)S(1)} %add_convert_fusion.10), channel_id=1, source_target_pairs={{0,4},{1,5},{2,6},{3,7},{4,0},{5,1},{6,2},{7,3},{8,12},{9,13},{10,... | collective-permute-start | bytes 442376 | tf_op jit(solution)/shard_map/ppermute | solution.py:28
  227.1 16.8 %collective-permute-start.64 = (bf16[4,48,896]{2,1,0:T(8,128)(2,1)S(1)}, bf16[4,48,896]{2,1,0:T(8,128)(2,1)S(1)}, u32[]{:S(2)}, u32[]{:S(2)}) collective-permute-start(bf16[4,48,896]{2,1,0:T(8,128)(2,1)S(1)} %get-tuple-element.397), channel_id=1, source_target_pairs={{0,1},{1,0},{2,3},{3,2},{4,5},{5,4},{6,7},{7,6},{8,9},{9,8},{10,11... | collective-permute-start | bytes 1032200 | tf_op jit(solution)/shard_map/ppermute | solution.py:28
  228.9 12.7 %collective-permute-start.67 = (bf16[2,48,768]{2,1,0:T(8,128)(2,1)S(1)}, bf16[2,48,768]{2,1,0:T(8,128)(2,1)S(1)}, u32[]{:S(2)}, u32[]{:S(2)}) collective-permute-start(bf16[2,48,768]{2,1,0:T(8,128)(2,1)S(1)} %get-tuple-element.399), channel_id=1, source_target_pairs={{0,2},{1,3},{2,0},{3,1},{4,6},{5,7},{6,4},{7,5},{8,10},{9,11},{10,... | collective-permute-start | bytes 442376 | tf_op jit(solution)/shard_map/ppermute | solution.py:28
  233.0 13.0 %collective-permute-start.71 = (bf16[4,24,768]{2,1,0:T(8,128)(2,1)S(1)}, bf16[4,24,768]{2,1,0:T(8,128)(2,1)S(1)}, u32[]{:S(2)}, u32[]{:S(2)}) collective-permute-start(bf16[4,24,768]{2,1,0:T(8,128)(2,1)S(1)} %get-tuple-element.401), channel_id=1, source_target_pairs={{0,1},{1,0},{2,3},{3,2},{4,5},{5,4},{6,7},{7,6},{8,9},{9,8},{10,11... | collective-permute-start | bytes 442376 | tf_op jit(solution)/shard_map/ppermute | solution.py:28
  241.7 12.5 %collective-permute-start.74 = (bf16[1,48,768]{2,1,0:T(8,128)(2,1)S(1)}, bf16[1,48,768]{2,1,0:T(8,128)(2,1)S(1)}, u32[]{:S(2)}, u32[]{:S(2)}) collective-permute-start(bf16[1,48,768]{2,1,0:T(8,128)(2,1)S(1)} %add_convert_fusion.19), channel_id=1, source_target_pairs={{0,4},{1,5},{2,6},{3,7},{4,0},{5,1},{6,2},{7,3},{8,12},{9,13},{10,... | collective-permute-start | bytes 221192 | tf_op jit(solution)/shard_map/ppermute | solution.py:28
  242.8 12.5 %collective-permute-start.73 = (bf16[96,1536]{1,0:T(8,128)(2,1)S(1)}, bf16[96,1536]{1,0:T(8,128)(2,1)S(1)}, u32[]{:S(2)}, u32[]{:S(2)}) collective-permute-start(bf16[96,1536]{1,0:T(8,128)(2,1)S(1)} %fusion.18), channel_id=1, source_target_pairs={{0,16},{8,24},{16,0},{24,8},{1,17},{9,25},{17,1},{25,9},{2,18},{10... | collective-permute-start | bytes 884744 | tf_op jit(solution)/shard_map/ppermute | solution.py:28
  246.3 13.6 %collective-permute-start.77 = (bf16[192,384]{1,0:T(8,128)(2,1)S(1)}, bf16[192,384]{1,0:T(8,128)(2,1)S(1)}, u32[]{:S(2)}, u32[]{:S(2)}) collective-permute-start(bf16[192,384]{1,0:T(8,128)(2,1)S(1)} %fusion.28), channel_id=1, source_target_pairs={{0,16},{8,24},{16,0},{24,8},{1,17},{9,25},{17,1},{25,9},{2,18},{10... | collective-permute-start | bytes 442376 | tf_op jit(solution)/shard_map/ppermute | solution.py:28
  255.4 11.6 %collective-permute-start.84 = (bf16[96,1536]{1,0:T(8,128)(2,1)S(1)}, bf16[96,1536]{1,0:T(8,128)(2,1)S(1)}, u32[]{:S(2)}, u32[]{:S(2)}) collective-permute-start(bf16[96,1536]{1,0:T(8,128)(2,1)S(1)} %add_convert_fusion), channel_id=1, source_target_pairs={{0,8},{8,0},{16,24},{24,16},{1,9},{9,1},{17,25},{25,17},{2,10},{10... | collective-permute-start | bytes 884744 | tf_op jit(solution)/shard_map/ppermute | solution.py:28
  (61 other events, 317.2 us)

commit v5 on v4

--- a/solution.py
+++ b/solution.py
@@ -163,7 +163,35 @@
 
 
 COSTS = {"assemble": 1.5, "project": 10.8, "mix_segments": 1.1, "intra_forward": 5.9, "inter_forward": 16.5, "expand": 0.285, "contract": 6.0, "turn": 22.5, "back_to_heads": 11.8, "intra_backward": 10.3, "inter_backward": 4.6, "input_grad": 4.0, "vector_rows": 1.5, "down": 6.0, "up": 1.2, "outq": 3.36, "kv": 3.36}
-TAIL = ('kv0+kv1', 'up', 'grad', 'down', 'outq', 'kv1', 'kv0', 'kv1', 'up', 'outq', 'kv0', 'down', 'outq', 'kv0', 'kv1', 'up', 'outq', 'kv1', 'kv0', 'down', 'outq', 'close', 'kv0', 'kv1', 'outq', 'close', 'kv0', 'kv1')
+TAIL = (
+    "kv0+kv1",
+    "grad",
+    "outq",
+    "down",
+    "kv1",
+    "up",
+    "kv0",
+    "outq",
+    "kv1",
+    "down",
+    "kv0",
+    "up",
+    "outq",
+    "kv1",
+    "kv0",
+    "up",
+    "down",
+    "outq",
+    "kv1",
+    "kv0",
+    "outq",
+    "kv1",
+    "down",
+    "kv0",
+    "outq",
+    "kv1",
+    "kv0",
+)
 FLOPS_PER_US = 6.0e8
 
 
@@ -877,20 +905,10 @@
         keep, send = add_low(keep[:half], received[:half]), add_low(keep[half:], received[half:])
 
 
-def reduce_stages(x, core, large=False):
+def reduce_stages(x, core):
     half = x.shape[1] // 2
     bits = axis_bits("fsdp")
     keep, send = x[0, :half], x[0, half:]
-    if large and half >= 4:
-        axis, bit = bits.pop(0)
-        middle, first = half // 2, half // 4
-        (received,) = yield [(send[first:], axis, bit)]
-        after = add_low(keep[middle:], received[middle - first :])
-        beside = add_low(keep[first:middle], received[: middle - first])
-        rest, after = lax.optimization_barrier((send[:first], after))
-        (received,) = yield [(rest, axis, bit)]
-        keep = jnp.concatenate([add_low(keep[:first], received), beside], axis=0)
-        send, keep = lax.optimization_barrier((after, keep))
     x = yield from halving_stages(keep, send, bits)
     for axis, bit in axis_bits("group")[1:]:
         (received,) = yield [(x, axis, bit)]
@@ -899,13 +917,44 @@
     return ordered(x, other, core == 0, -1).astype(f32)
 
 
-def share_stages(x, core, chip):
+def share_stages(x, core, chip, twice=False):
     axis, bit = axis_bits("group")[1]
     half = x.shape[1] // 2
-    (received,) = yield [(x[1], axis, bit)]
-    keep, send = add_low(x[0, :half], received[:half]), add_low(x[0, half:], received[half:])
+    if twice:
+        (received,) = yield [(x[1, half:], axis, bit)]
+        rest, send = lax.optimization_barrier((x[1, :half], add_low(x[0, half:], received)))
+        (received,) = yield [(rest, axis, bit)]
+        send, keep = lax.optimization_barrier((send, add_low(x[0, :half], received)))
+    else:
+        (received,) = yield [(x[1], axis, bit)]
+        keep, send = add_low(x[0, :half], received[:half]), add_low(x[0, half:], received[half:])
     x = yield from halving_stages(keep, send, axis_bits("fsdp"))
     (other,) = yield [(x, axis, bit)]
+    x = ordered(x, other, chip == 0, 0)
+    other = yield from core_stage(x)
+    return ordered(x, other, core == 0, -1).astype(f32)
+
+
+def large_stages(x, core, chip):
+    (axis, bit), *bits = axis_bits("fsdp")
+    group_axis, group_bit = axis_bits("group")[1]
+    half = x.shape[1] // 2
+    first = half // 4
+    keep, send = x[:, :half], x[:, half:]
+    (received,) = yield [(send[:, first:], axis, bit)]
+    later = add_low(keep[:, first:], received)
+    rest, later = lax.optimization_barrier((send[:, :first], later))
+    (received,) = yield [(rest, axis, bit)]
+    head = add_low(keep[:, :first], received)
+    theirs = jnp.concatenate([head[1], later[1]], axis=0)
+    (received,) = yield [(theirs, group_axis, group_bit)]
+    head, later = head[0], later[0]
+    quarter = half // 2
+    ours = jnp.concatenate([head, later[: quarter - first]], axis=0)
+    keep = add_low(ours, received[:quarter])
+    send = add_low(later[quarter - first :], received[quarter:])
+    x = yield from halving_stages(keep, send, bits)
+    (other,) = yield [(x, group_axis, group_bit)]
     x = ordered(x, other, chip == 0, 0)
     other = yield from core_stage(x)
     return ordered(x, other, core == 0, -1).astype(f32)
@@ -1072,8 +1121,8 @@
     grads.slot(d_lower_other, only=("d_upper",))
     two = chips == 2
 
-    def reduction(part):
-        return share_stages(part, core, chip) if two else reduce_stages(part, core)
+    def reduction(part, twice=False):
+        return share_stages(part, core, chip, twice) if two else reduce_stages(part, core)
 
     split = 2 if two else 1
     (down_part,) = weight_grad(
@@ -1081,12 +1130,13 @@
         "down",
     )
     d_upper_other = grads.read("d_upper", down_part)
-    grads.add("down", reduction(down_part))
+    grads.add("down", reduction(down_part, True))
     grads.slot(d_upper_other, only=("down",))
     (up_part,) = weight_grad(
-        ids, [(low1, low1_other, tie(d_upper, *grads.started), d_upper_other)], fsdp, [1], "up",
-    )
-    grads.add("up", reduce_stages(up_part, core, True))
+        ids, [(low1, low1_other, tie(d_upper, *grads.started), d_upper_other)], fsdp, [split], "up",
+    )
+    large = two and fsdp >= 8
+    grads.add("up", large_stages(up_part, core, chip) if large else reduction(up_part))
     grads.slot(only=("up",))
     d_res1, d_mixed, d_mixed_half, d_num, d_den, sums, *back = back_to_heads(
         ids, tie(d_upper, *grads.started), d_res2, hat1, inv1, rden, att, q, cos, sin, w_qo,
@@ -1094,7 +1144,9 @@
     )
     grads.add("state", trade_stages(back))
     grads.slot(only=("state",))
-    grads.slot(d_num, only=("state",))
+    if two:
+        grads.slot(d_num, only=("down",))
+    grads.slot(*grads.started, d_num, only=("state",))
     grads.add("d_mixed", core_stage(d_mixed_half))
     grads.slot(*grads.started, only=("d_mixed",))
     grads.slot(*grads.started, only=("up",))
@@ -1104,14 +1156,13 @@
     mixed = mix_segments(from_descendants, far, near)
     grads.add("path", trade_stages(mixed))
     grads.slot(only=("path",))
+    grads.slot(*grads.started, only=("up",))
     d_q, d_q_half, d_k, d_v = intra_backward(
         ids, tie(q, *grads.started), k, v, d_num, d_den, cos, sin, wave, wave_t, *path
     )
     grads.add("d_q", core_stage(d_q_half))
-    grads.arrive(d_q, only=("up",))
-    grads.slot(*grads.started, only=("path", "d_q"))
-    grads.slot(*grads.started, only=("up",))
-    grads.arrive(*grads.started, only=("down",))
+    grads.slot(d_q, only=("path", "d_q"))
+    grads.arrive(*grads.started, only=("up", "down"))
     d_q_other = grads.read("d_q", *grads.started)
     (outq_part,) = weight_grad(
         ids,
@@ -1123,12 +1174,14 @@
     )
     grads.add("outq", reduction(outq_part))
     grads.slot(only=("outq",))
+    grads.slot(*grads.started, only=("up",))
     back = grads.finish("path", *grads.started, only=("path",))
     d_kv = inter_backward(ids, k, v, d_k, d_v, cos, sin, *back)
     grads.add("d_kv", core_stage(d_kv[1]))
-    grads.slot(only=("d_kv",))
+    grads.arrive(d_kv, only=("up",))
+    grads.slot(*grads.started, only=("d_kv",))
+    grads.slot(*grads.started, only=("up",))
     grads.slot(*grads.started, only=("down",))
-    grads.arrive(*grads.started, only=("up",))
     d_kv_other = grads.read("d_kv", *grads.started)
     kv_parts = weight_grad(
         ids, [(tokens, tokens_other, d_kv[0], d_kv_other)], fsdp, [2, 1] if two else [1], "kv",
@@ -1147,18 +1200,28 @@
         out_grad = jnp.concatenate([ours[:, :half], others[:, :half]], axis=1)
         return q_grad, out_grad, sums.T, sums[:, B_UP : B_UP + ff // D].T.reshape(-1)
 
+    written = set()
+
+    def write():
+        nonlocal closed
+        if not closed and "outq" in grads.finished:
+            closed = close(grads.finished["outq"])
+            grads.started += closed
+        for n in ("up", "down"):
+            if n in grads.finished and n not in written:
+                written.add(n)
+                grads.started += (grads.finished[n],)
+
     for step in TAIL:
         if step == "grad":
             tokens_grad = input_grad(ids, d_q, tie(d_kv, *grads.started), d_res1, w_qo, w_kv)
             grads.started = (tokens_grad,)
-        elif step == "close":
-            if not closed and "outq" in grads.finished:
-                closed = close(grads.finished["outq"])
-                grads.started += closed
         elif grads.names(step.split("+")):
             grads.slot(*grads.started, only=step.split("+"))
+            write()
     while grads.running:
         grads.slot(*grads.started)
+        write()
     done = grads.finished
     q_grad, out_grad, sums, b_up_grad = closed or close(done["outq"])
     kv_grad = jnp.concatenate([done[n] for n in ("kv0", "kv1") if n in done], axis=0)

time: 270 us -> 269 us (level)
  starting transfers between devices: 84.9 us -> 91.6 us
  waiting for transfers between devices: 72.2 us -> 65.9 us
  other arithmetic: 17.6 us -> 14.9 us
    ppermute x86 -> x88, starting transfers between devices: 84.9 us -> 91.6 us  [exchange(): return lax.ppermute(x, axis, [(i, i ^ offset) for i in range(size)])]
    ppermute x86 -> x88, waiting for transfers between devices: 72.2 us -> 65.9 us  [exchange(): return lax.ppermute(x, axis, [(i, i ^ offset) for i in range(size)])]
  transfers between devices with their start and end apart: 86 -> 88, of which waited for: 40 -> 35; matrix products, arithmetic and copies ran while one was open for 9% -> 8% of each run, Pallas kernels for 28% -> 29%
where the time goes in v5:
time: 269 us; the launch traced here: 268 us
  starting transfers between devices  91.6 us (34%)
  Pallas kernels  79.2 us (29%)
  waiting for transfers between devices  65.9 us (24%)
  other arithmetic  14.9 us (6%)
  local copies, waits for them, and re-layouts  11.1 us (4%)
  matrix products  3.7 us (1%)
    ppermute x88, starting transfers between devices, exchange(): return lax.ppermute(x, axis, [(i, i ^ offset) for i in range(size)])  91.6 us
    ppermute x88, waiting for transfers between devices, exchange(): return lax.ppermute(x, axis, [(i, i ^ offset) for i in range(size)])  65.9 us
    pallas_call x4, Pallas kernels, weight_grad(): call(kernel, 'weight_grad', tuple((shape_of((n, fsdp, share // n, width),...  14 us
    pallas_call x1, Pallas kernels, back_to_heads(): call(kernel, 'back_to_heads', (shape_of((rows, D), f32), shape_of((rows,...  9.94 us
    pallas_call x1, Pallas kernels, intra_backward(): call(kernel, 'intra_backward', (shape_of((rows, D), bf16), shape_of((rows...  8.77 us
    pallas_call x1, Pallas kernels, expand(): call(kernel, 'expand', (shape_of((rows, D), f32), shape_of((rows, LANES),...  7.46 us
    pallas_call x1, Pallas kernels, intra_forward(): call(kernel, 'intra_forward', (shape_of((rows, D), bf16), wide, wide), [V...  5.87 us
  transfers between devices with their start and end apart: 88, of which 35 were waited for; matrix products, arithmetic and copies ran while one was open for 8% of the time, Pallas kernels for 29%

profile of v5, /device:TPU:0, one launch (start us, length us, event | category | flops | bytes accessed | tf_op | source)
XLA Modules:
  0.0 268.3 jit_solution(3871328352813154291)
XLA Ops:
  1.5 4.0 %collective-permute-start = (bf16[1,24,1536]{2,1,0:T(8,128)(2,1)S(1)}, bf16[1,24,1536]{2,1,0:T(8,128)(2,1)S(1)}, u32[]{:S(2)}, u32[]{:S(2)}) collective-permute-start(bf16[1,24,1536]{2,1,0:T(8,128)(2,1)S(1)} %slice_bitcast_fusion.15), channel_id=1, source_target_pairs={{0,4},{1,5},{2,6},{3,7},{4,0},{5,1},{6,2},{7,3},{8,12},{9,13},{10,... | collective-permute-start | bytes 221192 | tf_op jit(solution)/shard_map/ppermute | solution.py:28
  12.4 1.8 fusion.22
  15.2 1.6 collective-permute-start.4
  19.3 2.3 collective-permute-start.2
  22.0 1.6 collective-permute-start.6
  27.4 3.0 %collective-permute-start.11 = (bf16[1,24,3072]{2,1,0:T(8,128)(2,1)}, bf16[1,24,3072]{2,1,0:T(8,128)(2,1)S(1)}, u32[]{:S(2)}, u32[]{:S(2)}) collective-permute-start(bf16[1,24,3072]{2,1,0:T(8,128)(2,1)} %bitcast.15), channel_id=1, source_target_pairs={{0,4},{1,5},{2,6},{3,7},{4,0},{5,1},{6,2},{7,3},{8,12},{9,13},{10,... | collective-permute-start | bytes 442376 | tf_op jit(solution)/shard_map/ppermute | solution.py:28
  32.7 2.6 collective-permute-done.11
  38.4 5.1 %project.1 = (bf16[512,768]{1,0:T(8,128)(2,1)S(1)}, bf16[512,768]{1,0:T(8,128)(2,1)S(1)}, bf16[2,2,104,128]{3,2,1,0:T(8,128)(2,1)S(1)}, bf16[2,2,104,128]{3,2,1,...) custom-call(s32[3]{0:T(128)S(1)} %pad_add_fusion.ids_ref, ...), custom_call_target="tpu_custom_call" | custom-call | flops 6480000000 | tf_op jit(solution)/shard_map/project/pallas_call | solution.py:381
  46.0 3.1 %collective-permute-start.17 = (bf16[2,2,104,128]{3,2,1,0:T(8,128)(2,1)S(1)}, bf16[2,2,104,128]{3,2,1,0:T(8,128)(2,1)S(1)}, u32[]{:S(2)}, u32[]{:S(2)}) collective-permute-start(bf16[2,2,104,128]{3,2,1,0:T(8,128)(2,1)S(1)} %get-tuple-element.259), channel_id=1, source_target_pairs={{0,4},{1,5},{2,6},{3,7},{4,0},{5,1},{6,2},{7,3},{8,12},{9,13},{10,... | collective-permute-start | bytes 319496 | tf_op jit(solution)/shard_map/ppermute | solution.py:28
  50.4 4.5 %collective-permute-done.16.refs_1_ = bf16[2,2,104,128]{3,2,1,0:T(8,128)(2,1)S(1)} collective-permute-done((bf16[2,2,104,128]{3,2,1,0:T(8,128)(2,1)S(1)}, bf16[2,2,104,128]{3,2,1,0:T(8,128)(2,1)S(1)}, u32[]{:S(2)}, u32[]{:S(2)}) %collective-permute-start.16) | collective-permute-done | bytes 106528 | tf_op jit(solution)/shard_map/ppermute | solution.py:28
  58.3 3.3 %collective-permute-done.21 = bf16[2,24,3072]{2,1,0:T(8,128)(2,1)S(1)} collective-permute-done((bf16[2,24,3072]{2,1,0:T(8,128)(2,1)S(1)}, bf16[2,24,3072]{2,1,0:T(8,128)(2,1)S(1)}, u32[]{:S(2)}, u32[]{:S(2)}) %collective-permute-start.21) | collective-permute-done | bytes 294944 | tf_op jit(solution)/shard_map/ppermute | solution.py:28
  65.9 5.9 %intra_forward.1 = (bf16[512,768]{1,0:T(8,128)(2,1)S(1)}, f32[512,768]{1,0:T(8,128)S(1)}, f32[512,768]{1,0:T(8,128)S(1)}) custom-call(bf16[512,768]{1,0:T(8,128)(2,1)S(1)} %copy-done.8, bf16[768,1792]{1,0:T(8,128)(2,1)S(1)} %bitcast.103, bf16[512,768]{1,0:T(8,128)(2,1)S(1)} %get-tuple-element.250.k_ref, bf16[512,768]{1,0:T(8,128)(2,1)S(1)} %get-tuple-element.267.v_ref, ...), custom_call_target="tpu_custom_call" | custom-call | flops 3540000000 | tf_op jit(solution)/shard_map/intra_forward/pallas_call | solution.py:439
  77.3 2.3 collective-permute-start.28
  79.8 1.8 collective-permute-done.26.refs_1_
  81.6 3.1 %collective-permute-done.27.refs_2_ = bf16[2,2,104,128]{3,2,1,0:T(8,128)(2,1)S(1)} collective-permute-done((bf16[2,2,104,128]{3,2,1,0:T(8,128)(2,1)S(1)}, bf16[2,2,104,128]{3,2,1,0:T(8,128)(2,1)S(1)}, u32[]{:S(2)}, u32[]{:S(2)}) %collective-permute-start.27) | collective-permute-done | bytes 106528 | tf_op jit(solution)/shard_map/ppermute | solution.py:28
  86.6 1.8 collective-permute-start.29
  91.8 3.5 %collective-permute-done.30.refs_4_ = bf16[4,2,104,128]{3,2,1,0:T(8,128)(2,1)S(1)} collective-permute-done((bf16[4,2,104,128]{3,2,1,0:T(8,128)(2,1)S(1)}, bf16[4,2,104,128]{3,2,1,0:T(8,128)(2,1)S(1)}, u32[]{:S(2)}, u32[]{:S(2)}) %collective-permute-start.30) | collective-permute-done | bytes 213024 | tf_op jit(solution)/shard_map/ppermute | solution.py:28
  97.8 4.0 %inter_forward.1 = (bf16[512,768]{1,0:T(8,128)(2,1)S(1)}, f32[512,768]{1,0:T(8,128)S(1)}) custom-call(s32[3]{0:T(128)S(1)} %pad_add_fusion.ids_ref, bf16[512,768]{1,0:T(8,128)(2,1)S(1)} %get-tuple-element.377.q_ref, f32[512,768]{1,0:T(8,128)S(1)} %get-tuple-element.306.num_ref, f32[512,768]{1,0:T(8,128)S(1)} %get-tuple-element.307.den_ref, ...), custom_call_target="tpu_custom_call" | custom-call | flops 9900000256 | tf_op jit(solution)/shard_map/inter_forward/pallas_call | solution.py:480
  101.9 2.1 collective-permute-done.36
  106.0 1.7 collective-permute-start.39
  107.7 7.5 %expand.1 = (f32[512,768]{1,0:T(8,128)S(1)}, f32[512,128]{1,0:T(8,128)S(1)}, bf16[512,768]{1,0:T(8,128)(2,1)S(1)}, bf16[512,3072]{1,0:T(8,128)(2,1)S(1)}, bf16[512,3072]{1,0:T(8,128)(2,1)S(1)}) custom-call(bf16[512,768]{1,0:T(8,128)(2,1)S(1)} %get-tuple-element.314.att_ref.refs_0_, bf16[512,768]{1,0:T(8,128)(2,1)S(1)} %copy-done.8, ...), custom_call_target="tpu_custom_call" | custom-call | flops 171000000 | tf_op jit(solution)/shard_map/expand/pallas_call | solution.py:535
  115.1 4.1 %collective-permute-done.38 = bf16[8,96,384]{2,1,0:T(8,128)(2,1)S(1)} collective-permute-done((bf16[8,96,384]{2,1,0:T(8,128)(2,1)S(1)}, bf16[8,96,384]{2,1,0:T(8,128)(2,1)S(1)}, u32[]{:S(2)}, u32[]{:S(2)}) %collective-permute-start.38) | collective-permute-done | bytes 589856 | tf_op jit(solution)/shard_map/ppermute | solution.py:28
  120.4 2.3 collective-permute-done.40.refs_1_
  122.8 1.7 collective-permute-done.41.refs_3_
  126.3 5.3 %contract.1 = (bf16[512,768]{1,0:T(8,128)(2,1)}, f32[512,768]{1,0:T(8,128)S(1)}, bf16[512,768]{1,0:T(8,128)(2,1)S(1)}, bf16[512,384]{1,0:T(8,128)(2,1)S(1)}, f32[16,768]{1,0:T(8,128)S(1)}) custom-call(s32[3]{0:T(128)S(1)} %pad_add_fusion.ids_ref, bf16[512,3072]{1,0:T(8,128)(2,1)S(1)} %get-tuple-element.329.gelu_ref.refs_0_, ...), custom_call_target="tpu_custom_call" | custom-call | flops 3600000000 | tf_op jit(solution)/shard_map/contract/pallas_call | solution.py:579
  132.7 5.0 %turn.1 = (bf16[512,3072]{1,0:T(8,128)(2,1)S(1)}, bf16[512,1536]{1,0:T(8,128)(2,1)S(1)}, f32[16,768]{1,0:T(8,128)S(1)}) custom-call(s32[3]{0:T(128)S(1)} %pad_add_fusion.ids_ref, bf16[512,768]{1,0:T(8,128)(2,1)S(1)} %get-tuple-element.339.dlow_ref.refs_2_, bf16[512,3072]{1,0:T(8,128)(2,1)S(1)} %get-tuple-element.333.slope_ref, ...), custom_call_target="tpu_custom_call" | custom-call | flops 13500000256 | tf_op jit(solution)/shard_map/turn/pallas_call | solution.py:620
  138.2 5.7 %weight_grad.4 = bf16[2,8,192,384]{3,2,1,0:T(8,128)(2,1)S(1)} custom-call(s32[3]{0:T(128)S(1)} %pad_add_fusion.ids_ref, bf16[512,3072]{1,0:T(8,128)(2,1)S(1)} %get-tuple-element.329.gelu_ref.refs_0_, bf16[512,3072]{1,0:T(8,128)(2,1)S(1)} %collective-permute-done.43.refs_1_, bf16[512,768]{1,0:T(8,128)(2,1)S(1)} %get-tuple-element.339.dlow_ref.refs_2_, ...), custom_call_target="tpu_custom_call" | custom-call | flops 3600000000 | tf_op jit(solution)/shard_map/weight_grad/pallas_call | solution.py:881
  145.5 3.2 %weight_grad.5 = bf16[2,8,48,1536]{3,2,1,0:T(8,128)(2,1)S(1)} custom-call(s32[3]{0:T(128)S(1)} %pad_add_fusion.ids_ref, bf16[512,768]{1,0:T(8,128)(2,1)S(1)} %get-tuple-element.325.refs_0_, bf16[512,768]{1,0:T(8,128)(2,1)S(1)} %collective-permute-done.42.refs_1_, bf16[512,3072]{1,0:T(8,128)(2,1)S(1)} %get-tuple-element.343.refs_2_.dup_ref, ...), custom_call_target="tpu_custom_call" | custom-call | flops 720000000 | tf_op jit(solution)/shard_map/weight_grad/pallas_call | solution.py:881
  149.5 9.9 %back_to_heads.1 = (f32[512,768]{1,0:T(8,128)S(1)}, bf16[512,768]{1,0:T(8,128)(2,1)S(1)}, bf16[512,384]{1,0:T(8,128)(2,1)S(1)}, bf16[512,768]{1,0:T(8,128)(2,1)S...) custom-call(s32[3]{0:T(128)S(1)} %pad_add_fusion.ids_ref, ...), custom_call_target="tpu_custom_call" | custom-call | flops 7080000000 | tf_op jit(solution)/shard_map/back_to_heads/pallas_call | solution.py:684
  161.8 2.2 collective-permute-start.49
  165.6 5.7 %collective-permute-done.48.refs_2_ = bf16[2,2,104,128]{3,2,1,0:T(8,128)(2,1)S(1)} collective-permute-done((bf16[2,2,104,128]{3,2,1,0:T(8,128)(2,1)S(1)}, bf16[2,2,104,128]{3,2,1,0:T(8,128)(2,1)S(1)}, u32[]{:S(2)}, u32[]{:S(2)}) %collective-permute-start.48) | collective-permute-done | bytes 106528 | tf_op jit(solution)/shard_map/ppermute | solution.py:28
  173.9 4.2 %collective-permute-done.54 = bf16[4,192,384]{2,1,0:T(8,128)(2,1)S(1)} collective-permute-done((bf16[4,192,384]{2,1,0:T(8,128)(2,1)S(1)}, bf16[4,192,384]{2,1,0:T(8,128)(2,1)S(1)}, u32[]{:S(2)}, u32[]{:S(2)}) %collective-permute-start.54) | collective-permute-done | bytes 589856 | tf_op jit(solution)/shard_map/ppermute | solution.py:28
  178.5 3.0 %collective-permute-start.55 = (bf16[2,2,104,128]{3,2,1,0:T(8,128)(2,1)S(1)}, bf16[2,2,104,128]{3,2,1,0:T(8,128)(2,1)S(1)}, u32[]{:S(2)}, u32[]{:S(2)}) collective-permute-start(bf16[2,2,104,128]{3,2,1,0:T(8,128)(2,1)S(1)} %get-tuple-element.371), channel_id=1, source_target_pairs={{0,2},{1,3},{2,0},{3,1},{4,6},{5,7},{6,4},{7,5},{8,10},{9,11},{10,... | collective-permute-start | bytes 319496 | tf_op jit(solution)/shard_map/ppermute | solution.py:28
  181.6 2.4 collective-permute-start.57
  184.2 1.8 collective-permute-start.60
  186.2 8.8 %intra_backward.1 = (bf16[512,768]{1,0:T(8,128)(2,1)S(1)}, bf16[512,384]{1,0:T(8,128)(2,1)S(1)}, f32[512,768]{1,0:T(8,128)S(1)}, f32[512,768]{1,0:T(8,128)S(1)}) custom-call(s32[3]{0:T(128)S(1)} %pad_add_fusion.ids_ref, bf16[512,768]{1,0:T(8,128)(2,1)S(1)} %get-tuple-element.377.q_ref, bf16[512,768]{1,0:T(8,128)(2,1)S(1)} %get-tuple-element.250.k_ref, ...), custom_call_target="tpu_custom_call" | custom-call | flops 6179999744 | tf_op jit(solution)/shard_map/intra_backward/pallas_call | solution.py:753
  195.1 1.8 collective-permute-start.58
  198.4 2.4 collective-permute-done.59
  203.0 2.4 weight_grad.6
  206.5 2.1 collective-permute-start.62
  208.5 4.1 %inter_backward.1.dkv_ref = bf16[2,512,768]{2,1,0:T(8,128)(2,1)S(1)} custom-call(s32[3]{0:T(128)S(1)} %pad_add_fusion.ids_ref, bf16[512,768]{1,0:T(8,128)(2,1)S(1)} %get-tuple-element.250.k_ref, bf16[512,768]{1,0:T(8,128)(2,1)S(1)} %get-tuple-element.267.v_ref, f32[512,768]{1,0:T(8,128)S(1)} %get-tuple-element.380.dk_ref, ...), custom_call_target="tpu_custom_call" | custom-call | flops 2760000000 | tf_op jit(solution)/shard_map/inter_backward/pallas_call | solution.py:801
  221.0 2.7 %weight_grad.7 = (bf16[2,8,24,768]{3,2,1,0:T(8,128)(2,1)S(1)}, bf16[1,8,48,768]{3,2,1,0:T(8,128)(2,1)S(1)}) custom-call(s32[3]{0:T(128)S(1)} %pad_add_fusion.ids_ref, bf16[512,768]{1,0:T(8,128)(2,1)S(1)} %copy-done.8, bf16[512,768]{1,0:T(8,128)(2,1)S(1)} %copy-done.17, bf16[512,768]{1,0:T(8,128)(2,1)S(1)} %copy-done.9, ...), custom_call_target="tpu_custom_call" | custom-call | flops 2016000000 | tf_op jit(solution)/shard_map/weight_grad/pallas_call | solution.py:881
  225.9 4.2 %input_grad.1 = f32[512,768]{1,0:T(8,128)} custom-call(s32[3]{0:T(128)S(1)} %pad_add_fusion.ids_ref, bf16[512,768]{1,0:T(8,128)(2,1)S(1)} %copy-done.11, bf16[2,512,768]{2,1,0:T(8,128)(2,1)S(1)} %copy-done.3, f32[512,768]{1,0:T(8,128)S(1)} %copy-done.5, bf16[768,1792]{1,0:T(8,128)(2,1)S(1)} %bitcast.107, bf16[768,1536]{1,0:T(8,128)(2,1)S(1)} %bitcast.111), custom_call_target="tpu_custom_call" | custom-call | flops 2400000000 | tf_op jit(solution)/shard_map/input_grad/pallas_call | solution.py:825
  230.1 3.5 %collective-permute-done.64 = bf16[8,48,896]{2,1,0:T(8,128)(2,1)S(1)} collective-permute-done((bf16[8,48,896]{2,1,0:T(8,128)(2,1)}, bf16[8,48,896]{2,1,0:T(8,128)(2,1)S(1)}, u32[]{:S(2)}, u32[]{:S(2)}) %collective-permute-start.64) | collective-permute-done | bytes 688160 | tf_op jit(solution)/shard_map/ppermute | solution.py:28
  241.3 2.9 %collective-permute-done.65 = bf16[4,48,896]{2,1,0:T(8,128)(2,1)S(1)} collective-permute-done((bf16[4,48,896]{2,1,0:T(8,128)(2,1)S(1)}, bf16[4,48,896]{2,1,0:T(8,128)(2,1)S(1)}, u32[]{:S(2)}, u32[]{:S(2)}) %collective-permute-start.65) | collective-permute-done | bytes 344096 | tf_op jit(solution)/shard_map/ppermute | solution.py:28
  249.4 1.9 collective-permute-done.70
  253.3 2.6 collective-permute-start.81
  260.5 2.2 collective-permute-done.80
  (331 shorter events, 102.1 us)
Async XLA Ops:
  1.5 7.9 %collective-permute-start = (bf16[1,24,1536]{2,1,0:T(8,128)(2,1)S(1)}, bf16[1,24,1536]{2,1,0:T(8,128)(2,1)S(1)}, u32[]{:S(2)}, u32[]{:S(2)}) collective-permute-start(bf16[1,24,1536]{2,1,0:T(8,128)(2,1)S(1)} %slice_bitcast_fusion.15), channel_id=1, source_target_pairs={{0,4},{1,5},{2,6},{3,7},{4,0},{5,1},{6,2},{7,3},{8,12},{9,13},{10,... | collective-permute-start | bytes 221192 | tf_op jit(solution)/shard_map/ppermute | solution.py:28
  5.6 31.2 %collective-permute-start.10 = (bf16[512,768]{1,0:T(8,128)(2,1)}, bf16[512,768]{1,0:T(8,128)(2,1)S(1)}, u32[]{:S(2)}, u32[]{:S(2)}) collective-permute-start(bf16[512,768]{1,0:T(8,128)(2,1)} %refs_0_.1), channel_id=1, source_target_pairs={{0,8},{8,0},{16,24},{24,16},{1,9},{9,1},{17,25},{25,17},{2,10},{10... | collective-permute-start | bytes 2359304 | tf_op jit(solution)/shard_map/ppermute | solution.py:28
  22.0 8.8 %collective-permute-start.6 = (bf16[8,24,768]{2,1,0:T(8,128)(2,1)S(1)}, bf16[8,24,768]{2,1,0:T(8,128)(2,1)S(1)}, u32[]{:S(2)}, u32[]{:S(2)}) collective-permute-start(bf16[8,24,768]{2,1,0:T(8,128)(2,1)S(1)} %pad_maximum_fusion.21), channel_id=1, source_target_pairs={{0,1},{1,0},{2,3},{3,2},{4,5},{5,4},{6,7},{7,6},{8,9},{9,8},{10,11... | collective-permute-start | bytes 884744 | tf_op jit(solution)/shard_map/ppermute | solution.py:28
  27.4 7.9 %collective-permute-start.11 = (bf16[1,24,3072]{2,1,0:T(8,128)(2,1)}, bf16[1,24,3072]{2,1,0:T(8,128)(2,1)S(1)}, u32[]{:S(2)}, u32[]{:S(2)}) collective-permute-start(bf16[1,24,3072]{2,1,0:T(8,128)(2,1)} %bitcast.15), channel_id=1, source_target_pairs={{0,4},{1,5},{2,6},{3,7},{4,0},{5,1},{6,2},{7,3},{8,12},{9,13},{10,... | collective-permute-start | bytes 442376 | tf_op jit(solution)/shard_map/ppermute | solution.py:28
  31.5 12.0 %collective-permute-start.9 = (bf16[4,24,896]{2,1,0:T(8,128)(2,1)S(1)}, bf16[4,24,896]{2,1,0:T(8,128)(2,1)S(1)}, u32[]{:S(2)}, u32[]{:S(2)}) collective-permute-start(bf16[4,24,896]{2,1,0:T(8,128)(2,1)S(1)} %get-tuple-element.487), channel_id=1, source_target_pairs={{0,16},{8,24},{16,0},{24,8},{1,17},{9,25},{17,1},{25,9},{2,18},{10... | collective-permute-start | bytes 516104 | tf_op jit(solution)/shard_map/ppermute | solution.py:28
  35.3 8.2 %collective-permute-start.8 = (bf16[4,24,896]{2,1,0:T(8,128)(2,1)S(1)}, bf16[4,24,896]{2,1,0:T(8,128)(2,1)S(1)}, u32[]{:S(2)}, u32[]{:S(2)}) collective-permute-start(bf16[4,24,896]{2,1,0:T(8,128)(2,1)S(1)} %get-tuple-element.488), channel_id=1, source_target_pairs={{0,1},{1,0},{2,3},{3,2},{4,5},{5,4},{6,7},{7,6},{8,9},{9,8},{10,11... | collective-permute-start | bytes 516104 | tf_op jit(solution)/shard_map/ppermute | solution.py:28
  43.6 13.2 %collective-permute-start.14 = (bf16[8,24,896]{2,1,0:T(8,128)(2,1)S(1)}, bf16[8,24,896]{2,1,0:T(8,128)(2,1)S(1)}, u32[]{:S(2)}, u32[]{:S(2)}) collective-permute-start(bf16[8,24,896]{2,1,0:T(8,128)(2,1)S(1)} %get-tuple-element.256), channel_id=1, source_target_pairs={{0,16},{8,24},{16,0},{24,8},{1,17},{9,25},{17,1},{25,9},{2,18},{10... | collective-permute-start | bytes 1032200 | tf_op jit(solution)/shard_map/ppermute | solution.py:28
  44.5 12.3 %collective-permute-start.15 = (bf16[8,24,896]{2,1,0:T(8,128)(2,1)S(1)}, bf16[8,24,896]{2,1,0:T(8,128)(2,1)S(1)}, u32[]{:S(2)}, u32[]{:S(2)}) collective-permute-start(bf16[8,24,896]{2,1,0:T(8,128)(2,1)S(1)} %get-tuple-element.257), channel_id=1, source_target_pairs={{0,1},{1,0},{2,3},{3,2},{4,5},{5,4},{6,7},{7,6},{8,9},{9,8},{10,11... | collective-permute-start | bytes 1032200 | tf_op jit(solution)/shard_map/ppermute | solution.py:28
  46.0 8.9 %collective-permute-start.16 = (bf16[2,2,104,128]{3,2,1,0:T(8,128)(2,1)S(1)}, bf16[2,2,104,128]{3,2,1,0:T(8,128)(2,1)S(1)}, u32[]{:S(2)}, u32[]{:S(2)}) collective-permute-start(bf16[2,2,104,128]{3,2,1,0:T(8,128)(2,1)S(1)} %get-tuple-element.258), channel_id=1, source_target_pairs={{0,2},{1,3},{2,0},{3,1},{4,6},{5,7},{6,4},{7,5},{8,10},{9,11},{10,... | collective-permute-start | bytes 319496 | tf_op jit(solution)/shard_map/ppermute | solution.py:28
  46.0 9.5 %collective-permute-start.17 = (bf16[2,2,104,128]{3,2,1,0:T(8,128)(2,1)S(1)}, bf16[2,2,104,128]{3,2,1,0:T(8,128)(2,1)S(1)}, u32[]{:S(2)}, u32[]{:S(2)}) collective-permute-start(bf16[2,2,104,128]{3,2,1,0:T(8,128)(2,1)S(1)} %get-tuple-element.259), channel_id=1, source_target_pairs={{0,4},{1,5},{2,6},{3,7},{4,0},{5,1},{6,2},{7,3},{8,12},{9,13},{10,... | collective-permute-start | bytes 319496 | tf_op jit(solution)/shard_map/ppermute | solution.py:28
  49.1 7.7 %collective-permute-start.18 = (bf16[2,2,104,128]{3,2,1,0:T(8,128)(2,1)S(1)}, bf16[2,2,104,128]{3,2,1,0:T(8,128)(2,1)S(1)}, u32[]{:S(2)}, u32[]{:S(2)}) collective-permute-start(bf16[2,2,104,128]{3,2,1,0:T(8,128)(2,1)S(1)} %get-tuple-element.260), channel_id=1, source_target_pairs={{0,6},{1,7},{2,4},{3,5},{4,2},{5,3},{6,0},{7,1},{8,14},{9,15},{10,... | collective-permute-start | bytes 319496 | tf_op jit(solution)/shard_map/ppermute | solution.py:28
  56.9 14.9 %collective-permute-start.25 = (bf16[4,2,104,128]{3,2,1,0:T(8,128)(2,1)S(1)}, bf16[4,2,104,128]{3,2,1,0:T(8,128)(2,1)S(1)}, u32[]{:S(2)}, u32[]{:S(2)}) collective-permute-start(bf16[4,2,104,128]{3,2,1,0:T(8,128)(2,1)S(1)} %pad_maximum_fusion.27), channel_id=1, source_target_pairs={{0,1},{1,0},{2,3},{3,2},{4,5},{5,4},{6,7},{7,6},{8,9},{9,8},{10,11... | collective-permute-start | bytes 638984 | tf_op jit(solution)/shard_map/ppermute | solution.py:28
  62.6 9.5 %collective-permute-start.22 = (bf16[4,24,1536]{2,1,0:T(8,128)(2,1)S(1)}, bf16[4,24,1536]{2,1,0:T(8,128)(2,1)S(1)}, u32[]{:S(2)}, u32[]{:S(2)}) collective-permute-start(bf16[4,24,1536]{2,1,0:T(8,128)(2,1)S(1)} %get-tuple-element.274), channel_id=1, source_target_pairs={{0,1},{1,0},{2,3},{3,2},{4,5},{5,4},{6,7},{7,6},{8,9},{9,8},{10,11... | collective-permute-start | bytes 884744 | tf_op jit(solution)/shard_map/ppermute | solution.py:28
  63.5 8.6 %collective-permute-start.23 = (bf16[4,24,1536]{2,1,0:T(8,128)(2,1)S(1)}, bf16[4,24,1536]{2,1,0:T(8,128)(2,1)S(1)}, u32[]{:S(2)}, u32[]{:S(2)}) collective-permute-start(bf16[4,24,1536]{2,1,0:T(8,128)(2,1)S(1)} %get-tuple-element.275), channel_id=1, source_target_pairs={{0,16},{8,24},{16,0},{24,8},{1,17},{9,25},{17,1},{25,9},{2,18},{10... | collective-permute-start | bytes 884744 | tf_op jit(solution)/shard_map/ppermute | solution.py:28
  72.7 12.2 %collective-permute-start.31 = (bf16[8,24,1536]{2,1,0:T(8,128)(2,1)S(1)}, bf16[8,24,1536]{2,1,0:T(8,128)(2,1)S(1)}, u32[]{:S(2)}, u32[]{:S(2)}) collective-permute-start(bf16[8,24,1536]{2,1,0:T(8,128)(2,1)S(1)} %pad_maximum_fusion.10), channel_id=1, source_target_pairs={{0,16},{8,24},{16,0},{24,8},{1,17},{9,25},{17,1},{25,9},{2,18},{10... | collective-permute-start | bytes 1769480 | tf_op jit(solution)/shard_map/ppermute | solution.py:28
  74.0 11.7 %collective-permute-start.32 = (bf16[8,24,1536]{2,1,0:T(8,128)(2,1)S(1)}, bf16[8,24,1536]{2,1,0:T(8,128)(2,1)S(1)}, u32[]{:S(2)}, u32[]{:S(2)}) collective-permute-start(bf16[8,24,1536]{2,1,0:T(8,128)(2,1)S(1)} %pad_maximum_fusion.11), channel_id=1, source_target_pairs={{0,1},{1,0},{2,3},{3,2},{4,5},{5,4},{6,7},{7,6},{8,9},{9,8},{10,11... | collective-permute-start | bytes 1769480 | tf_op jit(solution)/shard_map/ppermute | solution.py:28
  76.3 8.3 %collective-permute-start.27 = (bf16[2,2,104,128]{3,2,1,0:T(8,128)(2,1)S(1)}, bf16[2,2,104,128]{3,2,1,0:T(8,128)(2,1)S(1)}, u32[]{:S(2)}, u32[]{:S(2)}) collective-permute-start(bf16[2,2,104,128]{3,2,1,0:T(8,128)(2,1)S(1)} %get-tuple-element.285), channel_id=1, source_target_pairs={{0,4},{1,5},{2,6},{3,7},{4,0},{5,1},{6,2},{7,3},{8,12},{9,13},{10,... | collective-permute-start | bytes 319496 | tf_op jit(solution)/shard_map/ppermute | solution.py:28
  77.3 7.3 %collective-permute-start.28 = (bf16[2,2,104,128]{3,2,1,0:T(8,128)(2,1)S(1)}, bf16[2,2,104,128]{3,2,1,0:T(8,128)(2,1)S(1)}, u32[]{:S(2)}, u32[]{:S(2)}) collective-permute-start(bf16[2,2,104,128]{3,2,1,0:T(8,128)(2,1)S(1)} %get-tuple-element.286), channel_id=1, source_target_pairs={{0,6},{1,7},{2,4},{3,5},{4,2},{5,3},{6,0},{7,1},{8,14},{9,15},{10,... | collective-permute-start | bytes 319496 | tf_op jit(solution)/shard_map/ppermute | solution.py:28
  86.6 9.0 %collective-permute-start.29 = (bf16[2,96,768]{2,1,0:T(8,128)(2,1)S(1)}, bf16[2,96,768]{2,1,0:T(8,128)(2,1)S(1)}, u32[]{:S(2)}, u32[]{:S(2)}) collective-permute-start(bf16[2,96,768]{2,1,0:T(8,128)(2,1)S(1)} %pad_maximum_fusion.23), channel_id=1, source_target_pairs={{0,2},{1,3},{2,0},{3,1},{4,6},{5,7},{6,4},{7,5},{8,10},{9,11},{10,... | collective-permute-start | bytes 884744 | tf_op jit(solution)/shard_map/ppermute | solution.py:28
  95.7 8.2 %collective-permute-start.36 = (bf16[4,96,384]{2,1,0:T(8,128)(2,1)S(1)}, bf16[4,96,384]{2,1,0:T(8,128)(2,1)S(1)}, u32[]{:S(2)}, u32[]{:S(2)}) collective-permute-start(bf16[4,96,384]{2,1,0:T(8,128)(2,1)S(1)} %get-tuple-element.303), channel_id=1, source_target_pairs={{0,1},{1,0},{2,3},{3,2},{4,5},{5,4},{6,7},{7,6},{8,9},{9,8},{10,11... | collective-permute-start | bytes 884744 | tf_op jit(solution)/shard_map/ppermute | solution.py:28
  97.2 8.2 %collective-permute-start.37 = (bf16[4,96,384]{2,1,0:T(8,128)(2,1)S(1)}, bf16[4,96,384]{2,1,0:T(8,128)(2,1)S(1)}, u32[]{:S(2)}, u32[]{:S(2)}) collective-permute-start(bf16[4,96,384]{2,1,0:T(8,128)(2,1)S(1)} %get-tuple-element.304), channel_id=1, source_target_pairs={{0,16},{8,24},{16,0},{24,8},{1,17},{9,25},{17,1},{25,9},{2,18},{10... | collective-permute-start | bytes 884744 | tf_op jit(solution)/shard_map/ppermute | solution.py:28
  105.6 13.7 %collective-permute-start.38 = (bf16[8,96,384]{2,1,0:T(8,128)(2,1)S(1)}, bf16[8,96,384]{2,1,0:T(8,128)(2,1)S(1)}, u32[]{:S(2)}, u32[]{:S(2)}) collective-permute-start(bf16[8,96,384]{2,1,0:T(8,128)(2,1)S(1)} %pad_maximum_fusion.13), channel_id=1, source_target_pairs={{0,16},{8,24},{16,0},{24,8},{1,17},{9,25},{17,1},{25,9},{2,18},{10... | collective-permute-start | bytes 1769480 | tf_op jit(solution)/shard_map/ppermute | solution.py:28
  106.0 13.5 %collective-permute-start.39 = (bf16[8,96,384]{2,1,0:T(8,128)(2,1)S(1)}, bf16[8,96,384]{2,1,0:T(8,128)(2,1)S(1)}, u32[]{:S(2)}, u32[]{:S(2)}) collective-permute-start(bf16[8,96,384]{2,1,0:T(8,128)(2,1)S(1)} %pad_maximum_fusion.14), channel_id=1, source_target_pairs={{0,1},{1,0},{2,3},{3,2},{4,5},{5,4},{6,7},{7,6},{8,9},{9,8},{10,11... | collective-permute-start | bytes 1769480 | tf_op jit(solution)/shard_map/ppermute | solution.py:28
  144.0 19.9 %collective-permute-start.50 = (bf16[4,192,384]{2,1,0:T(8,128)(2,1)S(1)}, bf16[4,192,384]{2,1,0:T(8,128)(2,1)S(1)}, u32[]{:S(2)}, u32[]{:S(2)}) collective-permute-start(bf16[4,192,384]{2,1,0:T(8,128)(2,1)S(1)} %get-tuple-element.341), channel_id=1, source_target_pairs={{0,16},{8,24},{16,0},{24,8},{1,17},{9,25},{17,1},{25,9},{2,18},{10... | collective-permute-start | bytes 1769480 | tf_op jit(solution)/shard_map/ppermute | solution.py:28
  148.9 24.1 %collective-permute-start.46 = (bf16[2,3,48,1536]{3,2,1,0:T(8,128)(2,1)S(1)}, bf16[2,3,48,1536]{3,2,1,0:T(8,128)(2,1)S(1)}, u32[]{:S(2)}, u32[]{:S(2)}) collective-permute-start(bf16[2,3,48,1536]{3,2,1,0:T(8,128)(2,1)S(1)} %slice.454), channel_id=1, source_target_pairs={{0,1},{1,0},{2,3},{3,2},{4,5},{5,4},{6,7},{7,6},{8,9},{9,8},{10,11... | collective-permute-start | bytes 2654216 | tf_op jit(solution)/shard_map/ppermute | solution.py:28
  160.8 10.5 %collective-permute-start.48 = (bf16[2,2,104,128]{3,2,1,0:T(8,128)(2,1)S(1)}, bf16[2,2,104,128]{3,2,1,0:T(8,128)(2,1)S(1)}, u32[]{:S(2)}, u32[]{:S(2)}) collective-permute-start(bf16[2,2,104,128]{3,2,1,0:T(8,128)(2,1)S(1)} %get-tuple-element.351), channel_id=1, source_target_pairs={{0,4},{1,5},{2,6},{3,7},{4,0},{5,1},{6,2},{7,3},{8,12},{9,13},{10,... | collective-permute-start | bytes 319496 | tf_op jit(solution)/shard_map/ppermute | solution.py:28
  161.8 9.5 %collective-permute-start.49 = (bf16[2,2,104,128]{3,2,1,0:T(8,128)(2,1)S(1)}, bf16[2,2,104,128]{3,2,1,0:T(8,128)(2,1)S(1)}, u32[]{:S(2)}, u32[]{:S(2)}) collective-permute-start(bf16[2,2,104,128]{3,2,1,0:T(8,128)(2,1)S(1)} %get-tuple-element.352), channel_id=1, source_target_pairs={{0,6},{1,7},{2,4},{3,5},{4,2},{5,3},{6,0},{7,1},{8,14},{9,15},{10,... | collective-permute-start | bytes 319496 | tf_op jit(solution)/shard_map/ppermute | solution.py:28
  164.1 14.0 %collective-permute-start.54 = (bf16[4,192,384]{2,1,0:T(8,128)(2,1)S(1)}, bf16[4,192,384]{2,1,0:T(8,128)(2,1)S(1)}, u32[]{:S(2)}, u32[]{:S(2)}) collective-permute-start(bf16[4,192,384]{2,1,0:T(8,128)(2,1)S(1)} %get-tuple-element.356), channel_id=1, source_target_pairs={{0,16},{8,24},{16,0},{24,8},{1,17},{9,25},{17,1},{25,9},{2,18},{10... | collective-permute-start | bytes 1769480 | tf_op jit(solution)/shard_map/ppermute | solution.py:28
  173.3 10.7 %collective-permute-start.51 = (bf16[2,1,48,1536]{3,2,1,0:T(8,128)(2,1)S(1)}, bf16[2,1,48,1536]{3,2,1,0:T(8,128)(2,1)S(1)}, u32[]{:S(2)}, u32[]{:S(2)}) collective-permute-start(bf16[2,1,48,1536]{3,2,1,0:T(8,128)(2,1)S(1)} %slice.452), channel_id=1, source_target_pairs={{0,1},{1,0},{2,3},{3,2},{4,5},{5,4},{6,7},{7,6},{8,9},{9,8},{10,11... | collective-permute-start | bytes 884744 | tf_op jit(solution)/shard_map/ppermute | solution.py:28
  178.5 16.5 %collective-permute-start.55 = (bf16[2,2,104,128]{3,2,1,0:T(8,128)(2,1)S(1)}, bf16[2,2,104,128]{3,2,1,0:T(8,128)(2,1)S(1)}, u32[]{:S(2)}, u32[]{:S(2)}) collective-permute-start(bf16[2,2,104,128]{3,2,1,0:T(8,128)(2,1)S(1)} %get-tuple-element.371), channel_id=1, source_target_pairs={{0,2},{1,3},{2,0},{3,1},{4,6},{5,7},{6,4},{7,5},{8,10},{9,11},{10,... | collective-permute-start | bytes 319496 | tf_op jit(solution)/shard_map/ppermute | solution.py:28
  181.5 13.5 %collective-permute-start.56 = (bf16[2,2,104,128]{3,2,1,0:T(8,128)(2,1)S(1)}, bf16[2,2,104,128]{3,2,1,0:T(8,128)(2,1)S(1)}, u32[]{:S(2)}, u32[]{:S(2)}) collective-permute-start(bf16[2,2,104,128]{3,2,1,0:T(8,128)(2,1)S(1)} %get-tuple-element.372), channel_id=1, source_target_pairs={{0,4},{1,5},{2,6},{3,7},{4,0},{5,1},{6,2},{7,3},{8,12},{9,13},{10,... | collective-permute-start | bytes 319496 | tf_op jit(solution)/shard_map/ppermute | solution.py:28
  181.6 13.5 %collective-permute-start.57 = (bf16[2,2,104,128]{3,2,1,0:T(8,128)(2,1)S(1)}, bf16[2,2,104,128]{3,2,1,0:T(8,128)(2,1)S(1)}, u32[]{:S(2)}, u32[]{:S(2)}) collective-permute-start(bf16[2,2,104,128]{3,2,1,0:T(8,128)(2,1)S(1)} %get-tuple-element.373), channel_id=1, source_target_pairs={{0,6},{1,7},{2,4},{3,5},{4,2},{5,3},{6,0},{7,1},{8,14},{9,15},{10,... | collective-permute-start | bytes 319496 | tf_op jit(solution)/shard_map/ppermute | solution.py:28
  184.2 14.2 %collective-permute-start.60 = (bf16[4,48,1536]{2,1,0:T(8,128)(2,1)S(1)}, bf16[4,48,1536]{2,1,0:T(8,128)(2,1)S(1)}, u32[]{:S(2)}, u32[]{:S(2)}) collective-permute-start(bf16[4,48,1536]{2,1,0:T(8,128)(2,1)S(1)} %pad_maximum_fusion.15), channel_id=1, source_target_pairs={{0,16},{8,24},{16,0},{24,8},{1,17},{9,25},{17,1},{25,9},{2,18},{10... | collective-permute-start | bytes 1769480 | tf_op jit(solution)/shard_map/ppermute | solution.py:28
  185.9 14.9 %collective-permute-start.59 = (bf16[4,192,384]{2,1,0:T(8,128)(2,1)S(1)}, bf16[4,192,384]{2,1,0:T(8,128)(2,1)S(1)}, u32[]{:S(2)}, u32[]{:S(2)}) collective-permute-start(bf16[4,192,384]{2,1,0:T(8,128)(2,1)S(1)} %fusion.1), channel_id=1, source_target_pairs={{0,1},{1,0},{2,3},{3,2},{4,5},{5,4},{6,7},{7,6},{8,9},{9,8},{10,11... | collective-permute-start | bytes 1769480 | tf_op jit(solution)/shard_map/ppermute | solution.py:28
  195.1 13.4 %collective-permute-start.58 = (bf16[4,2,104,128]{3,2,1,0:T(8,128)(2,1)S(1)}, bf16[4,2,104,128]{3,2,1,0:T(8,128)(2,1)S(1)}, u32[]{:S(2)}, u32[]{:S(2)}) collective-permute-start(bf16[4,2,104,128]{3,2,1,0:T(8,128)(2,1)S(1)} %pad_maximum_fusion.30), channel_id=1, source_target_pairs={{0,1},{1,0},{2,3},{3,2},{4,5},{5,4},{6,7},{7,6},{8,9},{9,8},{10,11... | collective-permute-start | bytes 638984 | tf_op jit(solution)/shard_map/ppermute | solution.py:28
  206.5 7.8 %collective-permute-start.62 = (bf16[2,48,1536]{2,1,0:T(8,128)(2,1)S(1)}, bf16[2,48,1536]{2,1,0:T(8,128)(2,1)S(1)}, u32[]{:S(2)}, u32[]{:S(2)}) collective-permute-start(bf16[2,48,1536]{2,1,0:T(8,128)(2,1)S(1)} %get-tuple-element.395), channel_id=1, source_target_pairs={{0,2},{1,3},{2,0},{3,1},{4,6},{5,7},{6,4},{7,5},{8,10},{9,11},{10,... | collective-permute-start | bytes 884744 | tf_op jit(solution)/shard_map/ppermute | solution.py:28
  215.1 18.4 %collective-permute-start.64 = (bf16[8,48,896]{2,1,0:T(8,128)(2,1)}, bf16[8,48,896]{2,1,0:T(8,128)(2,1)S(1)}, u32[]{:S(2)}, u32[]{:S(2)}) collective-permute-start(bf16[8,48,896]{2,1,0:T(8,128)(2,1)} %slice_bitcast_fusion.2), channel_id=1, source_target_pairs={{0,16},{8,24},{16,0},{24,8},{1,17},{9,25},{17,1},{25,9},{2,18},{10... | collective-permute-start | bytes 2064392 | tf_op jit(solution)/shard_map/ppermute | solution.py:28
  216.4 21.2 %collective-permute-start.67 = (bf16[1,48,1536]{2,1,0:T(8,128)(2,1)}, bf16[1,48,1536]{2,1,0:T(8,128)(2,1)S(1)}, u32[]{:S(2)}, u32[]{:S(2)}) collective-permute-start(bf16[1,48,1536]{2,1,0:T(8,128)(2,1)} %add_convert_fusion.12), channel_id=1, source_target_pairs={{0,4},{1,5},{2,6},{3,7},{4,0},{5,1},{6,2},{7,3},{8,12},{9,13},{10,... | collective-permute-start | bytes 442376 | tf_op jit(solution)/shard_map/ppermute | solution.py:28
  217.6 17.5 %collective-permute-start.69 = (bf16[2,192,384]{2,1,0:T(8,128)(2,1)}, bf16[2,192,384]{2,1,0:T(8,128)(2,1)S(1)}, u32[]{:S(2)}, u32[]{:S(2)}) collective-permute-start(bf16[2,192,384]{2,1,0:T(8,128)(2,1)} %get-tuple-element.400), channel_id=1, source_target_pairs={{0,2},{1,3},{2,0},{3,1},{4,6},{5,7},{6,4},{7,5},{8,10},{9,11},{10,... | collective-permute-start | bytes 884744 | tf_op jit(solution)/shard_map/ppermute | solution.py:28
  223.8 16.1 %collective-permute-start.66 = (bf16[8,24,768]{2,1,0:T(8,128)(2,1)S(1)}, bf16[8,24,768]{2,1,0:T(8,128)(2,1)S(1)}, u32[]{:S(2)}, u32[]{:S(2)}) collective-permute-start(bf16[8,24,768]{2,1,0:T(8,128)(2,1)S(1)} %slice_bitcast_fusion.11), channel_id=1, source_target_pairs={{0,16},{8,24},{16,0},{24,8},{1,17},{9,25},{17,1},{25,9},{2,18},{10... | collective-permute-start | bytes 884744 | tf_op jit(solution)/shard_map/ppermute | solution.py:28
  224.5 11.9 %collective-permute-start.68 = (bf16[4,48,768]{2,1,0:T(8,128)(2,1)S(1)}, bf16[4,48,768]{2,1,0:T(8,128)(2,1)S(1)}, u32[]{:S(2)}, u32[]{:S(2)}) collective-permute-start(bf16[4,48,768]{2,1,0:T(8,128)(2,1)S(1)} %slice_bitcast_fusion.10), channel_id=1, source_target_pairs={{0,1},{1,0},{2,3},{3,2},{4,5},{5,4},{6,7},{7,6},{8,9},{9,8},{10,11... | collective-permute-start | bytes 884744 | tf_op jit(solution)/shard_map/ppermute | solution.py:28
  233.7 10.5 %collective-permute-start.65 = (bf16[4,48,896]{2,1,0:T(8,128)(2,1)S(1)}, bf16[4,48,896]{2,1,0:T(8,128)(2,1)S(1)}, u32[]{:S(2)}, u32[]{:S(2)}) collective-permute-start(bf16[4,48,896]{2,1,0:T(8,128)(2,1)S(1)} %get-tuple-element.409), channel_id=1, source_target_pairs={{0,1},{1,0},{2,3},{3,2},{4,5},{5,4},{6,7},{7,6},{8,9},{9,8},{10,11... | collective-permute-start | bytes 1032200 | tf_op jit(solution)/shard_map/ppermute | solution.py:28
  235.2 11.5 %collective-permute-start.73 = (bf16[1,192,384]{2,1,0:T(8,128)(2,1)S(1)}, bf16[1,192,384]{2,1,0:T(8,128)(2,1)S(1)}, u32[]{:S(2)}, u32[]{:S(2)}) collective-permute-start(bf16[1,192,384]{2,1,0:T(8,128)(2,1)S(1)} %add_convert_fusion.10), channel_id=1, source_target_pairs={{0,4},{1,5},{2,6},{3,7},{4,0},{5,1},{6,2},{7,3},{8,12},{9,13},{10,... | collective-permute-start | bytes 442376 | tf_op jit(solution)/shard_map/ppermute | solution.py:28
  236.5 8.8 %collective-permute-start.74 = (bf16[2,48,768]{2,1,0:T(8,128)(2,1)S(1)}, bf16[2,48,768]{2,1,0:T(8,128)(2,1)S(1)}, u32[]{:S(2)}, u32[]{:S(2)}) collective-permute-start(bf16[2,48,768]{2,1,0:T(8,128)(2,1)S(1)} %get-tuple-element.413), channel_id=1, source_target_pairs={{0,2},{1,3},{2,0},{3,1},{4,6},{5,7},{6,4},{7,5},{8,10},{9,11},{10,... | collective-permute-start | bytes 442376 | tf_op jit(solution)/shard_map/ppermute | solution.py:28
  237.7 11.6 %collective-permute-start.71 = (bf16[48,1536]{1,0:T(8,128)(2,1)S(1)}, bf16[48,1536]{1,0:T(8,128)(2,1)S(1)}, u32[]{:S(2)}, u32[]{:S(2)}) collective-permute-start(bf16[48,1536]{1,0:T(8,128)(2,1)S(1)} %fusion.25), channel_id=1, source_target_pairs={{0,16},{8,24},{16,0},{24,8},{1,17},{9,25},{17,1},{25,9},{2,18},{10... | collective-permute-start | bytes 442376 | tf_op jit(solution)/shard_map/ppermute | solution.py:28
  239.9 8.3 %collective-permute-start.72 = (bf16[4,24,768]{2,1,0:T(8,128)(2,1)S(1)}, bf16[4,24,768]{2,1,0:T(8,128)(2,1)S(1)}, u32[]{:S(2)}, u32[]{:S(2)}) collective-permute-start(bf16[4,24,768]{2,1,0:T(8,128)(2,1)S(1)} %get-tuple-element.417), channel_id=1, source_target_pairs={{0,1},{1,0},{2,3},{3,2},{4,5},{5,4},{6,7},{7,6},{8,9},{9,8},{10,11... | collective-permute-start | bytes 442376 | tf_op jit(solution)/shard_map/ppermute | solution.py:28
  246.8 10.3 %collective-permute-start.76 = (bf16[192,384]{1,0:T(8,128)(2,1)S(1)}, bf16[192,384]{1,0:T(8,128)(2,1)S(1)}, u32[]{:S(2)}, u32[]{:S(2)}) collective-permute-start(bf16[192,384]{1,0:T(8,128)(2,1)S(1)} %fusion.26), channel_id=1, source_target_pairs={{0,16},{8,24},{16,0},{24,8},{1,17},{9,25},{17,1},{25,9},{2,18},{10... | collective-permute-start | bytes 442376 | tf_op jit(solution)/shard_map/ppermute | solution.py:28
  251.9 7.7 %collective-permute-start.82 = (bf16[48,768]{1,0:T(8,128)(2,1)S(1)}, bf16[48,768]{1,0:T(8,128)(2,1)S(1)}, u32[]{:S(2)}, u32[]{:S(2)}) collective-permute-start(bf16[48,768]{1,0:T(8,128)(2,1)S(1)} %fusion.29), channel_id=1, source_target_pairs={{0,16},{8,24},{16,0},{24,8},{1,17},{9,25},{17,1},{25,9},{2,18},{10... | collective-permute-start | bytes 221192 | tf_op jit(solution)/shard_map/ppermute | solution.py:28
  (66 other events, 337.0 us)

commit v6 on v5

--- a/solution.py
+++ b/solution.py
@@ -840,7 +840,7 @@
     block = height // fsdp
     bits = fsdp.bit_length() - 1
     share = block // len(splits)
-    group = block if block % 128 == 0 else height
+    group = min(4, fsdp) * block if block % 128 == 0 else height
     extra = [] if sums is None else [sums]
 
     def kernel(ids_ref, *refs):

time: 269 us -> 268 us (level)
  no operation moved by 1% of the time
where the time goes in v6:
time: 268 us; the launch traced here: 267 us
  starting transfers between devices  91.4 us (34%)
  Pallas kernels  78 us (29%)
  waiting for transfers between devices  66.1 us (25%)
  other arithmetic  14.9 us (6%)
  local copies, waits for them, and re-layouts  11.1 us (4%)
  matrix products  3.7 us (1%)
    ppermute x88, starting transfers between devices, exchange(): return lax.ppermute(x, axis, [(i, i ^ offset) for i in range(size)])  91.4 us
    ppermute x88, waiting for transfers between devices, exchange(): return lax.ppermute(x, axis, [(i, i ^ offset) for i in range(size)])  66.1 us
    pallas_call x4, Pallas kernels, weight_grad(): call(kernel, 'weight_grad', tuple((shape_of((n, fsdp, share // n, width),...  12.8 us
    pallas_call x1, Pallas kernels, back_to_heads(): call(kernel, 'back_to_heads', (shape_of((rows, D), f32), shape_of((rows,...  9.93 us
    pallas_call x1, Pallas kernels, intra_backward(): call(kernel, 'intra_backward', (shape_of((rows, D), bf16), shape_of((rows...  8.77 us
    pallas_call x1, Pallas kernels, expand(): call(kernel, 'expand', (shape_of((rows, D), f32), shape_of((rows, LANES),...  7.46 us
    pallas_call x1, Pallas kernels, intra_forward(): call(kernel, 'intra_forward', (shape_of((rows, D), bf16), wide, wide), [V...  5.87 us
  transfers between devices with their start and end apart: 88, of which 35 were waited for; matrix products, arithmetic and copies ran while one was open for 8% of the time, Pallas kernels for 29%

profile of v6, /device:TPU:0, one launch (start us, length us, event | category | flops | bytes accessed | tf_op | source)
XLA Modules:
  0.0 267.1 jit_solution(15357128493793134289)
XLA Ops:
  1.5 4.0 %collective-permute-start = (bf16[1,24,1536]{2,1,0:T(8,128)(2,1)S(1)}, bf16[1,24,1536]{2,1,0:T(8,128)(2,1)S(1)}, u32[]{:S(2)}, u32[]{:S(2)}) collective-permute-start(bf16[1,24,1536]{2,1,0:T(8,128)(2,1)S(1)} %slice_bitcast_fusion.15), channel_id=1, source_target_pairs={{0,4},{1,5},{2,6},{3,7},{4,0},{5,1},{6,2},{7,3},{8,12},{9,13},{10,... | collective-permute-start | bytes 221192 | tf_op jit(solution)/shard_map/ppermute | solution.py:28
  12.4 1.8 fusion.22
  15.2 1.6 collective-permute-start.4
  19.3 2.3 collective-permute-start.2
  22.0 1.6 collective-permute-start.6
  27.4 3.0 %collective-permute-start.11 = (bf16[1,24,3072]{2,1,0:T(8,128)(2,1)}, bf16[1,24,3072]{2,1,0:T(8,128)(2,1)S(1)}, u32[]{:S(2)}, u32[]{:S(2)}) collective-permute-start(bf16[1,24,3072]{2,1,0:T(8,128)(2,1)} %bitcast.15), channel_id=1, source_target_pairs={{0,4},{1,5},{2,6},{3,7},{4,0},{5,1},{6,2},{7,3},{8,12},{9,13},{10,... | collective-permute-start | bytes 442376 | tf_op jit(solution)/shard_map/ppermute | solution.py:28
  32.7 2.6 collective-permute-done.11
  38.4 5.1 %project.1 = (bf16[512,768]{1,0:T(8,128)(2,1)S(1)}, bf16[512,768]{1,0:T(8,128)(2,1)S(1)}, bf16[2,2,104,128]{3,2,1,0:T(8,128)(2,1)S(1)}, bf16[2,2,104,128]{3,2,1,...) custom-call(s32[3]{0:T(128)S(1)} %pad_add_fusion.ids_ref, ...), custom_call_target="tpu_custom_call" | custom-call | flops 6480000000 | tf_op jit(solution)/shard_map/project/pallas_call | solution.py:381
  46.0 3.1 %collective-permute-start.17 = (bf16[2,2,104,128]{3,2,1,0:T(8,128)(2,1)S(1)}, bf16[2,2,104,128]{3,2,1,0:T(8,128)(2,1)S(1)}, u32[]{:S(2)}, u32[]{:S(2)}) collective-permute-start(bf16[2,2,104,128]{3,2,1,0:T(8,128)(2,1)S(1)} %get-tuple-element.259), channel_id=1, source_target_pairs={{0,4},{1,5},{2,6},{3,7},{4,0},{5,1},{6,2},{7,3},{8,12},{9,13},{10,... | collective-permute-start | bytes 319496 | tf_op jit(solution)/shard_map/ppermute | solution.py:28
  50.4 4.5 %collective-permute-done.16.refs_1_ = bf16[2,2,104,128]{3,2,1,0:T(8,128)(2,1)S(1)} collective-permute-done((bf16[2,2,104,128]{3,2,1,0:T(8,128)(2,1)S(1)}, bf16[2,2,104,128]{3,2,1,0:T(8,128)(2,1)S(1)}, u32[]{:S(2)}, u32[]{:S(2)}) %collective-permute-start.16) | collective-permute-done | bytes 106528 | tf_op jit(solution)/shard_map/ppermute | solution.py:28
  58.3 3.3 %collective-permute-done.21 = bf16[2,24,3072]{2,1,0:T(8,128)(2,1)S(1)} collective-permute-done((bf16[2,24,3072]{2,1,0:T(8,128)(2,1)S(1)}, bf16[2,24,3072]{2,1,0:T(8,128)(2,1)S(1)}, u32[]{:S(2)}, u32[]{:S(2)}) %collective-permute-start.21) | collective-permute-done | bytes 294944 | tf_op jit(solution)/shard_map/ppermute | solution.py:28
  65.9 5.9 %intra_forward.1 = (bf16[512,768]{1,0:T(8,128)(2,1)S(1)}, f32[512,768]{1,0:T(8,128)S(1)}, f32[512,768]{1,0:T(8,128)S(1)}) custom-call(bf16[512,768]{1,0:T(8,128)(2,1)S(1)} %copy-done.8, bf16[768,1792]{1,0:T(8,128)(2,1)S(1)} %bitcast.103, bf16[512,768]{1,0:T(8,128)(2,1)S(1)} %get-tuple-element.250.k_ref, bf16[512,768]{1,0:T(8,128)(2,1)S(1)} %get-tuple-element.267.v_ref, ...), custom_call_target="tpu_custom_call" | custom-call | flops 3540000000 | tf_op jit(solution)/shard_map/intra_forward/pallas_call | solution.py:439
  77.3 2.3 collective-permute-start.28
  79.8 1.8 collective-permute-done.26.refs_1_
  81.6 3.1 %collective-permute-done.27.refs_2_ = bf16[2,2,104,128]{3,2,1,0:T(8,128)(2,1)S(1)} collective-permute-done((bf16[2,2,104,128]{3,2,1,0:T(8,128)(2,1)S(1)}, bf16[2,2,104,128]{3,2,1,0:T(8,128)(2,1)S(1)}, u32[]{:S(2)}, u32[]{:S(2)}) %collective-permute-start.27) | collective-permute-done | bytes 106528 | tf_op jit(solution)/shard_map/ppermute | solution.py:28
  86.6 1.8 collective-permute-start.29
  91.8 3.5 %collective-permute-done.30.refs_4_ = bf16[4,2,104,128]{3,2,1,0:T(8,128)(2,1)S(1)} collective-permute-done((bf16[4,2,104,128]{3,2,1,0:T(8,128)(2,1)S(1)}, bf16[4,2,104,128]{3,2,1,0:T(8,128)(2,1)S(1)}, u32[]{:S(2)}, u32[]{:S(2)}) %collective-permute-start.30) | collective-permute-done | bytes 213024 | tf_op jit(solution)/shard_map/ppermute | solution.py:28
  97.8 4.0 %inter_forward.1 = (bf16[512,768]{1,0:T(8,128)(2,1)S(1)}, f32[512,768]{1,0:T(8,128)S(1)}) custom-call(s32[3]{0:T(128)S(1)} %pad_add_fusion.ids_ref, bf16[512,768]{1,0:T(8,128)(2,1)S(1)} %get-tuple-element.377.q_ref, f32[512,768]{1,0:T(8,128)S(1)} %get-tuple-element.306.num_ref, f32[512,768]{1,0:T(8,128)S(1)} %get-tuple-element.307.den_ref, ...), custom_call_target="tpu_custom_call" | custom-call | flops 9900000256 | tf_op jit(solution)/shard_map/inter_forward/pallas_call | solution.py:480
  101.9 2.1 collective-permute-done.36
  106.0 1.7 collective-permute-start.39
  107.7 7.5 %expand.1 = (f32[512,768]{1,0:T(8,128)S(1)}, f32[512,128]{1,0:T(8,128)S(1)}, bf16[512,768]{1,0:T(8,128)(2,1)S(1)}, bf16[512,3072]{1,0:T(8,128)(2,1)S(1)}, bf16[512,3072]{1,0:T(8,128)(2,1)S(1)}) custom-call(bf16[512,768]{1,0:T(8,128)(2,1)S(1)} %get-tuple-element.314.att_ref.refs_0_, bf16[512,768]{1,0:T(8,128)(2,1)S(1)} %copy-done.8, ...), custom_call_target="tpu_custom_call" | custom-call | flops 171000000 | tf_op jit(solution)/shard_map/expand/pallas_call | solution.py:535
  115.1 4.1 %collective-permute-done.38 = bf16[8,96,384]{2,1,0:T(8,128)(2,1)S(1)} collective-permute-done((bf16[8,96,384]{2,1,0:T(8,128)(2,1)S(1)}, bf16[8,96,384]{2,1,0:T(8,128)(2,1)S(1)}, u32[]{:S(2)}, u32[]{:S(2)}) %collective-permute-start.38) | collective-permute-done | bytes 589856 | tf_op jit(solution)/shard_map/ppermute | solution.py:28
  120.4 2.3 collective-permute-done.40.refs_1_
  122.8 1.7 collective-permute-done.41.refs_3_
  126.3 5.3 %contract.1 = (bf16[512,768]{1,0:T(8,128)(2,1)}, f32[512,768]{1,0:T(8,128)S(1)}, bf16[512,768]{1,0:T(8,128)(2,1)S(1)}, bf16[512,384]{1,0:T(8,128)(2,1)S(1)}, f32[16,768]{1,0:T(8,128)S(1)}) custom-call(s32[3]{0:T(128)S(1)} %pad_add_fusion.ids_ref, bf16[512,3072]{1,0:T(8,128)(2,1)S(1)} %get-tuple-element.329.gelu_ref.refs_0_, ...), custom_call_target="tpu_custom_call" | custom-call | flops 3600000000 | tf_op jit(solution)/shard_map/contract/pallas_call | solution.py:579
  132.7 5.0 %turn.1 = (bf16[512,3072]{1,0:T(8,128)(2,1)S(1)}, bf16[512,1536]{1,0:T(8,128)(2,1)S(1)}, f32[16,768]{1,0:T(8,128)S(1)}) custom-call(s32[3]{0:T(128)S(1)} %pad_add_fusion.ids_ref, bf16[512,768]{1,0:T(8,128)(2,1)S(1)} %get-tuple-element.339.dlow_ref.refs_2_, bf16[512,3072]{1,0:T(8,128)(2,1)S(1)} %get-tuple-element.333.slope_ref, ...), custom_call_target="tpu_custom_call" | custom-call | flops 13500000256 | tf_op jit(solution)/shard_map/turn/pallas_call | solution.py:620
  138.2 4.5 %weight_grad.4 = bf16[2,8,192,384]{3,2,1,0:T(8,128)(2,1)S(1)} custom-call(s32[3]{0:T(128)S(1)} %pad_add_fusion.ids_ref, bf16[512,3072]{1,0:T(8,128)(2,1)S(1)} %get-tuple-element.329.gelu_ref.refs_0_, bf16[512,3072]{1,0:T(8,128)(2,1)S(1)} %collective-permute-done.43.refs_1_, bf16[512,768]{1,0:T(8,128)(2,1)S(1)} %get-tuple-element.339.dlow_ref.refs_2_, ...), custom_call_target="tpu_custom_call" | custom-call | flops 3600000000 | tf_op jit(solution)/shard_map/weight_grad/pallas_call | solution.py:881
  144.3 3.2 %weight_grad.5 = bf16[2,8,48,1536]{3,2,1,0:T(8,128)(2,1)S(1)} custom-call(s32[3]{0:T(128)S(1)} %pad_add_fusion.ids_ref, bf16[512,768]{1,0:T(8,128)(2,1)S(1)} %get-tuple-element.325.refs_0_, bf16[512,768]{1,0:T(8,128)(2,1)S(1)} %collective-permute-done.42.refs_1_, bf16[512,3072]{1,0:T(8,128)(2,1)S(1)} %get-tuple-element.343.refs_2_.dup_ref, ...), custom_call_target="tpu_custom_call" | custom-call | flops 720000000 | tf_op jit(solution)/shard_map/weight_grad/pallas_call | solution.py:881
  148.3 9.9 %back_to_heads.1 = (f32[512,768]{1,0:T(8,128)S(1)}, bf16[512,768]{1,0:T(8,128)(2,1)S(1)}, bf16[512,384]{1,0:T(8,128)(2,1)S(1)}, bf16[512,768]{1,0:T(8,128)(2,1)S...) custom-call(s32[3]{0:T(128)S(1)} %pad_add_fusion.ids_ref, ...), custom_call_target="tpu_custom_call" | custom-call | flops 7080000000 | tf_op jit(solution)/shard_map/back_to_heads/pallas_call | solution.py:684
  160.5 2.2 collective-permute-start.49
  164.4 5.7 %collective-permute-done.48.refs_2_ = bf16[2,2,104,128]{3,2,1,0:T(8,128)(2,1)S(1)} collective-permute-done((bf16[2,2,104,128]{3,2,1,0:T(8,128)(2,1)S(1)}, bf16[2,2,104,128]{3,2,1,0:T(8,128)(2,1)S(1)}, u32[]{:S(2)}, u32[]{:S(2)}) %collective-permute-start.48) | collective-permute-done | bytes 106528 | tf_op jit(solution)/shard_map/ppermute | solution.py:28
  172.7 4.2 %collective-permute-done.54 = bf16[4,192,384]{2,1,0:T(8,128)(2,1)S(1)} collective-permute-done((bf16[4,192,384]{2,1,0:T(8,128)(2,1)S(1)}, bf16[4,192,384]{2,1,0:T(8,128)(2,1)S(1)}, u32[]{:S(2)}, u32[]{:S(2)}) %collective-permute-start.54) | collective-permute-done | bytes 589856 | tf_op jit(solution)/shard_map/ppermute | solution.py:28
  177.3 3.0 %collective-permute-start.55 = (bf16[2,2,104,128]{3,2,1,0:T(8,128)(2,1)S(1)}, bf16[2,2,104,128]{3,2,1,0:T(8,128)(2,1)S(1)}, u32[]{:S(2)}, u32[]{:S(2)}) collective-permute-start(bf16[2,2,104,128]{3,2,1,0:T(8,128)(2,1)S(1)} %get-tuple-element.371), channel_id=1, source_target_pairs={{0,2},{1,3},{2,0},{3,1},{4,6},{5,7},{6,4},{7,5},{8,10},{9,11},{10,... | collective-permute-start | bytes 319496 | tf_op jit(solution)/shard_map/ppermute | solution.py:28
  180.3 2.4 collective-permute-start.57
  182.9 1.8 collective-permute-start.60
  185.0 8.8 %intra_backward.1 = (bf16[512,768]{1,0:T(8,128)(2,1)S(1)}, bf16[512,384]{1,0:T(8,128)(2,1)S(1)}, f32[512,768]{1,0:T(8,128)S(1)}, f32[512,768]{1,0:T(8,128)S(1)}) custom-call(s32[3]{0:T(128)S(1)} %pad_add_fusion.ids_ref, bf16[512,768]{1,0:T(8,128)(2,1)S(1)} %get-tuple-element.377.q_ref, bf16[512,768]{1,0:T(8,128)(2,1)S(1)} %get-tuple-element.250.k_ref, ...), custom_call_target="tpu_custom_call" | custom-call | flops 6179999744 | tf_op jit(solution)/shard_map/intra_backward/pallas_call | solution.py:753
  193.9 1.8 collective-permute-start.58
  197.1 2.5 collective-permute-done.59
  201.8 2.4 weight_grad.6
  205.3 2.1 collective-permute-start.62
  207.3 4.1 %inter_backward.1.dkv_ref = bf16[2,512,768]{2,1,0:T(8,128)(2,1)S(1)} custom-call(s32[3]{0:T(128)S(1)} %pad_add_fusion.ids_ref, bf16[512,768]{1,0:T(8,128)(2,1)S(1)} %get-tuple-element.250.k_ref, bf16[512,768]{1,0:T(8,128)(2,1)S(1)} %get-tuple-element.267.v_ref, f32[512,768]{1,0:T(8,128)S(1)} %get-tuple-element.380.dk_ref, ...), custom_call_target="tpu_custom_call" | custom-call | flops 2760000000 | tf_op jit(solution)/shard_map/inter_backward/pallas_call | solution.py:801
  219.7 2.7 %weight_grad.7 = (bf16[2,8,24,768]{3,2,1,0:T(8,128)(2,1)S(1)}, bf16[1,8,48,768]{3,2,1,0:T(8,128)(2,1)S(1)}) custom-call(s32[3]{0:T(128)S(1)} %pad_add_fusion.ids_ref, bf16[512,768]{1,0:T(8,128)(2,1)S(1)} %copy-done.8, bf16[512,768]{1,0:T(8,128)(2,1)S(1)} %copy-done.17, bf16[512,768]{1,0:T(8,128)(2,1)S(1)} %copy-done.9, ...), custom_call_target="tpu_custom_call" | custom-call | flops 2016000000 | tf_op jit(solution)/shard_map/weight_grad/pallas_call | solution.py:881
  224.6 4.2 %input_grad.1 = f32[512,768]{1,0:T(8,128)} custom-call(s32[3]{0:T(128)S(1)} %pad_add_fusion.ids_ref, bf16[512,768]{1,0:T(8,128)(2,1)S(1)} %copy-done.11, bf16[2,512,768]{2,1,0:T(8,128)(2,1)S(1)} %copy-done.3, f32[512,768]{1,0:T(8,128)S(1)} %copy-done.5, bf16[768,1792]{1,0:T(8,128)(2,1)S(1)} %bitcast.107, bf16[768,1536]{1,0:T(8,128)(2,1)S(1)} %bitcast.111), custom_call_target="tpu_custom_call" | custom-call | flops 2400000000 | tf_op jit(solution)/shard_map/input_grad/pallas_call | solution.py:825
  228.8 3.5 %collective-permute-done.64 = bf16[8,48,896]{2,1,0:T(8,128)(2,1)S(1)} collective-permute-done((bf16[8,48,896]{2,1,0:T(8,128)(2,1)}, bf16[8,48,896]{2,1,0:T(8,128)(2,1)S(1)}, u32[]{:S(2)}, u32[]{:S(2)}) %collective-permute-start.64) | collective-permute-done | bytes 688160 | tf_op jit(solution)/shard_map/ppermute | solution.py:28
  240.1 2.9 %collective-permute-done.65 = bf16[4,48,896]{2,1,0:T(8,128)(2,1)S(1)} collective-permute-done((bf16[4,48,896]{2,1,0:T(8,128)(2,1)S(1)}, bf16[4,48,896]{2,1,0:T(8,128)(2,1)S(1)}, u32[]{:S(2)}, u32[]{:S(2)}) %collective-permute-start.65) | collective-permute-done | bytes 344096 | tf_op jit(solution)/shard_map/ppermute | solution.py:28
  248.2 2.0 collective-permute-done.70
  252.1 2.6 collective-permute-start.81
  259.3 2.2 collective-permute-done.80
  (331 shorter events, 102.0 us)
Async XLA Ops:
  1.5 7.9 %collective-permute-start = (bf16[1,24,1536]{2,1,0:T(8,128)(2,1)S(1)}, bf16[1,24,1536]{2,1,0:T(8,128)(2,1)S(1)}, u32[]{:S(2)}, u32[]{:S(2)}) collective-permute-start(bf16[1,24,1536]{2,1,0:T(8,128)(2,1)S(1)} %slice_bitcast_fusion.15), channel_id=1, source_target_pairs={{0,4},{1,5},{2,6},{3,7},{4,0},{5,1},{6,2},{7,3},{8,12},{9,13},{10,... | collective-permute-start | bytes 221192 | tf_op jit(solution)/shard_map/ppermute | solution.py:28
  5.6 31.2 %collective-permute-start.10 = (bf16[512,768]{1,0:T(8,128)(2,1)}, bf16[512,768]{1,0:T(8,128)(2,1)S(1)}, u32[]{:S(2)}, u32[]{:S(2)}) collective-permute-start(bf16[512,768]{1,0:T(8,128)(2,1)} %refs_0_.1), channel_id=1, source_target_pairs={{0,8},{8,0},{16,24},{24,16},{1,9},{9,1},{17,25},{25,17},{2,10},{10... | collective-permute-start | bytes 2359304 | tf_op jit(solution)/shard_map/ppermute | solution.py:28
  22.0 8.8 %collective-permute-start.6 = (bf16[8,24,768]{2,1,0:T(8,128)(2,1)S(1)}, bf16[8,24,768]{2,1,0:T(8,128)(2,1)S(1)}, u32[]{:S(2)}, u32[]{:S(2)}) collective-permute-start(bf16[8,24,768]{2,1,0:T(8,128)(2,1)S(1)} %pad_maximum_fusion.21), channel_id=1, source_target_pairs={{0,1},{1,0},{2,3},{3,2},{4,5},{5,4},{6,7},{7,6},{8,9},{9,8},{10,11... | collective-permute-start | bytes 884744 | tf_op jit(solution)/shard_map/ppermute | solution.py:28
  27.4 7.9 %collective-permute-start.11 = (bf16[1,24,3072]{2,1,0:T(8,128)(2,1)}, bf16[1,24,3072]{2,1,0:T(8,128)(2,1)S(1)}, u32[]{:S(2)}, u32[]{:S(2)}) collective-permute-start(bf16[1,24,3072]{2,1,0:T(8,128)(2,1)} %bitcast.15), channel_id=1, source_target_pairs={{0,4},{1,5},{2,6},{3,7},{4,0},{5,1},{6,2},{7,3},{8,12},{9,13},{10,... | collective-permute-start | bytes 442376 | tf_op jit(solution)/shard_map/ppermute | solution.py:28
  31.5 12.0 %collective-permute-start.9 = (bf16[4,24,896]{2,1,0:T(8,128)(2,1)S(1)}, bf16[4,24,896]{2,1,0:T(8,128)(2,1)S(1)}, u32[]{:S(2)}, u32[]{:S(2)}) collective-permute-start(bf16[4,24,896]{2,1,0:T(8,128)(2,1)S(1)} %get-tuple-element.487), channel_id=1, source_target_pairs={{0,16},{8,24},{16,0},{24,8},{1,17},{9,25},{17,1},{25,9},{2,18},{10... | collective-permute-start | bytes 516104 | tf_op jit(solution)/shard_map/ppermute | solution.py:28
  35.3 8.2 %collective-permute-start.8 = (bf16[4,24,896]{2,1,0:T(8,128)(2,1)S(1)}, bf16[4,24,896]{2,1,0:T(8,128)(2,1)S(1)}, u32[]{:S(2)}, u32[]{:S(2)}) collective-permute-start(bf16[4,24,896]{2,1,0:T(8,128)(2,1)S(1)} %get-tuple-element.488), channel_id=1, source_target_pairs={{0,1},{1,0},{2,3},{3,2},{4,5},{5,4},{6,7},{7,6},{8,9},{9,8},{10,11... | collective-permute-start | bytes 516104 | tf_op jit(solution)/shard_map/ppermute | solution.py:28
  43.6 13.2 %collective-permute-start.14 = (bf16[8,24,896]{2,1,0:T(8,128)(2,1)S(1)}, bf16[8,24,896]{2,1,0:T(8,128)(2,1)S(1)}, u32[]{:S(2)}, u32[]{:S(2)}) collective-permute-start(bf16[8,24,896]{2,1,0:T(8,128)(2,1)S(1)} %get-tuple-element.256), channel_id=1, source_target_pairs={{0,16},{8,24},{16,0},{24,8},{1,17},{9,25},{17,1},{25,9},{2,18},{10... | collective-permute-start | bytes 1032200 | tf_op jit(solution)/shard_map/ppermute | solution.py:28
  44.5 12.3 %collective-permute-start.15 = (bf16[8,24,896]{2,1,0:T(8,128)(2,1)S(1)}, bf16[8,24,896]{2,1,0:T(8,128)(2,1)S(1)}, u32[]{:S(2)}, u32[]{:S(2)}) collective-permute-start(bf16[8,24,896]{2,1,0:T(8,128)(2,1)S(1)} %get-tuple-element.257), channel_id=1, source_target_pairs={{0,1},{1,0},{2,3},{3,2},{4,5},{5,4},{6,7},{7,6},{8,9},{9,8},{10,11... | collective-permute-start | bytes 1032200 | tf_op jit(solution)/shard_map/ppermute | solution.py:28
  46.0 8.9 %collective-permute-start.16 = (bf16[2,2,104,128]{3,2,1,0:T(8,128)(2,1)S(1)}, bf16[2,2,104,128]{3,2,1,0:T(8,128)(2,1)S(1)}, u32[]{:S(2)}, u32[]{:S(2)}) collective-permute-start(bf16[2,2,104,128]{3,2,1,0:T(8,128)(2,1)S(1)} %get-tuple-element.258), channel_id=1, source_target_pairs={{0,2},{1,3},{2,0},{3,1},{4,6},{5,7},{6,4},{7,5},{8,10},{9,11},{10,... | collective-permute-start | bytes 319496 | tf_op jit(solution)/shard_map/ppermute | solution.py:28
  46.0 9.5 %collective-permute-start.17 = (bf16[2,2,104,128]{3,2,1,0:T(8,128)(2,1)S(1)}, bf16[2,2,104,128]{3,2,1,0:T(8,128)(2,1)S(1)}, u32[]{:S(2)}, u32[]{:S(2)}) collective-permute-start(bf16[2,2,104,128]{3,2,1,0:T(8,128)(2,1)S(1)} %get-tuple-element.259), channel_id=1, source_target_pairs={{0,4},{1,5},{2,6},{3,7},{4,0},{5,1},{6,2},{7,3},{8,12},{9,13},{10,... | collective-permute-start | bytes 319496 | tf_op jit(solution)/shard_map/ppermute | solution.py:28
  49.1 7.7 %collective-permute-start.18 = (bf16[2,2,104,128]{3,2,1,0:T(8,128)(2,1)S(1)}, bf16[2,2,104,128]{3,2,1,0:T(8,128)(2,1)S(1)}, u32[]{:S(2)}, u32[]{:S(2)}) collective-permute-start(bf16[2,2,104,128]{3,2,1,0:T(8,128)(2,1)S(1)} %get-tuple-element.260), channel_id=1, source_target_pairs={{0,6},{1,7},{2,4},{3,5},{4,2},{5,3},{6,0},{7,1},{8,14},{9,15},{10,... | collective-permute-start | bytes 319496 | tf_op jit(solution)/shard_map/ppermute | solution.py:28
  56.9 14.9 %collective-permute-start.25 = (bf16[4,2,104,128]{3,2,1,0:T(8,128)(2,1)S(1)}, bf16[4,2,104,128]{3,2,1,0:T(8,128)(2,1)S(1)}, u32[]{:S(2)}, u32[]{:S(2)}) collective-permute-start(bf16[4,2,104,128]{3,2,1,0:T(8,128)(2,1)S(1)} %pad_maximum_fusion.27), channel_id=1, source_target_pairs={{0,1},{1,0},{2,3},{3,2},{4,5},{5,4},{6,7},{7,6},{8,9},{9,8},{10,11... | collective-permute-start | bytes 638984 | tf_op jit(solution)/shard_map/ppermute | solution.py:28
  62.6 9.5 %collective-permute-start.22 = (bf16[4,24,1536]{2,1,0:T(8,128)(2,1)S(1)}, bf16[4,24,1536]{2,1,0:T(8,128)(2,1)S(1)}, u32[]{:S(2)}, u32[]{:S(2)}) collective-permute-start(bf16[4,24,1536]{2,1,0:T(8,128)(2,1)S(1)} %get-tuple-element.274), channel_id=1, source_target_pairs={{0,1},{1,0},{2,3},{3,2},{4,5},{5,4},{6,7},{7,6},{8,9},{9,8},{10,11... | collective-permute-start | bytes 884744 | tf_op jit(solution)/shard_map/ppermute | solution.py:28
  63.5 8.6 %collective-permute-start.23 = (bf16[4,24,1536]{2,1,0:T(8,128)(2,1)S(1)}, bf16[4,24,1536]{2,1,0:T(8,128)(2,1)S(1)}, u32[]{:S(2)}, u32[]{:S(2)}) collective-permute-start(bf16[4,24,1536]{2,1,0:T(8,128)(2,1)S(1)} %get-tuple-element.275), channel_id=1, source_target_pairs={{0,16},{8,24},{16,0},{24,8},{1,17},{9,25},{17,1},{25,9},{2,18},{10... | collective-permute-start | bytes 884744 | tf_op jit(solution)/shard_map/ppermute | solution.py:28
  72.7 12.2 %collective-permute-start.31 = (bf16[8,24,1536]{2,1,0:T(8,128)(2,1)S(1)}, bf16[8,24,1536]{2,1,0:T(8,128)(2,1)S(1)}, u32[]{:S(2)}, u32[]{:S(2)}) collective-permute-start(bf16[8,24,1536]{2,1,0:T(8,128)(2,1)S(1)} %pad_maximum_fusion.10), channel_id=1, source_target_pairs={{0,16},{8,24},{16,0},{24,8},{1,17},{9,25},{17,1},{25,9},{2,18},{10... | collective-permute-start | bytes 1769480 | tf_op jit(solution)/shard_map/ppermute | solution.py:28
  74.0 11.7 %collective-permute-start.32 = (bf16[8,24,1536]{2,1,0:T(8,128)(2,1)S(1)}, bf16[8,24,1536]{2,1,0:T(8,128)(2,1)S(1)}, u32[]{:S(2)}, u32[]{:S(2)}) collective-permute-start(bf16[8,24,1536]{2,1,0:T(8,128)(2,1)S(1)} %pad_maximum_fusion.11), channel_id=1, source_target_pairs={{0,1},{1,0},{2,3},{3,2},{4,5},{5,4},{6,7},{7,6},{8,9},{9,8},{10,11... | collective-permute-start | bytes 1769480 | tf_op jit(solution)/shard_map/ppermute | solution.py:28
  76.3 8.3 %collective-permute-start.27 = (bf16[2,2,104,128]{3,2,1,0:T(8,128)(2,1)S(1)}, bf16[2,2,104,128]{3,2,1,0:T(8,128)(2,1)S(1)}, u32[]{:S(2)}, u32[]{:S(2)}) collective-permute-start(bf16[2,2,104,128]{3,2,1,0:T(8,128)(2,1)S(1)} %get-tuple-element.285), channel_id=1, source_target_pairs={{0,4},{1,5},{2,6},{3,7},{4,0},{5,1},{6,2},{7,3},{8,12},{9,13},{10,... | collective-permute-start | bytes 319496 | tf_op jit(solution)/shard_map/ppermute | solution.py:28
  77.3 7.3 %collective-permute-start.28 = (bf16[2,2,104,128]{3,2,1,0:T(8,128)(2,1)S(1)}, bf16[2,2,104,128]{3,2,1,0:T(8,128)(2,1)S(1)}, u32[]{:S(2)}, u32[]{:S(2)}) collective-permute-start(bf16[2,2,104,128]{3,2,1,0:T(8,128)(2,1)S(1)} %get-tuple-element.286), channel_id=1, source_target_pairs={{0,6},{1,7},{2,4},{3,5},{4,2},{5,3},{6,0},{7,1},{8,14},{9,15},{10,... | collective-permute-start | bytes 319496 | tf_op jit(solution)/shard_map/ppermute | solution.py:28
  86.6 9.0 %collective-permute-start.29 = (bf16[2,96,768]{2,1,0:T(8,128)(2,1)S(1)}, bf16[2,96,768]{2,1,0:T(8,128)(2,1)S(1)}, u32[]{:S(2)}, u32[]{:S(2)}) collective-permute-start(bf16[2,96,768]{2,1,0:T(8,128)(2,1)S(1)} %pad_maximum_fusion.23), channel_id=1, source_target_pairs={{0,2},{1,3},{2,0},{3,1},{4,6},{5,7},{6,4},{7,5},{8,10},{9,11},{10,... | collective-permute-start | bytes 884744 | tf_op jit(solution)/shard_map/ppermute | solution.py:28
  95.7 8.2 %collective-permute-start.36 = (bf16[4,96,384]{2,1,0:T(8,128)(2,1)S(1)}, bf16[4,96,384]{2,1,0:T(8,128)(2,1)S(1)}, u32[]{:S(2)}, u32[]{:S(2)}) collective-permute-start(bf16[4,96,384]{2,1,0:T(8,128)(2,1)S(1)} %get-tuple-element.303), channel_id=1, source_target_pairs={{0,1},{1,0},{2,3},{3,2},{4,5},{5,4},{6,7},{7,6},{8,9},{9,8},{10,11... | collective-permute-start | bytes 884744 | tf_op jit(solution)/shard_map/ppermute | solution.py:28
  97.2 8.2 %collective-permute-start.37 = (bf16[4,96,384]{2,1,0:T(8,128)(2,1)S(1)}, bf16[4,96,384]{2,1,0:T(8,128)(2,1)S(1)}, u32[]{:S(2)}, u32[]{:S(2)}) collective-permute-start(bf16[4,96,384]{2,1,0:T(8,128)(2,1)S(1)} %get-tuple-element.304), channel_id=1, source_target_pairs={{0,16},{8,24},{16,0},{24,8},{1,17},{9,25},{17,1},{25,9},{2,18},{10... | collective-permute-start | bytes 884744 | tf_op jit(solution)/shard_map/ppermute | solution.py:28
  105.6 13.7 %collective-permute-start.38 = (bf16[8,96,384]{2,1,0:T(8,128)(2,1)S(1)}, bf16[8,96,384]{2,1,0:T(8,128)(2,1)S(1)}, u32[]{:S(2)}, u32[]{:S(2)}) collective-permute-start(bf16[8,96,384]{2,1,0:T(8,128)(2,1)S(1)} %pad_maximum_fusion.13), channel_id=1, source_target_pairs={{0,16},{8,24},{16,0},{24,8},{1,17},{9,25},{17,1},{25,9},{2,18},{10... | collective-permute-start | bytes 1769480 | tf_op jit(solution)/shard_map/ppermute | solution.py:28
  106.0 13.5 %collective-permute-start.39 = (bf16[8,96,384]{2,1,0:T(8,128)(2,1)S(1)}, bf16[8,96,384]{2,1,0:T(8,128)(2,1)S(1)}, u32[]{:S(2)}, u32[]{:S(2)}) collective-permute-start(bf16[8,96,384]{2,1,0:T(8,128)(2,1)S(1)} %pad_maximum_fusion.14), channel_id=1, source_target_pairs={{0,1},{1,0},{2,3},{3,2},{4,5},{5,4},{6,7},{7,6},{8,9},{9,8},{10,11... | collective-permute-start | bytes 1769480 | tf_op jit(solution)/shard_map/ppermute | solution.py:28
  142.8 19.9 %collective-permute-start.50 = (bf16[4,192,384]{2,1,0:T(8,128)(2,1)S(1)}, bf16[4,192,384]{2,1,0:T(8,128)(2,1)S(1)}, u32[]{:S(2)}, u32[]{:S(2)}) collective-permute-start(bf16[4,192,384]{2,1,0:T(8,128)(2,1)S(1)} %get-tuple-element.341), channel_id=1, source_target_pairs={{0,16},{8,24},{16,0},{24,8},{1,17},{9,25},{17,1},{25,9},{2,18},{10... | collective-permute-start | bytes 1769480 | tf_op jit(solution)/shard_map/ppermute | solution.py:28
  147.6 24.0 %collective-permute-start.46 = (bf16[2,3,48,1536]{3,2,1,0:T(8,128)(2,1)S(1)}, bf16[2,3,48,1536]{3,2,1,0:T(8,128)(2,1)S(1)}, u32[]{:S(2)}, u32[]{:S(2)}) collective-permute-start(bf16[2,3,48,1536]{3,2,1,0:T(8,128)(2,1)S(1)} %slice.454), channel_id=1, source_target_pairs={{0,1},{1,0},{2,3},{3,2},{4,5},{5,4},{6,7},{7,6},{8,9},{9,8},{10,11... | collective-permute-start | bytes 2654216 | tf_op jit(solution)/shard_map/ppermute | solution.py:28
  159.5 10.5 %collective-permute-start.48 = (bf16[2,2,104,128]{3,2,1,0:T(8,128)(2,1)S(1)}, bf16[2,2,104,128]{3,2,1,0:T(8,128)(2,1)S(1)}, u32[]{:S(2)}, u32[]{:S(2)}) collective-permute-start(bf16[2,2,104,128]{3,2,1,0:T(8,128)(2,1)S(1)} %get-tuple-element.351), channel_id=1, source_target_pairs={{0,4},{1,5},{2,6},{3,7},{4,0},{5,1},{6,2},{7,3},{8,12},{9,13},{10,... | collective-permute-start | bytes 319496 | tf_op jit(solution)/shard_map/ppermute | solution.py:28
  160.5 9.5 %collective-permute-start.49 = (bf16[2,2,104,128]{3,2,1,0:T(8,128)(2,1)S(1)}, bf16[2,2,104,128]{3,2,1,0:T(8,128)(2,1)S(1)}, u32[]{:S(2)}, u32[]{:S(2)}) collective-permute-start(bf16[2,2,104,128]{3,2,1,0:T(8,128)(2,1)S(1)} %get-tuple-element.352), channel_id=1, source_target_pairs={{0,6},{1,7},{2,4},{3,5},{4,2},{5,3},{6,0},{7,1},{8,14},{9,15},{10,... | collective-permute-start | bytes 319496 | tf_op jit(solution)/shard_map/ppermute | solution.py:28
  162.8 14.0 %collective-permute-start.54 = (bf16[4,192,384]{2,1,0:T(8,128)(2,1)S(1)}, bf16[4,192,384]{2,1,0:T(8,128)(2,1)S(1)}, u32[]{:S(2)}, u32[]{:S(2)}) collective-permute-start(bf16[4,192,384]{2,1,0:T(8,128)(2,1)S(1)} %get-tuple-element.356), channel_id=1, source_target_pairs={{0,16},{8,24},{16,0},{24,8},{1,17},{9,25},{17,1},{25,9},{2,18},{10... | collective-permute-start | bytes 1769480 | tf_op jit(solution)/shard_map/ppermute | solution.py:28
  172.0 10.7 %collective-permute-start.51 = (bf16[2,1,48,1536]{3,2,1,0:T(8,128)(2,1)S(1)}, bf16[2,1,48,1536]{3,2,1,0:T(8,128)(2,1)S(1)}, u32[]{:S(2)}, u32[]{:S(2)}) collective-permute-start(bf16[2,1,48,1536]{3,2,1,0:T(8,128)(2,1)S(1)} %slice.452), channel_id=1, source_target_pairs={{0,1},{1,0},{2,3},{3,2},{4,5},{5,4},{6,7},{7,6},{8,9},{9,8},{10,11... | collective-permute-start | bytes 884744 | tf_op jit(solution)/shard_map/ppermute | solution.py:28
  177.3 16.5 %collective-permute-start.55 = (bf16[2,2,104,128]{3,2,1,0:T(8,128)(2,1)S(1)}, bf16[2,2,104,128]{3,2,1,0:T(8,128)(2,1)S(1)}, u32[]{:S(2)}, u32[]{:S(2)}) collective-permute-start(bf16[2,2,104,128]{3,2,1,0:T(8,128)(2,1)S(1)} %get-tuple-element.371), channel_id=1, source_target_pairs={{0,2},{1,3},{2,0},{3,1},{4,6},{5,7},{6,4},{7,5},{8,10},{9,11},{10,... | collective-permute-start | bytes 319496 | tf_op jit(solution)/shard_map/ppermute | solution.py:28
  180.3 13.5 %collective-permute-start.56 = (bf16[2,2,104,128]{3,2,1,0:T(8,128)(2,1)S(1)}, bf16[2,2,104,128]{3,2,1,0:T(8,128)(2,1)S(1)}, u32[]{:S(2)}, u32[]{:S(2)}) collective-permute-start(bf16[2,2,104,128]{3,2,1,0:T(8,128)(2,1)S(1)} %get-tuple-element.372), channel_id=1, source_target_pairs={{0,4},{1,5},{2,6},{3,7},{4,0},{5,1},{6,2},{7,3},{8,12},{9,13},{10,... | collective-permute-start | bytes 319496 | tf_op jit(solution)/shard_map/ppermute | solution.py:28
  180.3 13.5 %collective-permute-start.57 = (bf16[2,2,104,128]{3,2,1,0:T(8,128)(2,1)S(1)}, bf16[2,2,104,128]{3,2,1,0:T(8,128)(2,1)S(1)}, u32[]{:S(2)}, u32[]{:S(2)}) collective-permute-start(bf16[2,2,104,128]{3,2,1,0:T(8,128)(2,1)S(1)} %get-tuple-element.373), channel_id=1, source_target_pairs={{0,6},{1,7},{2,4},{3,5},{4,2},{5,3},{6,0},{7,1},{8,14},{9,15},{10,... | collective-permute-start | bytes 319496 | tf_op jit(solution)/shard_map/ppermute | solution.py:28
  182.9 14.2 %collective-permute-start.60 = (bf16[4,48,1536]{2,1,0:T(8,128)(2,1)S(1)}, bf16[4,48,1536]{2,1,0:T(8,128)(2,1)S(1)}, u32[]{:S(2)}, u32[]{:S(2)}) collective-permute-start(bf16[4,48,1536]{2,1,0:T(8,128)(2,1)S(1)} %pad_maximum_fusion.15), channel_id=1, source_target_pairs={{0,16},{8,24},{16,0},{24,8},{1,17},{9,25},{17,1},{25,9},{2,18},{10... | collective-permute-start | bytes 1769480 | tf_op jit(solution)/shard_map/ppermute | solution.py:28
  184.7 14.9 %collective-permute-start.59 = (bf16[4,192,384]{2,1,0:T(8,128)(2,1)S(1)}, bf16[4,192,384]{2,1,0:T(8,128)(2,1)S(1)}, u32[]{:S(2)}, u32[]{:S(2)}) collective-permute-start(bf16[4,192,384]{2,1,0:T(8,128)(2,1)S(1)} %fusion.1), channel_id=1, source_target_pairs={{0,1},{1,0},{2,3},{3,2},{4,5},{5,4},{6,7},{7,6},{8,9},{9,8},{10,11... | collective-permute-start | bytes 1769480 | tf_op jit(solution)/shard_map/ppermute | solution.py:28
  193.9 13.4 %collective-permute-start.58 = (bf16[4,2,104,128]{3,2,1,0:T(8,128)(2,1)S(1)}, bf16[4,2,104,128]{3,2,1,0:T(8,128)(2,1)S(1)}, u32[]{:S(2)}, u32[]{:S(2)}) collective-permute-start(bf16[4,2,104,128]{3,2,1,0:T(8,128)(2,1)S(1)} %pad_maximum_fusion.30), channel_id=1, source_target_pairs={{0,1},{1,0},{2,3},{3,2},{4,5},{5,4},{6,7},{7,6},{8,9},{9,8},{10,11... | collective-permute-start | bytes 638984 | tf_op jit(solution)/shard_map/ppermute | solution.py:28
  205.3 7.8 %collective-permute-start.62 = (bf16[2,48,1536]{2,1,0:T(8,128)(2,1)S(1)}, bf16[2,48,1536]{2,1,0:T(8,128)(2,1)S(1)}, u32[]{:S(2)}, u32[]{:S(2)}) collective-permute-start(bf16[2,48,1536]{2,1,0:T(8,128)(2,1)S(1)} %get-tuple-element.395), channel_id=1, source_target_pairs={{0,2},{1,3},{2,0},{3,1},{4,6},{5,7},{6,4},{7,5},{8,10},{9,11},{10,... | collective-permute-start | bytes 884744 | tf_op jit(solution)/shard_map/ppermute | solution.py:28
  213.9 18.4 %collective-permute-start.64 = (bf16[8,48,896]{2,1,0:T(8,128)(2,1)}, bf16[8,48,896]{2,1,0:T(8,128)(2,1)S(1)}, u32[]{:S(2)}, u32[]{:S(2)}) collective-permute-start(bf16[8,48,896]{2,1,0:T(8,128)(2,1)} %slice_bitcast_fusion.2), channel_id=1, source_target_pairs={{0,16},{8,24},{16,0},{24,8},{1,17},{9,25},{17,1},{25,9},{2,18},{10... | collective-permute-start | bytes 2064392 | tf_op jit(solution)/shard_map/ppermute | solution.py:28
  215.2 21.2 %collective-permute-start.67 = (bf16[1,48,1536]{2,1,0:T(8,128)(2,1)}, bf16[1,48,1536]{2,1,0:T(8,128)(2,1)S(1)}, u32[]{:S(2)}, u32[]{:S(2)}) collective-permute-start(bf16[1,48,1536]{2,1,0:T(8,128)(2,1)} %add_convert_fusion.12), channel_id=1, source_target_pairs={{0,4},{1,5},{2,6},{3,7},{4,0},{5,1},{6,2},{7,3},{8,12},{9,13},{10,... | collective-permute-start | bytes 442376 | tf_op jit(solution)/shard_map/ppermute | solution.py:28
  216.4 17.5 %collective-permute-start.69 = (bf16[2,192,384]{2,1,0:T(8,128)(2,1)}, bf16[2,192,384]{2,1,0:T(8,128)(2,1)S(1)}, u32[]{:S(2)}, u32[]{:S(2)}) collective-permute-start(bf16[2,192,384]{2,1,0:T(8,128)(2,1)} %get-tuple-element.400), channel_id=1, source_target_pairs={{0,2},{1,3},{2,0},{3,1},{4,6},{5,7},{6,4},{7,5},{8,10},{9,11},{10,... | collective-permute-start | bytes 884744 | tf_op jit(solution)/shard_map/ppermute | solution.py:28
  222.5 16.1 %collective-permute-start.66 = (bf16[8,24,768]{2,1,0:T(8,128)(2,1)S(1)}, bf16[8,24,768]{2,1,0:T(8,128)(2,1)S(1)}, u32[]{:S(2)}, u32[]{:S(2)}) collective-permute-start(bf16[8,24,768]{2,1,0:T(8,128)(2,1)S(1)} %slice_bitcast_fusion.11), channel_id=1, source_target_pairs={{0,16},{8,24},{16,0},{24,8},{1,17},{9,25},{17,1},{25,9},{2,18},{10... | collective-permute-start | bytes 884744 | tf_op jit(solution)/shard_map/ppermute | solution.py:28
  223.3 11.9 %collective-permute-start.68 = (bf16[4,48,768]{2,1,0:T(8,128)(2,1)S(1)}, bf16[4,48,768]{2,1,0:T(8,128)(2,1)S(1)}, u32[]{:S(2)}, u32[]{:S(2)}) collective-permute-start(bf16[4,48,768]{2,1,0:T(8,128)(2,1)S(1)} %slice_bitcast_fusion.10), channel_id=1, source_target_pairs={{0,1},{1,0},{2,3},{3,2},{4,5},{5,4},{6,7},{7,6},{8,9},{9,8},{10,11... | collective-permute-start | bytes 884744 | tf_op jit(solution)/shard_map/ppermute | solution.py:28
  232.5 10.5 %collective-permute-start.65 = (bf16[4,48,896]{2,1,0:T(8,128)(2,1)S(1)}, bf16[4,48,896]{2,1,0:T(8,128)(2,1)S(1)}, u32[]{:S(2)}, u32[]{:S(2)}) collective-permute-start(bf16[4,48,896]{2,1,0:T(8,128)(2,1)S(1)} %get-tuple-element.409), channel_id=1, source_target_pairs={{0,1},{1,0},{2,3},{3,2},{4,5},{5,4},{6,7},{7,6},{8,9},{9,8},{10,11... | collective-permute-start | bytes 1032200 | tf_op jit(solution)/shard_map/ppermute | solution.py:28
  233.9 11.5 %collective-permute-start.73 = (bf16[1,192,384]{2,1,0:T(8,128)(2,1)S(1)}, bf16[1,192,384]{2,1,0:T(8,128)(2,1)S(1)}, u32[]{:S(2)}, u32[]{:S(2)}) collective-permute-start(bf16[1,192,384]{2,1,0:T(8,128)(2,1)S(1)} %add_convert_fusion.10), channel_id=1, source_target_pairs={{0,4},{1,5},{2,6},{3,7},{4,0},{5,1},{6,2},{7,3},{8,12},{9,13},{10,... | collective-permute-start | bytes 442376 | tf_op jit(solution)/shard_map/ppermute | solution.py:28
  235.3 8.8 %collective-permute-start.74 = (bf16[2,48,768]{2,1,0:T(8,128)(2,1)S(1)}, bf16[2,48,768]{2,1,0:T(8,128)(2,1)S(1)}, u32[]{:S(2)}, u32[]{:S(2)}) collective-permute-start(bf16[2,48,768]{2,1,0:T(8,128)(2,1)S(1)} %get-tuple-element.413), channel_id=1, source_target_pairs={{0,2},{1,3},{2,0},{3,1},{4,6},{5,7},{6,4},{7,5},{8,10},{9,11},{10,... | collective-permute-start | bytes 442376 | tf_op jit(solution)/shard_map/ppermute | solution.py:28
  236.5 11.5 %collective-permute-start.71 = (bf16[48,1536]{1,0:T(8,128)(2,1)S(1)}, bf16[48,1536]{1,0:T(8,128)(2,1)S(1)}, u32[]{:S(2)}, u32[]{:S(2)}) collective-permute-start(bf16[48,1536]{1,0:T(8,128)(2,1)S(1)} %fusion.25), channel_id=1, source_target_pairs={{0,16},{8,24},{16,0},{24,8},{1,17},{9,25},{17,1},{25,9},{2,18},{10... | collective-permute-start | bytes 442376 | tf_op jit(solution)/shard_map/ppermute | solution.py:28
  238.7 8.2 %collective-permute-start.72 = (bf16[4,24,768]{2,1,0:T(8,128)(2,1)S(1)}, bf16[4,24,768]{2,1,0:T(8,128)(2,1)S(1)}, u32[]{:S(2)}, u32[]{:S(2)}) collective-permute-start(bf16[4,24,768]{2,1,0:T(8,128)(2,1)S(1)} %get-tuple-element.417), channel_id=1, source_target_pairs={{0,1},{1,0},{2,3},{3,2},{4,5},{5,4},{6,7},{7,6},{8,9},{9,8},{10,11... | collective-permute-start | bytes 442376 | tf_op jit(solution)/shard_map/ppermute | solution.py:28
  245.6 10.3 %collective-permute-start.76 = (bf16[192,384]{1,0:T(8,128)(2,1)S(1)}, bf16[192,384]{1,0:T(8,128)(2,1)S(1)}, u32[]{:S(2)}, u32[]{:S(2)}) collective-permute-start(bf16[192,384]{1,0:T(8,128)(2,1)S(1)} %fusion.26), channel_id=1, source_target_pairs={{0,16},{8,24},{16,0},{24,8},{1,17},{9,25},{17,1},{25,9},{2,18},{10... | collective-permute-start | bytes 442376 | tf_op jit(solution)/shard_map/ppermute | solution.py:28
  250.6 7.7 %collective-permute-start.82 = (bf16[48,768]{1,0:T(8,128)(2,1)S(1)}, bf16[48,768]{1,0:T(8,128)(2,1)S(1)}, u32[]{:S(2)}, u32[]{:S(2)}) collective-permute-start(bf16[48,768]{1,0:T(8,128)(2,1)S(1)} %fusion.29), channel_id=1, source_target_pairs={{0,16},{8,24},{16,0},{24,8},{1,17},{9,25},{17,1},{25,9},{2,18},{10... | collective-permute-start | bytes 221192 | tf_op jit(solution)/shard_map/ppermute | solution.py:28
  (66 other events, 336.0 us)

commit v7 on v6

--- a/solution.py
+++ b/solution.py
@@ -226,12 +226,12 @@
     return lax.dot_general(a, b, (((0,), (0,)), ((), ())), preferred_element_type=f32)
 
 
-def loop(count, body):
+def loop(count, body, unroll=1):
     def step(i, carry):
         body(i)
         return carry
 
-    lax.fori_loop(0, count, step, 0)
+    lax.fori_loop(0, count, step, 0, unroll=unroll)
 
 
 def rows_at(i):
@@ -300,7 +300,7 @@
         for n, wave in ((p, cos), (PAIRS + p, sin)):
             norm_scr[pl.ds(norm_row(n, fsdp), 1), :] = jnp.sum(wide * wave, axis=0, keepdims=True)
 
-    loop(PAIRS, pair)
+    loop(PAIRS, pair, 3)
     for r in range(fsdp):
         j = own ^ r
         at = pl.ds(pl.multiple_of(chunk * j, 8), chunk)
@@ -431,7 +431,7 @@
                 num_ref[at, lanes] = both[:, :LANES]
                 den_ref[at, lanes] = both[:, LANES:]
 
-            loop(PAIRS, pair)
+            loop(PAIRS, pair, 3)
 
         loop(rows // SEG, segment)
 
@@ -473,7 +473,7 @@
                 att_ref[at, lanes] = ((num_ref[at, lanes] + carried) * inverse).astype(bf16)
                 rden_ref[at, lanes] = inverse
 
-            loop(PAIRS, pair)
+            loop(PAIRS, pair, 3)
 
         loop(rows // SEG, segment)
 
@@ -744,7 +744,7 @@
                 d_q += sine * (dot_nt(dn, sin_part) + dd * norm_sin)
                 dq_ref[at, lanes] = jnp.where(qs.astype(f32) > 0.0, d_q, 0.0).astype(bf16)
 
-            loop(PAIRS, pair)
+            loop(PAIRS, pair, 3)
             theirs = 1 - ids_ref[0]
             dq_half_ref[at, :] = dq_ref[at, pl.ds(pl.multiple_of(theirs * (D // 2), 128), D // 2)]
 
@@ -794,7 +794,7 @@
                 out_ref[core, at, lanes] = jnp.where(ks > 0.0, d_k, 0.0).astype(bf16)
                 out_ref[1 - core, at, lanes] = d_v.astype(bf16)
 
-            loop(PAIRS, pair)
+            loop(PAIRS, pair, 3)
 
         loop(rows // SEG, segment)
 

time: 268 us -> 262 us (0.978)
  Pallas kernels: 78 us -> 68.5 us
  waiting for transfers between devices: 66.1 us -> 73.9 us
  starting transfers between devices: 91.4 us -> 88 us
    ppermute x88, waiting for transfers between devices: 66.1 us -> 73.9 us  [exchange(): return lax.ppermute(x, axis, [(i, i ^ offset) for i in range(size)])]
    ppermute x88, starting transfers between devices: 91.4 us -> 88 us  [exchange(): return lax.ppermute(x, axis, [(i, i ^ offset) for i in range(size)])]
  transfers between devices with their start and end apart: 88 -> 88, of which waited for: 35 -> 40; matrix products, arithmetic and copies ran while one was open for 8% -> 9% of each run, Pallas kernels for 29% -> 26%
where the time goes in v7:
time: 262 us
  starting transfers between devices  88 us (34%)
  waiting for transfers between devices  73.9 us (28%)
  Pallas kernels  68.5 us (26%)
  other arithmetic  14.9 us (6%)
  local copies, waits for them, and re-layouts  11.1 us (4%)
  matrix products  3.7 us (1%)
    ppermute x88, starting transfers between devices, exchange(): return lax.ppermute(x, axis, [(i, i ^ offset) for i in range(size)])  88 us
    ppermute x88, waiting for transfers between devices, exchange(): return lax.ppermute(x, axis, [(i, i ^ offset) for i in range(size)])  73.9 us
    pallas_call x4, Pallas kernels, weight_grad(): call(kernel, 'weight_grad', tuple((shape_of((n, fsdp, share // n, width),...  12.8 us
    pallas_call x1, Pallas kernels, back_to_heads(): call(kernel, 'back_to_heads', (shape_of((rows, D), f32), shape_of((rows,...  8.44 us
    pallas_call x1, Pallas kernels, intra_backward(): call(kernel, 'intra_backward', (shape_of((rows, D), bf16), shape_of((rows...  7.67 us
    pallas_call x1, Pallas kernels, expand(): call(kernel, 'expand', (shape_of((rows, D), f32), shape_of((rows, LANES),...  7.45 us
    pallas_call x1, Pallas kernels, contract(): call(kernel, 'contract', (shape_of((rows, D), bf16), shape_of((rows, D),...  5.33 us
  transfers between devices with their start and end apart: 88, of which 40 were waited for; matrix products, arithmetic and copies ran while one was open for 9% of the time, Pallas kernels for 26%

profile of v7, /device:TPU:0, one launch (start us, length us, event | category | flops | bytes accessed | tf_op | source)
XLA Modules:
  0.0 261.8 jit_solution(7425256785309390612)
XLA Ops:
  1.5 4.0 %collective-permute-start = (bf16[1,24,1536]{2,1,0:T(8,128)(2,1)S(1)}, bf16[1,24,1536]{2,1,0:T(8,128)(2,1)S(1)}, u32[]{:S(2)}, u32[]{:S(2)}) collective-permute-start(bf16[1,24,1536]{2,1,0:T(8,128)(2,1)S(1)} %slice_bitcast_fusion.15), channel_id=1, source_target_pairs={{0,4},{1,5},{2,6},{3,7},{4,0},{5,1},{6,2},{7,3},{8,12},{9,13},{10,... | collective-permute-start | bytes 221192 | tf_op jit(solution)/shard_map/ppermute | solution.py:28
  12.4 1.8 fusion.22
  19.3 2.3 collective-permute-start.2
  27.4 3.0 %collective-permute-start.11 = (bf16[1,24,3072]{2,1,0:T(8,128)(2,1)}, bf16[1,24,3072]{2,1,0:T(8,128)(2,1)S(1)}, u32[]{:S(2)}, u32[]{:S(2)}) collective-permute-start(bf16[1,24,3072]{2,1,0:T(8,128)(2,1)} %bitcast.15), channel_id=1, source_target_pairs={{0,4},{1,5},{2,6},{3,7},{4,0},{5,1},{6,2},{7,3},{8,12},{9,13},{10,... | collective-permute-start | bytes 442376 | tf_op jit(solution)/shard_map/ppermute | solution.py:28
  32.7 2.6 %collective-permute-done.11 = bf16[1,24,3072]{2,1,0:T(8,128)(2,1)S(1)} collective-permute-done((bf16[1,24,3072]{2,1,0:T(8,128)(2,1)}, bf16[1,24,3072]{2,1,0:T(8,128)(2,1)S(1)}, u32[]{:S(2)}, u32[]{:S(2)}) %collective-permute-start.11) | collective-permute-done | bytes 147488 | tf_op jit(solution)/shard_map/ppermute | solution.py:28
  38.4 3.6 %project.1 = (bf16[512,768]{1,0:T(8,128)(2,1)S(1)}, bf16[512,768]{1,0:T(8,128)(2,1)S(1)}, bf16[2,2,104,128]{3,2,1,0:T(8,128)(2,1)S(1)}, bf16[2,2,104,128]{3,2,1,...) custom-call(s32[3]{0:T(128)S(1)} %pad_add_fusion.ids_ref, ...), custom_call_target="tpu_custom_call" | custom-call | flops 6480000000 | tf_op jit(solution)/shard_map/project/pallas_call | solution.py:381
  44.5 3.1 %collective-permute-start.17 = (bf16[2,2,104,128]{3,2,1,0:T(8,128)(2,1)S(1)}, bf16[2,2,104,128]{3,2,1,0:T(8,128)(2,1)S(1)}, u32[]{:S(2)}, u32[]{:S(2)}) collective-permute-start(bf16[2,2,104,128]{3,2,1,0:T(8,128)(2,1)S(1)} %get-tuple-element.259), channel_id=1, source_target_pairs={{0,4},{1,5},{2,6},{3,7},{4,0},{5,1},{6,2},{7,3},{8,12},{9,13},{10,... | collective-permute-start | bytes 319496 | tf_op jit(solution)/shard_map/ppermute | solution.py:28
  48.9 4.5 %collective-permute-done.16.refs_1_ = bf16[2,2,104,128]{3,2,1,0:T(8,128)(2,1)S(1)} collective-permute-done((bf16[2,2,104,128]{3,2,1,0:T(8,128)(2,1)S(1)}, bf16[2,2,104,128]{3,2,1,0:T(8,128)(2,1)S(1)}, u32[]{:S(2)}, u32[]{:S(2)}) %collective-permute-start.16) | collective-permute-done | bytes 106528 | tf_op jit(solution)/shard_map/ppermute | solution.py:28
  56.8 3.3 %collective-permute-done.21 = bf16[2,24,3072]{2,1,0:T(8,128)(2,1)S(1)} collective-permute-done((bf16[2,24,3072]{2,1,0:T(8,128)(2,1)S(1)}, bf16[2,24,3072]{2,1,0:T(8,128)(2,1)S(1)}, u32[]{:S(2)}, u32[]{:S(2)}) %collective-permute-start.21) | collective-permute-done | bytes 294944 | tf_op jit(solution)/shard_map/ppermute | solution.py:28
  64.4 3.7 %intra_forward.1 = (bf16[512,768]{1,0:T(8,128)(2,1)S(1)}, f32[512,768]{1,0:T(8,128)S(1)}, f32[512,768]{1,0:T(8,128)S(1)}) custom-call(bf16[512,768]{1,0:T(8,128)(2,1)S(1)} %copy-done.8, bf16[768,1792]{1,0:T(8,128)(2,1)S(1)} %bitcast.103, bf16[512,768]{1,0:T(8,128)(2,1)S(1)} %get-tuple-element.250.k_ref, bf16[512,768]{1,0:T(8,128)(2,1)S(1)} %get-tuple-element.267.v_ref, ...), custom_call_target="tpu_custom_call" | custom-call | flops 3540000000 | tf_op jit(solution)/shard_map/intra_forward/pallas_call | solution.py:439
  68.8 2.2 collective-permute-done.24
  73.7 2.0 collective-permute-start.27
  75.7 2.4 collective-permute-start.28
  79.6 2.7 %collective-permute-done.28.refs_3_ = bf16[2,2,104,128]{3,2,1,0:T(8,128)(2,1)S(1)} collective-permute-done((bf16[2,2,104,128]{3,2,1,0:T(8,128)(2,1)S(1)}, bf16[2,2,104,128]{3,2,1,0:T(8,128)(2,1)S(1)}, u32[]{:S(2)}, u32[]{:S(2)}) %collective-permute-start.28) | collective-permute-done | bytes 106528 | tf_op jit(solution)/shard_map/ppermute | solution.py:28
  89.7 2.0 collective-permute-done.30.refs_4_
  91.8 1.8 collective-permute-done.29
  95.7 2.3 inter_forward.1
  98.1 3.7 %collective-permute-done.36 = bf16[4,96,384]{2,1,0:T(8,128)(2,1)S(1)} collective-permute-done((bf16[4,96,384]{2,1,0:T(8,128)(2,1)S(1)}, bf16[4,96,384]{2,1,0:T(8,128)(2,1)S(1)}, u32[]{:S(2)}, u32[]{:S(2)}) %collective-permute-start.36) | collective-permute-done | bytes 294944 | tf_op jit(solution)/shard_map/ppermute | solution.py:28
  104.9 7.5 %expand.1 = (f32[512,768]{1,0:T(8,128)S(1)}, f32[512,128]{1,0:T(8,128)S(1)}, bf16[512,768]{1,0:T(8,128)(2,1)S(1)}, bf16[512,3072]{1,0:T(8,128)(2,1)S(1)}, bf16[512,3072]{1,0:T(8,128)(2,1)S(1)}) custom-call(bf16[512,768]{1,0:T(8,128)(2,1)S(1)} %get-tuple-element.314.att_ref.refs_0_, bf16[512,768]{1,0:T(8,128)(2,1)S(1)} %copy-done.8, ...), custom_call_target="tpu_custom_call" | custom-call | flops 171000000 | tf_op jit(solution)/shard_map/expand/pallas_call | solution.py:535
  112.4 3.8 %collective-permute-done.38 = bf16[8,96,384]{2,1,0:T(8,128)(2,1)S(1)} collective-permute-done((bf16[8,96,384]{2,1,0:T(8,128)(2,1)S(1)}, bf16[8,96,384]{2,1,0:T(8,128)(2,1)S(1)}, u32[]{:S(2)}, u32[]{:S(2)}) %collective-permute-start.38) | collective-permute-done | bytes 589856 | tf_op jit(solution)/shard_map/ppermute | solution.py:28
  117.7 2.3 collective-permute-done.40.refs_1_
  123.6 5.3 %contract.1 = (bf16[512,768]{1,0:T(8,128)(2,1)}, f32[512,768]{1,0:T(8,128)S(1)}, bf16[512,768]{1,0:T(8,128)(2,1)S(1)}, bf16[512,384]{1,0:T(8,128)(2,1)S(1)}, f32[16,768]{1,0:T(8,128)S(1)}) custom-call(s32[3]{0:T(128)S(1)} %pad_add_fusion.ids_ref, bf16[512,3072]{1,0:T(8,128)(2,1)S(1)} %get-tuple-element.329.gelu_ref.refs_0_, ...), custom_call_target="tpu_custom_call" | custom-call | flops 3600000000 | tf_op jit(solution)/shard_map/contract/pallas_call | solution.py:579
  130.0 5.0 %turn.1 = (bf16[512,3072]{1,0:T(8,128)(2,1)S(1)}, bf16[512,1536]{1,0:T(8,128)(2,1)S(1)}, f32[16,768]{1,0:T(8,128)S(1)}) custom-call(s32[3]{0:T(128)S(1)} %pad_add_fusion.ids_ref, bf16[512,768]{1,0:T(8,128)(2,1)S(1)} %get-tuple-element.339.dlow_ref.refs_2_, bf16[512,3072]{1,0:T(8,128)(2,1)S(1)} %get-tuple-element.333.slope_ref, ...), custom_call_target="tpu_custom_call" | custom-call | flops 13500000256 | tf_op jit(solution)/shard_map/turn/pallas_call | solution.py:620
  135.5 4.5 %weight_grad.4 = bf16[2,8,192,384]{3,2,1,0:T(8,128)(2,1)S(1)} custom-call(s32[3]{0:T(128)S(1)} %pad_add_fusion.ids_ref, bf16[512,3072]{1,0:T(8,128)(2,1)S(1)} %get-tuple-element.329.gelu_ref.refs_0_, bf16[512,3072]{1,0:T(8,128)(2,1)S(1)} %collective-permute-done.43.refs_1_, bf16[512,768]{1,0:T(8,128)(2,1)S(1)} %get-tuple-element.339.dlow_ref.refs_2_, ...), custom_call_target="tpu_custom_call" | custom-call | flops 3600000000 | tf_op jit(solution)/shard_map/weight_grad/pallas_call | solution.py:881
  141.3 3.2 %weight_grad.5 = bf16[2,8,48,1536]{3,2,1,0:T(8,128)(2,1)S(1)} custom-call(s32[3]{0:T(128)S(1)} %pad_add_fusion.ids_ref, bf16[512,768]{1,0:T(8,128)(2,1)S(1)} %get-tuple-element.325.refs_0_, bf16[512,768]{1,0:T(8,128)(2,1)S(1)} %collective-permute-done.42.refs_1_, bf16[512,3072]{1,0:T(8,128)(2,1)S(1)} %get-tuple-element.343.refs_2_.dup_ref, ...), custom_call_target="tpu_custom_call" | custom-call | flops 720000000 | tf_op jit(solution)/shard_map/weight_grad/pallas_call | solution.py:881
  145.5 8.4 %back_to_heads.1 = (f32[512,768]{1,0:T(8,128)S(1)}, bf16[512,768]{1,0:T(8,128)(2,1)S(1)}, bf16[512,384]{1,0:T(8,128)(2,1)S(1)}, bf16[512,768]{1,0:T(8,128)(2,1)S...) custom-call(s32[3]{0:T(128)S(1)} %pad_add_fusion.ids_ref, ...), custom_call_target="tpu_custom_call" | custom-call | flops 7080000000 | tf_op jit(solution)/shard_map/back_to_heads/pallas_call | solution.py:684
  154.7 1.9 collective-permute-start.48
  156.7 1.8 collective-permute-start.49
  159.9 5.6 %collective-permute-done.48.refs_2_ = bf16[2,2,104,128]{3,2,1,0:T(8,128)(2,1)S(1)} collective-permute-done((bf16[2,2,104,128]{3,2,1,0:T(8,128)(2,1)S(1)}, bf16[2,2,104,128]{3,2,1,0:T(8,128)(2,1)S(1)}, u32[]{:S(2)}, u32[]{:S(2)}) %collective-permute-start.48) | collective-permute-done | bytes 106528 | tf_op jit(solution)/shard_map/ppermute | solution.py:28
  168.1 4.6 %collective-permute-done.54 = bf16[4,192,384]{2,1,0:T(8,128)(2,1)S(1)} collective-permute-done((bf16[4,192,384]{2,1,0:T(8,128)(2,1)S(1)}, bf16[4,192,384]{2,1,0:T(8,128)(2,1)S(1)}, u32[]{:S(2)}, u32[]{:S(2)}) %collective-permute-start.54) | collective-permute-done | bytes 589856 | tf_op jit(solution)/shard_map/ppermute | solution.py:28
  173.1 2.1 collective-permute-start.55
  180.3 7.7 %intra_backward.1 = (bf16[512,768]{1,0:T(8,128)(2,1)S(1)}, bf16[512,384]{1,0:T(8,128)(2,1)S(1)}, f32[512,768]{1,0:T(8,128)S(1)}, f32[512,768]{1,0:T(8,128)S(1)}) custom-call(s32[3]{0:T(128)S(1)} %pad_add_fusion.ids_ref, bf16[512,768]{1,0:T(8,128)(2,1)S(1)} %get-tuple-element.377.q_ref, bf16[512,768]{1,0:T(8,128)(2,1)S(1)} %get-tuple-element.250.k_ref, ...), custom_call_target="tpu_custom_call" | custom-call | flops 6179999744 | tf_op jit(solution)/shard_map/intra_backward/pallas_call | solution.py:753
  188.9 3.1 %collective-permute-done.60 = bf16[4,48,1536]{2,1,0:T(8,128)(2,1)S(1)} collective-permute-done((bf16[4,48,1536]{2,1,0:T(8,128)(2,1)S(1)}, bf16[4,48,1536]{2,1,0:T(8,128)(2,1)S(1)}, u32[]{:S(2)}, u32[]{:S(2)}) %collective-permute-start.60) | collective-permute-done | bytes 589856 | tf_op jit(solution)/shard_map/ppermute | solution.py:28
  192.0 3.1 %collective-permute-done.59 = bf16[4,192,384]{2,1,0:T(8,128)(2,1)S(1)} collective-permute-done((bf16[4,192,384]{2,1,0:T(8,128)(2,1)S(1)}, bf16[4,192,384]{2,1,0:T(8,128)(2,1)S(1)}, u32[]{:S(2)}, u32[]{:S(2)}) %collective-permute-start.59) | collective-permute-done | bytes 589856 | tf_op jit(solution)/shard_map/ppermute | solution.py:28
  197.3 2.4 weight_grad.6
  200.7 1.7 collective-permute-start.62
  202.4 2.8 %inter_backward.1.dkv_ref = bf16[2,512,768]{2,1,0:T(8,128)(2,1)S(1)} custom-call(s32[3]{0:T(128)S(1)} %pad_add_fusion.ids_ref, bf16[512,768]{1,0:T(8,128)(2,1)S(1)} %get-tuple-element.250.k_ref, bf16[512,768]{1,0:T(8,128)(2,1)S(1)} %get-tuple-element.267.v_ref, f32[512,768]{1,0:T(8,128)S(1)} %get-tuple-element.380.dk_ref, ...), custom_call_target="tpu_custom_call" | custom-call | flops 2760000000 | tf_op jit(solution)/shard_map/inter_backward/pallas_call | solution.py:801
  209.2 2.2 collective-permute-start.67
  213.9 2.7 %weight_grad.7 = (bf16[2,8,24,768]{3,2,1,0:T(8,128)(2,1)S(1)}, bf16[1,8,48,768]{3,2,1,0:T(8,128)(2,1)S(1)}) custom-call(s32[3]{0:T(128)S(1)} %pad_add_fusion.ids_ref, bf16[512,768]{1,0:T(8,128)(2,1)S(1)} %copy-done.8, bf16[512,768]{1,0:T(8,128)(2,1)S(1)} %copy-done.17, bf16[512,768]{1,0:T(8,128)(2,1)S(1)} %copy-done.9, ...), custom_call_target="tpu_custom_call" | custom-call | flops 2016000000 | tf_op jit(solution)/shard_map/weight_grad/pallas_call | solution.py:881
  218.8 3.9 %input_grad.1 = f32[512,768]{1,0:T(8,128)} custom-call(s32[3]{0:T(128)S(1)} %pad_add_fusion.ids_ref, bf16[512,768]{1,0:T(8,128)(2,1)S(1)} %copy-done.11, bf16[2,512,768]{2,1,0:T(8,128)(2,1)S(1)} %copy-done.3, f32[512,768]{1,0:T(8,128)S(1)} %copy-done.5, bf16[768,1792]{1,0:T(8,128)(2,1)S(1)} %bitcast.107, bf16[768,1536]{1,0:T(8,128)(2,1)S(1)} %bitcast.111), custom_call_target="tpu_custom_call" | custom-call | flops 2400000000 | tf_op jit(solution)/shard_map/input_grad/pallas_call | solution.py:825
  222.7 4.0 %collective-permute-done.64 = bf16[8,48,896]{2,1,0:T(8,128)(2,1)S(1)} collective-permute-done((bf16[8,48,896]{2,1,0:T(8,128)(2,1)}, bf16[8,48,896]{2,1,0:T(8,128)(2,1)S(1)}, u32[]{:S(2)}, u32[]{:S(2)}) %collective-permute-start.64) | collective-permute-done | bytes 688160 | tf_op jit(solution)/shard_map/ppermute | solution.py:28
  228.0 2.2 collective-permute-start.73
  234.1 3.2 %collective-permute-done.65 = bf16[4,48,896]{2,1,0:T(8,128)(2,1)S(1)} collective-permute-done((bf16[4,48,896]{2,1,0:T(8,128)(2,1)S(1)}, bf16[4,48,896]{2,1,0:T(8,128)(2,1)S(1)}, u32[]{:S(2)}, u32[]{:S(2)}) %collective-permute-start.65) | collective-permute-done | bytes 344096 | tf_op jit(solution)/shard_map/ppermute | solution.py:28
  237.5 1.8 collective-permute-start.70
  241.2 1.8 collective-permute-start.77
  243.7 2.5 collective-permute-start.75
  249.6 1.8 collective-permute-done.75
  253.8 2.5 collective-permute-done.80
  (331 shorter events, 103.7 us)
Async XLA Ops:
  1.5 7.9 %collective-permute-start = (bf16[1,24,1536]{2,1,0:T(8,128)(2,1)S(1)}, bf16[1,24,1536]{2,1,0:T(8,128)(2,1)S(1)}, u32[]{:S(2)}, u32[]{:S(2)}) collective-permute-start(bf16[1,24,1536]{2,1,0:T(8,128)(2,1)S(1)} %slice_bitcast_fusion.15), channel_id=1, source_target_pairs={{0,4},{1,5},{2,6},{3,7},{4,0},{5,1},{6,2},{7,3},{8,12},{9,13},{10,... | collective-permute-start | bytes 221192 | tf_op jit(solution)/shard_map/ppermute | solution.py:28
  5.6 31.2 %collective-permute-start.10 = (bf16[512,768]{1,0:T(8,128)(2,1)}, bf16[512,768]{1,0:T(8,128)(2,1)S(1)}, u32[]{:S(2)}, u32[]{:S(2)}) collective-permute-start(bf16[512,768]{1,0:T(8,128)(2,1)} %refs_0_.1), channel_id=1, source_target_pairs={{0,8},{8,0},{16,24},{24,16},{1,9},{9,1},{17,25},{25,17},{2,10},{10... | collective-permute-start | bytes 2359304 | tf_op jit(solution)/shard_map/ppermute | solution.py:28
  22.0 8.8 %collective-permute-start.6 = (bf16[8,24,768]{2,1,0:T(8,128)(2,1)S(1)}, bf16[8,24,768]{2,1,0:T(8,128)(2,1)S(1)}, u32[]{:S(2)}, u32[]{:S(2)}) collective-permute-start(bf16[8,24,768]{2,1,0:T(8,128)(2,1)S(1)} %pad_maximum_fusion.21), channel_id=1, source_target_pairs={{0,1},{1,0},{2,3},{3,2},{4,5},{5,4},{6,7},{7,6},{8,9},{9,8},{10,11... | collective-permute-start | bytes 884744 | tf_op jit(solution)/shard_map/ppermute | solution.py:28
  23.5 7.2 %collective-permute-start.5 = (bf16[8,24,768]{2,1,0:T(8,128)(2,1)S(1)}, bf16[8,24,768]{2,1,0:T(8,128)(2,1)S(1)}, u32[]{:S(2)}, u32[]{:S(2)}) collective-permute-start(bf16[8,24,768]{2,1,0:T(8,128)(2,1)S(1)} %pad_maximum_fusion.20), channel_id=1, source_target_pairs={{0,16},{8,24},{16,0},{24,8},{1,17},{9,25},{17,1},{25,9},{2,18},{10... | collective-permute-start | bytes 884744 | tf_op jit(solution)/shard_map/ppermute | solution.py:28
  27.4 7.9 %collective-permute-start.11 = (bf16[1,24,3072]{2,1,0:T(8,128)(2,1)}, bf16[1,24,3072]{2,1,0:T(8,128)(2,1)S(1)}, u32[]{:S(2)}, u32[]{:S(2)}) collective-permute-start(bf16[1,24,3072]{2,1,0:T(8,128)(2,1)} %bitcast.15), channel_id=1, source_target_pairs={{0,4},{1,5},{2,6},{3,7},{4,0},{5,1},{6,2},{7,3},{8,12},{9,13},{10,... | collective-permute-start | bytes 442376 | tf_op jit(solution)/shard_map/ppermute | solution.py:28
  31.5 10.4 %collective-permute-start.9 = (bf16[4,24,896]{2,1,0:T(8,128)(2,1)S(1)}, bf16[4,24,896]{2,1,0:T(8,128)(2,1)S(1)}, u32[]{:S(2)}, u32[]{:S(2)}) collective-permute-start(bf16[4,24,896]{2,1,0:T(8,128)(2,1)S(1)} %get-tuple-element.487), channel_id=1, source_target_pairs={{0,16},{8,24},{16,0},{24,8},{1,17},{9,25},{17,1},{25,9},{2,18},{10... | collective-permute-start | bytes 516104 | tf_op jit(solution)/shard_map/ppermute | solution.py:28
  42.1 13.2 %collective-permute-start.14 = (bf16[8,24,896]{2,1,0:T(8,128)(2,1)S(1)}, bf16[8,24,896]{2,1,0:T(8,128)(2,1)S(1)}, u32[]{:S(2)}, u32[]{:S(2)}) collective-permute-start(bf16[8,24,896]{2,1,0:T(8,128)(2,1)S(1)} %get-tuple-element.256), channel_id=1, source_target_pairs={{0,16},{8,24},{16,0},{24,8},{1,17},{9,25},{17,1},{25,9},{2,18},{10... | collective-permute-start | bytes 1032200 | tf_op jit(solution)/shard_map/ppermute | solution.py:28
  43.0 12.3 %collective-permute-start.15 = (bf16[8,24,896]{2,1,0:T(8,128)(2,1)S(1)}, bf16[8,24,896]{2,1,0:T(8,128)(2,1)S(1)}, u32[]{:S(2)}, u32[]{:S(2)}) collective-permute-start(bf16[8,24,896]{2,1,0:T(8,128)(2,1)S(1)} %get-tuple-element.257), channel_id=1, source_target_pairs={{0,1},{1,0},{2,3},{3,2},{4,5},{5,4},{6,7},{7,6},{8,9},{9,8},{10,11... | collective-permute-start | bytes 1032200 | tf_op jit(solution)/shard_map/ppermute | solution.py:28
  44.5 8.9 %collective-permute-start.16 = (bf16[2,2,104,128]{3,2,1,0:T(8,128)(2,1)S(1)}, bf16[2,2,104,128]{3,2,1,0:T(8,128)(2,1)S(1)}, u32[]{:S(2)}, u32[]{:S(2)}) collective-permute-start(bf16[2,2,104,128]{3,2,1,0:T(8,128)(2,1)S(1)} %get-tuple-element.258), channel_id=1, source_target_pairs={{0,2},{1,3},{2,0},{3,1},{4,6},{5,7},{6,4},{7,5},{8,10},{9,11},{10,... | collective-permute-start | bytes 319496 | tf_op jit(solution)/shard_map/ppermute | solution.py:28
  44.5 9.5 %collective-permute-start.17 = (bf16[2,2,104,128]{3,2,1,0:T(8,128)(2,1)S(1)}, bf16[2,2,104,128]{3,2,1,0:T(8,128)(2,1)S(1)}, u32[]{:S(2)}, u32[]{:S(2)}) collective-permute-start(bf16[2,2,104,128]{3,2,1,0:T(8,128)(2,1)S(1)} %get-tuple-element.259), channel_id=1, source_target_pairs={{0,4},{1,5},{2,6},{3,7},{4,0},{5,1},{6,2},{7,3},{8,12},{9,13},{10,... | collective-permute-start | bytes 319496 | tf_op jit(solution)/shard_map/ppermute | solution.py:28
  47.5 7.7 %collective-permute-start.18 = (bf16[2,2,104,128]{3,2,1,0:T(8,128)(2,1)S(1)}, bf16[2,2,104,128]{3,2,1,0:T(8,128)(2,1)S(1)}, u32[]{:S(2)}, u32[]{:S(2)}) collective-permute-start(bf16[2,2,104,128]{3,2,1,0:T(8,128)(2,1)S(1)} %get-tuple-element.260), channel_id=1, source_target_pairs={{0,6},{1,7},{2,4},{3,5},{4,2},{5,3},{6,0},{7,1},{8,14},{9,15},{10,... | collective-permute-start | bytes 319496 | tf_op jit(solution)/shard_map/ppermute | solution.py:28
  55.3 12.8 %collective-permute-start.25 = (bf16[4,2,104,128]{3,2,1,0:T(8,128)(2,1)S(1)}, bf16[4,2,104,128]{3,2,1,0:T(8,128)(2,1)S(1)}, u32[]{:S(2)}, u32[]{:S(2)}) collective-permute-start(bf16[4,2,104,128]{3,2,1,0:T(8,128)(2,1)S(1)} %pad_maximum_fusion.27), channel_id=1, source_target_pairs={{0,1},{1,0},{2,3},{3,2},{4,5},{5,4},{6,7},{7,6},{8,9},{9,8},{10,11... | collective-permute-start | bytes 638984 | tf_op jit(solution)/shard_map/ppermute | solution.py:28
  61.1 7.3 %collective-permute-start.22 = (bf16[4,24,1536]{2,1,0:T(8,128)(2,1)S(1)}, bf16[4,24,1536]{2,1,0:T(8,128)(2,1)S(1)}, u32[]{:S(2)}, u32[]{:S(2)}) collective-permute-start(bf16[4,24,1536]{2,1,0:T(8,128)(2,1)S(1)} %get-tuple-element.274), channel_id=1, source_target_pairs={{0,1},{1,0},{2,3},{3,2},{4,5},{5,4},{6,7},{7,6},{8,9},{9,8},{10,11... | collective-permute-start | bytes 884744 | tf_op jit(solution)/shard_map/ppermute | solution.py:28
  63.9 7.1 %collective-permute-start.24 = (bf16[1,96,768]{2,1,0:T(8,128)(2,1)S(1)}, bf16[1,96,768]{2,1,0:T(8,128)(2,1)S(1)}, u32[]{:S(2)}, u32[]{:S(2)}) collective-permute-start(bf16[1,96,768]{2,1,0:T(8,128)(2,1)S(1)} %bitcast.118), channel_id=1, source_target_pairs={{0,4},{1,5},{2,6},{3,7},{4,0},{5,1},{6,2},{7,3},{8,12},{9,13},{10,... | collective-permute-start | bytes 442376 | tf_op jit(solution)/shard_map/ppermute | solution.py:28
  71.2 11.9 %collective-permute-start.31 = (bf16[8,24,1536]{2,1,0:T(8,128)(2,1)S(1)}, bf16[8,24,1536]{2,1,0:T(8,128)(2,1)S(1)}, u32[]{:S(2)}, u32[]{:S(2)}) collective-permute-start(bf16[8,24,1536]{2,1,0:T(8,128)(2,1)S(1)} %pad_maximum_fusion.10), channel_id=1, source_target_pairs={{0,16},{8,24},{16,0},{24,8},{1,17},{9,25},{17,1},{25,9},{2,18},{10... | collective-permute-start | bytes 1769480 | tf_op jit(solution)/shard_map/ppermute | solution.py:28
  72.5 11.1 %collective-permute-start.32 = (bf16[8,24,1536]{2,1,0:T(8,128)(2,1)S(1)}, bf16[8,24,1536]{2,1,0:T(8,128)(2,1)S(1)}, u32[]{:S(2)}, u32[]{:S(2)}) collective-permute-start(bf16[8,24,1536]{2,1,0:T(8,128)(2,1)S(1)} %pad_maximum_fusion.11), channel_id=1, source_target_pairs={{0,1},{1,0},{2,3},{3,2},{4,5},{5,4},{6,7},{7,6},{8,9},{9,8},{10,11... | collective-permute-start | bytes 1769480 | tf_op jit(solution)/shard_map/ppermute | solution.py:28
  84.5 9.0 %collective-permute-start.29 = (bf16[2,96,768]{2,1,0:T(8,128)(2,1)S(1)}, bf16[2,96,768]{2,1,0:T(8,128)(2,1)S(1)}, u32[]{:S(2)}, u32[]{:S(2)}) collective-permute-start(bf16[2,96,768]{2,1,0:T(8,128)(2,1)S(1)} %pad_maximum_fusion.23), channel_id=1, source_target_pairs={{0,2},{1,3},{2,0},{3,1},{4,6},{5,7},{6,4},{7,5},{8,10},{9,11},{10,... | collective-permute-start | bytes 884744 | tf_op jit(solution)/shard_map/ppermute | solution.py:28
  84.7 7.1 %collective-permute-start.30 = (bf16[4,2,104,128]{3,2,1,0:T(8,128)(2,1)S(1)}, bf16[4,2,104,128]{3,2,1,0:T(8,128)(2,1)S(1)}, u32[]{:S(2)}, u32[]{:S(2)}) collective-permute-start(bf16[4,2,104,128]{3,2,1,0:T(8,128)(2,1)S(1)} %pad_maximum_fusion.28), channel_id=1, source_target_pairs={{0,1},{1,0},{2,3},{3,2},{4,5},{5,4},{6,7},{7,6},{8,9},{9,8},{10,11... | collective-permute-start | bytes 638984 | tf_op jit(solution)/shard_map/ppermute | solution.py:28
  93.6 8.2 %collective-permute-start.36 = (bf16[4,96,384]{2,1,0:T(8,128)(2,1)S(1)}, bf16[4,96,384]{2,1,0:T(8,128)(2,1)S(1)}, u32[]{:S(2)}, u32[]{:S(2)}) collective-permute-start(bf16[4,96,384]{2,1,0:T(8,128)(2,1)S(1)} %get-tuple-element.303), channel_id=1, source_target_pairs={{0,1},{1,0},{2,3},{3,2},{4,5},{5,4},{6,7},{7,6},{8,9},{9,8},{10,11... | collective-permute-start | bytes 884744 | tf_op jit(solution)/shard_map/ppermute | solution.py:28
  94.8 7.9 %collective-permute-start.37 = (bf16[4,96,384]{2,1,0:T(8,128)(2,1)S(1)}, bf16[4,96,384]{2,1,0:T(8,128)(2,1)S(1)}, u32[]{:S(2)}, u32[]{:S(2)}) collective-permute-start(bf16[4,96,384]{2,1,0:T(8,128)(2,1)S(1)} %get-tuple-element.304), channel_id=1, source_target_pairs={{0,16},{8,24},{16,0},{24,8},{1,17},{9,25},{17,1},{25,9},{2,18},{10... | collective-permute-start | bytes 884744 | tf_op jit(solution)/shard_map/ppermute | solution.py:28
  102.8 13.3 %collective-permute-start.38 = (bf16[8,96,384]{2,1,0:T(8,128)(2,1)S(1)}, bf16[8,96,384]{2,1,0:T(8,128)(2,1)S(1)}, u32[]{:S(2)}, u32[]{:S(2)}) collective-permute-start(bf16[8,96,384]{2,1,0:T(8,128)(2,1)S(1)} %pad_maximum_fusion.13), channel_id=1, source_target_pairs={{0,16},{8,24},{16,0},{24,8},{1,17},{9,25},{17,1},{25,9},{2,18},{10... | collective-permute-start | bytes 1769480 | tf_op jit(solution)/shard_map/ppermute | solution.py:28
  103.8 13.0 %collective-permute-start.39 = (bf16[8,96,384]{2,1,0:T(8,128)(2,1)S(1)}, bf16[8,96,384]{2,1,0:T(8,128)(2,1)S(1)}, u32[]{:S(2)}, u32[]{:S(2)}) collective-permute-start(bf16[8,96,384]{2,1,0:T(8,128)(2,1)S(1)} %pad_maximum_fusion.14), channel_id=1, source_target_pairs={{0,1},{1,0},{2,3},{3,2},{4,5},{5,4},{6,7},{7,6},{8,9},{9,8},{10,11... | collective-permute-start | bytes 1769480 | tf_op jit(solution)/shard_map/ppermute | solution.py:28
  140.1 18.4 %collective-permute-start.50 = (bf16[4,192,384]{2,1,0:T(8,128)(2,1)S(1)}, bf16[4,192,384]{2,1,0:T(8,128)(2,1)S(1)}, u32[]{:S(2)}, u32[]{:S(2)}) collective-permute-start(bf16[4,192,384]{2,1,0:T(8,128)(2,1)S(1)} %get-tuple-element.341), channel_id=1, source_target_pairs={{0,16},{8,24},{16,0},{24,8},{1,17},{9,25},{17,1},{25,9},{2,18},{10... | collective-permute-start | bytes 1769480 | tf_op jit(solution)/shard_map/ppermute | solution.py:28
  144.6 22.2 %collective-permute-start.46 = (bf16[2,3,48,1536]{3,2,1,0:T(8,128)(2,1)S(1)}, bf16[2,3,48,1536]{3,2,1,0:T(8,128)(2,1)S(1)}, u32[]{:S(2)}, u32[]{:S(2)}) collective-permute-start(bf16[2,3,48,1536]{3,2,1,0:T(8,128)(2,1)S(1)} %slice.454), channel_id=1, source_target_pairs={{0,1},{1,0},{2,3},{3,2},{4,5},{5,4},{6,7},{7,6},{8,9},{9,8},{10,11... | collective-permute-start | bytes 2654216 | tf_op jit(solution)/shard_map/ppermute | solution.py:28
  154.7 10.8 %collective-permute-start.48 = (bf16[2,2,104,128]{3,2,1,0:T(8,128)(2,1)S(1)}, bf16[2,2,104,128]{3,2,1,0:T(8,128)(2,1)S(1)}, u32[]{:S(2)}, u32[]{:S(2)}) collective-permute-start(bf16[2,2,104,128]{3,2,1,0:T(8,128)(2,1)S(1)} %get-tuple-element.351), channel_id=1, source_target_pairs={{0,4},{1,5},{2,6},{3,7},{4,0},{5,1},{6,2},{7,3},{8,12},{9,13},{10,... | collective-permute-start | bytes 319496 | tf_op jit(solution)/shard_map/ppermute | solution.py:28
  156.7 8.8 %collective-permute-start.49 = (bf16[2,2,104,128]{3,2,1,0:T(8,128)(2,1)S(1)}, bf16[2,2,104,128]{3,2,1,0:T(8,128)(2,1)S(1)}, u32[]{:S(2)}, u32[]{:S(2)}) collective-permute-start(bf16[2,2,104,128]{3,2,1,0:T(8,128)(2,1)S(1)} %get-tuple-element.352), channel_id=1, source_target_pairs={{0,6},{1,7},{2,4},{3,5},{4,2},{5,3},{6,0},{7,1},{8,14},{9,15},{10,... | collective-permute-start | bytes 319496 | tf_op jit(solution)/shard_map/ppermute | solution.py:28
  158.6 14.0 %collective-permute-start.54 = (bf16[4,192,384]{2,1,0:T(8,128)(2,1)S(1)}, bf16[4,192,384]{2,1,0:T(8,128)(2,1)S(1)}, u32[]{:S(2)}, u32[]{:S(2)}) collective-permute-start(bf16[4,192,384]{2,1,0:T(8,128)(2,1)S(1)} %get-tuple-element.356), channel_id=1, source_target_pairs={{0,16},{8,24},{16,0},{24,8},{1,17},{9,25},{17,1},{25,9},{2,18},{10... | collective-permute-start | bytes 1769480 | tf_op jit(solution)/shard_map/ppermute | solution.py:28
  165.6 7.3 %collective-permute-start.52 = (bf16[4,2,104,128]{3,2,1,0:T(8,128)(2,1)S(1)}, bf16[4,2,104,128]{3,2,1,0:T(8,128)(2,1)S(1)}, u32[]{:S(2)}, u32[]{:S(2)}) collective-permute-start(bf16[4,2,104,128]{3,2,1,0:T(8,128)(2,1)S(1)} %pad_maximum_fusion.29), channel_id=1, source_target_pairs={{0,1},{1,0},{2,3},{3,2},{4,5},{5,4},{6,7},{7,6},{8,9},{9,8},{10,11... | collective-permute-start | bytes 638984 | tf_op jit(solution)/shard_map/ppermute | solution.py:28
  167.2 10.9 %collective-permute-start.51 = (bf16[2,1,48,1536]{3,2,1,0:T(8,128)(2,1)S(1)}, bf16[2,1,48,1536]{3,2,1,0:T(8,128)(2,1)S(1)}, u32[]{:S(2)}, u32[]{:S(2)}) collective-permute-start(bf16[2,1,48,1536]{3,2,1,0:T(8,128)(2,1)S(1)} %slice.452), channel_id=1, source_target_pairs={{0,1},{1,0},{2,3},{3,2},{4,5},{5,4},{6,7},{7,6},{8,9},{9,8},{10,11... | collective-permute-start | bytes 884744 | tf_op jit(solution)/shard_map/ppermute | solution.py:28
  173.1 14.9 %collective-permute-start.55 = (bf16[2,2,104,128]{3,2,1,0:T(8,128)(2,1)S(1)}, bf16[2,2,104,128]{3,2,1,0:T(8,128)(2,1)S(1)}, u32[]{:S(2)}, u32[]{:S(2)}) collective-permute-start(bf16[2,2,104,128]{3,2,1,0:T(8,128)(2,1)S(1)} %get-tuple-element.371), channel_id=1, source_target_pairs={{0,2},{1,3},{2,0},{3,1},{4,6},{5,7},{6,4},{7,5},{8,10},{9,11},{10,... | collective-permute-start | bytes 319496 | tf_op jit(solution)/shard_map/ppermute | solution.py:28
  175.3 12.7 %collective-permute-start.56 = (bf16[2,2,104,128]{3,2,1,0:T(8,128)(2,1)S(1)}, bf16[2,2,104,128]{3,2,1,0:T(8,128)(2,1)S(1)}, u32[]{:S(2)}, u32[]{:S(2)}) collective-permute-start(bf16[2,2,104,128]{3,2,1,0:T(8,128)(2,1)S(1)} %get-tuple-element.372), channel_id=1, source_target_pairs={{0,4},{1,5},{2,6},{3,7},{4,0},{5,1},{6,2},{7,3},{8,12},{9,13},{10,... | collective-permute-start | bytes 319496 | tf_op jit(solution)/shard_map/ppermute | solution.py:28
  176.6 11.4 %collective-permute-start.57 = (bf16[2,2,104,128]{3,2,1,0:T(8,128)(2,1)S(1)}, bf16[2,2,104,128]{3,2,1,0:T(8,128)(2,1)S(1)}, u32[]{:S(2)}, u32[]{:S(2)}) collective-permute-start(bf16[2,2,104,128]{3,2,1,0:T(8,128)(2,1)S(1)} %get-tuple-element.373), channel_id=1, source_target_pairs={{0,6},{1,7},{2,4},{3,5},{4,2},{5,3},{6,0},{7,1},{8,14},{9,15},{10,... | collective-permute-start | bytes 319496 | tf_op jit(solution)/shard_map/ppermute | solution.py:28
  178.2 13.8 %collective-permute-start.60 = (bf16[4,48,1536]{2,1,0:T(8,128)(2,1)S(1)}, bf16[4,48,1536]{2,1,0:T(8,128)(2,1)S(1)}, u32[]{:S(2)}, u32[]{:S(2)}) collective-permute-start(bf16[4,48,1536]{2,1,0:T(8,128)(2,1)S(1)} %pad_maximum_fusion.15), channel_id=1, source_target_pairs={{0,16},{8,24},{16,0},{24,8},{1,17},{9,25},{17,1},{25,9},{2,18},{10... | collective-permute-start | bytes 1769480 | tf_op jit(solution)/shard_map/ppermute | solution.py:28
  179.0 16.1 %collective-permute-start.59 = (bf16[4,192,384]{2,1,0:T(8,128)(2,1)S(1)}, bf16[4,192,384]{2,1,0:T(8,128)(2,1)S(1)}, u32[]{:S(2)}, u32[]{:S(2)}) collective-permute-start(bf16[4,192,384]{2,1,0:T(8,128)(2,1)S(1)} %fusion.1), channel_id=1, source_target_pairs={{0,1},{1,0},{2,3},{3,2},{4,5},{5,4},{6,7},{7,6},{8,9},{9,8},{10,11... | collective-permute-start | bytes 1769480 | tf_op jit(solution)/shard_map/ppermute | solution.py:28
  188.1 14.3 %collective-permute-start.58 = (bf16[4,2,104,128]{3,2,1,0:T(8,128)(2,1)S(1)}, bf16[4,2,104,128]{3,2,1,0:T(8,128)(2,1)S(1)}, u32[]{:S(2)}, u32[]{:S(2)}) collective-permute-start(bf16[4,2,104,128]{3,2,1,0:T(8,128)(2,1)S(1)} %pad_maximum_fusion.30), channel_id=1, source_target_pairs={{0,1},{1,0},{2,3},{3,2},{4,5},{5,4},{6,7},{7,6},{8,9},{9,8},{10,11... | collective-permute-start | bytes 638984 | tf_op jit(solution)/shard_map/ppermute | solution.py:28
  188.9 7.3 %collective-permute-start.61 = (bf16[512,384]{1,0:T(8,128)(2,1)S(1)}, bf16[512,384]{1,0:T(8,128)(2,1)S(1)}, u32[]{:S(2)}, u32[]{:S(2)}) collective-permute-start(bf16[512,384]{1,0:T(8,128)(2,1)S(1)} %get-tuple-element.388), channel_id=1, source_target_pairs={{0,8},{8,0},{16,24},{24,16},{1,9},{9,1},{17,25},{25,17},{2,10},{10... | collective-permute-start | bytes 1179656 | tf_op jit(solution)/shard_map/ppermute | solution.py:28
  208.2 18.4 %collective-permute-start.64 = (bf16[8,48,896]{2,1,0:T(8,128)(2,1)}, bf16[8,48,896]{2,1,0:T(8,128)(2,1)S(1)}, u32[]{:S(2)}, u32[]{:S(2)}) collective-permute-start(bf16[8,48,896]{2,1,0:T(8,128)(2,1)} %slice_bitcast_fusion.2), channel_id=1, source_target_pairs={{0,16},{8,24},{16,0},{24,8},{1,17},{9,25},{17,1},{25,9},{2,18},{10... | collective-permute-start | bytes 2064392 | tf_op jit(solution)/shard_map/ppermute | solution.py:28
  209.2 21.4 %collective-permute-start.67 = (bf16[1,48,1536]{2,1,0:T(8,128)(2,1)}, bf16[1,48,1536]{2,1,0:T(8,128)(2,1)S(1)}, u32[]{:S(2)}, u32[]{:S(2)}) collective-permute-start(bf16[1,48,1536]{2,1,0:T(8,128)(2,1)} %add_convert_fusion.12), channel_id=1, source_target_pairs={{0,4},{1,5},{2,6},{3,7},{4,0},{5,1},{6,2},{7,3},{8,12},{9,13},{10,... | collective-permute-start | bytes 442376 | tf_op jit(solution)/shard_map/ppermute | solution.py:28
  211.4 16.6 %collective-permute-start.69 = (bf16[2,192,384]{2,1,0:T(8,128)(2,1)}, bf16[2,192,384]{2,1,0:T(8,128)(2,1)S(1)}, u32[]{:S(2)}, u32[]{:S(2)}) collective-permute-start(bf16[2,192,384]{2,1,0:T(8,128)(2,1)} %get-tuple-element.400), channel_id=1, source_target_pairs={{0,2},{1,3},{2,0},{3,1},{4,6},{5,7},{6,4},{7,5},{8,10},{9,11},{10,... | collective-permute-start | bytes 884744 | tf_op jit(solution)/shard_map/ppermute | solution.py:28
  216.7 16.3 %collective-permute-start.66 = (bf16[8,24,768]{2,1,0:T(8,128)(2,1)S(1)}, bf16[8,24,768]{2,1,0:T(8,128)(2,1)S(1)}, u32[]{:S(2)}, u32[]{:S(2)}) collective-permute-start(bf16[8,24,768]{2,1,0:T(8,128)(2,1)S(1)} %slice_bitcast_fusion.11), channel_id=1, source_target_pairs={{0,16},{8,24},{16,0},{24,8},{1,17},{9,25},{17,1},{25,9},{2,18},{10... | collective-permute-start | bytes 884744 | tf_op jit(solution)/shard_map/ppermute | solution.py:28
  218.0 12.1 %collective-permute-start.68 = (bf16[4,48,768]{2,1,0:T(8,128)(2,1)S(1)}, bf16[4,48,768]{2,1,0:T(8,128)(2,1)S(1)}, u32[]{:S(2)}, u32[]{:S(2)}) collective-permute-start(bf16[4,48,768]{2,1,0:T(8,128)(2,1)S(1)} %slice_bitcast_fusion.10), channel_id=1, source_target_pairs={{0,1},{1,0},{2,3},{3,2},{4,5},{5,4},{6,7},{7,6},{8,9},{9,8},{10,11... | collective-permute-start | bytes 884744 | tf_op jit(solution)/shard_map/ppermute | solution.py:28
  226.9 10.5 %collective-permute-start.65 = (bf16[4,48,896]{2,1,0:T(8,128)(2,1)S(1)}, bf16[4,48,896]{2,1,0:T(8,128)(2,1)S(1)}, u32[]{:S(2)}, u32[]{:S(2)}) collective-permute-start(bf16[4,48,896]{2,1,0:T(8,128)(2,1)S(1)} %get-tuple-element.409), channel_id=1, source_target_pairs={{0,1},{1,0},{2,3},{3,2},{4,5},{5,4},{6,7},{7,6},{8,9},{9,8},{10,11... | collective-permute-start | bytes 1032200 | tf_op jit(solution)/shard_map/ppermute | solution.py:28
  228.0 12.3 %collective-permute-start.73 = (bf16[1,192,384]{2,1,0:T(8,128)(2,1)S(1)}, bf16[1,192,384]{2,1,0:T(8,128)(2,1)S(1)}, u32[]{:S(2)}, u32[]{:S(2)}) collective-permute-start(bf16[1,192,384]{2,1,0:T(8,128)(2,1)S(1)} %add_convert_fusion.10), channel_id=1, source_target_pairs={{0,4},{1,5},{2,6},{3,7},{4,0},{5,1},{6,2},{7,3},{8,12},{9,13},{10,... | collective-permute-start | bytes 442376 | tf_op jit(solution)/shard_map/ppermute | solution.py:28
  230.2 9.0 %collective-permute-start.74 = (bf16[2,48,768]{2,1,0:T(8,128)(2,1)S(1)}, bf16[2,48,768]{2,1,0:T(8,128)(2,1)S(1)}, u32[]{:S(2)}, u32[]{:S(2)}) collective-permute-start(bf16[2,48,768]{2,1,0:T(8,128)(2,1)S(1)} %get-tuple-element.413), channel_id=1, source_target_pairs={{0,2},{1,3},{2,0},{3,1},{4,6},{5,7},{6,4},{7,5},{8,10},{9,11},{10,... | collective-permute-start | bytes 442376 | tf_op jit(solution)/shard_map/ppermute | solution.py:28
  230.6 12.4 %collective-permute-start.71 = (bf16[48,1536]{1,0:T(8,128)(2,1)S(1)}, bf16[48,1536]{1,0:T(8,128)(2,1)S(1)}, u32[]{:S(2)}, u32[]{:S(2)}) collective-permute-start(bf16[48,1536]{1,0:T(8,128)(2,1)S(1)} %fusion.25), channel_id=1, source_target_pairs={{0,16},{8,24},{16,0},{24,8},{1,17},{9,25},{17,1},{25,9},{2,18},{10... | collective-permute-start | bytes 442376 | tf_op jit(solution)/shard_map/ppermute | solution.py:28
  233.1 8.1 %collective-permute-start.72 = (bf16[4,24,768]{2,1,0:T(8,128)(2,1)S(1)}, bf16[4,24,768]{2,1,0:T(8,128)(2,1)S(1)}, u32[]{:S(2)}, u32[]{:S(2)}) collective-permute-start(bf16[4,24,768]{2,1,0:T(8,128)(2,1)S(1)} %get-tuple-element.417), channel_id=1, source_target_pairs={{0,1},{1,0},{2,3},{3,2},{4,5},{5,4},{6,7},{7,6},{8,9},{9,8},{10,11... | collective-permute-start | bytes 442376 | tf_op jit(solution)/shard_map/ppermute | solution.py:28
  240.3 9.2 %collective-permute-start.76 = (bf16[192,384]{1,0:T(8,128)(2,1)S(1)}, bf16[192,384]{1,0:T(8,128)(2,1)S(1)}, u32[]{:S(2)}, u32[]{:S(2)}) collective-permute-start(bf16[192,384]{1,0:T(8,128)(2,1)S(1)} %fusion.26), channel_id=1, source_target_pairs={{0,16},{8,24},{16,0},{24,8},{1,17},{9,25},{17,1},{25,9},{2,18},{10... | collective-permute-start | bytes 442376 | tf_op jit(solution)/shard_map/ppermute | solution.py:28
  243.7 7.7 %collective-permute-start.75 = (bf16[1,48,896]{2,1,0:T(8,128)(2,1)S(1)}, bf16[1,48,896]{2,1,0:T(8,128)(2,1)S(1)}, u32[]{:S(2)}, u32[]{:S(2)}) collective-permute-start(bf16[1,48,896]{2,1,0:T(8,128)(2,1)S(1)} %add_convert_fusion.14), channel_id=1, source_target_pairs={{0,4},{1,5},{2,6},{3,7},{4,0},{5,1},{6,2},{7,3},{8,12},{9,13},{10,... | collective-permute-start | bytes 258056 | tf_op jit(solution)/shard_map/ppermute | solution.py:28
  (66 other events, 330.8 us)

commit v8 on v7

--- a/solution.py
+++ b/solution.py
@@ -528,7 +528,7 @@
                     gelu_ref[at, columns] = (upper * cdf).astype(bf16)
                     slope_ref[at, columns] = (cdf + upper * pdf).astype(bf16)
 
-            loop(ff // D, part)
+            loop(ff // D, part, 2)
 
         loop(rows // SEG, block)
 
@@ -609,7 +609,7 @@
                         d_up.astype(f32), axis=0, keepdims=True
                     )
 
-            loop(ff // D, part)
+            loop(ff // D, part, 2)
             theirs = 1 - ids_ref[0]
             dup_half_ref[at, :] = dup_ref[
                 at, pl.ds(pl.multiple_of(theirs * (ff // 2), 128), ff // 2)

time: 262 us -> 262 us (level)
  transfers between devices with their start and end apart: 88 -> 88, of which waited for: 40 -> 40; matrix products, arithmetic and copies ran while one was open for 9% -> 9% of each run, Pallas kernels for 26% -> 25%
where the time goes in v8:
time: 262 us; the launch traced here: 261 us
  starting transfers between devices  88 us (34%)
  waiting for transfers between devices  74.1 us (28%)
  Pallas kernels  67.6 us (26%)
  other arithmetic  14.9 us (6%)
  local copies, waits for them, and re-layouts  11.1 us (4%)
  matrix products  3.7 us (1%)
    ppermute x88, starting transfers between devices, exchange(): return lax.ppermute(x, axis, [(i, i ^ offset) for i in range(size)])  88 us
    ppermute x88, waiting for transfers between devices, exchange(): return lax.ppermute(x, axis, [(i, i ^ offset) for i in range(size)])  74.1 us
    pallas_call x4, Pallas kernels, weight_grad(): call(kernel, 'weight_grad', tuple((shape_of((n, fsdp, share // n, width),...  12.8 us
    pallas_call x1, Pallas kernels, back_to_heads(): call(kernel, 'back_to_heads', (shape_of((rows, D), f32), shape_of((rows,...  8.43 us
    pallas_call x1, Pallas kernels, intra_backward(): call(kernel, 'intra_backward', (shape_of((rows, D), bf16), shape_of((rows...  7.93 us
    pallas_call x1, Pallas kernels, expand(): call(kernel, 'expand', (shape_of((rows, D), f32), shape_of((rows, LANES),...  7.28 us
    pallas_call x1, Pallas kernels, contract(): call(kernel, 'contract', (shape_of((rows, D), bf16), shape_of((rows, D),...  5.33 us
  transfers between devices with their start and end apart: 88, of which 40 were waited for; matrix products, arithmetic and copies ran while one was open for 9% of the time, Pallas kernels for 25%

profile of v8, /device:TPU:0, one launch (start us, length us, event | category | flops | bytes accessed | tf_op | source)
XLA Modules:
  0.0 261.2 jit_solution(9472317754790865033)
XLA Ops:
  1.5 4.0 %collective-permute-start = (bf16[1,24,1536]{2,1,0:T(8,128)(2,1)S(1)}, bf16[1,24,1536]{2,1,0:T(8,128)(2,1)S(1)}, u32[]{:S(2)}, u32[]{:S(2)}) collective-permute-start(bf16[1,24,1536]{2,1,0:T(8,128)(2,1)S(1)} %slice_bitcast_fusion.15), channel_id=1, source_target_pairs={{0,4},{1,5},{2,6},{3,7},{4,0},{5,1},{6,2},{7,3},{8,12},{9,13},{10,... | collective-permute-start | bytes 221192 | tf_op jit(solution)/shard_map/ppermute | solution.py:28
  12.4 1.8 fusion.22
  19.3 2.3 collective-permute-start.2
  27.4 3.0 %collective-permute-start.11 = (bf16[1,24,3072]{2,1,0:T(8,128)(2,1)}, bf16[1,24,3072]{2,1,0:T(8,128)(2,1)S(1)}, u32[]{:S(2)}, u32[]{:S(2)}) collective-permute-start(bf16[1,24,3072]{2,1,0:T(8,128)(2,1)} %bitcast.15), channel_id=1, source_target_pairs={{0,4},{1,5},{2,6},{3,7},{4,0},{5,1},{6,2},{7,3},{8,12},{9,13},{10,... | collective-permute-start | bytes 442376 | tf_op jit(solution)/shard_map/ppermute | solution.py:28
  32.7 2.6 %collective-permute-done.11 = bf16[1,24,3072]{2,1,0:T(8,128)(2,1)S(1)} collective-permute-done((bf16[1,24,3072]{2,1,0:T(8,128)(2,1)}, bf16[1,24,3072]{2,1,0:T(8,128)(2,1)S(1)}, u32[]{:S(2)}, u32[]{:S(2)}) %collective-permute-start.11) | collective-permute-done | bytes 147488 | tf_op jit(solution)/shard_map/ppermute | solution.py:28
  38.4 3.6 %project.1 = (bf16[512,768]{1,0:T(8,128)(2,1)S(1)}, bf16[512,768]{1,0:T(8,128)(2,1)S(1)}, bf16[2,2,104,128]{3,2,1,0:T(8,128)(2,1)S(1)}, bf16[2,2,104,128]{3,2,1,...) custom-call(s32[3]{0:T(128)S(1)} %pad_add_fusion.ids_ref, ...), custom_call_target="tpu_custom_call" | custom-call | flops 6480000000 | tf_op jit(solution)/shard_map/project/pallas_call | solution.py:381
  44.5 3.1 %collective-permute-start.17 = (bf16[2,2,104,128]{3,2,1,0:T(8,128)(2,1)S(1)}, bf16[2,2,104,128]{3,2,1,0:T(8,128)(2,1)S(1)}, u32[]{:S(2)}, u32[]{:S(2)}) collective-permute-start(bf16[2,2,104,128]{3,2,1,0:T(8,128)(2,1)S(1)} %get-tuple-element.259), channel_id=1, source_target_pairs={{0,4},{1,5},{2,6},{3,7},{4,0},{5,1},{6,2},{7,3},{8,12},{9,13},{10,... | collective-permute-start | bytes 319496 | tf_op jit(solution)/shard_map/ppermute | solution.py:28
  48.9 4.5 %collective-permute-done.16.refs_1_ = bf16[2,2,104,128]{3,2,1,0:T(8,128)(2,1)S(1)} collective-permute-done((bf16[2,2,104,128]{3,2,1,0:T(8,128)(2,1)S(1)}, bf16[2,2,104,128]{3,2,1,0:T(8,128)(2,1)S(1)}, u32[]{:S(2)}, u32[]{:S(2)}) %collective-permute-start.16) | collective-permute-done | bytes 106528 | tf_op jit(solution)/shard_map/ppermute | solution.py:28
  56.8 3.3 %collective-permute-done.21 = bf16[2,24,3072]{2,1,0:T(8,128)(2,1)S(1)} collective-permute-done((bf16[2,24,3072]{2,1,0:T(8,128)(2,1)S(1)}, bf16[2,24,3072]{2,1,0:T(8,128)(2,1)S(1)}, u32[]{:S(2)}, u32[]{:S(2)}) %collective-permute-start.21) | collective-permute-done | bytes 294944 | tf_op jit(solution)/shard_map/ppermute | solution.py:28
  64.4 3.7 %intra_forward.1 = (bf16[512,768]{1,0:T(8,128)(2,1)S(1)}, f32[512,768]{1,0:T(8,128)S(1)}, f32[512,768]{1,0:T(8,128)S(1)}) custom-call(bf16[512,768]{1,0:T(8,128)(2,1)S(1)} %copy-done.8, bf16[768,1792]{1,0:T(8,128)(2,1)S(1)} %bitcast.103, bf16[512,768]{1,0:T(8,128)(2,1)S(1)} %get-tuple-element.250.k_ref, bf16[512,768]{1,0:T(8,128)(2,1)S(1)} %get-tuple-element.267.v_ref, ...), custom_call_target="tpu_custom_call" | custom-call | flops 3540000000 | tf_op jit(solution)/shard_map/intra_forward/pallas_call | solution.py:439
  68.8 2.2 collective-permute-done.24
  73.7 2.0 collective-permute-start.27
  75.7 2.4 collective-permute-start.28
  79.6 2.7 %collective-permute-done.28.refs_3_ = bf16[2,2,104,128]{3,2,1,0:T(8,128)(2,1)S(1)} collective-permute-done((bf16[2,2,104,128]{3,2,1,0:T(8,128)(2,1)S(1)}, bf16[2,2,104,128]{3,2,1,0:T(8,128)(2,1)S(1)}, u32[]{:S(2)}, u32[]{:S(2)}) %collective-permute-start.28) | collective-permute-done | bytes 106528 | tf_op jit(solution)/shard_map/ppermute | solution.py:28
  89.7 2.0 collective-permute-done.30.refs_4_
  91.8 1.8 collective-permute-done.29
  95.7 2.3 inter_forward.1
  98.1 3.7 %collective-permute-done.36 = bf16[4,96,384]{2,1,0:T(8,128)(2,1)S(1)} collective-permute-done((bf16[4,96,384]{2,1,0:T(8,128)(2,1)S(1)}, bf16[4,96,384]{2,1,0:T(8,128)(2,1)S(1)}, u32[]{:S(2)}, u32[]{:S(2)}) %collective-permute-start.36) | collective-permute-done | bytes 294944 | tf_op jit(solution)/shard_map/ppermute | solution.py:28
  104.9 7.3 %expand.1 = (f32[512,768]{1,0:T(8,128)S(1)}, f32[512,128]{1,0:T(8,128)S(1)}, bf16[512,768]{1,0:T(8,128)(2,1)S(1)}, bf16[512,3072]{1,0:T(8,128)(2,1)S(1)}, bf16[512,3072]{1,0:T(8,128)(2,1)S(1)}) custom-call(bf16[512,768]{1,0:T(8,128)(2,1)S(1)} %get-tuple-element.314.att_ref.refs_0_, bf16[512,768]{1,0:T(8,128)(2,1)S(1)} %copy-done.8, ...), custom_call_target="tpu_custom_call" | custom-call | flops 171000000 | tf_op jit(solution)/shard_map/expand/pallas_call | solution.py:535
  112.2 4.0 %collective-permute-done.38 = bf16[8,96,384]{2,1,0:T(8,128)(2,1)S(1)} collective-permute-done((bf16[8,96,384]{2,1,0:T(8,128)(2,1)S(1)}, bf16[8,96,384]{2,1,0:T(8,128)(2,1)S(1)}, u32[]{:S(2)}, u32[]{:S(2)}) %collective-permute-start.38) | collective-permute-done | bytes 589856 | tf_op jit(solution)/shard_map/ppermute | solution.py:28
  117.7 2.3 collective-permute-done.40.refs_1_
  123.6 5.3 %contract.1 = (bf16[512,768]{1,0:T(8,128)(2,1)}, f32[512,768]{1,0:T(8,128)S(1)}, bf16[512,768]{1,0:T(8,128)(2,1)S(1)}, bf16[512,384]{1,0:T(8,128)(2,1)S(1)}, f32[16,768]{1,0:T(8,128)S(1)}) custom-call(s32[3]{0:T(128)S(1)} %pad_add_fusion.ids_ref, bf16[512,3072]{1,0:T(8,128)(2,1)S(1)} %get-tuple-element.329.gelu_ref.refs_0_, ...), custom_call_target="tpu_custom_call" | custom-call | flops 3600000000 | tf_op jit(solution)/shard_map/contract/pallas_call | solution.py:579
  130.0 4.3 %turn.1 = (bf16[512,3072]{1,0:T(8,128)(2,1)S(1)}, bf16[512,1536]{1,0:T(8,128)(2,1)S(1)}, f32[16,768]{1,0:T(8,128)S(1)}) custom-call(s32[3]{0:T(128)S(1)} %pad_add_fusion.ids_ref, bf16[512,768]{1,0:T(8,128)(2,1)S(1)} %get-tuple-element.339.dlow_ref.refs_2_, bf16[512,3072]{1,0:T(8,128)(2,1)S(1)} %get-tuple-element.333.slope_ref, ...), custom_call_target="tpu_custom_call" | custom-call | flops 13500000256 | tf_op jit(solution)/shard_map/turn/pallas_call | solution.py:620
  134.8 4.5 %weight_grad.4 = bf16[2,8,192,384]{3,2,1,0:T(8,128)(2,1)S(1)} custom-call(s32[3]{0:T(128)S(1)} %pad_add_fusion.ids_ref, bf16[512,3072]{1,0:T(8,128)(2,1)S(1)} %get-tuple-element.329.gelu_ref.refs_0_, bf16[512,3072]{1,0:T(8,128)(2,1)S(1)} %collective-permute-done.43.refs_1_, bf16[512,768]{1,0:T(8,128)(2,1)S(1)} %get-tuple-element.339.dlow_ref.refs_2_, ...), custom_call_target="tpu_custom_call" | custom-call | flops 3600000000 | tf_op jit(solution)/shard_map/weight_grad/pallas_call | solution.py:881
  140.6 3.2 %weight_grad.5 = bf16[2,8,48,1536]{3,2,1,0:T(8,128)(2,1)S(1)} custom-call(s32[3]{0:T(128)S(1)} %pad_add_fusion.ids_ref, bf16[512,768]{1,0:T(8,128)(2,1)S(1)} %get-tuple-element.325.refs_0_, bf16[512,768]{1,0:T(8,128)(2,1)S(1)} %collective-permute-done.42.refs_1_, bf16[512,3072]{1,0:T(8,128)(2,1)S(1)} %get-tuple-element.343.refs_2_.dup_ref, ...), custom_call_target="tpu_custom_call" | custom-call | flops 720000000 | tf_op jit(solution)/shard_map/weight_grad/pallas_call | solution.py:881
  144.9 8.4 %back_to_heads.1 = (f32[512,768]{1,0:T(8,128)S(1)}, bf16[512,768]{1,0:T(8,128)(2,1)S(1)}, bf16[512,384]{1,0:T(8,128)(2,1)S(1)}, bf16[512,768]{1,0:T(8,128)(2,1)S...) custom-call(s32[3]{0:T(128)S(1)} %pad_add_fusion.ids_ref, ...), custom_call_target="tpu_custom_call" | custom-call | flops 7080000000 | tf_op jit(solution)/shard_map/back_to_heads/pallas_call | solution.py:684
  154.0 1.9 collective-permute-start.48
  156.0 1.8 collective-permute-start.49
  159.3 5.6 %collective-permute-done.48.refs_2_ = bf16[2,2,104,128]{3,2,1,0:T(8,128)(2,1)S(1)} collective-permute-done((bf16[2,2,104,128]{3,2,1,0:T(8,128)(2,1)S(1)}, bf16[2,2,104,128]{3,2,1,0:T(8,128)(2,1)S(1)}, u32[]{:S(2)}, u32[]{:S(2)}) %collective-permute-start.48) | collective-permute-done | bytes 106528 | tf_op jit(solution)/shard_map/ppermute | solution.py:28
  167.4 4.6 %collective-permute-done.54 = bf16[4,192,384]{2,1,0:T(8,128)(2,1)S(1)} collective-permute-done((bf16[4,192,384]{2,1,0:T(8,128)(2,1)S(1)}, bf16[4,192,384]{2,1,0:T(8,128)(2,1)S(1)}, u32[]{:S(2)}, u32[]{:S(2)}) %collective-permute-start.54) | collective-permute-done | bytes 589856 | tf_op jit(solution)/shard_map/ppermute | solution.py:28
  172.5 2.1 collective-permute-start.55
  179.6 7.9 %intra_backward.1 = (bf16[512,768]{1,0:T(8,128)(2,1)S(1)}, bf16[512,384]{1,0:T(8,128)(2,1)S(1)}, f32[512,768]{1,0:T(8,128)S(1)}, f32[512,768]{1,0:T(8,128)S(1)}) custom-call(s32[3]{0:T(128)S(1)} %pad_add_fusion.ids_ref, bf16[512,768]{1,0:T(8,128)(2,1)S(1)} %get-tuple-element.377.q_ref, bf16[512,768]{1,0:T(8,128)(2,1)S(1)} %get-tuple-element.250.k_ref, ...), custom_call_target="tpu_custom_call" | custom-call | flops 6179999744 | tf_op jit(solution)/shard_map/intra_backward/pallas_call | solution.py:753
  188.5 2.8 %collective-permute-done.60 = bf16[4,48,1536]{2,1,0:T(8,128)(2,1)S(1)} collective-permute-done((bf16[4,48,1536]{2,1,0:T(8,128)(2,1)S(1)}, bf16[4,48,1536]{2,1,0:T(8,128)(2,1)S(1)}, u32[]{:S(2)}, u32[]{:S(2)}) %collective-permute-start.60) | collective-permute-done | bytes 589856 | tf_op jit(solution)/shard_map/ppermute | solution.py:28
  191.4 3.1 %collective-permute-done.59 = bf16[4,192,384]{2,1,0:T(8,128)(2,1)S(1)} collective-permute-done((bf16[4,192,384]{2,1,0:T(8,128)(2,1)S(1)}, bf16[4,192,384]{2,1,0:T(8,128)(2,1)S(1)}, u32[]{:S(2)}, u32[]{:S(2)}) %collective-permute-start.59) | collective-permute-done | bytes 589856 | tf_op jit(solution)/shard_map/ppermute | solution.py:28
  196.6 2.4 weight_grad.6
  200.1 1.7 collective-permute-start.62
  201.8 2.5 inter_backward.1.dkv_ref
  208.5 2.2 collective-permute-start.67
  213.3 2.7 %weight_grad.7 = (bf16[2,8,24,768]{3,2,1,0:T(8,128)(2,1)S(1)}, bf16[1,8,48,768]{3,2,1,0:T(8,128)(2,1)S(1)}) custom-call(s32[3]{0:T(128)S(1)} %pad_add_fusion.ids_ref, bf16[512,768]{1,0:T(8,128)(2,1)S(1)} %copy-done.8, bf16[512,768]{1,0:T(8,128)(2,1)S(1)} %copy-done.17, bf16[512,768]{1,0:T(8,128)(2,1)S(1)} %copy-done.9, ...), custom_call_target="tpu_custom_call" | custom-call | flops 2016000000 | tf_op jit(solution)/shard_map/weight_grad/pallas_call | solution.py:881
  218.1 3.9 %input_grad.1 = f32[512,768]{1,0:T(8,128)} custom-call(s32[3]{0:T(128)S(1)} %pad_add_fusion.ids_ref, bf16[512,768]{1,0:T(8,128)(2,1)S(1)} %copy-done.11, bf16[2,512,768]{2,1,0:T(8,128)(2,1)S(1)} %copy-done.3, f32[512,768]{1,0:T(8,128)S(1)} %copy-done.5, bf16[768,1792]{1,0:T(8,128)(2,1)S(1)} %bitcast.107, bf16[768,1536]{1,0:T(8,128)(2,1)S(1)} %bitcast.111), custom_call_target="tpu_custom_call" | custom-call | flops 2400000000 | tf_op jit(solution)/shard_map/input_grad/pallas_call | solution.py:825
  222.1 4.0 %collective-permute-done.64 = bf16[8,48,896]{2,1,0:T(8,128)(2,1)S(1)} collective-permute-done((bf16[8,48,896]{2,1,0:T(8,128)(2,1)}, bf16[8,48,896]{2,1,0:T(8,128)(2,1)S(1)}, u32[]{:S(2)}, u32[]{:S(2)}) %collective-permute-start.64) | collective-permute-done | bytes 688160 | tf_op jit(solution)/shard_map/ppermute | solution.py:28
  227.3 2.2 collective-permute-start.73
  233.5 3.2 %collective-permute-done.65 = bf16[4,48,896]{2,1,0:T(8,128)(2,1)S(1)} collective-permute-done((bf16[4,48,896]{2,1,0:T(8,128)(2,1)S(1)}, bf16[4,48,896]{2,1,0:T(8,128)(2,1)S(1)}, u32[]{:S(2)}, u32[]{:S(2)}) %collective-permute-start.65) | collective-permute-done | bytes 344096 | tf_op jit(solution)/shard_map/ppermute | solution.py:28
  236.8 1.8 collective-permute-start.70
  240.5 1.8 collective-permute-start.77
  243.1 2.5 collective-permute-start.75
  249.0 1.8 collective-permute-done.75
  253.1 2.5 collective-permute-done.80
  (331 shorter events, 104.0 us)
Async XLA Ops:
  1.5 7.9 %collective-permute-start = (bf16[1,24,1536]{2,1,0:T(8,128)(2,1)S(1)}, bf16[1,24,1536]{2,1,0:T(8,128)(2,1)S(1)}, u32[]{:S(2)}, u32[]{:S(2)}) collective-permute-start(bf16[1,24,1536]{2,1,0:T(8,128)(2,1)S(1)} %slice_bitcast_fusion.15), channel_id=1, source_target_pairs={{0,4},{1,5},{2,6},{3,7},{4,0},{5,1},{6,2},{7,3},{8,12},{9,13},{10,... | collective-permute-start | bytes 221192 | tf_op jit(solution)/shard_map/ppermute | solution.py:28
  5.6 31.2 %collective-permute-start.10 = (bf16[512,768]{1,0:T(8,128)(2,1)}, bf16[512,768]{1,0:T(8,128)(2,1)S(1)}, u32[]{:S(2)}, u32[]{:S(2)}) collective-permute-start(bf16[512,768]{1,0:T(8,128)(2,1)} %refs_0_.1), channel_id=1, source_target_pairs={{0,8},{8,0},{16,24},{24,16},{1,9},{9,1},{17,25},{25,17},{2,10},{10... | collective-permute-start | bytes 2359304 | tf_op jit(solution)/shard_map/ppermute | solution.py:28
  22.0 8.8 %collective-permute-start.6 = (bf16[8,24,768]{2,1,0:T(8,128)(2,1)S(1)}, bf16[8,24,768]{2,1,0:T(8,128)(2,1)S(1)}, u32[]{:S(2)}, u32[]{:S(2)}) collective-permute-start(bf16[8,24,768]{2,1,0:T(8,128)(2,1)S(1)} %pad_maximum_fusion.21), channel_id=1, source_target_pairs={{0,1},{1,0},{2,3},{3,2},{4,5},{5,4},{6,7},{7,6},{8,9},{9,8},{10,11... | collective-permute-start | bytes 884744 | tf_op jit(solution)/shard_map/ppermute | solution.py:28
  23.5 7.2 %collective-permute-start.5 = (bf16[8,24,768]{2,1,0:T(8,128)(2,1)S(1)}, bf16[8,24,768]{2,1,0:T(8,128)(2,1)S(1)}, u32[]{:S(2)}, u32[]{:S(2)}) collective-permute-start(bf16[8,24,768]{2,1,0:T(8,128)(2,1)S(1)} %pad_maximum_fusion.20), channel_id=1, source_target_pairs={{0,16},{8,24},{16,0},{24,8},{1,17},{9,25},{17,1},{25,9},{2,18},{10... | collective-permute-start | bytes 884744 | tf_op jit(solution)/shard_map/ppermute | solution.py:28
  27.4 7.9 %collective-permute-start.11 = (bf16[1,24,3072]{2,1,0:T(8,128)(2,1)}, bf16[1,24,3072]{2,1,0:T(8,128)(2,1)S(1)}, u32[]{:S(2)}, u32[]{:S(2)}) collective-permute-start(bf16[1,24,3072]{2,1,0:T(8,128)(2,1)} %bitcast.15), channel_id=1, source_target_pairs={{0,4},{1,5},{2,6},{3,7},{4,0},{5,1},{6,2},{7,3},{8,12},{9,13},{10,... | collective-permute-start | bytes 442376 | tf_op jit(solution)/shard_map/ppermute | solution.py:28
  31.5 10.4 %collective-permute-start.9 = (bf16[4,24,896]{2,1,0:T(8,128)(2,1)S(1)}, bf16[4,24,896]{2,1,0:T(8,128)(2,1)S(1)}, u32[]{:S(2)}, u32[]{:S(2)}) collective-permute-start(bf16[4,24,896]{2,1,0:T(8,128)(2,1)S(1)} %get-tuple-element.487), channel_id=1, source_target_pairs={{0,16},{8,24},{16,0},{24,8},{1,17},{9,25},{17,1},{25,9},{2,18},{10... | collective-permute-start | bytes 516104 | tf_op jit(solution)/shard_map/ppermute | solution.py:28
  42.1 13.2 %collective-permute-start.14 = (bf16[8,24,896]{2,1,0:T(8,128)(2,1)S(1)}, bf16[8,24,896]{2,1,0:T(8,128)(2,1)S(1)}, u32[]{:S(2)}, u32[]{:S(2)}) collective-permute-start(bf16[8,24,896]{2,1,0:T(8,128)(2,1)S(1)} %get-tuple-element.256), channel_id=1, source_target_pairs={{0,16},{8,24},{16,0},{24,8},{1,17},{9,25},{17,1},{25,9},{2,18},{10... | collective-permute-start | bytes 1032200 | tf_op jit(solution)/shard_map/ppermute | solution.py:28
  43.0 12.3 %collective-permute-start.15 = (bf16[8,24,896]{2,1,0:T(8,128)(2,1)S(1)}, bf16[8,24,896]{2,1,0:T(8,128)(2,1)S(1)}, u32[]{:S(2)}, u32[]{:S(2)}) collective-permute-start(bf16[8,24,896]{2,1,0:T(8,128)(2,1)S(1)} %get-tuple-element.257), channel_id=1, source_target_pairs={{0,1},{1,0},{2,3},{3,2},{4,5},{5,4},{6,7},{7,6},{8,9},{9,8},{10,11... | collective-permute-start | bytes 1032200 | tf_op jit(solution)/shard_map/ppermute | solution.py:28
  44.5 8.9 %collective-permute-start.16 = (bf16[2,2,104,128]{3,2,1,0:T(8,128)(2,1)S(1)}, bf16[2,2,104,128]{3,2,1,0:T(8,128)(2,1)S(1)}, u32[]{:S(2)}, u32[]{:S(2)}) collective-permute-start(bf16[2,2,104,128]{3,2,1,0:T(8,128)(2,1)S(1)} %get-tuple-element.258), channel_id=1, source_target_pairs={{0,2},{1,3},{2,0},{3,1},{4,6},{5,7},{6,4},{7,5},{8,10},{9,11},{10,... | collective-permute-start | bytes 319496 | tf_op jit(solution)/shard_map/ppermute | solution.py:28
  44.5 9.5 %collective-permute-start.17 = (bf16[2,2,104,128]{3,2,1,0:T(8,128)(2,1)S(1)}, bf16[2,2,104,128]{3,2,1,0:T(8,128)(2,1)S(1)}, u32[]{:S(2)}, u32[]{:S(2)}) collective-permute-start(bf16[2,2,104,128]{3,2,1,0:T(8,128)(2,1)S(1)} %get-tuple-element.259), channel_id=1, source_target_pairs={{0,4},{1,5},{2,6},{3,7},{4,0},{5,1},{6,2},{7,3},{8,12},{9,13},{10,... | collective-permute-start | bytes 319496 | tf_op jit(solution)/shard_map/ppermute | solution.py:28
  47.5 7.7 %collective-permute-start.18 = (bf16[2,2,104,128]{3,2,1,0:T(8,128)(2,1)S(1)}, bf16[2,2,104,128]{3,2,1,0:T(8,128)(2,1)S(1)}, u32[]{:S(2)}, u32[]{:S(2)}) collective-permute-start(bf16[2,2,104,128]{3,2,1,0:T(8,128)(2,1)S(1)} %get-tuple-element.260), channel_id=1, source_target_pairs={{0,6},{1,7},{2,4},{3,5},{4,2},{5,3},{6,0},{7,1},{8,14},{9,15},{10,... | collective-permute-start | bytes 319496 | tf_op jit(solution)/shard_map/ppermute | solution.py:28
  55.3 12.8 %collective-permute-start.25 = (bf16[4,2,104,128]{3,2,1,0:T(8,128)(2,1)S(1)}, bf16[4,2,104,128]{3,2,1,0:T(8,128)(2,1)S(1)}, u32[]{:S(2)}, u32[]{:S(2)}) collective-permute-start(bf16[4,2,104,128]{3,2,1,0:T(8,128)(2,1)S(1)} %pad_maximum_fusion.27), channel_id=1, source_target_pairs={{0,1},{1,0},{2,3},{3,2},{4,5},{5,4},{6,7},{7,6},{8,9},{9,8},{10,11... | collective-permute-start | bytes 638984 | tf_op jit(solution)/shard_map/ppermute | solution.py:28
  61.1 7.3 %collective-permute-start.22 = (bf16[4,24,1536]{2,1,0:T(8,128)(2,1)S(1)}, bf16[4,24,1536]{2,1,0:T(8,128)(2,1)S(1)}, u32[]{:S(2)}, u32[]{:S(2)}) collective-permute-start(bf16[4,24,1536]{2,1,0:T(8,128)(2,1)S(1)} %get-tuple-element.274), channel_id=1, source_target_pairs={{0,1},{1,0},{2,3},{3,2},{4,5},{5,4},{6,7},{7,6},{8,9},{9,8},{10,11... | collective-permute-start | bytes 884744 | tf_op jit(solution)/shard_map/ppermute | solution.py:28
  63.9 7.1 %collective-permute-start.24 = (bf16[1,96,768]{2,1,0:T(8,128)(2,1)S(1)}, bf16[1,96,768]{2,1,0:T(8,128)(2,1)S(1)}, u32[]{:S(2)}, u32[]{:S(2)}) collective-permute-start(bf16[1,96,768]{2,1,0:T(8,128)(2,1)S(1)} %bitcast.118), channel_id=1, source_target_pairs={{0,4},{1,5},{2,6},{3,7},{4,0},{5,1},{6,2},{7,3},{8,12},{9,13},{10,... | collective-permute-start | bytes 442376 | tf_op jit(solution)/shard_map/ppermute | solution.py:28
  71.2 11.9 %collective-permute-start.31 = (bf16[8,24,1536]{2,1,0:T(8,128)(2,1)S(1)}, bf16[8,24,1536]{2,1,0:T(8,128)(2,1)S(1)}, u32[]{:S(2)}, u32[]{:S(2)}) collective-permute-start(bf16[8,24,1536]{2,1,0:T(8,128)(2,1)S(1)} %pad_maximum_fusion.10), channel_id=1, source_target_pairs={{0,16},{8,24},{16,0},{24,8},{1,17},{9,25},{17,1},{25,9},{2,18},{10... | collective-permute-start | bytes 1769480 | tf_op jit(solution)/shard_map/ppermute | solution.py:28
  72.5 11.1 %collective-permute-start.32 = (bf16[8,24,1536]{2,1,0:T(8,128)(2,1)S(1)}, bf16[8,24,1536]{2,1,0:T(8,128)(2,1)S(1)}, u32[]{:S(2)}, u32[]{:S(2)}) collective-permute-start(bf16[8,24,1536]{2,1,0:T(8,128)(2,1)S(1)} %pad_maximum_fusion.11), channel_id=1, source_target_pairs={{0,1},{1,0},{2,3},{3,2},{4,5},{5,4},{6,7},{7,6},{8,9},{9,8},{10,11... | collective-permute-start | bytes 1769480 | tf_op jit(solution)/shard_map/ppermute | solution.py:28
  84.5 9.0 %collective-permute-start.29 = (bf16[2,96,768]{2,1,0:T(8,128)(2,1)S(1)}, bf16[2,96,768]{2,1,0:T(8,128)(2,1)S(1)}, u32[]{:S(2)}, u32[]{:S(2)}) collective-permute-start(bf16[2,96,768]{2,1,0:T(8,128)(2,1)S(1)} %pad_maximum_fusion.23), channel_id=1, source_target_pairs={{0,2},{1,3},{2,0},{3,1},{4,6},{5,7},{6,4},{7,5},{8,10},{9,11},{10,... | collective-permute-start | bytes 884744 | tf_op jit(solution)/shard_map/ppermute | solution.py:28
  84.7 7.1 %collective-permute-start.30 = (bf16[4,2,104,128]{3,2,1,0:T(8,128)(2,1)S(1)}, bf16[4,2,104,128]{3,2,1,0:T(8,128)(2,1)S(1)}, u32[]{:S(2)}, u32[]{:S(2)}) collective-permute-start(bf16[4,2,104,128]{3,2,1,0:T(8,128)(2,1)S(1)} %pad_maximum_fusion.28), channel_id=1, source_target_pairs={{0,1},{1,0},{2,3},{3,2},{4,5},{5,4},{6,7},{7,6},{8,9},{9,8},{10,11... | collective-permute-start | bytes 638984 | tf_op jit(solution)/shard_map/ppermute | solution.py:28
  93.6 8.2 %collective-permute-start.36 = (bf16[4,96,384]{2,1,0:T(8,128)(2,1)S(1)}, bf16[4,96,384]{2,1,0:T(8,128)(2,1)S(1)}, u32[]{:S(2)}, u32[]{:S(2)}) collective-permute-start(bf16[4,96,384]{2,1,0:T(8,128)(2,1)S(1)} %get-tuple-element.303), channel_id=1, source_target_pairs={{0,1},{1,0},{2,3},{3,2},{4,5},{5,4},{6,7},{7,6},{8,9},{9,8},{10,11... | collective-permute-start | bytes 884744 | tf_op jit(solution)/shard_map/ppermute | solution.py:28
  94.8 7.9 %collective-permute-start.37 = (bf16[4,96,384]{2,1,0:T(8,128)(2,1)S(1)}, bf16[4,96,384]{2,1,0:T(8,128)(2,1)S(1)}, u32[]{:S(2)}, u32[]{:S(2)}) collective-permute-start(bf16[4,96,384]{2,1,0:T(8,128)(2,1)S(1)} %get-tuple-element.304), channel_id=1, source_target_pairs={{0,16},{8,24},{16,0},{24,8},{1,17},{9,25},{17,1},{25,9},{2,18},{10... | collective-permute-start | bytes 884744 | tf_op jit(solution)/shard_map/ppermute | solution.py:28
  102.8 13.3 %collective-permute-start.38 = (bf16[8,96,384]{2,1,0:T(8,128)(2,1)S(1)}, bf16[8,96,384]{2,1,0:T(8,128)(2,1)S(1)}, u32[]{:S(2)}, u32[]{:S(2)}) collective-permute-start(bf16[8,96,384]{2,1,0:T(8,128)(2,1)S(1)} %pad_maximum_fusion.13), channel_id=1, source_target_pairs={{0,16},{8,24},{16,0},{24,8},{1,17},{9,25},{17,1},{25,9},{2,18},{10... | collective-permute-start | bytes 1769480 | tf_op jit(solution)/shard_map/ppermute | solution.py:28
  103.8 13.0 %collective-permute-start.39 = (bf16[8,96,384]{2,1,0:T(8,128)(2,1)S(1)}, bf16[8,96,384]{2,1,0:T(8,128)(2,1)S(1)}, u32[]{:S(2)}, u32[]{:S(2)}) collective-permute-start(bf16[8,96,384]{2,1,0:T(8,128)(2,1)S(1)} %pad_maximum_fusion.14), channel_id=1, source_target_pairs={{0,1},{1,0},{2,3},{3,2},{4,5},{5,4},{6,7},{7,6},{8,9},{9,8},{10,11... | collective-permute-start | bytes 1769480 | tf_op jit(solution)/shard_map/ppermute | solution.py:28
  139.4 18.4 %collective-permute-start.50 = (bf16[4,192,384]{2,1,0:T(8,128)(2,1)S(1)}, bf16[4,192,384]{2,1,0:T(8,128)(2,1)S(1)}, u32[]{:S(2)}, u32[]{:S(2)}) collective-permute-start(bf16[4,192,384]{2,1,0:T(8,128)(2,1)S(1)} %get-tuple-element.341), channel_id=1, source_target_pairs={{0,16},{8,24},{16,0},{24,8},{1,17},{9,25},{17,1},{25,9},{2,18},{10... | collective-permute-start | bytes 1769480 | tf_op jit(solution)/shard_map/ppermute | solution.py:28
  143.9 22.2 %collective-permute-start.46 = (bf16[2,3,48,1536]{3,2,1,0:T(8,128)(2,1)S(1)}, bf16[2,3,48,1536]{3,2,1,0:T(8,128)(2,1)S(1)}, u32[]{:S(2)}, u32[]{:S(2)}) collective-permute-start(bf16[2,3,48,1536]{3,2,1,0:T(8,128)(2,1)S(1)} %slice.454), channel_id=1, source_target_pairs={{0,1},{1,0},{2,3},{3,2},{4,5},{5,4},{6,7},{7,6},{8,9},{9,8},{10,11... | collective-permute-start | bytes 2654216 | tf_op jit(solution)/shard_map/ppermute | solution.py:28
  154.0 10.8 %collective-permute-start.48 = (bf16[2,2,104,128]{3,2,1,0:T(8,128)(2,1)S(1)}, bf16[2,2,104,128]{3,2,1,0:T(8,128)(2,1)S(1)}, u32[]{:S(2)}, u32[]{:S(2)}) collective-permute-start(bf16[2,2,104,128]{3,2,1,0:T(8,128)(2,1)S(1)} %get-tuple-element.351), channel_id=1, source_target_pairs={{0,4},{1,5},{2,6},{3,7},{4,0},{5,1},{6,2},{7,3},{8,12},{9,13},{10,... | collective-permute-start | bytes 319496 | tf_op jit(solution)/shard_map/ppermute | solution.py:28
  156.0 8.8 %collective-permute-start.49 = (bf16[2,2,104,128]{3,2,1,0:T(8,128)(2,1)S(1)}, bf16[2,2,104,128]{3,2,1,0:T(8,128)(2,1)S(1)}, u32[]{:S(2)}, u32[]{:S(2)}) collective-permute-start(bf16[2,2,104,128]{3,2,1,0:T(8,128)(2,1)S(1)} %get-tuple-element.352), channel_id=1, source_target_pairs={{0,6},{1,7},{2,4},{3,5},{4,2},{5,3},{6,0},{7,1},{8,14},{9,15},{10,... | collective-permute-start | bytes 319496 | tf_op jit(solution)/shard_map/ppermute | solution.py:28
  158.0 14.0 %collective-permute-start.54 = (bf16[4,192,384]{2,1,0:T(8,128)(2,1)S(1)}, bf16[4,192,384]{2,1,0:T(8,128)(2,1)S(1)}, u32[]{:S(2)}, u32[]{:S(2)}) collective-permute-start(bf16[4,192,384]{2,1,0:T(8,128)(2,1)S(1)} %get-tuple-element.356), channel_id=1, source_target_pairs={{0,16},{8,24},{16,0},{24,8},{1,17},{9,25},{17,1},{25,9},{2,18},{10... | collective-permute-start | bytes 1769480 | tf_op jit(solution)/shard_map/ppermute | solution.py:28
  164.9 7.3 %collective-permute-start.52 = (bf16[4,2,104,128]{3,2,1,0:T(8,128)(2,1)S(1)}, bf16[4,2,104,128]{3,2,1,0:T(8,128)(2,1)S(1)}, u32[]{:S(2)}, u32[]{:S(2)}) collective-permute-start(bf16[4,2,104,128]{3,2,1,0:T(8,128)(2,1)S(1)} %pad_maximum_fusion.29), channel_id=1, source_target_pairs={{0,1},{1,0},{2,3},{3,2},{4,5},{5,4},{6,7},{7,6},{8,9},{9,8},{10,11... | collective-permute-start | bytes 638984 | tf_op jit(solution)/shard_map/ppermute | solution.py:28
  166.5 10.9 %collective-permute-start.51 = (bf16[2,1,48,1536]{3,2,1,0:T(8,128)(2,1)S(1)}, bf16[2,1,48,1536]{3,2,1,0:T(8,128)(2,1)S(1)}, u32[]{:S(2)}, u32[]{:S(2)}) collective-permute-start(bf16[2,1,48,1536]{3,2,1,0:T(8,128)(2,1)S(1)} %slice.452), channel_id=1, source_target_pairs={{0,1},{1,0},{2,3},{3,2},{4,5},{5,4},{6,7},{7,6},{8,9},{9,8},{10,11... | collective-permute-start | bytes 884744 | tf_op jit(solution)/shard_map/ppermute | solution.py:28
  172.5 15.1 %collective-permute-start.55 = (bf16[2,2,104,128]{3,2,1,0:T(8,128)(2,1)S(1)}, bf16[2,2,104,128]{3,2,1,0:T(8,128)(2,1)S(1)}, u32[]{:S(2)}, u32[]{:S(2)}) collective-permute-start(bf16[2,2,104,128]{3,2,1,0:T(8,128)(2,1)S(1)} %get-tuple-element.371), channel_id=1, source_target_pairs={{0,2},{1,3},{2,0},{3,1},{4,6},{5,7},{6,4},{7,5},{8,10},{9,11},{10,... | collective-permute-start | bytes 319496 | tf_op jit(solution)/shard_map/ppermute | solution.py:28
  174.6 13.0 %collective-permute-start.56 = (bf16[2,2,104,128]{3,2,1,0:T(8,128)(2,1)S(1)}, bf16[2,2,104,128]{3,2,1,0:T(8,128)(2,1)S(1)}, u32[]{:S(2)}, u32[]{:S(2)}) collective-permute-start(bf16[2,2,104,128]{3,2,1,0:T(8,128)(2,1)S(1)} %get-tuple-element.372), channel_id=1, source_target_pairs={{0,4},{1,5},{2,6},{3,7},{4,0},{5,1},{6,2},{7,3},{8,12},{9,13},{10,... | collective-permute-start | bytes 319496 | tf_op jit(solution)/shard_map/ppermute | solution.py:28
  176.0 11.6 %collective-permute-start.57 = (bf16[2,2,104,128]{3,2,1,0:T(8,128)(2,1)S(1)}, bf16[2,2,104,128]{3,2,1,0:T(8,128)(2,1)S(1)}, u32[]{:S(2)}, u32[]{:S(2)}) collective-permute-start(bf16[2,2,104,128]{3,2,1,0:T(8,128)(2,1)S(1)} %get-tuple-element.373), channel_id=1, source_target_pairs={{0,6},{1,7},{2,4},{3,5},{4,2},{5,3},{6,0},{7,1},{8,14},{9,15},{10,... | collective-permute-start | bytes 319496 | tf_op jit(solution)/shard_map/ppermute | solution.py:28
  177.6 13.8 %collective-permute-start.60 = (bf16[4,48,1536]{2,1,0:T(8,128)(2,1)S(1)}, bf16[4,48,1536]{2,1,0:T(8,128)(2,1)S(1)}, u32[]{:S(2)}, u32[]{:S(2)}) collective-permute-start(bf16[4,48,1536]{2,1,0:T(8,128)(2,1)S(1)} %pad_maximum_fusion.15), channel_id=1, source_target_pairs={{0,16},{8,24},{16,0},{24,8},{1,17},{9,25},{17,1},{25,9},{2,18},{10... | collective-permute-start | bytes 1769480 | tf_op jit(solution)/shard_map/ppermute | solution.py:28
  178.4 16.1 %collective-permute-start.59 = (bf16[4,192,384]{2,1,0:T(8,128)(2,1)S(1)}, bf16[4,192,384]{2,1,0:T(8,128)(2,1)S(1)}, u32[]{:S(2)}, u32[]{:S(2)}) collective-permute-start(bf16[4,192,384]{2,1,0:T(8,128)(2,1)S(1)} %fusion.1), channel_id=1, source_target_pairs={{0,1},{1,0},{2,3},{3,2},{4,5},{5,4},{6,7},{7,6},{8,9},{9,8},{10,11... | collective-permute-start | bytes 1769480 | tf_op jit(solution)/shard_map/ppermute | solution.py:28
  187.7 14.0 %collective-permute-start.58 = (bf16[4,2,104,128]{3,2,1,0:T(8,128)(2,1)S(1)}, bf16[4,2,104,128]{3,2,1,0:T(8,128)(2,1)S(1)}, u32[]{:S(2)}, u32[]{:S(2)}) collective-permute-start(bf16[4,2,104,128]{3,2,1,0:T(8,128)(2,1)S(1)} %pad_maximum_fusion.30), channel_id=1, source_target_pairs={{0,1},{1,0},{2,3},{3,2},{4,5},{5,4},{6,7},{7,6},{8,9},{9,8},{10,11... | collective-permute-start | bytes 638984 | tf_op jit(solution)/shard_map/ppermute | solution.py:28
  188.5 7.1 %collective-permute-start.61 = (bf16[512,384]{1,0:T(8,128)(2,1)S(1)}, bf16[512,384]{1,0:T(8,128)(2,1)S(1)}, u32[]{:S(2)}, u32[]{:S(2)}) collective-permute-start(bf16[512,384]{1,0:T(8,128)(2,1)S(1)} %get-tuple-element.388), channel_id=1, source_target_pairs={{0,8},{8,0},{16,24},{24,16},{1,9},{9,1},{17,25},{25,17},{2,10},{10... | collective-permute-start | bytes 1179656 | tf_op jit(solution)/shard_map/ppermute | solution.py:28
  207.6 18.4 %collective-permute-start.64 = (bf16[8,48,896]{2,1,0:T(8,128)(2,1)}, bf16[8,48,896]{2,1,0:T(8,128)(2,1)S(1)}, u32[]{:S(2)}, u32[]{:S(2)}) collective-permute-start(bf16[8,48,896]{2,1,0:T(8,128)(2,1)} %slice_bitcast_fusion.2), channel_id=1, source_target_pairs={{0,16},{8,24},{16,0},{24,8},{1,17},{9,25},{17,1},{25,9},{2,18},{10... | collective-permute-start | bytes 2064392 | tf_op jit(solution)/shard_map/ppermute | solution.py:28
  208.5 21.4 %collective-permute-start.67 = (bf16[1,48,1536]{2,1,0:T(8,128)(2,1)}, bf16[1,48,1536]{2,1,0:T(8,128)(2,1)S(1)}, u32[]{:S(2)}, u32[]{:S(2)}) collective-permute-start(bf16[1,48,1536]{2,1,0:T(8,128)(2,1)} %add_convert_fusion.12), channel_id=1, source_target_pairs={{0,4},{1,5},{2,6},{3,7},{4,0},{5,1},{6,2},{7,3},{8,12},{9,13},{10,... | collective-permute-start | bytes 442376 | tf_op jit(solution)/shard_map/ppermute | solution.py:28
  210.7 16.6 %collective-permute-start.69 = (bf16[2,192,384]{2,1,0:T(8,128)(2,1)}, bf16[2,192,384]{2,1,0:T(8,128)(2,1)S(1)}, u32[]{:S(2)}, u32[]{:S(2)}) collective-permute-start(bf16[2,192,384]{2,1,0:T(8,128)(2,1)} %get-tuple-element.400), channel_id=1, source_target_pairs={{0,2},{1,3},{2,0},{3,1},{4,6},{5,7},{6,4},{7,5},{8,10},{9,11},{10,... | collective-permute-start | bytes 884744 | tf_op jit(solution)/shard_map/ppermute | solution.py:28
  216.0 16.3 %collective-permute-start.66 = (bf16[8,24,768]{2,1,0:T(8,128)(2,1)S(1)}, bf16[8,24,768]{2,1,0:T(8,128)(2,1)S(1)}, u32[]{:S(2)}, u32[]{:S(2)}) collective-permute-start(bf16[8,24,768]{2,1,0:T(8,128)(2,1)S(1)} %slice_bitcast_fusion.11), channel_id=1, source_target_pairs={{0,16},{8,24},{16,0},{24,8},{1,17},{9,25},{17,1},{25,9},{2,18},{10... | collective-permute-start | bytes 884744 | tf_op jit(solution)/shard_map/ppermute | solution.py:28
  217.4 12.1 %collective-permute-start.68 = (bf16[4,48,768]{2,1,0:T(8,128)(2,1)S(1)}, bf16[4,48,768]{2,1,0:T(8,128)(2,1)S(1)}, u32[]{:S(2)}, u32[]{:S(2)}) collective-permute-start(bf16[4,48,768]{2,1,0:T(8,128)(2,1)S(1)} %slice_bitcast_fusion.10), channel_id=1, source_target_pairs={{0,1},{1,0},{2,3},{3,2},{4,5},{5,4},{6,7},{7,6},{8,9},{9,8},{10,11... | collective-permute-start | bytes 884744 | tf_op jit(solution)/shard_map/ppermute | solution.py:28
  226.2 10.5 %collective-permute-start.65 = (bf16[4,48,896]{2,1,0:T(8,128)(2,1)S(1)}, bf16[4,48,896]{2,1,0:T(8,128)(2,1)S(1)}, u32[]{:S(2)}, u32[]{:S(2)}) collective-permute-start(bf16[4,48,896]{2,1,0:T(8,128)(2,1)S(1)} %get-tuple-element.409), channel_id=1, source_target_pairs={{0,1},{1,0},{2,3},{3,2},{4,5},{5,4},{6,7},{7,6},{8,9},{9,8},{10,11... | collective-permute-start | bytes 1032200 | tf_op jit(solution)/shard_map/ppermute | solution.py:28
  227.3 12.3 %collective-permute-start.73 = (bf16[1,192,384]{2,1,0:T(8,128)(2,1)S(1)}, bf16[1,192,384]{2,1,0:T(8,128)(2,1)S(1)}, u32[]{:S(2)}, u32[]{:S(2)}) collective-permute-start(bf16[1,192,384]{2,1,0:T(8,128)(2,1)S(1)} %add_convert_fusion.10), channel_id=1, source_target_pairs={{0,4},{1,5},{2,6},{3,7},{4,0},{5,1},{6,2},{7,3},{8,12},{9,13},{10,... | collective-permute-start | bytes 442376 | tf_op jit(solution)/shard_map/ppermute | solution.py:28
  229.6 9.0 %collective-permute-start.74 = (bf16[2,48,768]{2,1,0:T(8,128)(2,1)S(1)}, bf16[2,48,768]{2,1,0:T(8,128)(2,1)S(1)}, u32[]{:S(2)}, u32[]{:S(2)}) collective-permute-start(bf16[2,48,768]{2,1,0:T(8,128)(2,1)S(1)} %get-tuple-element.413), channel_id=1, source_target_pairs={{0,2},{1,3},{2,0},{3,1},{4,6},{5,7},{6,4},{7,5},{8,10},{9,11},{10,... | collective-permute-start | bytes 442376 | tf_op jit(solution)/shard_map/ppermute | solution.py:28
  230.0 12.4 %collective-permute-start.71 = (bf16[48,1536]{1,0:T(8,128)(2,1)S(1)}, bf16[48,1536]{1,0:T(8,128)(2,1)S(1)}, u32[]{:S(2)}, u32[]{:S(2)}) collective-permute-start(bf16[48,1536]{1,0:T(8,128)(2,1)S(1)} %fusion.25), channel_id=1, source_target_pairs={{0,16},{8,24},{16,0},{24,8},{1,17},{9,25},{17,1},{25,9},{2,18},{10... | collective-permute-start | bytes 442376 | tf_op jit(solution)/shard_map/ppermute | solution.py:28
  232.4 8.1 %collective-permute-start.72 = (bf16[4,24,768]{2,1,0:T(8,128)(2,1)S(1)}, bf16[4,24,768]{2,1,0:T(8,128)(2,1)S(1)}, u32[]{:S(2)}, u32[]{:S(2)}) collective-permute-start(bf16[4,24,768]{2,1,0:T(8,128)(2,1)S(1)} %get-tuple-element.417), channel_id=1, source_target_pairs={{0,1},{1,0},{2,3},{3,2},{4,5},{5,4},{6,7},{7,6},{8,9},{9,8},{10,11... | collective-permute-start | bytes 442376 | tf_op jit(solution)/shard_map/ppermute | solution.py:28
  239.7 9.2 %collective-permute-start.76 = (bf16[192,384]{1,0:T(8,128)(2,1)S(1)}, bf16[192,384]{1,0:T(8,128)(2,1)S(1)}, u32[]{:S(2)}, u32[]{:S(2)}) collective-permute-start(bf16[192,384]{1,0:T(8,128)(2,1)S(1)} %fusion.26), channel_id=1, source_target_pairs={{0,16},{8,24},{16,0},{24,8},{1,17},{9,25},{17,1},{25,9},{2,18},{10... | collective-permute-start | bytes 442376 | tf_op jit(solution)/shard_map/ppermute | solution.py:28
  243.1 7.7 %collective-permute-start.75 = (bf16[1,48,896]{2,1,0:T(8,128)(2,1)S(1)}, bf16[1,48,896]{2,1,0:T(8,128)(2,1)S(1)}, u32[]{:S(2)}, u32[]{:S(2)}) collective-permute-start(bf16[1,48,896]{2,1,0:T(8,128)(2,1)S(1)} %add_convert_fusion.14), channel_id=1, source_target_pairs={{0,4},{1,5},{2,6},{3,7},{4,0},{5,1},{6,2},{7,3},{8,12},{9,13},{10,... | collective-permute-start | bytes 258056 | tf_op jit(solution)/shard_map/ppermute | solution.py:28
  (66 other events, 329.8 us)
